TPU v7x, 32 devices: a whole 2x2x4 slice. The times are simulated.
32 devices in a mesh: seq: 4 (over y, x), row: 8 (over z, core).
Axes of the slice: x: 2, y: 2, z: 4, core: 2. Of those that a mesh axis runs over, the one named last changes fastest.
Arguments:
- tokens: bfloat16 [16, 1024, 512], P('row', 'seq'), may hold values from -7.2 to 7.2
- cotangent: bfloat16 [16, 1024, 512], P('row', 'seq'), may hold values from -6 to 6
- contig_lengths: int32 [16, 8], P('row'), may hold values from 1 to 256, 1024 in all within a row
- conv_weight: float32 [9, 512, 512], P(None, 'row'), may hold values from -0.09375 to 0.09375
- inner_weight: float32 [512, 2048], P('row'), may hold values from -0.25 to 0.25
- outer_weight: float32 [2048, 512], P('row'), may hold values from -0.125 to 0.125
- vectors: float32 [10, 512], replicated, may hold values from -0.75 to 1.4, as said below
- conv_moments: float32 [2, 9, 512, 512], P(None, None, 'row'), may hold values from -0.00015623207 to 0.00015623207, as said below
- inner_moments: float32 [2, 512, 2048], P(None, 'row'), may hold values from -0.00015623207 to 0.00015623207, as said below
- outer_moments: float32 [2, 2048, 512], P(None, 'row'), may hold values from -0.00015623207 to 0.00015623207, as said below
- vector_moments: float32 [2, 10, 512], replicated, may hold values from -0.00015623207 to 0.00015623207, as said below
Outputs:
- layer_out: bfloat16 [16, 1024, 512], P('row', 'seq')
- input_grad: float32 [16, 1024, 512], P('row', 'seq')
- global_norm: float32 [], replicated
- new_conv: float32 [9, 512, 512], P(None, 'row')
- conv_first: float32 [9, 512, 512], P(None, 'row')
- new_inner: float32 [512, 2048], P('row')
- inner_first: float32 [512, 2048], P('row')
- new_outer: float32 [2048, 512], P('row')
- outer_first: float32 [2048, 512], P('row')
- new_vectors: float32 [10, 512], replicated
- vector_first: float32 [10, 512], replicated
- second_moments: float32 [512, 8714], P('row')
Inputs may be any that keep to these rules, and one draw needn't show every extreme that they name: `contig_lengths`: each row's contig lengths sum to 1024; contigs lie one after another from base 0. `vectors`: rows 1 and 4 lie in 0.6 to 1.4. `conv_moments`: second moments are positive. `inner_moments`: second moments are positive. `outer_moments`: second moments are positive. `vector_moments`: second moments are positive.
All inputs are finite; a program needn't handle non-finite values.
Results may differ from a plain program's by a relative error of at most 0.0062.
Values may be sent and summed in bfloat16 or wider, within the bound.
No kernel may reach another device: no remote copies, remote signals or barrier semaphores. Data moves between devices by JAX's collectives and lax.ppermute only.
A program may use at most 128 MiB of HBM per device.

v0:
```python
import jax
import jax.numpy as jnp
from jax import lax
from jax.sharding import PartitionSpec as P

DILATION_STEP = 8


beta_one = 0.9
beta_two = 0.999
adam_eps = 1e-08
weight_decay = 0.1
matrix_rate = 0.03
vector_rate = 0.3
clip_level = 1.0
step_count = 10
norm_eps = 1e-05


def padded(value, sides, width):
    for axis, dim in sides:
        size, length = (lax.axis_size(axis), value.shape[dim])
        up = [(i, (i + 1) % size) for i in range(size - 1)]
        down = [(j, i) for i, j in up]
        last = lax.slice_in_dim(value, length - width, length, axis=dim)
        initial = lax.slice_in_dim(value, 0, width, axis=dim)
        before = lax.ppermute(last, axis, up)
        after = lax.ppermute(initial, axis, down)
        value = jnp.concatenate([before, value, after], axis=dim)
    return value


def layer_norm(feature, gain_row, shift_row):
    average = jnp.mean(feature, axis=-1, keepdims=True)
    centered = feature - average
    variance = jnp.mean(centered * centered, axis=-1, keepdims=True)
    return centered * lax.rsqrt(variance + norm_eps) * gain_row + shift_row


def gelu_exact(preact):
    return jax.nn.gelu(preact, approximate=False)


def conv_norm(preact, gain_row, shift_row):
    return layer_norm(gelu_exact(preact), gain_row, shift_row)


def window_masks(contig_lengths, local_len, first_base, row_length, count_of_taps, half_span_width):
    starts = jnp.cumsum(contig_lengths, axis=1)[:, :-1]
    position = (
        first_base - half_span_width + jnp.arange(local_len + 2 * half_span_width, dtype=jnp.int32)
    )
    contig_of = jnp.sum((position[None, :, None] >= starts[:, None, :]).astype(jnp.int32), axis=2)
    inside = (position >= 0) & (position < row_length)
    centre = contig_of[:, half_span_width : half_span_width + local_len]
    mask_list = []
    for kernel_tap_index in range(count_of_taps):
        begin_position = kernel_tap_index * DILATION_STEP
        mask_list.append(
            (contig_of[:, begin_position : begin_position + local_len] == centre)
            & inside[None, begin_position : begin_position + local_len]
        )
    return mask_list


def adamw(weight, moments, gradient, clip_scale, step_rate, decay_rate):
    clipped = gradient * clip_scale
    first_moment = beta_one * moments[0] + (1.0 - beta_one) * clipped
    second_moment = beta_two * moments[1] + (1.0 - beta_two) * clipped * clipped
    first_hat = first_moment / (1.0 - beta_one**step_count)
    second_hat = second_moment / (1.0 - beta_two**step_count)
    updated = weight - step_rate * (
        first_hat / (jnp.sqrt(second_hat) + adam_eps) + decay_rate * weight
    )
    return (updated, first_moment, second_moment)


def per_device(
    tokens,
    cotangent,
    contig_lengths,
    conv_weight,
    inner_weight,
    outer_weight,
    vectors,
    conv_moments,
    inner_moments,
    outer_moments,
    vector_moments,
):
    conv_full, inner_full, outer_full = (
        lax.all_gather(conv_weight.astype(jnp.bfloat16), "row", axis=1, tiled=True),
        lax.all_gather(inner_weight.astype(jnp.bfloat16), "row", axis=0, tiled=True),
        lax.all_gather(outer_weight.astype(jnp.bfloat16), "row", axis=0, tiled=True),
    )
    row_count, local_len, feature_count = tokens.shape
    count_of_taps = conv_full.shape[0]
    half_span_width = DILATION_STEP * (count_of_taps // 2)
    row_length = local_len * lax.axis_size("seq")
    first_base = lax.axis_index("seq") * local_len
    mask_list = window_masks(
        contig_lengths, local_len, first_base, row_length, count_of_taps, half_span_width
    )
    extended = padded(tokens, (("seq", 1),), half_span_width)
    conv_pre = vectors[0]
    for kernel_tap_index in range(count_of_taps):
        begin_position = kernel_tap_index * DILATION_STEP
        receptive_span = extended[:, begin_position : begin_position + local_len]
        product = jnp.einsum(
            "rld,de->rle",
            receptive_span,
            conv_full[kernel_tap_index],
            preferred_element_type=jnp.float32,
        )
        conv_pre = conv_pre + jnp.where(mask_list[kernel_tap_index][:, :, None], product, 0.0)
    conv_branch, conv_back = jax.vjp(conv_norm, conv_pre, vectors[1], vectors[2])
    after_conv = tokens.astype(jnp.float32) + conv_branch
    after_low = after_conv.astype(jnp.bfloat16)
    inner_pre = jnp.einsum(
        "rld,df->rlf", after_low, inner_full, preferred_element_type=jnp.float32
    ) + vectors[6:].reshape(-1)
    hidden, hidden_back = jax.vjp(gelu_exact, inner_pre)
    hidden_low = hidden.astype(jnp.bfloat16)
    outer_pre = (
        jnp.einsum("rlf,fd->rld", hidden_low, outer_full, preferred_element_type=jnp.float32)
        + vectors[3]
    )
    ffn_branch, ffn_back = jax.vjp(layer_norm, outer_pre, vectors[4], vectors[5])
    layer_out = (after_conv + ffn_branch).astype(jnp.bfloat16)
    upstream = cotangent.astype(jnp.float32)
    outer_grad, gain_two, shift_two = ffn_back(upstream)
    outer_low = outer_grad.astype(jnp.bfloat16)
    outer_weight_grad = jnp.einsum(
        "rlf,rld->fd", hidden_low, outer_low, preferred_element_type=jnp.float32
    )
    outer_bias = jnp.sum(outer_low, axis=(0, 1), dtype=jnp.float32)
    (inner_grad,) = hidden_back(
        jnp.einsum("rld,fd->rlf", outer_low, outer_full, preferred_element_type=jnp.float32)
    )
    inner_low = inner_grad.astype(jnp.bfloat16)
    inner_weight_grad = jnp.einsum(
        "rld,rlf->df", after_low, inner_low, preferred_element_type=jnp.float32
    )
    inner_bias = jnp.sum(inner_low, axis=(0, 1), dtype=jnp.float32)
    after_grad = upstream + jnp.einsum(
        "rlf,df->rld", inner_low, inner_full, preferred_element_type=jnp.float32
    )
    conv_grad, gain_one, shift_one = conv_back(after_grad)
    conv_low = conv_grad.astype(jnp.bfloat16)
    conv_bias = jnp.sum(conv_low, axis=(0, 1), dtype=jnp.float32)
    extended_grad = jnp.zeros(
        (row_count, local_len + 2 * half_span_width, feature_count), jnp.float32
    )
    tap_grads = []
    for kernel_tap_index in range(count_of_taps):
        begin_position = kernel_tap_index * DILATION_STEP
        receptive_span = extended[:, begin_position : begin_position + local_len]
        masked = jnp.where(
            mask_list[kernel_tap_index][:, :, None], conv_low, jnp.zeros((), jnp.bfloat16)
        )
        tap_grads.append(
            jnp.einsum("rld,rle->de", receptive_span, masked, preferred_element_type=jnp.float32)
        )
        spread_back = jnp.einsum(
            "rle,de->rld", masked, conv_full[kernel_tap_index], preferred_element_type=jnp.float32
        )
        extended_grad = extended_grad.at[:, begin_position : begin_position + local_len].add(
            spread_back
        )
    conv_weight_grad = jnp.stack(tap_grads)
    rim_grads = jnp.concatenate(
        [extended_grad[:, :half_span_width], extended_grad[:, local_len + half_span_width :]],
        axis=1,
    )
    arrived = padded(rim_grads.astype(jnp.bfloat16), (("seq", 1),), half_span_width).astype(
        rim_grads.dtype
    )
    local_grad = extended_grad[:, half_span_width : half_span_width + local_len]
    local_grad = local_grad.at[:, :half_span_width].add(arrived[:, :half_span_width])
    local_grad = local_grad.at[:, local_len - half_span_width :].add(
        arrived[:, 3 * half_span_width :]
    )
    input_grad = after_grad + local_grad
    vector_grad = jnp.concatenate(
        [
            jnp.stack([conv_bias, gain_one, shift_one, outer_bias, gain_two, shift_two]),
            inner_bias.reshape(-1, feature_count),
        ],
        axis=0,
    )
    row_index = lax.axis_index("row")
    conv_rows = conv_weight.shape[1]
    inner_rows = inner_weight.shape[0]
    outer_rows = outer_weight.shape[0]
    conv_sum, inner_sum, outer_sum, vector_sum = lax.psum(
        (conv_weight_grad, inner_weight_grad, outer_weight_grad, vector_grad), ("seq", "row")
    )
    squares = (
        jnp.sum(conv_sum * conv_sum)
        + jnp.sum(inner_sum * inner_sum)
        + jnp.sum(outer_sum * outer_sum)
        + jnp.sum(vector_sum * vector_sum)
    )
    conv_part = lax.dynamic_slice_in_dim(conv_sum, row_index * conv_rows, conv_rows, 1)
    inner_part = lax.dynamic_slice_in_dim(inner_sum, row_index * inner_rows, inner_rows, 0)
    outer_part = lax.dynamic_slice_in_dim(outer_sum, row_index * outer_rows, outer_rows, 0)
    global_norm = jnp.sqrt(squares)
    clip_scale = clip_level / jnp.maximum(global_norm, clip_level)
    new_conv, conv_first, conv_second = adamw(
        conv_weight, conv_moments, conv_part, clip_scale, matrix_rate, weight_decay
    )
    new_inner, inner_first, inner_second = adamw(
        inner_weight, inner_moments, inner_part, clip_scale, matrix_rate, weight_decay
    )
    new_outer, outer_first, outer_second = adamw(
        outer_weight, outer_moments, outer_part, clip_scale, matrix_rate, weight_decay
    )
    new_vectors, vector_first, vector_second = adamw(
        vectors, vector_moments, vector_sum, clip_scale, vector_rate, 0.0
    )
    vector_rows = lax.dynamic_slice_in_dim(
        jnp.transpose(vector_second), row_index * conv_rows, conv_rows, 0
    )
    second_moments = jnp.concatenate(
        [
            jnp.transpose(conv_second, (1, 0, 2)).reshape(conv_rows, -1),
            inner_second,
            outer_second.reshape(conv_rows, -1),
            vector_rows,
        ],
        axis=1,
    )
    return (
        layer_out,
        input_grad,
        global_norm,
        new_conv,
        conv_first,
        new_inner,
        inner_first,
        new_outer,
        outer_first,
        new_vectors,
        vector_first,
        second_moments,
    )


def solution(mesh):
    in_specs = (
        P("row", "seq", None),
        P("row", "seq", None),
        P("row", None),
        P(None, "row", None),
        P("row", None),
        P("row", None),
        P(),
        P(None, None, "row", None),
        P(None, "row", None),
        P(None, "row", None),
        P(),
    )
    out_specs = (
        P("row", "seq", None),
        P("row", "seq", None),
        P(),
        P(None, "row", None),
        P(None, "row", None),
        P("row", None),
        P("row", None),
        P("row", None),
        P("row", None),
        P(),
        P(),
        P("row", None),
    )
    return jax.shard_map(
        per_device, mesh=mesh, in_specs=in_specs, out_specs=out_specs, check_vma=False
    )
```

profile of v0, /device:TPU:0, one launch (start us, length us, event | category | flops | bytes accessed | tf_op | source)
XLA Modules:
  0.0 486.7 jit_solution(6041598314879058906)
XLA Ops:
  7.3 2.2 convert_element_type.51
  9.5 1.8 convert_element_type.53
  12.3 4.8 collective-permute-start
  18.4 1.8 convert_element_type.55
  21.2 2.1 collective-permute-done.1
  23.3 41.3 %all-gather.4.cloned.1.call-done = bf16[9,512,512]{2,1,0:T(8,128)(2,1)} async-done(((bf16[9,64,512]{2,1,0:T(8,128)(2,1)}), bf16[9,512,512]{2,1,0:T(8,128)(2,1)}) %all-gather.4.cloned.1.call-update) | async-done | bytes 4718608 | tf_op jit(solution)/shard_map/all_gather | solution.py:92
  64.6 1.6 convolution_select_fusion
  71.4 3.6 fusion.129
  75.6 19.2 %all-gather.6.cloned.1.call-done = bf16[512,2048]{1,0:T(8,128)(2,1)} async-done(((bf16[64,2048]{1,0:T(8,128)(2,1)}), bf16[512,2048]{1,0:T(8,128)(2,1)}) %all-gather.6.cloned.1.call-update) | async-done | bytes 2097168 | tf_op jit(solution)/shard_map/all_gather | solution.py:93
  94.8 4.1 fusion.55
  98.9 1.9 copy-done.8
  100.8 10.8 %multiply_convert_fusion = (bf16[2,256,2048]{2,1,0:T(8,128)(2,1)}, f32[2,256,2048]{2,1,0:T(8,128)}) fusion(f32[2,256,2048]{2,1,0:T(8,128)S(1)} %get-tuple-element.225, f32[2048]{0:T(1024)S(1)} %bitcast.192, u8[256,2048]{1,0:T(8,128)(4,1)S(1)} %get-tuple-element.157, u8[256,2048]{1,0:T(8,128)(4,1)S(1)} %get-tuple-element.156), kind=kLoop, calls=%fused_computation.12 | loop fusion | flops 74448896 | bytes 11542528 | tf_op jit(solution)/shard_map/convert_element_type | solution.py:123
  111.7 13.9 %all-gather.8.cloned.1.call-done = bf16[2048,512]{1,0:T(8,128)(2,1)} async-done(((bf16[256,512]{1,0:T(8,128)(2,1)}), bf16[2048,512]{1,0:T(8,128)(2,1)}) %all-gather.8.cloned.1.call-update) | async-done | bytes 2097168 | tf_op jit(solution)/shard_map/all_gather | solution.py:94
  125.6 3.5 fusion.135
  130.8 3.4 convolution_bitcast_fusion
  135.5 3.0 convert_reduce_fusion
  138.6 3.3 convolution_bitcast_fusion.1
  141.9 1.6 fusion.123
  144.1 2.3 convert_reduce_fusion.3
  160.9 1.7 fusion.59
  162.8 1.6 fusion.28
  164.4 1.7 fusion.27
  172.7 4.5 collective-permute-start.2
  177.4 41.5 %psum.31 = f32[10,512]{1,0:T(8,128)S(1)} all-reduce(f32[10,512]{1,0:T(8,128)S(1)} %concatenate.50), channel_id=1, replica_groups=mesh['seq'=4,'row'=8] {'seq','row'}, use_global_device_ids=true, to_apply=%region_23.24 | all-reduce | flops 5120 | bytes 40960 | tf_op jit(solution)/shard_map/psum | solution.py:195
  221.8 2.4 add.319
  224.2 228.8 %all-reduce.4.cloned.1.call-done = (f32[9,512,512]{2,1,0:T(8,128)}, f32[512,2048]{1,0:T(8,128)}, f32[2048,512]{1,0:T(8,128)}) async-done(((f32[9,512,512]{2,1,0:T(8,128)}, f32[512,2048]{1,0:T(8,128)}, f32[2048,512]{1,0:T(8,128)}), (f32[9,512,512]{2,1,0:T(8,128)}, f32[512,2048]{1,0:T(8,128)}, f32[2048,512]{1,0:T(8,128)})) %all-reduce.4.cloned.1.call-update) | async-done | bytes 17825808 | tf_op jit(solution)/shard_map/psum | solution.py:195
  453.0 6.9 %multiply_reduce_fusion = f32[]{:T(128)} fusion(f32[9,512,512]{2,1,0:T(8,128)} %get-tuple-element.167), kind=kLoop, calls=%fused_computation | loop fusion | flops 4718591 | bytes 9437188 | tf_op jit(solution)/shard_map/reduce_sum | solution.py:199
  459.9 1.7 multiply_reduce_fusion.2
  462.1 1.7 multiply_reduce_fusion.1
  466.5 4.4 multiply_subtract_fusion
  470.9 2.7 multiply_subtract_fusion.2
  474.4 2.7 multiply_subtract_fusion.1
  (137 shorter events, 39.6 us)
Async XLA Ops:
  7.2 13.9 %copy-start.2 = (bf16[2,256,512]{2,1,0:T(8,128)(2,1)S(1)}, bf16[2,256,512]{2,1,0:T(8,128)(2,1)}, u32[]{:S(2)}) copy-start(bf16[2,256,512]{2,1,0:T(8,128)(2,1)} %param.33) | copy-start | bytes 1572868
  7.2 13.2 %copy-start.21 = (f32[10,512]{1,0:T(8,128)S(1)}, f32[10,512]{1,0:T(8,128)}, u32[]{:S(2)}) copy-start(f32[10,512]{1,0:T(8,128)} %param.39) | copy-start | bytes 61444
  7.2 13.2 %copy-start.23 = (s32[2,8]{1,0:T(2,128)S(1)}, s32[2,8]{1,0:T(2,128)}, u32[]{:S(2)}) copy-start(s32[2,8]{1,0:T(2,128)} %param.35) | copy-start | bytes 196
  7.2 57.4 %all-gather.4.cloned.1.call-start = ((), (), s32[]{:S(2)}) async-start(), calls=%async_computation | async-start | bytes 5308416 | tf_op jit(solution)/shard_map/all_gather | solution.py:92
  9.5 85.3 %all-gather.6.cloned.1.call-start = ((), (), s32[]{:S(2)}) async-start(), calls=%async_computation.1 | async-start | bytes 2359296 | tf_op jit(solution)/shard_map/all_gather | solution.py:93
  11.3 114.3 %all-gather.8.cloned.1.call-start = ((), (), s32[]{:S(2)}) async-start(), calls=%async_computation.2 | async-start | bytes 2359296 | tf_op jit(solution)/shard_map/all_gather | solution.py:94
  12.3 8.8 %collective-permute-start = (bf16[2,32,512]{2,1,0:T(8,128)(2,1)S(1)}, bf16[2,32,512]{2,1,0:T(8,128)(2,1)S(1)}, u32[]{:S(2)}, u32[]{:S(2)}) collective-permute-start(bf16[2,32,512]{2,1,0:T(8,128)(2,1)S(1)} %get-tuple-element.194), channel_id=1, source_target_pairs={{0,8},{8,16},{16,24},{1,9},{9,17},{17,25},{2,10},{10,18},{18,26},{... | collective-permute-start | bytes 196616 | tf_op jit(solution)/shard_map/ppermute | solution.py:27
  17.1 6.2 %collective-permute-start.1 = (bf16[2,32,512]{2,1,0:T(8,128)(2,1)S(1)}, bf16[2,32,512]{2,1,0:T(8,128)(2,1)S(1)}, u32[]{:S(2)}, u32[]{:S(2)}) collective-permute-start(bf16[2,32,512]{2,1,0:T(8,128)(2,1)S(1)} %get-tuple-element.195), channel_id=1, source_target_pairs={{8,0},{16,8},{24,16},{9,1},{17,9},{25,17},{10,2},{18,10},{26,18},{... | collective-permute-start | bytes 196616 | tf_op jit(solution)/shard_map/ppermute | solution.py:28
  20.3 432.7 %all-reduce.4.cloned.1.call-start = ((), (), s32[]{:S(2)}) async-start(), calls=%async_computation.3 | async-start | bytes 35651584 | tf_op jit(solution)/shard_map/psum | solution.py:195
  21.2 49.3 %copy-start.17 = (bf16[2,288,512]{2,1,0:T(8,128)(2,1)}, bf16[2,288,512]{2,1,0:T(8,128)(2,1)S(1)}, u32[]{:S(2)}) copy-start(bf16[2,288,512]{2,1,0:T(8,128)(2,1)S(1)} %get-tuple-element.192) | copy-start | bytes 1769476
  23.3 45.3 %copy-start.19 = (bf16[2,288,512]{2,1,0:T(8,128)(2,1)}, bf16[2,288,512]{2,1,0:T(8,128)(2,1)S(1)}, u32[]{:S(2)}) copy-start(bf16[2,288,512]{2,1,0:T(8,128)(2,1)S(1)} %constant_dynamic-update-slice_fusion.2) | copy-start | bytes 1769476
  64.6 3.1 copy-start.7
  75.6 23.3 %copy-start.15 = (bf16[2,256,512]{2,1,0:T(8,128)(2,1)}, bf16[2,256,512]{2,1,0:T(8,128)(2,1)S(1)}, u32[]{:S(2)}) copy-start(bf16[2,256,512]{2,1,0:T(8,128)(2,1)S(1)} %fusion.58) | copy-start | bytes 1572868
  111.7 17.5 %copy-start.6 = (bf16[2,256,512]{2,1,0:T(8,128)(2,1)S(1)}, bf16[2,256,512]{2,1,0:T(8,128)(2,1)}, u32[]{:S(2)}) copy-start(bf16[2,256,512]{2,1,0:T(8,128)(2,1)} %param.34) | copy-start | bytes 1572868
  129.7 4.5 copy-start.25
  130.4 3.9 copy-start.10
  130.8 4.7 copy-start.9
  135.5 3.0 copy-start.16
  138.5 3.4 copy-start.24
  141.9 2.2 copy-start.11
  143.5 2.9 copy-start
  143.5 2.9 copy-start.18
  149.4 4.6 copy-start.20
  160.9 6.8 %slice-start = ((s8[4718592]{0:T(1024)(128)(4,1)}), s8[4194304]{0:T(1024)(128)(4,1)S(1)}, s32[]{:S(2)}) async-start(s8[4718592]{0:T(1024)(128)(4,1)} %bitcast.185), calls=%async_computation.4 | async-start | bytes 8388608
  162.8 4.9 %slice-start.1 = ((s8[4718592]{0:T(1024)(128)(4,1)}), s8[524288]{0:T(1024)(128)(4,1)S(1)}, s32[]{:S(2)}) async-start(s8[4718592]{0:T(1024)(128)(4,1)} %bitcast.185), calls=%async_computation.5 | async-start | bytes 1048576
  169.7 52.0 %copy-start.1 = (f32[2,256,512]{2,1,0:T(8,128)S(1)}, f32[2,256,512]{2,1,0:T(8,128)}, u32[]{:S(2)}) copy-start(f32[2,256,512]{2,1,0:T(8,128)} %copy-done) | copy-start | bytes 3145732
  171.4 48.1 %collective-permute-start.3 = (bf16[2,32,512]{2,1,0:T(8,128)(2,1)S(1)}, bf16[2,32,512]{2,1,0:T(8,128)(2,1)S(1)}, u32[]{:S(2)}, u32[]{:S(2)}) collective-permute-start(bf16[2,32,512]{2,1,0:T(8,128)(2,1)S(1)} %slice.673), channel_id=1, source_target_pairs={{8,0},{16,8},{24,16},{9,1},{17,9},{25,17},{10,2},{18,10},{26,18},{... | collective-permute-start | bytes 196616 | tf_op jit(solution)/shard_map/ppermute | solution.py:28
  172.7 46.8 %collective-permute-start.2 = (bf16[2,32,512]{2,1,0:T(8,128)(2,1)S(1)}, bf16[2,32,512]{2,1,0:T(8,128)(2,1)S(1)}, u32[]{:S(2)}, u32[]{:S(2)}) collective-permute-start(bf16[2,32,512]{2,1,0:T(8,128)(2,1)S(1)} %slice.674), channel_id=1, source_target_pairs={{0,8},{8,16},{16,24},{1,9},{9,17},{17,25},{2,10},{10,18},{18,26},{... | collective-permute-start | bytes 196616 | tf_op jit(solution)/shard_map/ppermute | solution.py:27
  453.0 6.9 %copy-start.4 = (f32[512,2048]{1,0:T(8,128)S(1)}, f32[512,2048]{1,0:T(8,128)}, u32[]{:S(2)}) copy-start(f32[512,2048]{1,0:T(8,128)} %get-tuple-element.168) | copy-start | bytes 12582916
  459.9 6.6 %copy-start.5 = (f32[9,64,512]{2,1,0:T(8,128)S(1)}, f32[9,64,512]{2,1,0:T(8,128)}, u32[]{:S(2)}) copy-start(f32[9,64,512]{2,1,0:T(8,128)} %param.36) | copy-start | bytes 3538948
  463.7 7.1 %copy-start.13 = (f32[64,2048]{1,0:T(8,128)S(1)}, f32[64,2048]{1,0:T(8,128)}, u32[]{:S(2)}) copy-start(f32[64,2048]{1,0:T(8,128)} %param.37) | copy-start | bytes 1572868
  466.5 7.9 %copy-start.14 = (f32[256,512]{1,0:T(8,128)S(1)}, f32[256,512]{1,0:T(8,128)}, u32[]{:S(2)}) copy-start(f32[256,512]{1,0:T(8,128)} %param.38) | copy-start | bytes 1572868
  (4 other events, 6.6 us)
Sparse Core Ops, SparseCore 0:
  10.2 54.3 all-gather.3
  66.8 27.9 all-gather.5
  97.0 28.5 all-gather.7
  160.3 292.7 all-reduce.3
where the time goes:
time: 487 us
  waiting for transfers between devices  305 us (63%)
  other arithmetic  53.2 us (11%)
  matrix products  48.4 us (10%)
  blocking collectives  41.5 us (9%)
  between operations  18.2 us (4%)
  starting transfers between devices  12.1 us (2%)
  local copies, waits for them, and re-layouts  7.68 us (2%)
    psum x1, waiting for transfers between devices, per_device(): lax.psum((conv_weight_grad, inner_weight_grad, outer_weight_grad, vector_...  229 us
    psum x1, blocking collectives, per_device(): lax.psum((conv_weight_grad, inner_weight_grad, outer_weight_grad, vector_...  41.5 us
    all_gather x1, waiting for transfers between devices, per_device(): lax.all_gather(conv_weight.astype(jnp.bfloat16), 'row', axis=1, tiled=True)  41.3 us
    all_gather x1, waiting for transfers between devices, per_device(): lax.all_gather(inner_weight.astype(jnp.bfloat16), 'row', axis=0, tiled=True)  19.2 us
    all_gather x1, waiting for transfers between devices, per_device(): lax.all_gather(outer_weight.astype(jnp.bfloat16), 'row', axis=0, tiled=True)  13.9 us
    dot_general x9, matrix products, per_device(): jnp.einsum('rld,rle->de', receptive_span, masked, preferred_element_type=...  13.7 us
    convert_element_type x1, other arithmetic, per_device(): hidden_low = hidden.astype(jnp.bfloat16)  10.8 us
    sub x4, other arithmetic, adamw(): weight - step_rate * (first_hat / (jnp.sqrt(second_hat) + adam_eps) + dec...  10.5 us
  transfers between devices with their start and end apart: 8, of which 5 were waited for; matrix products, arithmetic and copies ran while one was open for 10% of the time, Pallas kernels for 0%

commit v1 on v0

v1 whole, which is shorter than its diff:
```python
import functools

import jax
import jax.numpy as jnp
from jax import lax
from jax.experimental import pallas as pl
from jax.experimental.pallas import tpu as pltpu
from jax.sharding import PartitionSpec as P

DILATION_STEP = 8

beta_one = 0.9
beta_two = 0.999
adam_eps = 1e-08
weight_decay = 0.1
matrix_rate = 0.03
vector_rate = 0.3
clip_level = 1.0
step_count = 10
norm_eps = 1e-05

F32 = jnp.float32
BF = jnp.bfloat16
VEC_PAD = 16
LANES = 128
SQRT_HALF = 0.7071067811865476
PDF_SCALE = 0.3989422804014327


def exchange(value, axis, mask):
    size = lax.axis_size(axis)
    return lax.ppermute(value, axis, [(i, i ^ mask) for i in range(size)])


def shift_along(value, axis, step):
    size = lax.axis_size(axis)
    pairs = [(i, i + step) for i in range(size) if 0 <= i + step < size]
    return lax.ppermute(value, axis, pairs)


def gelu_parts(v):
    cdf = 0.5 + 0.5 * lax.erf(v * SQRT_HALF)
    return v * cdf, cdf


def gelu_slope(v, cdf):
    return cdf + v * (jnp.exp(-0.5 * v * v) * PDF_SCALE)


def mean_of(v):
    return jnp.mean(v, axis=-1, keepdims=True)


def normalized(v):
    centred = v - mean_of(v)
    scale = lax.rsqrt(mean_of(centred * centred) + norm_eps)
    return centred * scale, scale


def fold_rows(v):
    rows, cols = v.shape
    return jnp.sum(v.reshape(rows // 8, 8, cols), axis=0)


def column_sum(acc):
    return jnp.sum(acc, axis=0, keepdims=True)


def loop_rows(total, step, body, init=0):
    return lax.fori_loop(
        0, total // step, lambda i, carry: body(pl.multiple_of(i * step, step), carry), init
    )


def dot(a, b):
    return jnp.dot(a, b, preferred_element_type=F32)


def dot_nt(a, b):
    return lax.dot_general(a, b, (((1,), (1,)), ((), ())), preferred_element_type=F32)


def dot_tn(a, b):
    return lax.dot_general(a, b, (((0,), (0,)), ((), ())), preferred_element_type=F32)


def place():
    seq_at = lax.axis_index("seq")
    row_at = lax.axis_index("row")
    return seq_at, row_at // 2, row_at % 2


def at(index, step):
    return pl.ds(pl.multiple_of(index * step, step), step)


def vmem_call(kernel, outs, scratch=(), smem=0, inputs=0, flops=0, nbytes=0, **kw):
    return pl.pallas_call(
        kernel,
        out_shape=[jax.ShapeDtypeStruct(shape, dtype) for shape, dtype in outs],
        in_specs=[pl.BlockSpec(memory_space=pltpu.SMEM)] * smem
        + [pl.BlockSpec(memory_space=pltpu.VMEM)] * inputs,
        out_specs=[pl.BlockSpec(memory_space=pltpu.VMEM)] * len(outs),
        scratch_shapes=list(scratch),
        cost_estimate=pl.CostEstimate(flops=flops, bytes_accessed=nbytes, transcendentals=0),
        compiler_params=pltpu.CompilerParams(vmem_limit_bytes=60 * 1024 * 1024),
        **kw,
    )


def contigs(lens_ref, row, positions, row_length):
    found = jnp.zeros(positions.shape, jnp.int32)
    start = jnp.int32(0)
    for j in range(lens_ref.shape[1] - 1):
        start = start + lens_ref[row, j]
        found = found + (positions >= start).astype(jnp.int32)
    found = jnp.where(positions < 0, -1, found)
    return jnp.where(positions >= row_length, lens_ref.shape[1], found)


def masked_taps(src, cid, length, taps, half, store):
    centre = cid[pl.ds(half, length), :]

    def body(tap, carry):
        begin = pl.multiple_of(tap * DILATION_STEP, DILATION_STEP)
        keep = cid[pl.ds(begin, length), :] == centre
        for a in range(src.shape[1] // LANES):
            part = src[pl.ds(begin, length), a * LANES : (a + 1) * LANES]
            store(tap, a, jnp.where(keep, part, 0.0).astype(BF))
        return carry

    lax.fori_loop(0, taps, body, 0)


def conv_kernel(taps, nz, ns, *refs):
    lens, tok, left, right, vec, own, other = refs[:7]
    pieces = (refs[7 : 7 + ns], refs[7 + ns : 7 + 2 * ns])
    pre, after, full, ext, cid, cat = refs[7 + 2 * ns :]
    seq_at, z_at, core_at = place()
    rows, length, width = tok.shape
    in_rows = own.shape[1]
    quarter = width // ns
    half = DILATION_STEP * (taps // 2)
    for i, whole in enumerate((own, other)):
        block = z_at * 2 + (core_at ^ i)
        for t in range(taps):
            full[t, at(block, in_rows), :] = whole[t]
        for j in range(1, nz):
            block = (z_at ^ j) * 2 + (core_at ^ i)
            for k in range(ns):
                for t in range(taps):
                    full[t, at(block, in_rows), at(seq_at ^ k, quarter)] = pieces[i][k][j - 1, t]
    span = length + 2 * half
    base = seq_at * length - half
    positions = base + lax.broadcasted_iota(jnp.int32, (span, LANES), 0)
    for r in range(rows):
        ext[0:half, :] = left[r].astype(F32)
        ext[half : half + length, :] = tok[r].astype(F32)
        ext[half + length :, :] = right[r].astype(F32)
        cid[...] = contigs(lens, r, positions, length * ns)

        def store(tap, a, value, r=r):
            cat[r * length : (r + 1) * length, at(tap * (width // LANES) + a, LANES)] = value

        masked_taps(ext, cid, length, taps, half, store)
    weights = full.reshape(taps * width, width)

    def product(r, carry):
        where = at(r, length)
        pre[where, :] = dot(cat[where, :], weights[...]) + vec[0:1, :]
        return carry

    lax.fori_loop(0, rows, product, 0)

    for r in range(rows):

        def norm(begin, carry, r=r):
            where = pl.ds(r * length + begin, 32)
            active, _ = gelu_parts(pre[where, :])
            unit, _ = normalized(active)
            after[where, :] = (
                tok[r, pl.ds(begin, 32), :].astype(F32) + unit * vec[1:2, :] + vec[2:3, :]
            )
            return carry

        loop_rows(length, 32, norm)


def ffn_kernel(nz, ns, *refs):
    pre, after, cot, vec, inner_own, outer_own, inner_other, outer_other = refs[:8]
    pieces = (refs[8 : 8 + ns], refs[8 + ns : 8 + 2 * ns])
    rest = refs[8 + 2 * ns :]
    layer, after_grad, conv_grad = rest[:3]
    sends = rest[3 : 3 + ns]
    low, hidden, outer_grad, inner_grad, inner, outer, slope, tmp, sums = rest[3 + ns :]
    seq_at, z_at, core_at = place()
    count, width = pre.shape
    in_rows, hid = inner_own.shape
    out_rows = outer_own.shape[0]
    part = out_rows // ns
    quarter = hid // ns
    blocks = hid // width
    for i, (one, two) in enumerate(((inner_own, outer_own), (inner_other, outer_other))):
        block = z_at * 2 + (core_at ^ i)
        inner[at(block, in_rows), :] = one[...]
        outer[at(block, out_rows), :] = two[...]
        for j in range(1, nz):
            block = (z_at ^ j) * 2 + (core_at ^ i)
            for k in range(ns):
                inner[at(block, in_rows), at(seq_at ^ k, quarter)] = pieces[i][k][j - 1, :in_rows]
                outer[at(block * ns + (seq_at ^ k), part), :] = pieces[i][k][j - 1, in_rows:]

    def lower(begin, carry):
        where = pl.ds(begin, 64)
        low[where, :] = after[where, :].astype(BF)
        return carry

    loop_rows(count, 64, lower)

    def up(b, carry):
        cols = at(b, width)
        tmp[...] = dot(low[...], inner[:, cols]) + vec[pl.ds(6 + b, 1), :]

        def act(begin, inside):
            where = pl.ds(begin, 32)
            v = tmp[where, :]
            active, cdf = gelu_parts(v)
            hidden[where, cols] = active.astype(BF)
            slope[where, cols] = gelu_slope(v, cdf)
            return inside

        loop_rows(count, 32, act)
        return carry

    lax.fori_loop(0, blocks, up, 0)
    tmp[...] = dot(hidden[...], outer[...]) + vec[3:4, :]
    zero = jnp.zeros((8, width), F32)

    def second(begin, carry):
        bias_sum, gain_sum, shift_sum = carry
        where = pl.ds(begin, 32)
        unit, scale = normalized(tmp[where, :])
        gain = vec[4:5, :]
        layer[where, :] = (after[where, :] + unit * gain + vec[5:6, :]).astype(BF)
        dy = cot[where, :].astype(F32)
        u = dy * gain
        grad = (scale * (u - mean_of(u) - unit * mean_of(u * unit))).astype(BF)
        outer_grad[where, :] = grad
        return (
            bias_sum + fold_rows(grad.astype(F32)),
            gain_sum + fold_rows(dy * unit),
            shift_sum + fold_rows(dy),
        )

    totals = loop_rows(count, 32, second, (zero, zero, zero))
    sums[...] = jnp.zeros(sums.shape, F32)
    for i, total in enumerate(totals):
        sums[3 + i : 4 + i, :] = column_sum(total)

    def down(b, carry):
        cols = at(b, width)
        tmp[...] = dot_nt(outer_grad[...], outer[cols, :])

        def act(begin, total):
            where = pl.ds(begin, 32)
            grad = (tmp[where, :] * slope[where, cols]).astype(BF)
            inner_grad[where, cols] = grad
            return total + fold_rows(grad.astype(F32))

        total = loop_rows(count, 32, act, zero)
        sums[pl.ds(6 + b, 1), :] = column_sum(total)
        return carry

    lax.fori_loop(0, blocks, down, 0)
    tmp[...] = dot_nt(inner_grad[...], inner[...])

    def first(begin, carry):
        bias_sum, gain_sum, shift_sum = carry
        where = pl.ds(begin, 32)
        upstream = cot[where, :].astype(F32) + tmp[where, :]
        after_grad[where, :] = upstream
        v = pre[where, :]
        active, cdf = gelu_parts(v)
        unit, scale = normalized(active)
        u = upstream * vec[1:2, :]
        grad = scale * (u - mean_of(u) - unit * mean_of(u * unit))
        grad = (grad * gelu_slope(v, cdf)).astype(BF)
        conv_grad[where, :] = grad
        return (
            bias_sum + fold_rows(grad.astype(F32)),
            gain_sum + fold_rows(upstream * unit),
            shift_sum + fold_rows(upstream),
        )

    totals = loop_rows(count, 32, first, (zero, zero, zero))
    for i, total in enumerate(totals):
        sums[i : i + 1, :] = column_sum(total)
    span = width // ns
    for k in range(ns):
        sends[k][0:count, :] = conv_grad[:, at(seq_at ^ k, span)]
        encode(sends[k], count, spread(sums[...]))


def spread(v):
    return jnp.concatenate(
        [v[:, a * LANES : (a + 1) * LANES] for a in range(v.shape[1] // LANES)], axis=0
    )


def gathered(v):
    return jnp.concatenate(
        [v[a * VEC_PAD : (a + 1) * VEC_PAD, :] for a in range(v.shape[0] // VEC_PAD)], axis=1
    )


def encode(ref, begin, v):
    rows = v.shape[0]
    high = v.astype(BF)
    ref[begin : begin + rows, :] = high
    ref[begin + rows : begin + 2 * rows, :] = (v - high.astype(F32)).astype(BF)


def decode(ref, begin, rows):
    high = ref[begin : begin + rows, :].astype(F32)
    return high + ref[begin + rows : begin + 2 * rows, :].astype(F32)


def tree_sum(values):
    values = list(values)
    while len(values) > 1:
        values = [values[i] + values[i + 1] for i in range(0, len(values), 2)]
    return values[0]


def ffn_weight_kernel(nz, ns, in_rows, out_rows, *refs):
    low, hidden, outer_grad, inner_grad, mine, theirs, outer_sum, inner_sum = refs
    seq_at, z_at, core_at = place()
    width = low.shape[1]
    hid = hidden.shape[1]
    part = out_rows // ns
    quarter = hid // ns

    def product(b, carry):
        cols = at(b, width)
        outer_sum[cols, :] = dot_tn(hidden[:, cols], outer_grad[...]).astype(BF)
        inner_sum[:, cols] = dot_tn(low[...], inner_grad[:, cols]).astype(BF)
        return carry

    lax.fori_loop(0, hid // width, product, 0)
    for i, out in enumerate((mine, theirs)):
        for k in range(ns):
            for j in range(nz):
                block = (z_at ^ j) * 2 + (core_at ^ i)
                out[k, j, :in_rows] = inner_sum[at(block, in_rows), at(seq_at ^ k, quarter)]
                out[k, j, in_rows:] = outer_sum[at(block * ns + (seq_at ^ k), part), :]


def conv_weight_kernel(taps, nz, ns, in_rows, *refs):
    lens = refs[0]
    toks = refs[1 : 1 + ns]
    grads = refs[1 + ns : 1 + 2 * ns]
    mine, theirs, padded, cid, cat, total = refs[1 + 2 * ns :]
    seq_at, z_at, core_at = place()
    rows, length, width = toks[0].shape
    span = width // ns
    half = DILATION_STEP * (taps // 2)
    row_length = ns * length
    count = rows * length
    positions = lax.broadcasted_iota(jnp.int32, (row_length + 2 * half, LANES), 0) - half
    edge = jnp.zeros((half, span), F32)
    for r in range(rows):
        padded[0:half, :] = edge
        padded[half + row_length :, :] = edge
        cid[...] = contigs(lens, r, positions, row_length)
        for k in range(ns):
            padded[pl.ds(half + (seq_at ^ k) * length, length), :] = grads[k][
                r * length : (r + 1) * length, :
            ].astype(F32)
        for k in range(ns):
            base = (seq_at ^ k) * length
            centre = cid[pl.ds(pl.multiple_of(base + half, 8), length), :]
            for t in range(taps):
                begin = pl.multiple_of(base + DILATION_STEP * (taps - 1 - t), 8)
                keep = cid[pl.ds(begin, length), :] == centre
                value = jnp.where(keep, padded[pl.ds(begin, length), :], 0.0)
                low_row = k * count + r * length
                cat[low_row : low_row + length, t * span : (t + 1) * span] = value.astype(BF)
    for k in range(ns):
        value = tree_sum(
            [
                dot_tn(toks[k][r], cat[k * count + r * length : k * count + (r + 1) * length, :])
                for r in range(rows)
            ]
        )
        if k == 0:
            total[...] = value
        else:
            total[...] += value
    for i, out in enumerate((mine, theirs)):
        for j in range(nz):
            block = (z_at ^ j) * 2 + (core_at ^ i)
            for t in range(taps):
                begin = (j * taps + t) * in_rows
                out[begin : begin + in_rows, :] = total[
                    at(block, in_rows), t * span : (t + 1) * span
                ].astype(BF)
    vec_rows = (grads[0].shape[0] - count) // 2
    summed = tree_sum([decode(g, count, vec_rows) for g in grads])
    for out in (mine, theirs):
        encode(out, nz * taps * in_rows, summed)


def input_grad_kernel(taps, ns, *refs):
    lens, grad, left, right, after_grad, full, out, ext, cid, cat = refs
    seq_at = lax.axis_index("seq")
    rows, half, width = left.shape
    length = grad.shape[0] // rows
    base = seq_at * length - half
    positions = base + lax.broadcasted_iota(jnp.int32, (length + 2 * half, LANES), 0)
    for r in range(rows):
        ext[0:half, :] = left[r].astype(F32)
        ext[half : half + length, :] = grad[r * length : (r + 1) * length, :].astype(F32)
        ext[half + length :, :] = right[r].astype(F32)
        cid[...] = contigs(lens, r, positions, length * ns)

        def store(tap, a, value, r=r):
            flipped = taps - 1 - tap
            cat[
                flipped, r * length : (r + 1) * length, a * LANES : (a + 1) * LANES
            ] = value

        masked_taps(ext, cid, length, taps, half, store)

    out[...] = after_grad[...]

    def product(t, carry):
        out[...] += dot_nt(cat[t], full[t])
        return carry

    lax.fori_loop(0, taps, product, 0)


def split_sum_kernel(count, *refs):
    ins, outs = refs[:count], refs[count:]
    rows = outs[0].shape[0]
    for p, out in enumerate(outs):

        def body(begin, carry, p=p, out=out):
            where = pl.ds(p * rows + begin, 64)
            out[pl.ds(begin, 64), :] = tree_sum([v[where, :].astype(F32) for v in ins]).astype(BF)
            return carry

        loop_rows(rows, 64, body)


def split_sum(ins, parts):
    rows, cols = ins[0].shape
    return vmem_call(
        functools.partial(split_sum_kernel, len(ins)),
        [((rows // parts, cols), BF)] * parts,
        inputs=len(ins),
        flops=rows * cols * len(ins),
        nbytes=2 * rows * cols * (len(ins) + 1),
    )(*ins)


def conv_core_kernel(rows, mine, got, *outs):
    vec_rows = (mine.shape[0] - rows * len(outs)) // 2
    begin_vec = rows * len(outs)
    summed = decode(mine, begin_vec, vec_rows) + decode(got, begin_vec, vec_rows)
    for p, out in enumerate(outs):

        def body(begin, carry, p=p, out=out):
            where = pl.ds(p * rows + begin, 64)
            out[pl.ds(begin, 64), :] = (mine[where, :].astype(F32) + got[where, :].astype(F32)).astype(
                BF
            )
            return carry

        loop_rows(rows, 64, body)
        encode(out, rows, summed)


def final_kernel(count, vec_rows, *refs):
    ins, outs = refs[:count], refs[count:]
    out, square = outs[:2]
    rows = out.shape[0]

    def body(begin, carry):
        where = pl.ds(begin, 64)
        value = tree_sum([v[where, :].astype(F32) for v in ins]).astype(BF)
        out[where, :] = value
        wide = value.astype(F32)
        folded = fold_rows(wide * wide)
        return carry + sum(
            folded[:, a * LANES : (a + 1) * LANES] for a in range(folded.shape[1] // LANES)
        )

    square[...] = loop_rows(rows, 64, body, jnp.zeros((8, LANES), F32))
    if vec_rows:
        outs[2][...] = gathered(tree_sum([decode(v, rows, vec_rows) for v in ins]))


def adam_math(weight, first, second, gradient, clip, rate, decay):
    clipped = gradient * clip
    first = beta_one * first + (1.0 - beta_one) * clipped
    second = beta_two * second + (1.0 - beta_two) * clipped * clipped
    first_hat = first / (1.0 - beta_one**step_count)
    second_hat = second / (1.0 - beta_two**step_count)
    weight = weight - rate * (first_hat / (jnp.sqrt(second_hat) + adam_eps) + decay * weight)
    return weight, first, second


def adam_kernel(taps, ns, *refs):
    conv_grads, ffn_grads = refs[:ns], refs[ns : 2 * ns]
    vec_sum, squares, conv, inner, outer, vec, conv_m, inner_m, outer_m, vec_m = refs[
        2 * ns : 2 * ns + 10
    ]
    (
        norm,
        new_conv,
        conv_first,
        new_inner,
        inner_first,
        new_outer,
        outer_first,
        new_vec,
        vec_first,
        second,
        outer_second,
        vec_second,
    ) = refs[2 * ns + 10 :]
    seq_at, z_at, core_at = place()
    in_rows, width = conv.shape[1:]
    hid = inner.shape[1]
    out_rows = outer.shape[0]
    span = width // ns
    quarter = hid // ns
    part = out_rows // ns
    vec_count = vec.shape[0]
    vec_grad = vec_sum[0:vec_count, :]
    total = jnp.sum(squares[...]) + jnp.sum(vec_grad * vec_grad)
    value = jnp.sqrt(jnp.full((1, 1), total, F32))
    norm[...] = value
    clip = clip_level / jnp.maximum(value, clip_level)

    for k in range(ns):
        cols = at(seq_at ^ k, span)

        def conv_step(t, carry, k=k, cols=cols):
            w, m, v = adam_math(
                conv[t, :, cols],
                conv_m[0, t, :, cols],
                conv_m[1, t, :, cols],
                conv_grads[k][at(t, in_rows), :].astype(F32),
                clip,
                matrix_rate,
                weight_decay,
            )
            new_conv[t, :, cols] = w
            conv_first[t, :, cols] = m
            second[:, at(t * ns + (seq_at ^ k), span)] = v
            return carry

        lax.fori_loop(0, taps, conv_step, 0)
        for a in range(quarter // LANES):
            lanes = pl.ds(pl.multiple_of((seq_at ^ k) * quarter + a * LANES, LANES), LANES)
            w, m, v = adam_math(
                inner[:, lanes],
                inner_m[0, :, lanes],
                inner_m[1, :, lanes],
                ffn_grads[k][0:in_rows, a * LANES : (a + 1) * LANES].astype(F32),
                clip,
                matrix_rate,
                weight_decay,
            )
            new_inner[:, lanes] = w
            inner_first[:, lanes] = m
            second[
                :, pl.ds(pl.multiple_of(taps * width + (seq_at ^ k) * quarter + a * LANES, LANES), LANES)
            ] = v
        where = at(seq_at ^ k, part)
        for a in range(width // LANES):
            lanes = slice(a * LANES, (a + 1) * LANES)
            w, m, v = adam_math(
                outer[where, lanes],
                outer_m[0, where, lanes],
                outer_m[1, where, lanes],
                ffn_grads[k][in_rows:, lanes].astype(F32),
                clip,
                matrix_rate,
                weight_decay,
            )
            new_outer[where, lanes] = w
            outer_first[where, lanes] = m
            outer_second[a, where, :] = v
    ratio = out_rows // in_rows
    base = taps * width + hid
    for e in range(ratio):
        for a in range(width // LANES):
            begin = base + e * width + a * LANES
            second[:, begin : begin + LANES] = outer_second[a, pl.ds(e, in_rows, stride=ratio), :]
    w, m, v = adam_math(vec[...], vec_m[0], vec_m[1], vec_grad, clip, vector_rate, 0.0)
    new_vec[...] = w
    vec_first[...] = m
    v = jnp.concatenate([v, jnp.zeros((LANES - vec_count, width), F32)], axis=0)
    vec_second[...] = jnp.transpose(v)
    begin = base + ratio * width
    block = z_at * 2 + core_at
    second[:, begin : begin + vec_count] = vec_second[at(block, in_rows), :][:, 0:vec_count]


def per_device(
    tokens,
    cotangent,
    contig_lengths,
    conv_weight,
    inner_weight,
    outer_weight,
    vectors,
    conv_moments,
    inner_moments,
    outer_moments,
    vector_moments,
):
    ns = lax.axis_size("seq")
    nr = lax.axis_size("row")
    nz = nr // 2
    seq_at = lax.axis_index("seq")
    rows, length, width = tokens.shape
    taps, in_rows, _ = conv_weight.shape
    hid = inner_weight.shape[1]
    out_rows = outer_weight.shape[0]
    count = rows * length
    half = DILATION_STEP * (taps // 2)
    span = width // ns
    quarter = hid // ns
    part = out_rows // ns

    left = shift_along(tokens[:, length - half :], "seq", 1)
    right = shift_along(tokens[:, :half], "seq", -1)

    conv_own = conv_weight.astype(BF)
    conv_part = lax.dynamic_slice_in_dim(conv_weight, seq_at * span, span, 2).astype(BF)
    got = [exchange(conv_part, "row", 2 * j) for j in range(1, nz)]
    got = jnp.stack(got)
    conv_pieces = [got] + [exchange(got, "seq", k) for k in range(1, ns)]
    conv_other = exchange(conv_own, "row", 1)
    conv_other_pieces = [exchange(p, "row", 1) for p in conv_pieces]

    inner_own = inner_weight.astype(BF)
    outer_own = outer_weight.astype(BF)
    ffn_part = jnp.concatenate(
        [
            lax.dynamic_slice_in_dim(inner_weight, seq_at * quarter, quarter, 1),
            lax.dynamic_slice_in_dim(outer_weight, seq_at * part, part, 0),
        ],
        axis=0,
    ).astype(BF)
    got = jnp.stack([exchange(ffn_part, "row", 2 * j) for j in range(1, nz)])
    ffn_pieces = [got] + [exchange(got, "seq", k) for k in range(1, ns)]
    inner_other = exchange(inner_own, "row", 1)
    outer_other = exchange(outer_own, "row", 1)
    ffn_other_pieces = [exchange(p, "row", 1) for p in ffn_pieces]

    pre, after, conv_full = vmem_call(
        functools.partial(conv_kernel, taps, nz, ns),
        [((count, width), F32), ((count, width), F32), ((taps, width, width), BF)],
        [
            pltpu.VMEM((length + 2 * half, width), F32),
            pltpu.VMEM((length + 2 * half, LANES), jnp.int32),
            pltpu.VMEM((count, taps * width), BF),
        ],
        smem=1,
        inputs=6 + 2 * ns,
        flops=2 * count * taps * width * width,
        nbytes=4 * taps * width * width,
    )(
        contig_lengths,
        tokens,
        left,
        right,
        vectors,
        conv_own,
        conv_other,
        *conv_pieces,
        *conv_other_pieces,
    )

    tokens_late, _ = lax.optimization_barrier((tokens, ffn_pieces[-1]))
    token_pieces = [tokens] + [exchange(tokens_late, "seq", k) for k in range(1, ns)]

    results = vmem_call(
        functools.partial(ffn_kernel, nz, ns),
        [((count, width), BF), ((count, width), F32), ((count, width), BF)]
        + [((count + 2 * VEC_PAD * width // LANES, span), BF)] * ns
        + [((count, width), BF), ((count, hid), BF), ((count, width), BF), ((count, hid), BF)],
        [
            pltpu.VMEM((width, hid), BF),
            pltpu.VMEM((hid, width), BF),
            pltpu.VMEM((count, hid), F32),
            pltpu.VMEM((count, width), F32),
            pltpu.VMEM((VEC_PAD, width), F32),
        ],
        inputs=8 + 2 * ns,
        flops=8 * count * width * hid,
        nbytes=20 * width * hid,
    )(
        pre,
        after,
        cotangent.reshape(count, width),
        vectors,
        inner_own,
        outer_own,
        inner_other,
        outer_other,
        *ffn_pieces,
        *ffn_other_pieces,
    )
    layer_out, after_grad, conv_grad = results[:3]
    grad_pieces = list(results[3 : 3 + ns])
    low, hidden, outer_grad, inner_grad = results[3 + ns :]
    grad_pieces = grad_pieces[:1] + [exchange(grad_pieces[k], "seq", k) for k in range(1, ns)]

    conv_grad_rows = conv_grad.reshape(rows, length, width)
    grad_left = shift_along(conv_grad_rows[:, length - half :], "seq", 1)
    grad_right = shift_along(conv_grad_rows[:, :half], "seq", -1)

    ffn_rows = in_rows + part
    mine, theirs = vmem_call(
        functools.partial(ffn_weight_kernel, nz, ns, in_rows, out_rows),
        [((ns, nz, ffn_rows, width), BF)] * 2,
        [pltpu.VMEM((hid, width), BF), pltpu.VMEM((width, hid), BF)],
        inputs=4,
        flops=4 * count * width * hid,
        nbytes=8 * width * hid,
    )(low, hidden, outer_grad, inner_grad)
    arrived = exchange(theirs, "row", 1)
    flat = (ns * nz * ffn_rows, width)
    sums = split_sum([mine.reshape(flat), arrived.reshape(flat)], ns)
    sums = [sums[0]] + [exchange(sums[k], "seq", k) for k in range(1, ns)]
    sums = split_sum(sums, nz)
    sums = [sums[0]] + [exchange(sums[j], "row", 2 * j) for j in range(1, nz)]
    ffn_sum, ffn_square = vmem_call(
        functools.partial(final_kernel, nz, 0),
        [((ffn_rows, width), BF), ((8, LANES), F32)],
        inputs=nz,
        flops=ffn_rows * width * nz,
        nbytes=2 * ffn_rows * width * nz,
    )(*sums)
    ffn_sums = [ffn_sum] + [exchange(ffn_sum, "seq", k) for k in range(1, ns)]

    vec_rows = VEC_PAD * width // LANES
    conv_rows = taps * in_rows
    mine, theirs = vmem_call(
        functools.partial(conv_weight_kernel, taps, nz, ns, in_rows),
        [((nz * conv_rows + 2 * vec_rows, span), BF)] * 2,
        [
            pltpu.VMEM((ns * length + 2 * half, span), F32),
            pltpu.VMEM((ns * length + 2 * half, LANES), jnp.int32),
            pltpu.VMEM((ns * count, taps * span), BF),
            pltpu.VMEM((width, taps * span), F32),
        ],
        smem=1,
        inputs=2 * ns,
        flops=2 * ns * count * width * taps * span,
        nbytes=8 * count * width * ns,
    )(contig_lengths, *token_pieces, *grad_pieces)
    arrived = exchange(theirs, "row", 1)
    sums = vmem_call(
        functools.partial(conv_core_kernel, conv_rows),
        [((conv_rows + 2 * vec_rows, span), BF)] * nz,
        inputs=2,
        flops=4 * conv_rows * nz * span,
        nbytes=8 * conv_rows * nz * span,
    )(mine, arrived)
    sums = [sums[0]] + [exchange(sums[j], "row", 2 * j) for j in range(1, nz)]
    conv_sum, conv_square, vec_sum = vmem_call(
        functools.partial(final_kernel, nz, vec_rows),
        [((conv_rows, span), BF), ((8, LANES), F32), ((VEC_PAD, width), F32)],
        inputs=nz,
        flops=conv_rows * span * nz,
        nbytes=2 * conv_rows * span * nz,
    )(*sums)
    conv_sums = [conv_sum] + [exchange(conv_sum, "seq", k) for k in range(1, ns)]
    square = conv_square + ffn_square
    squares = lax.all_to_all(
        jnp.broadcast_to(square[None], (ns * nr, 8, LANES)), ("seq", "row"), 0, 0
    )

    (input_grad,) = vmem_call(
        functools.partial(input_grad_kernel, taps, ns),
        [((count, width), F32)],
        [
            pltpu.VMEM((length + 2 * half, width), F32),
            pltpu.VMEM((length + 2 * half, LANES), jnp.int32),
            pltpu.VMEM((taps, count, width), BF),
        ],
        smem=1,
        inputs=5,
        flops=2 * count * taps * width * width,
        nbytes=2 * taps * width * width,
    )(contig_lengths, conv_grad, grad_left, grad_right, after_grad, conv_full)

    second_width = taps * width + hid + (out_rows // in_rows) * width + vectors.shape[0]
    (
        norm,
        new_conv,
        conv_first,
        new_inner,
        inner_first,
        new_outer,
        outer_first,
        new_vectors,
        vector_first,
        second_moments,
    ) = vmem_call(
        functools.partial(adam_kernel, taps, ns),
        [
            ((1, 1), F32),
            (conv_weight.shape, F32),
            (conv_weight.shape, F32),
            (inner_weight.shape, F32),
            (inner_weight.shape, F32),
            (outer_weight.shape, F32),
            (outer_weight.shape, F32),
            (vectors.shape, F32),
            (vectors.shape, F32),
            ((in_rows, second_width), F32),
        ],
        [
            pltpu.VMEM((width // LANES, out_rows, LANES), F32),
            pltpu.VMEM((width, LANES), F32),
        ],
        inputs=2 * ns + 10,
        flops=20 * in_rows * second_width,
        nbytes=28 * in_rows * second_width,
    )(
        *conv_sums,
        *ffn_sums,
        vec_sum,
        squares,
        conv_weight,
        inner_weight,
        outer_weight,
        vectors,
        conv_moments,
        inner_moments,
        outer_moments,
        vector_moments,
    )
    return (
        layer_out.reshape(tokens.shape),
        input_grad.reshape(tokens.shape),
        norm.reshape(()),
        new_conv,
        conv_first,
        new_inner,
        inner_first,
        new_outer,
        outer_first,
        new_vectors,
        vector_first,
        second_moments,
    )


def solution(mesh):
    in_specs = (
        P("row", "seq", None),
        P("row", "seq", None),
        P("row", None),
        P(None, "row", None),
        P("row", None),
        P("row", None),
        P(),
        P(None, None, "row", None),
        P(None, "row", None),
        P(None, "row", None),
        P(),
    )
    out_specs = (
        P("row", "seq", None),
        P("row", "seq", None),
        P(),
        P(None, "row", None),
        P(None, "row", None),
        P("row", None),
        P("row", None),
        P("row", None),
        P("row", None),
        P(),
        P(),
        P("row", None),
    )
    return jax.shard_map(
        per_device, mesh=mesh, in_specs=in_specs, out_specs=out_specs, check_vma=False
    )
```

time: 487 us -> 247 us (0.51)
  waiting for transfers between devices: 305 us -> 77.2 us
  Pallas kernels: 0 us -> 85.5 us
  starting transfers between devices: 12.1 us -> 65.2 us
  other arithmetic: 53.2 us -> 1.97 us
  matrix products: 48.4 us -> 0 us
  blocking collectives: 41.5 us -> 0 us
  between operations: 18.2 us -> 1.2 us
  local copies, waits for them, and re-layouts: 7.68 us -> 14.9 us
    psum x1 -> x0, waiting for transfers between devices: 229 us -> none  [per_device(): lax.psum((conv_weight_grad, inner_weight_grad, outer_weight_grad, vector_...]
    pallas_call x0 -> x11, Pallas kernels: none -> 85.5 us  [the longest x1 25.1 us: per_device(): vmem_call(functools.partial(ffn_kernel, nz, ns), [((count, width), BF), (...]
    ppermute x4 -> x50, waiting for transfers between devices: 2.14 us -> 77.2 us  [the longest x46 74.4 us: exchange(): return lax.ppermute(value, axis, [(i, i ^ mask) for i in range(size)])]
    all_gather x3 -> x0, waiting for transfers between devices: 74.5 us -> none  [the longest x1 41.3 us: per_device(): lax.all_gather(conv_weight.astype(jnp.bfloat16), 'row', axis=1, tiled=True)]
    ppermute x4 -> x50, starting transfers between devices: 12 us -> 60.8 us  [the longest x46 52.1 us: exchange(): return lax.ppermute(value, axis, [(i, i ^ mask) for i in range(size)])]
    dot_general x33 -> x0, matrix products: 48.4 us -> none  [the longest x9 13.7 us: per_device(): jnp.einsum('rld,rle->de', receptive_span, masked, preferred_element_type=...]
    psum x1 -> x0, blocking collectives: 41.5 us -> none  [per_device(): lax.psum((conv_weight_grad, inner_weight_grad, outer_weight_grad, vector_...]
    reduce_sum x12 -> x0, other arithmetic: 19.2 us -> none  [the longest x1 6.86 us: per_device(): jnp.sum(conv_sum * conv_sum) + jnp.sum(inner_sum * inner_sum)]
  transfers between devices with their start and end apart: 8 -> 51, of which waited for: 5 -> 17; matrix products, arithmetic and copies ran while one was open for 10% -> 2% of each run, Pallas kernels for 0% -> 18%
where the time goes in v1:
time: 247 us; the launch traced here: 246 us
  Pallas kernels  85.5 us (35%)
  waiting for transfers between devices  77.2 us (31%)
  starting transfers between devices  65.2 us (26%)
  local copies, waits for them, and re-layouts  14.9 us (6%)
    ppermute x46, waiting for transfers between devices, exchange(): return lax.ppermute(value, axis, [(i, i ^ mask) for i in range(size)])  74.4 us
    ppermute x46, starting transfers between devices, exchange(): return lax.ppermute(value, axis, [(i, i ^ mask) for i in range(size)])  52.1 us
    pallas_call x1, Pallas kernels, per_device(): vmem_call(functools.partial(ffn_kernel, nz, ns), [((count, width), BF), (...  25.1 us
    pallas_call x1, Pallas kernels, per_device(): vmem_call(functools.partial(conv_kernel, taps, nz, ns), [((count, width),...  13.7 us
    pallas_call x1, Pallas kernels, per_device(): vmem_call(functools.partial(input_grad_kernel, taps, ns), [((count, width...  9.71 us
    unnamed x101, local copies, waits for them, and re-layouts  9.57 us
    pallas_call x1, Pallas kernels, per_device(): vmem_call(functools.partial(adam_kernel, taps, ns), [((1, 1), F32), (conv...  8.71 us
    ppermute x4, starting transfers between devices, shift_along(): return lax.ppermute(value, axis, pairs)  8.66 us
  transfers between devices with their start and end apart: 51, of which 17 were waited for; matrix products, arithmetic and copies ran while one was open for 2% of the time, Pallas kernels for 18%

profile of v1, /device:TPU:0, one launch (start us, length us, event | category | flops | bytes accessed | tf_op | source)
XLA Modules:
  0.0 246.0 jit_solution(8799598131991314356)
XLA Ops:
  2.6 3.1 %collective-permute-start.15 = (bf16[128,512]{1,0:T(8,128)(2,1)S(1)}, bf16[128,512]{1,0:T(8,128)(2,1)S(1)}, u32[]{:S(2)}, u32[]{:S(2)}) collective-permute-start(bf16[128,512]{1,0:T(8,128)(2,1)S(1)} %pad_maximum_fusion.2), channel_id=1, source_target_pairs={{0,2},{1,3},{2,0},{3,1},{4,6},{5,7},{6,4},{7,5},{8,10},{9,11},{10,... | collective-permute-start | bytes 393224 | tf_op jit(solution)/shard_map/ppermute | solution.py:32
  5.7 2.6 %collective-permute-start.16 = (bf16[128,512]{1,0:T(8,128)(2,1)S(1)}, bf16[128,512]{1,0:T(8,128)(2,1)S(1)}, u32[]{:S(2)}, u32[]{:S(2)}) collective-permute-start(bf16[128,512]{1,0:T(8,128)(2,1)S(1)} %pad_maximum_fusion.2), channel_id=1, source_target_pairs={{0,4},{1,5},{2,6},{3,7},{4,0},{5,1},{6,2},{7,3},{8,12},{9,13},{10,... | collective-permute-start | bytes 393224 | tf_op jit(solution)/shard_map/ppermute | solution.py:32
  10.3 3.5 %collective-permute-start.4 = (bf16[9,64,128]{2,1,0:T(8,128)(2,1)S(1)}, bf16[9,64,128]{2,1,0:T(8,128)(2,1)S(1)}, u32[]{:S(2)}, u32[]{:S(2)}) collective-permute-start(bf16[9,64,128]{2,1,0:T(8,128)(2,1)S(1)} %dynamic-slice_convert_fusion), channel_id=1, source_target_pairs={{0,4},{1,5},{2,6},{3,7},{4,0},{5,1},{6,2},{7,3},{8,12},{9,13},{10,... | collective-permute-start | bytes 442376 | tf_op jit(solution)/shard_map/ppermute | solution.py:32
  14.9 3.7 %collective-permute-done.16 = bf16[128,512]{1,0:T(8,128)(2,1)S(1)} collective-permute-done((bf16[128,512]{1,0:T(8,128)(2,1)S(1)}, bf16[128,512]{1,0:T(8,128)(2,1)S(1)}, u32[]{:S(2)}, u32[]{:S(2)}) %collective-permute-start.16) | collective-permute-done | bytes 131104 | tf_op jit(solution)/shard_map/ppermute | solution.py:32
  18.7 2.5 %collective-permute-start.20 = (bf16[3,128,512]{2,1,0:T(8,128)(2,1)S(1)}, bf16[3,128,512]{2,1,0:T(8,128)(2,1)}, u32[]{:S(2)}, u32[]{:S(2)}) collective-permute-start(bf16[3,128,512]{2,1,0:T(8,128)(2,1)S(1)} %pad_maximum_fusion.1.refs_8_), channel_id=1, source_target_pairs={{0,24},{8,16},{16,8},{24,0},{1,25},{9,17},{17,9},{25,1},{2,26},{10... | collective-permute-start | bytes 1179656 | tf_op jit(solution)/shard_map/ppermute | solution.py:32
  22.1 2.4 collective-permute-start
  24.6 6.4 %collective-permute-done.4 = bf16[9,64,128]{2,1,0:T(8,128)(2,1)S(1)} collective-permute-done((bf16[9,64,128]{2,1,0:T(8,128)(2,1)S(1)}, bf16[9,64,128]{2,1,0:T(8,128)(2,1)S(1)}, u32[]{:S(2)}, u32[]{:S(2)}) %collective-permute-start.4) | collective-permute-done | bytes 147488 | tf_op jit(solution)/shard_map/ppermute | solution.py:32
  32.2 2.7 %collective-permute-start.18 = (bf16[3,128,512]{2,1,0:T(8,128)(2,1)S(1)}, bf16[3,128,512]{2,1,0:T(8,128)(2,1)}, u32[]{:S(2)}, u32[]{:S(2)}) collective-permute-start(bf16[3,128,512]{2,1,0:T(8,128)(2,1)S(1)} %pad_maximum_fusion.1.refs_8_), channel_id=1, source_target_pairs={{0,8},{8,0},{16,24},{24,16},{1,9},{9,1},{17,25},{25,17},{2,10},{10... | collective-permute-start | bytes 1179656 | tf_op jit(solution)/shard_map/ppermute | solution.py:32
  35.1 2.7 %collective-permute-done.1.refs_3_ = bf16[2,32,512]{2,1,0:T(8,128)(2,1)S(1)} collective-permute-done((bf16[2,32,512]{2,1,0:T(8,128)(2,1)S(1)}, bf16[2,32,512]{2,1,0:T(8,128)(2,1)S(1)}, u32[]{:S(2)}, u32[]{:S(2)}) %collective-permute-start.1) | collective-permute-done | bytes 65568 | tf_op jit(solution)/shard_map/ppermute | solution.py:38
  42.5 3.9 %collective-permute-done.18.refs_9_ = bf16[3,128,512]{2,1,0:T(8,128)(2,1)} collective-permute-done((bf16[3,128,512]{2,1,0:T(8,128)(2,1)S(1)}, bf16[3,128,512]{2,1,0:T(8,128)(2,1)}, u32[]{:S(2)}, u32[]{:S(2)}) %collective-permute-start.18) | collective-permute-done | bytes 393248 | tf_op jit(solution)/shard_map/ppermute | solution.py:32
  46.4 17.3 %collective-permute-done.19.refs_10_ = bf16[3,128,512]{2,1,0:T(8,128)(2,1)} collective-permute-done((bf16[3,128,512]{2,1,0:T(8,128)(2,1)S(1)}, bf16[3,128,512]{2,1,0:T(8,128)(2,1)}, u32[]{:S(2)}, u32[]{:S(2)}) %collective-permute-start.19) | collective-permute-done | bytes 393248 | tf_op jit(solution)/shard_map/ppermute | solution.py:32
  69.1 13.7 %shard_map.202 = (f32[512,512]{1,0:T(8,128)}, f32[512,512]{1,0:T(8,128)}, bf16[9,512,512]{2,1,0:T(8,128)(2,1)}) custom-call(s32[2,8]{1,0:T(2,128)} %refs_0_.5, bf16[2,256,512]{2,1,0:T(8,128)(2,1)} %refs_1_.3, bf16[2,32,512]{2,1,0:T(8,128)(2,1)} %copy-done.46, bf16[2,32,512]{2,1,0:T(8,128)(2,1)} %copy-done.47, f32[10,512]{1,0:T(8,128)} %refs_13_.1, ...), custom_call_target="tpu_custom_call" | custom-call | flops 2415919104 | bytes 9437184 | tf_op jit(solution)/shard_map/pallas_call | solution.py:666
  82.8 25.1 %shard_map.203 = (bf16[512,512]{1,0:T(8,128)(2,1)}, f32[512,512]{1,0:T(8,128)}, bf16[512,512]{1,0:T(8,128)(2,1)}, bf16[640,128]{1,0:T(8,128)(2,1)}, bf16[640,128...) custom-call(f32[512,512]{1,0:T(8,128)} %get-tuple-element.58.refs_0_, ...), custom_call_target="tpu_custom_call" | custom-call | flops 4294967296 | bytes 20971520 | tf_op jit(solution)/shard_map/pallas_call | solution.py:693
  108.0 7.9 %shard_map.208 = (bf16[4,4,128,512]{3,2,1,0:T(8,128)(2,1)}, bf16[4,4,128,512]{3,2,1,0:T(8,128)(2,1)}) custom-call(bf16[512,512]{1,0:T(8,128)(2,1)} %get-tuple-element.76.refs_0_, bf16[512,2048]{1,0:T(8,128)(2,1)} %get-tuple-element.77.refs_1_, bf16[512,512]{1,0:T(8,128)(2,1)} %get-tuple-element.78.refs_2_, bf16[512,2048]{1,0:T(8,128)(2,1)} %get-tuple-element.79.refs_3_), custom_call_target="tpu_custom_call" | custom-call | flops 2147483648 | bytes 8388608 | tf_op jit(solution)/shard_map/pallas_call | solution.py:730
  116.1 2.8 %collective-permute-start.27 = (bf16[2,256,512]{2,1,0:T(8,128)(2,1)S(1)}, bf16[2,256,512]{2,1,0:T(8,128)(2,1)S(1)}, u32[]{:S(2)}, u32[]{:S(2)}) collective-permute-start(bf16[2,256,512]{2,1,0:T(8,128)(2,1)S(1)} %copy-done.27), channel_id=1, source_target_pairs={{0,8},{8,0},{16,24},{24,16},{1,9},{9,1},{17,25},{25,17},{2,10},{10... | collective-permute-start | bytes 1572872 | tf_op jit(solution)/shard_map/ppermute | solution.py:32
  122.4 9.2 %collective-permute-done.27.refs_2_ = bf16[2,256,512]{2,1,0:T(8,128)(2,1)S(1)} collective-permute-done((bf16[2,256,512]{2,1,0:T(8,128)(2,1)S(1)}, bf16[2,256,512]{2,1,0:T(8,128)(2,1)S(1)}, u32[]{:S(2)}, u32[]{:S(2)}) %collective-permute-start.27) | collective-permute-done | bytes 524320 | tf_op jit(solution)/shard_map/ppermute | solution.py:32
  132.1 12.8 %collective-permute-done.28.refs_3_ = bf16[2,256,512]{2,1,0:T(8,128)(2,1)S(1)} collective-permute-done((bf16[2,256,512]{2,1,0:T(8,128)(2,1)S(1)}, bf16[2,256,512]{2,1,0:T(8,128)(2,1)S(1)}, u32[]{:S(2)}, u32[]{:S(2)}) %collective-permute-start.28) | collective-permute-done | bytes 524320 | tf_op jit(solution)/shard_map/ppermute | solution.py:32
  146.4 2.8 %collective-permute-done.31.refs_7_ = bf16[640,128]{1,0:T(8,128)(2,1)S(1)} collective-permute-done((bf16[640,128]{1,0:T(8,128)(2,1)S(1)}, bf16[640,128]{1,0:T(8,128)(2,1)S(1)}, u32[]{:S(2)}, u32[]{:S(2)}) %collective-permute-start.31) | collective-permute-done | bytes 163872 | tf_op jit(solution)/shard_map/ppermute | solution.py:32
  151.8 7.4 %shard_map.205 = (bf16[2432,128]{1,0:T(8,128)(2,1)}, bf16[2432,128]{1,0:T(8,128)(2,1)}) custom-call(s32[2,8]{1,0:T(2,128)} %refs_0_.5, bf16[2,256,512]{2,1,0:T(8,128)(2,1)} %refs_1_.3, bf16[2,256,512]{2,1,0:T(8,128)(2,1)} %copy-done.30, bf16[2,256,512]{2,1,0:T(8,128)(2,1)} %copy-done.31, bf16[2,256,512]{2,1,0:T(8,128)(2,1)} %copy-done.32, ...), custom_call_target="tpu_custom_call" | custom-call | flops 2415919104 | bytes 8388608 | tf_op jit(solution)/shard_map/pallas_call | solution.py:755
  160.5 4.2 %shard_map.209 = (bf16[512,512]{1,0:T(8,128)(2,1)}, bf16[512,512]{1,0:T(8,128)(2,1)}, bf16[512,512]{1,0:T(8,128)(2,1)}, bf16[512,512]{1,0:T(8,128)(2,1)}) custom-call(bf16[2048,512]{1,0:T(8,128)(2,1)} %bitcast.13, bf16[2048,512]{1,0:T(8,128)(2,1)} %bitcast.14), custom_call_target="tpu_custom_call" | custom-call | flops 2097152 | bytes 6291456 | tf_op jit(solution)/shard_map/pallas_call | solution.py:458
  169.0 2.5 %shard_map.206 = (bf16[704,128]{1,0:T(8,128)(2,1)}, bf16[704,128]{1,0:T(8,128)(2,1)}, bf16[704,128]{1,0:T(8,128)(2,1)}, bf16[704,128]{1,0:T(8,128)(2,1)}) custom-call(bf16[2432,128]{1,0:T(8,128)(2,1)} %get-tuple-element.69.mine, bf16[2432,128]{1,0:T(8,128)(2,1)} %copy-done.3), custom_call_target="tpu_custom_call" | custom-call | flops 1179648 | bytes 2359296 | tf_op jit(solution)/shard_map/pallas_call | solution.py:770
  171.5 2.5 %collective-permute-start.34 = (bf16[704,128]{1,0:T(8,128)(2,1)}, bf16[704,128]{1,0:T(8,128)(2,1)S(1)}, u32[]{:S(2)}, u32[]{:S(2)}) collective-permute-start(bf16[704,128]{1,0:T(8,128)(2,1)} %get-tuple-element.72), channel_id=1, source_target_pairs={{0,2},{1,3},{2,0},{3,1},{4,6},{5,7},{6,4},{7,5},{8,10},{9,11},{10,... | collective-permute-start | bytes 540680 | tf_op jit(solution)/shard_map/ppermute | solution.py:32
  174.8 5.7 %collective-permute-done.34.refs_1_ = bf16[704,128]{1,0:T(8,128)(2,1)S(1)} collective-permute-done((bf16[704,128]{1,0:T(8,128)(2,1)}, bf16[704,128]{1,0:T(8,128)(2,1)S(1)}, u32[]{:S(2)}, u32[]{:S(2)}) %collective-permute-start.34) | collective-permute-done | bytes 180256 | tf_op jit(solution)/shard_map/ppermute | solution.py:32
  180.5 3.9 %collective-permute-start.36 = (bf16[704,128]{1,0:T(8,128)(2,1)}, bf16[704,128]{1,0:T(8,128)(2,1)S(1)}, u32[]{:S(2)}, u32[]{:S(2)}) collective-permute-start(bf16[704,128]{1,0:T(8,128)(2,1)} %get-tuple-element.74), channel_id=1, source_target_pairs={{0,6},{1,7},{2,4},{3,5},{4,2},{5,3},{6,0},{7,1},{8,14},{9,15},{10,... | collective-permute-start | bytes 540680 | tf_op jit(solution)/shard_map/ppermute | solution.py:32
  184.4 5.4 %collective-permute-done.35.refs_2_ = bf16[704,128]{1,0:T(8,128)(2,1)S(1)} collective-permute-done((bf16[704,128]{1,0:T(8,128)(2,1)}, bf16[704,128]{1,0:T(8,128)(2,1)S(1)}, u32[]{:S(2)}, u32[]{:S(2)}) %collective-permute-start.35) | collective-permute-done | bytes 180256 | tf_op jit(solution)/shard_map/ppermute | solution.py:32
  194.2 2.6 %shard_map.210 = (bf16[128,512]{1,0:T(8,128)(2,1)}, bf16[128,512]{1,0:T(8,128)(2,1)}, bf16[128,512]{1,0:T(8,128)(2,1)}, bf16[128,512]{1,0:T(8,128)(2,1)}) custom-call(bf16[512,512]{1,0:T(8,128)(2,1)} %get-tuple-element.82.refs_0_, bf16[512,512]{1,0:T(8,128)(2,1)} %copy-done.6, bf16[512,512]{1,0:T(8,128)(2,1)} %copy-done.7, bf16[512,512]{1,0:T(8,128)(2,1)} %copy-done.8), custom_call_target="tpu_custom_call" | custom-call | flops 1048576 | bytes 2621440 | tf_op jit(solution)/shard_map/pallas_call | solution.py:458
  196.8 3.1 %collective-permute-start.44 = (bf16[128,512]{1,0:T(8,128)(2,1)}, bf16[128,512]{1,0:T(8,128)(2,1)S(1)}, u32[]{:S(2)}, u32[]{:S(2)}) collective-permute-start(bf16[128,512]{1,0:T(8,128)(2,1)} %get-tuple-element.87), channel_id=1, source_target_pairs={{0,2},{1,3},{2,0},{3,1},{4,6},{5,7},{6,4},{7,5},{8,10},{9,11},{10,... | collective-permute-start | bytes 393224 | tf_op jit(solution)/shard_map/ppermute | solution.py:32
  203.1 3.6 %collective-permute-start.25 = (bf16[2,32,512]{2,1,0:T(8,128)(2,1)S(1)}, bf16[2,32,512]{2,1,0:T(8,128)(2,1)S(1)}, u32[]{:S(2)}, u32[]{:S(2)}) collective-permute-start(bf16[2,32,512]{2,1,0:T(8,128)(2,1)S(1)} %get-tuple-element.105), channel_id=1, source_target_pairs={{0,8},{8,16},{16,24},{1,9},{9,17},{17,25},{2,10},{10,18},{18,26},{... | collective-permute-start | bytes 196616 | tf_op jit(solution)/shard_map/ppermute | solution.py:38
  208.1 3.1 %collective-permute-done.45.refs_2_ = bf16[128,512]{1,0:T(8,128)(2,1)S(1)} collective-permute-done((bf16[128,512]{1,0:T(8,128)(2,1)}, bf16[128,512]{1,0:T(8,128)(2,1)S(1)}, u32[]{:S(2)}, u32[]{:S(2)}) %collective-permute-start.45) | collective-permute-done | bytes 131104 | tf_op jit(solution)/shard_map/ppermute | solution.py:32
  215.0 4.5 %all-to-all-start = ((f32[32,8,128]{2,1,0:T(8,128)}), f32[32,8,128]{2,1,0:T(8,128)S(1)}, u32[]{:S(2)}, u32[]{:S(2)}) async-start(f32[32,8,128]{2,1,0:T(8,128)} %broadcast_in_dim.2), calls=%async_computation | async-start | bytes 262144 | tf_op jit(solution)/shard_map/all_to_all | solution.py:787
  226.7 9.7 %shard_map.204 = f32[512,512]{1,0:T(8,128)} custom-call(s32[2,8]{1,0:T(2,128)} %refs_0_.5, bf16[512,512]{1,0:T(8,128)(2,1)} %get-tuple-element.61.refs_1_, bf16[2,32,512]{2,1,0:T(8,128)(2,1)} %copy-done.48, bf16[2,32,512]{2,1,0:T(8,128)(2,1)} %copy-done.49, f32[512,512]{1,0:T(8,128)} %get-tuple-element.62.refs_4_, bf16[9,512,512]{2,1,0:T(8,128)(2,1)} %get-tuple-element.63.refs_5_), custom_call_target="tpu_custom_call" | custom-call | flops 2415919104 | bytes 4718592 | tf_op jit(solution)/shard_map/pallas_call | solution.py:791
  237.3 8.7 %shard_map.212 = (f32[1,1]{1,0:T(1,128)}, f32[9,64,512]{2,1,0:T(8,128)}, f32[9,64,512]{2,1,0:T(8,128)}, f32[64,2048]{1,0:T(8,128)}, f32[64,2048]{1,0:T(8,128)}, ...) custom-call(bf16[576,128]{1,0:T(8,128)(2,1)} %get-tuple-element.75.r, ...), custom_call_target="tpu_custom_call" | custom-call | flops 11153920 | bytes 15615488 | tf_op jit(solution)/shard_map/pallas_call | solution.py:817
  (195 shorter events, 52.9 us)
Async XLA Ops:
  10.3 20.7 %collective-permute-start.4 = (bf16[9,64,128]{2,1,0:T(8,128)(2,1)S(1)}, bf16[9,64,128]{2,1,0:T(8,128)(2,1)S(1)}, u32[]{:S(2)}, u32[]{:S(2)}) collective-permute-start(bf16[9,64,128]{2,1,0:T(8,128)(2,1)S(1)} %dynamic-slice_convert_fusion), channel_id=1, source_target_pairs={{0,4},{1,5},{2,6},{3,7},{4,0},{5,1},{6,2},{7,3},{8,12},{9,13},{10,... | collective-permute-start | bytes 442376 | tf_op jit(solution)/shard_map/ppermute | solution.py:32
  14.8 17.4 %collective-permute-start.5 = (bf16[9,64,128]{2,1,0:T(8,128)(2,1)S(1)}, bf16[9,64,128]{2,1,0:T(8,128)(2,1)S(1)}, u32[]{:S(2)}, u32[]{:S(2)}) collective-permute-start(bf16[9,64,128]{2,1,0:T(8,128)(2,1)S(1)} %dynamic-slice_convert_fusion), channel_id=1, source_target_pairs={{0,6},{1,7},{2,4},{3,5},{4,2},{5,3},{6,0},{7,1},{8,14},{9,15},{10,... | collective-permute-start | bytes 442376 | tf_op jit(solution)/shard_map/ppermute | solution.py:32
  18.7 20.7 %collective-permute-start.13 = (bf16[64,2048]{1,0:T(8,128)(2,1)S(1)}, bf16[64,2048]{1,0:T(8,128)(2,1)S(1)}, u32[]{:S(2)}, u32[]{:S(2)}) collective-permute-start(bf16[64,2048]{1,0:T(8,128)(2,1)S(1)} %convert_element_type.15.refs_4_), channel_id=1, source_target_pairs={{0,1},{1,0},{2,3},{3,2},{4,5},{5,4},{6,7},{7,6},{8,9},{9,8},{10,11... | collective-permute-start | bytes 786440 | tf_op jit(solution)/shard_map/ppermute | solution.py:32
  18.7 21.2 %collective-permute-start.20 = (bf16[3,128,512]{2,1,0:T(8,128)(2,1)S(1)}, bf16[3,128,512]{2,1,0:T(8,128)(2,1)}, u32[]{:S(2)}, u32[]{:S(2)}) collective-permute-start(bf16[3,128,512]{2,1,0:T(8,128)(2,1)S(1)} %pad_maximum_fusion.1.refs_8_), channel_id=1, source_target_pairs={{0,24},{8,16},{16,8},{24,0},{1,25},{9,17},{17,9},{25,1},{2,26},{10... | collective-permute-start | bytes 1179656 | tf_op jit(solution)/shard_map/ppermute | solution.py:32
  32.2 14.1 %collective-permute-start.18 = (bf16[3,128,512]{2,1,0:T(8,128)(2,1)S(1)}, bf16[3,128,512]{2,1,0:T(8,128)(2,1)}, u32[]{:S(2)}, u32[]{:S(2)}) collective-permute-start(bf16[3,128,512]{2,1,0:T(8,128)(2,1)S(1)} %pad_maximum_fusion.1.refs_8_), channel_id=1, source_target_pairs={{0,8},{8,0},{16,24},{24,16},{1,9},{9,1},{17,25},{25,17},{2,10},{10... | collective-permute-start | bytes 1179656 | tf_op jit(solution)/shard_map/ppermute | solution.py:32
  35.0 28.7 %collective-permute-start.6 = (bf16[3,9,64,128]{3,2,1,0:T(8,128)(2,1)S(1)}, bf16[3,9,64,128]{3,2,1,0:T(8,128)(2,1)S(1)}, u32[]{:S(2)}, u32[]{:S(2)}) collective-permute-start(bf16[3,9,64,128]{3,2,1,0:T(8,128)(2,1)S(1)} %pad_maximum_fusion.refs_7_), channel_id=1, source_target_pairs={{0,8},{8,0},{16,24},{24,16},{1,9},{9,1},{17,25},{25,17},{2,10},{10... | collective-permute-start | bytes 1327112 | tf_op jit(solution)/shard_map/ppermute | solution.py:32
  37.9 26.4 %collective-permute-start.7 = (bf16[3,9,64,128]{3,2,1,0:T(8,128)(2,1)S(1)}, bf16[3,9,64,128]{3,2,1,0:T(8,128)(2,1)S(1)}, u32[]{:S(2)}, u32[]{:S(2)}) collective-permute-start(bf16[3,9,64,128]{3,2,1,0:T(8,128)(2,1)S(1)} %pad_maximum_fusion.refs_7_), channel_id=1, source_target_pairs={{0,16},{8,24},{16,0},{24,8},{1,17},{9,25},{17,1},{25,9},{2,18},{10... | collective-permute-start | bytes 1327112 | tf_op jit(solution)/shard_map/ppermute | solution.py:32
  39.4 24.3 %collective-permute-start.19 = (bf16[3,128,512]{2,1,0:T(8,128)(2,1)S(1)}, bf16[3,128,512]{2,1,0:T(8,128)(2,1)}, u32[]{:S(2)}, u32[]{:S(2)}) collective-permute-start(bf16[3,128,512]{2,1,0:T(8,128)(2,1)S(1)} %pad_maximum_fusion.1.refs_8_), channel_id=1, source_target_pairs={{0,16},{8,24},{16,0},{24,8},{1,17},{9,25},{17,1},{25,9},{2,18},{10... | collective-permute-start | bytes 1179656 | tf_op jit(solution)/shard_map/ppermute | solution.py:32
  40.1 24.2 %collective-permute-start.8 = (bf16[3,9,64,128]{3,2,1,0:T(8,128)(2,1)S(1)}, bf16[3,9,64,128]{3,2,1,0:T(8,128)(2,1)S(1)}, u32[]{:S(2)}, u32[]{:S(2)}) collective-permute-start(bf16[3,9,64,128]{3,2,1,0:T(8,128)(2,1)S(1)} %pad_maximum_fusion.refs_7_), channel_id=1, source_target_pairs={{0,24},{8,16},{16,8},{24,0},{1,25},{9,17},{17,9},{25,1},{2,26},{10... | collective-permute-start | bytes 1327112 | tf_op jit(solution)/shard_map/ppermute | solution.py:32
  46.4 19.3 %collective-permute-start.2 = (bf16[9,64,512]{2,1,0:T(8,128)(2,1)S(1)}, bf16[9,64,512]{2,1,0:T(8,128)(2,1)S(1)}, u32[]{:S(2)}, u32[]{:S(2)}) collective-permute-start(bf16[9,64,512]{2,1,0:T(8,128)(2,1)S(1)} %convert_element_type.13.refs_5_), channel_id=1, source_target_pairs={{0,1},{1,0},{2,3},{3,2},{4,5},{5,4},{6,7},{7,6},{8,9},{9,8},{10,11... | collective-permute-start | bytes 1769480 | tf_op jit(solution)/shard_map/ppermute | solution.py:32
  65.5 17.3 %collective-permute-start.21 = (bf16[3,128,512]{2,1,0:T(8,128)(2,1)S(1)}, bf16[3,128,512]{2,1,0:T(8,128)(2,1)}, u32[]{:S(2)}, u32[]{:S(2)}) collective-permute-start(bf16[3,128,512]{2,1,0:T(8,128)(2,1)S(1)} %pad_maximum_fusion.1.refs_8_), channel_id=1, source_target_pairs={{0,1},{1,0},{2,3},{3,2},{4,5},{5,4},{6,7},{7,6},{8,9},{9,8},{10,11... | collective-permute-start | bytes 1179656 | tf_op jit(solution)/shard_map/ppermute | solution.py:32
  65.6 17.2 %collective-permute-start.24 = (bf16[3,128,512]{2,1,0:T(8,128)(2,1)}, bf16[3,128,512]{2,1,0:T(8,128)(2,1)}, u32[]{:S(2)}, u32[]{:S(2)}) collective-permute-start(bf16[3,128,512]{2,1,0:T(8,128)(2,1)} %collective-permute-done.20.refs_11_), channel_id=1, source_target_pairs={{0,1},{1,0},{2,3},{3,2},{4,5},{5,4},{6,7},{7,6},{8,9},{9,8},{10,11... | collective-permute-start | bytes 1179656 | tf_op jit(solution)/shard_map/ppermute | solution.py:32
  66.1 16.7 %collective-permute-start.22 = (bf16[3,128,512]{2,1,0:T(8,128)(2,1)}, bf16[3,128,512]{2,1,0:T(8,128)(2,1)}, u32[]{:S(2)}, u32[]{:S(2)}) collective-permute-start(bf16[3,128,512]{2,1,0:T(8,128)(2,1)} %collective-permute-done.18.refs_9_), channel_id=1, source_target_pairs={{0,1},{1,0},{2,3},{3,2},{4,5},{5,4},{6,7},{7,6},{8,9},{9,8},{10,11... | collective-permute-start | bytes 1179656 | tf_op jit(solution)/shard_map/ppermute | solution.py:32
  67.7 15.1 %collective-permute-start.23 = (bf16[3,128,512]{2,1,0:T(8,128)(2,1)}, bf16[3,128,512]{2,1,0:T(8,128)(2,1)}, u32[]{:S(2)}, u32[]{:S(2)}) collective-permute-start(bf16[3,128,512]{2,1,0:T(8,128)(2,1)} %collective-permute-done.19.refs_10_), channel_id=1, source_target_pairs={{0,1},{1,0},{2,3},{3,2},{4,5},{5,4},{6,7},{7,6},{8,9},{9,8},{10,11... | collective-permute-start | bytes 1179656 | tf_op jit(solution)/shard_map/ppermute | solution.py:32
  68.8 14.0 %collective-permute-start.14 = (bf16[256,512]{1,0:T(8,128)(2,1)S(1)}, bf16[256,512]{1,0:T(8,128)(2,1)}, u32[]{:S(2)}, u32[]{:S(2)}) collective-permute-start(bf16[256,512]{1,0:T(8,128)(2,1)S(1)} %convert_element_type.16.refs_5_), channel_id=1, source_target_pairs={{0,1},{1,0},{2,3},{3,2},{4,5},{5,4},{6,7},{7,6},{8,9},{9,8},{10,11... | collective-permute-start | bytes 786440 | tf_op jit(solution)/shard_map/ppermute | solution.py:32
  115.8 43.4 %collective-permute-start.40 = (bf16[4,4,128,512]{3,2,1,0:T(8,128)(2,1)}, bf16[4,4,128,512]{3,2,1,0:T(8,128)(2,1)S(1)}, u32[]{:S(2)}, u32[]{:S(2)}) collective-permute-start(bf16[4,4,128,512]{3,2,1,0:T(8,128)(2,1)} %get-tuple-element.81), channel_id=1, source_target_pairs={{0,1},{1,0},{2,3},{3,2},{4,5},{5,4},{6,7},{7,6},{8,9},{9,8},{10,11... | collective-permute-start | bytes 6291464 | tf_op jit(solution)/shard_map/ppermute | solution.py:32
  116.1 15.5 %collective-permute-start.27 = (bf16[2,256,512]{2,1,0:T(8,128)(2,1)S(1)}, bf16[2,256,512]{2,1,0:T(8,128)(2,1)S(1)}, u32[]{:S(2)}, u32[]{:S(2)}) collective-permute-start(bf16[2,256,512]{2,1,0:T(8,128)(2,1)S(1)} %copy-done.27), channel_id=1, source_target_pairs={{0,8},{8,0},{16,24},{24,16},{1,9},{9,1},{17,25},{25,17},{2,10},{10... | collective-permute-start | bytes 1572872 | tf_op jit(solution)/shard_map/ppermute | solution.py:32
  118.9 26.0 %collective-permute-start.28 = (bf16[2,256,512]{2,1,0:T(8,128)(2,1)S(1)}, bf16[2,256,512]{2,1,0:T(8,128)(2,1)S(1)}, u32[]{:S(2)}, u32[]{:S(2)}) collective-permute-start(bf16[2,256,512]{2,1,0:T(8,128)(2,1)S(1)} %copy-done.27), channel_id=1, source_target_pairs={{0,16},{8,24},{16,0},{24,8},{1,17},{9,25},{17,1},{25,9},{2,18},{10... | collective-permute-start | bytes 1572872 | tf_op jit(solution)/shard_map/ppermute | solution.py:32
  118.9 26.0 %collective-permute-start.29 = (bf16[2,256,512]{2,1,0:T(8,128)(2,1)S(1)}, bf16[2,256,512]{2,1,0:T(8,128)(2,1)S(1)}, u32[]{:S(2)}, u32[]{:S(2)}) collective-permute-start(bf16[2,256,512]{2,1,0:T(8,128)(2,1)S(1)} %copy-done.27), channel_id=1, source_target_pairs={{0,24},{8,16},{16,8},{24,0},{1,25},{9,17},{17,9},{25,1},{2,26},{10... | collective-permute-start | bytes 1572872 | tf_op jit(solution)/shard_map/ppermute | solution.py:32
  120.3 26.0 %collective-permute-start.30 = (bf16[640,128]{1,0:T(8,128)(2,1)}, bf16[640,128]{1,0:T(8,128)(2,1)S(1)}, u32[]{:S(2)}, u32[]{:S(2)}) collective-permute-start(bf16[640,128]{1,0:T(8,128)(2,1)} %get-tuple-element.66), channel_id=1, source_target_pairs={{0,8},{8,0},{16,24},{24,16},{1,9},{9,1},{17,25},{25,17},{2,10},{10... | collective-permute-start | bytes 491528 | tf_op jit(solution)/shard_map/ppermute | solution.py:32
  131.6 17.6 %collective-permute-start.31 = (bf16[640,128]{1,0:T(8,128)(2,1)S(1)}, bf16[640,128]{1,0:T(8,128)(2,1)S(1)}, u32[]{:S(2)}, u32[]{:S(2)}) collective-permute-start(bf16[640,128]{1,0:T(8,128)(2,1)S(1)} %copy-done.42), channel_id=1, source_target_pairs={{0,16},{8,24},{16,0},{24,8},{1,17},{9,25},{17,1},{25,9},{2,18},{10... | collective-permute-start | bytes 491528 | tf_op jit(solution)/shard_map/ppermute | solution.py:32
  164.7 28.4 %collective-permute-start.41 = (bf16[512,512]{1,0:T(8,128)(2,1)}, bf16[512,512]{1,0:T(8,128)(2,1)S(1)}, u32[]{:S(2)}, u32[]{:S(2)}) collective-permute-start(bf16[512,512]{1,0:T(8,128)(2,1)} %get-tuple-element.83), channel_id=1, source_target_pairs={{0,8},{8,0},{16,24},{24,16},{1,9},{9,1},{17,25},{25,17},{2,10},{10... | collective-permute-start | bytes 1572872 | tf_op jit(solution)/shard_map/ppermute | solution.py:32
  165.5 27.6 %collective-permute-start.42 = (bf16[512,512]{1,0:T(8,128)(2,1)}, bf16[512,512]{1,0:T(8,128)(2,1)S(1)}, u32[]{:S(2)}, u32[]{:S(2)}) collective-permute-start(bf16[512,512]{1,0:T(8,128)(2,1)} %get-tuple-element.84), channel_id=1, source_target_pairs={{0,16},{8,24},{16,0},{24,8},{1,17},{9,25},{17,1},{25,9},{2,18},{10... | collective-permute-start | bytes 1572872 | tf_op jit(solution)/shard_map/ppermute | solution.py:32
  166.3 26.8 %collective-permute-start.43 = (bf16[512,512]{1,0:T(8,128)(2,1)}, bf16[512,512]{1,0:T(8,128)(2,1)S(1)}, u32[]{:S(2)}, u32[]{:S(2)}) collective-permute-start(bf16[512,512]{1,0:T(8,128)(2,1)} %get-tuple-element.85), channel_id=1, source_target_pairs={{0,24},{8,16},{16,8},{24,0},{1,25},{9,17},{17,9},{25,1},{2,26},{10... | collective-permute-start | bytes 1572872 | tf_op jit(solution)/shard_map/ppermute | solution.py:32
  174.0 15.7 %collective-permute-start.35 = (bf16[704,128]{1,0:T(8,128)(2,1)}, bf16[704,128]{1,0:T(8,128)(2,1)S(1)}, u32[]{:S(2)}, u32[]{:S(2)}) collective-permute-start(bf16[704,128]{1,0:T(8,128)(2,1)} %get-tuple-element.73), channel_id=1, source_target_pairs={{0,4},{1,5},{2,6},{3,7},{4,0},{5,1},{6,2},{7,3},{8,12},{9,13},{10,... | collective-permute-start | bytes 540680 | tf_op jit(solution)/shard_map/ppermute | solution.py:32
  192.5 32.7 %collective-permute-start.37 = (bf16[576,128]{1,0:T(8,128)(2,1)}, bf16[576,128]{1,0:T(8,128)(2,1)S(1)}, u32[]{:S(2)}, u32[]{:S(2)}) collective-permute-start(bf16[576,128]{1,0:T(8,128)(2,1)} %get-tuple-element.75.refs_0_), channel_id=1, source_target_pairs={{0,8},{8,0},{16,24},{24,16},{1,9},{9,1},{17,25},{25,17},{2,10},{10... | collective-permute-start | bytes 442376 | tf_op jit(solution)/shard_map/ppermute | solution.py:32
  203.1 20.1 %collective-permute-start.25 = (bf16[2,32,512]{2,1,0:T(8,128)(2,1)S(1)}, bf16[2,32,512]{2,1,0:T(8,128)(2,1)S(1)}, u32[]{:S(2)}, u32[]{:S(2)}) collective-permute-start(bf16[2,32,512]{2,1,0:T(8,128)(2,1)S(1)} %get-tuple-element.105), channel_id=1, source_target_pairs={{0,8},{8,16},{16,24},{1,9},{9,17},{17,25},{2,10},{10,18},{18,26},{... | collective-permute-start | bytes 196616 | tf_op jit(solution)/shard_map/ppermute | solution.py:38
  206.8 16.9 %collective-permute-start.26 = (bf16[2,32,512]{2,1,0:T(8,128)(2,1)S(1)}, bf16[2,32,512]{2,1,0:T(8,128)(2,1)S(1)}, u32[]{:S(2)}, u32[]{:S(2)}) collective-permute-start(bf16[2,32,512]{2,1,0:T(8,128)(2,1)S(1)} %get-tuple-element.104), channel_id=1, source_target_pairs={{8,0},{16,8},{24,16},{9,1},{17,9},{25,17},{10,2},{18,10},{26,18},{... | collective-permute-start | bytes 196616 | tf_op jit(solution)/shard_map/ppermute | solution.py:38
  215.0 21.4 %all-to-all-start = ((f32[32,8,128]{2,1,0:T(8,128)}), f32[32,8,128]{2,1,0:T(8,128)S(1)}, u32[]{:S(2)}, u32[]{:S(2)}) async-start(f32[32,8,128]{2,1,0:T(8,128)} %broadcast_in_dim.2), calls=%async_computation | async-start | bytes 262144 | tf_op jit(solution)/shard_map/all_to_all | solution.py:787
  220.2 16.2 %collective-permute-start.38 = (bf16[576,128]{1,0:T(8,128)(2,1)S(1)}, bf16[576,128]{1,0:T(8,128)(2,1)S(1)}, u32[]{:S(2)}, u32[]{:S(2)}) collective-permute-start(bf16[576,128]{1,0:T(8,128)(2,1)S(1)} %copy-done.16), channel_id=1, source_target_pairs={{0,16},{8,24},{16,0},{24,8},{1,17},{9,25},{17,1},{25,9},{2,18},{10... | collective-permute-start | bytes 442376 | tf_op jit(solution)/shard_map/ppermute | solution.py:32
  221.7 14.7 %collective-permute-start.39 = (bf16[576,128]{1,0:T(8,128)(2,1)S(1)}, bf16[576,128]{1,0:T(8,128)(2,1)S(1)}, u32[]{:S(2)}, u32[]{:S(2)}) collective-permute-start(bf16[576,128]{1,0:T(8,128)(2,1)S(1)} %copy-done.16), channel_id=1, source_target_pairs={{0,24},{8,16},{16,8},{24,0},{1,25},{9,17},{17,9},{25,1},{2,26},{10... | collective-permute-start | bytes 442376 | tf_op jit(solution)/shard_map/ppermute | solution.py:32
  223.2 13.2 %collective-permute-start.47 = (bf16[128,512]{1,0:T(8,128)(2,1)}, bf16[128,512]{1,0:T(8,128)(2,1)S(1)}, u32[]{:S(2)}, u32[]{:S(2)}) collective-permute-start(bf16[128,512]{1,0:T(8,128)(2,1)} %get-tuple-element.90.refs_4_), channel_id=1, source_target_pairs={{0,8},{8,0},{16,24},{24,16},{1,9},{9,1},{17,25},{25,17},{2,10},{10... | collective-permute-start | bytes 393224 | tf_op jit(solution)/shard_map/ppermute | solution.py:32
  (69 other events, 738.0 us)

commit v2 on v1

--- a/solution.py
+++ b/solution.py
@@ -94,18 +94,56 @@
     return pl.ds(pl.multiple_of(index * step, step), step)
 
 
-def vmem_call(kernel, outs, scratch=(), smem=0, inputs=0, flops=0, nbytes=0, **kw):
-    return pl.pallas_call(
-        kernel,
-        out_shape=[jax.ShapeDtypeStruct(shape, dtype) for shape, dtype in outs],
-        in_specs=[pl.BlockSpec(memory_space=pltpu.SMEM)] * smem
-        + [pl.BlockSpec(memory_space=pltpu.VMEM)] * inputs,
-        out_specs=[pl.BlockSpec(memory_space=pltpu.VMEM)] * len(outs),
-        scratch_shapes=list(scratch),
-        cost_estimate=pl.CostEstimate(flops=flops, bytes_accessed=nbytes, transcendentals=0),
-        compiler_params=pltpu.CompilerParams(vmem_limit_bytes=60 * 1024 * 1024),
-        **kw,
-    )
+def size_of(shape, dtype):
+    total = jnp.dtype(dtype).itemsize
+    for n in shape:
+        total *= n
+    return total
+
+
+def vmem_call(kernel, outs, scratch=(), smem=0, loose=(), kept=(), left=(), slack=6):
+    space = pl.BlockSpec(memory_space=pltpu.VMEM)
+    anywhere = pl.BlockSpec(memory_space=pl.ANY)
+    grant = slack * 1024 * 1024
+    grant += sum(size_of(v.shape, v.dtype) for v in scratch if hasattr(v, "shape") and v.dtype in (F32, BF, jnp.int32))
+    grant += sum(size_of(*outs[i]) for i in kept)
+
+    def call(*args):
+        fixed = [
+            a
+            if i < smem or i in loose
+            else pltpu.with_memory_space_constraint(a, pltpu.VMEM)
+            for i, a in enumerate(args)
+        ]
+        return pl.pallas_call(
+            kernel,
+            out_shape=[
+                jax.ShapeDtypeStruct(shape, dtype) if i in kept or i in left else pltpu.VMEM(shape, dtype)
+                for i, (shape, dtype) in enumerate(outs)
+            ],
+            in_specs=[
+                pl.BlockSpec(memory_space=pltpu.SMEM) if i < smem else anywhere if i in loose else space
+                for i in range(len(args))
+            ],
+            out_specs=[anywhere if i in left else space for i in range(len(outs))],
+            scratch_shapes=list(scratch),
+            cost_estimate=pl.CostEstimate(flops=1, bytes_accessed=1, transcendentals=0),
+            compiler_params=pltpu.CompilerParams(vmem_limit_bytes=grant),
+        )(*fixed)
+
+    return call
+
+
+def begin_copies(pairs, sems):
+    copies = [pltpu.make_async_copy(src, dst, sems.at[i]) for i, (src, dst) in enumerate(pairs)]
+    for copy in copies:
+        copy.start()
+    return copies
+
+
+def end_copies(copies):
+    for copy in copies:
+        copy.wait()
 
 
 def contigs(lens_ref, row, positions, row_length):
@@ -132,24 +170,51 @@
     lax.fori_loop(0, taps, body, 0)
 
 
-def conv_kernel(taps, nz, ns, *refs):
-    lens, tok, left, right, vec, own, other = refs[:7]
-    pieces = (refs[7 : 7 + ns], refs[7 + ns : 7 + 2 * ns])
-    pre, after, full, ext, cid, cat = refs[7 + 2 * ns :]
+def cut_kernel(ns, conv, tok, part, left_edge, right_edge):
+    seq_at = lax.axis_index("seq")
+    half = left_edge.shape[1]
+    part[...] = conv[:, :, at(seq_at, conv.shape[2] // ns)].astype(BF)
+    left_edge[...] = tok[:, :half, :]
+    right_edge[...] = tok[:, tok.shape[1] - half :, :]
+
+
+def round_kernel(ns, conv, inner, outer, vec_m, conv_own, ffn_own, ffn_part, vec_m_near):
+    seq_at = lax.axis_index("seq")
+    in_rows, hid = inner.shape
+    quarter = hid // ns
+    part = outer.shape[0] // ns
+    conv_own[...] = conv[...].astype(BF)
+    for k in range(ns):
+        ffn_own[k * in_rows : (k + 1) * in_rows, :] = inner[
+            :, k * quarter : (k + 1) * quarter
+        ].astype(BF)
+    ffn_own[ns * in_rows :, :] = outer[...].astype(BF)
+    ffn_part[:in_rows, :] = inner[:, at(seq_at, quarter)].astype(BF)
+    ffn_part[in_rows:, :] = outer[at(seq_at, part), :].astype(BF)
+    vec_m_near[...] = vec_m[...]
+
+
+def stack_kernel(*refs):
+    for i, ref in enumerate(refs[:-1]):
+        refs[-1][i] = ref[...]
+
+
+def conv_kernel(taps, nz, ns, lens, vec, tok, left, right, own, other, *rest):
+    pieces = (rest[:ns], rest[ns : 2 * ns])
+    pre, after, full, ext, cid, cat, sems = rest[2 * ns :]
     seq_at, z_at, core_at = place()
     rows, length, width = tok.shape
-    in_rows = own.shape[1]
     quarter = width // ns
     half = DILATION_STEP * (taps // 2)
+    pairs = []
     for i, whole in enumerate((own, other)):
-        block = z_at * 2 + (core_at ^ i)
-        for t in range(taps):
-            full[t, at(block, in_rows), :] = whole[t]
-        for j in range(1, nz):
-            block = (z_at ^ j) * 2 + (core_at ^ i)
-            for k in range(ns):
-                for t in range(taps):
-                    full[t, at(block, in_rows), at(seq_at ^ k, quarter)] = pieces[i][k][j - 1, t]
+        core = core_at ^ i
+        pairs.append((whole, full.at[:, z_at, core]))
+        for k in range(ns):
+            for j in range(1, nz):
+                cols = at(seq_at ^ k, quarter)
+                pairs.append((pieces[i][k].at[j - 1], full.at[:, z_at ^ j, core, :, cols]))
+    copies = begin_copies(pairs, sems)
     span = length + 2 * half
     base = seq_at * length - half
     positions = base + lax.broadcasted_iota(jnp.int32, (span, LANES), 0)
@@ -163,6 +228,7 @@
             cat[r * length : (r + 1) * length, at(tap * (width // LANES) + a, LANES)] = value
 
         masked_taps(ext, cid, length, taps, half, store)
+    end_copies(copies)
     weights = full.reshape(taps * width, width)
 
     def product(r, carry):
@@ -187,28 +253,44 @@
 
 
 def ffn_kernel(nz, ns, *refs):
-    pre, after, cot, vec, inner_own, outer_own, inner_other, outer_other = refs[:8]
-    pieces = (refs[8 : 8 + ns], refs[8 + ns : 8 + 2 * ns])
-    rest = refs[8 + 2 * ns :]
-    layer, after_grad, conv_grad = rest[:3]
-    sends = rest[3 : 3 + ns]
-    low, hidden, outer_grad, inner_grad, inner, outer, slope, tmp, sums = rest[3 + ns :]
+    after, cot, vec = refs[:3]
+    wholes = refs[3:5]
+    pieces = (refs[5 : 5 + ns], refs[5 + ns : 5 + 2 * ns])
+    rest = refs[5 + 2 * ns :]
+    layer, low, hidden, outer_grad, inner_grad, inner_full, sums, outer_full, slope, tmp, sems = rest
     seq_at, z_at, core_at = place()
-    count, width = pre.shape
-    in_rows, hid = inner_own.shape
-    out_rows = outer_own.shape[0]
-    part = out_rows // ns
+    count, width = after.shape
+    hid = inner_full.shape[3]
+    in_rows = inner_full.shape[2]
     quarter = hid // ns
     blocks = hid // width
-    for i, (one, two) in enumerate(((inner_own, outer_own), (inner_other, outer_other))):
-        block = z_at * 2 + (core_at ^ i)
-        inner[at(block, in_rows), :] = one[...]
-        outer[at(block, out_rows), :] = two[...]
-        for j in range(1, nz):
-            block = (z_at ^ j) * 2 + (core_at ^ i)
-            for k in range(ns):
-                inner[at(block, in_rows), at(seq_at ^ k, quarter)] = pieces[i][k][j - 1, :in_rows]
-                outer[at(block * ns + (seq_at ^ k), part), :] = pieces[i][k][j - 1, in_rows:]
+    inner = inner_full.reshape(width, hid)
+    outer = outer_full.reshape(hid, width)
+    part = outer_full.shape[3]
+    pairs = []
+    for i, whole in enumerate(wholes):
+        core = core_at ^ i
+        for q in range(ns):
+            pairs.append(
+                (
+                    whole.at[q * in_rows : (q + 1) * in_rows],
+                    inner_full.at[z_at, core, :, q * quarter : (q + 1) * quarter],
+                )
+            )
+            pairs.append(
+                (
+                    whole.at[ns * in_rows + q * part : ns * in_rows + (q + 1) * part],
+                    outer_full.at[z_at, core, q],
+                )
+            )
+        for k in range(ns):
+            piece = pieces[i][k]
+            q = seq_at ^ k
+            for j in range(1, nz):
+                z = z_at ^ j
+                pairs.append((piece.at[j - 1, :in_rows], inner_full.at[z, core, :, at(q, quarter)]))
+                pairs.append((piece.at[j - 1, in_rows:], outer_full.at[z, core, q]))
+    copies = begin_copies(pairs, sems)
 
     def lower(begin, carry):
         where = pl.ds(begin, 64)
@@ -216,6 +298,7 @@
         return carry
 
     loop_rows(count, 64, lower)
+    end_copies(copies)
 
     def up(b, carry):
         cols = at(b, width)
@@ -272,6 +355,17 @@
         return carry
 
     lax.fori_loop(0, blocks, down, 0)
+
+
+def back_kernel(ns, *refs):
+    pre, cot, vec, inner_grad, inner_full, partial_sums, after_grad, conv_grad = refs[:8]
+    inner = inner_full.reshape(pre.shape[1], inner_grad.shape[1])
+    sends = refs[8 : 8 + ns]
+    tmp, sums = refs[8 + ns :]
+    seq_at = lax.axis_index("seq")
+    count, width = pre.shape
+    zero = jnp.zeros((8, width), F32)
+    sums[...] = partial_sums[...]
     tmp[...] = dot_nt(inner_grad[...], inner[...])
 
     def first(begin, carry):
@@ -357,11 +451,12 @@
 
 def conv_weight_kernel(taps, nz, ns, in_rows, *refs):
     lens = refs[0]
-    toks = refs[1 : 1 + ns]
+    far = refs[1 : 1 + ns]
     grads = refs[1 + ns : 1 + 2 * ns]
-    mine, theirs, padded, cid, cat, total = refs[1 + 2 * ns :]
+    mine, theirs, padded, cid, cat, total, toks, sems = refs[1 + 2 * ns :]
+    copies = begin_copies([(far[k], toks.at[k]) for k in range(ns)], sems)
     seq_at, z_at, core_at = place()
-    rows, length, width = toks[0].shape
+    _, rows, length, width = toks.shape
     span = width // ns
     half = DILATION_STEP * (taps // 2)
     row_length = ns * length
@@ -385,10 +480,11 @@
                 value = jnp.where(keep, padded[pl.ds(begin, length), :], 0.0)
                 low_row = k * count + r * length
                 cat[low_row : low_row + length, t * span : (t + 1) * span] = value.astype(BF)
+    end_copies(copies)
     for k in range(ns):
         value = tree_sum(
             [
-                dot_tn(toks[k][r], cat[k * count + r * length : k * count + (r + 1) * length, :])
+                dot_tn(toks[k, r], cat[k * count + r * length : k * count + (r + 1) * length, :])
                 for r in range(rows)
             ]
         )
@@ -411,7 +507,8 @@
 
 
 def input_grad_kernel(taps, ns, *refs):
-    lens, grad, left, right, after_grad, full, out, ext, cid, cat = refs
+    lens, grad, left, right, after_grad, full_blocks, out, ext, cid, cat = refs
+    full = full_blocks.reshape(taps, grad.shape[1], grad.shape[1])
     seq_at = lax.axis_index("seq")
     rows, half, width = left.shape
     length = grad.shape[0] // rows
@@ -458,9 +555,7 @@
     return vmem_call(
         functools.partial(split_sum_kernel, len(ins)),
         [((rows // parts, cols), BF)] * parts,
-        inputs=len(ins),
-        flops=rows * cols * len(ins),
-        nbytes=2 * rows * cols * (len(ins) + 1),
+        slack=2,
     )(*ins)
 
 
@@ -481,24 +576,51 @@
         encode(out, rows, summed)
 
 
-def final_kernel(count, vec_rows, *refs):
-    ins, outs = refs[:count], refs[count:]
-    out, square = outs[:2]
-    rows = out.shape[0]
-
+def conv_final_kernel(count, vec_rows, *refs):
+    ins, (out, square, vec_sum) = refs[:count], refs[count:]
+    square[...] = summed_square(ins, out)
+    vec_sum[...] = gathered(tree_sum([decode(v, out.shape[0], vec_rows) for v in ins]))
+
+
+def summed_square(ins, out):
     def body(begin, carry):
         where = pl.ds(begin, 64)
         value = tree_sum([v[where, :].astype(F32) for v in ins]).astype(BF)
         out[where, :] = value
         wide = value.astype(F32)
-        folded = fold_rows(wide * wide)
-        return carry + sum(
-            folded[:, a * LANES : (a + 1) * LANES] for a in range(folded.shape[1] // LANES)
-        )
-
-    square[...] = loop_rows(rows, 64, body, jnp.zeros((8, LANES), F32))
-    if vec_rows:
-        outs[2][...] = gathered(tree_sum([decode(v, rows, vec_rows) for v in ins]))
+        return carry + lane_fold(fold_rows(wide * wide))
+
+    rows = ins[0].shape[0] // 64 * 64 if out.shape[0] % 64 else out.shape[0]
+    return loop_rows(min(rows, out.shape[0]), 64, body, jnp.zeros((8, LANES), F32))
+
+
+def lane_fold(v):
+    return sum(v[:, a * LANES : (a + 1) * LANES] for a in range(v.shape[1] // LANES))
+
+
+def ffn_final_kernel(count, *refs):
+    ins, (conv_square, out) = refs[:count], refs[count:]
+    rows = ins[0].shape[0]
+    square = summed_square(ins, out.at[0:rows]) + conv_square[...]
+    high = square.astype(BF)
+    low = (square - high.astype(F32)).astype(BF)
+    zero = jnp.zeros(high.shape, BF)
+    tail = jnp.concatenate([high, low] + [zero] * (out.shape[1] // LANES - 2), axis=1)
+    out[rows : rows + VEC_PAD, :] = jnp.concatenate([tail, jnp.zeros(tail.shape, BF)], axis=0)
+
+
+def square_kernel(count, *refs):
+    ins, out = refs[:count], refs[count]
+    rows = ins[0].shape[0] - VEC_PAD
+    parts = []
+    for v in ins:
+        tail = v[rows : rows + VEC_PAD, :].astype(F32)
+        parts.append(tail[:8, :LANES] + tail[:8, LANES : 2 * LANES])
+    out[...] = tree_sum(parts)
+
+
+def small_sum_kernel(*refs):
+    refs[-1][...] = tree_sum([v[...] for v in refs[:-1]])
 
 
 def adam_math(weight, first, second, gradient, clip, rate, decay):
@@ -512,24 +634,17 @@
 
 
 def adam_kernel(taps, ns, *refs):
-    conv_grads, ffn_grads = refs[:ns], refs[ns : 2 * ns]
-    vec_sum, squares, conv, inner, outer, vec, conv_m, inner_m, outer_m, vec_m = refs[
-        2 * ns : 2 * ns + 10
+    conv_grads = refs[:ns]
+    ffn_grads = refs[ns : 2 * ns]
+    vec_sum, one, two, conv, inner, outer, vec, conv_m, inner_m, outer_m, vec_m = refs[
+        2 * ns : 2 * ns + 11
     ]
-    (
-        norm,
-        new_conv,
-        conv_first,
-        new_inner,
-        inner_first,
-        new_outer,
-        outer_first,
-        new_vec,
-        vec_first,
-        second,
-        outer_second,
-        vec_second,
-    ) = refs[2 * ns + 10 :]
+    norm, new_vec, vec_first = refs[2 * ns + 11 : 2 * ns + 14]
+    outs = refs[2 * ns + 14 : 2 * ns + 21]
+    new_conv, conv_first, new_inner, inner_first, new_outer, outer_first, second = refs[
+        2 * ns + 21 : 2 * ns + 28
+    ]
+    outer_second, vec_second, sems = refs[2 * ns + 28 :]
     seq_at, z_at, core_at = place()
     in_rows, width = conv.shape[1:]
     hid = inner.shape[1]
@@ -539,15 +654,20 @@
     part = out_rows // ns
     vec_count = vec.shape[0]
     vec_grad = vec_sum[0:vec_count, :]
-    total = jnp.sum(squares[...]) + jnp.sum(vec_grad * vec_grad)
+    total = jnp.sum(one[...] + two[...]) + jnp.sum(vec_grad * vec_grad)
     value = jnp.sqrt(jnp.full((1, 1), total, F32))
     norm[...] = value
     clip = clip_level / jnp.maximum(value, clip_level)
-
-    for k in range(ns):
-        cols = at(seq_at ^ k, span)
-
-        def conv_step(t, carry, k=k, cols=cols):
+    going = []
+
+    def send(index, src, dst):
+        copy = pltpu.make_async_copy(src, dst, sems.at[index])
+        copy.start()
+        going.append(copy)
+
+    def conv_step(t, carry):
+        for k in range(ns):
+            cols = at(seq_at ^ k, span)
             w, m, v = adam_math(
                 conv[t, :, cols],
                 conv_m[0, t, :, cols],
@@ -560,33 +680,45 @@
             new_conv[t, :, cols] = w
             conv_first[t, :, cols] = m
             second[:, at(t * ns + (seq_at ^ k), span)] = v
-            return carry
-
-        lax.fori_loop(0, taps, conv_step, 0)
-        for a in range(quarter // LANES):
-            lanes = pl.ds(pl.multiple_of((seq_at ^ k) * quarter + a * LANES, LANES), LANES)
+        return carry
+
+    lax.fori_loop(0, taps, conv_step, 0)
+    send(0, new_conv, outs[0])
+    send(1, conv_first, outs[1])
+    send(2, second.at[:, : taps * width], outs[6].at[:, : taps * width])
+    chunks = quarter // LANES
+
+    for k in range(ns):
+
+        def inner_step(a, carry, k=k):
+            lanes = at((seq_at ^ k) * chunks + a, LANES)
             w, m, v = adam_math(
                 inner[:, lanes],
                 inner_m[0, :, lanes],
                 inner_m[1, :, lanes],
-                ffn_grads[k][0:in_rows, a * LANES : (a + 1) * LANES].astype(F32),
+                ffn_grads[k][0:in_rows, at(a, LANES)].astype(F32),
                 clip,
                 matrix_rate,
                 weight_decay,
             )
             new_inner[:, lanes] = w
             inner_first[:, lanes] = m
-            second[
-                :, pl.ds(pl.multiple_of(taps * width + (seq_at ^ k) * quarter + a * LANES, LANES), LANES)
-            ] = v
+            second[:, at(taps * width // LANES + (seq_at ^ k) * chunks + a, LANES)] = v
+            return carry
+
+        lax.fori_loop(0, chunks, inner_step, 0)
+    send(3, new_inner, outs[2])
+    send(4, inner_first, outs[3])
+    for k in range(ns):
         where = at(seq_at ^ k, part)
-        for a in range(width // LANES):
-            lanes = slice(a * LANES, (a + 1) * LANES)
+
+        def outer_step(a, carry, k=k, where=where):
+            lanes = at(a, LANES)
             w, m, v = adam_math(
                 outer[where, lanes],
                 outer_m[0, where, lanes],
                 outer_m[1, where, lanes],
-                ffn_grads[k][in_rows:, lanes].astype(F32),
+                ffn_grads[k][in_rows : in_rows + part, lanes].astype(F32),
                 clip,
                 matrix_rate,
                 weight_decay,
@@ -594,6 +726,11 @@
             new_outer[where, lanes] = w
             outer_first[where, lanes] = m
             outer_second[a, where, :] = v
+            return carry
+
+        lax.fori_loop(0, width // LANES, outer_step, 0)
+    send(5, new_outer, outs[4])
+    send(6, outer_first, outs[5])
     ratio = out_rows // in_rows
     base = taps * width + hid
     for e in range(ratio):
@@ -608,6 +745,8 @@
     begin = base + ratio * width
     block = z_at * 2 + core_at
     second[:, begin : begin + vec_count] = vec_second[at(block, in_rows), :][:, 0:vec_count]
+    send(7, second.at[:, taps * width :], outs[6].at[:, taps * width :])
+    end_copies(going)
 
 
 def per_device(
@@ -637,121 +776,120 @@
     quarter = hid // ns
     part = out_rows // ns
 
-    left = shift_along(tokens[:, length - half :], "seq", 1)
-    right = shift_along(tokens[:, :half], "seq", -1)
-
-    conv_own = conv_weight.astype(BF)
-    conv_part = lax.dynamic_slice_in_dim(conv_weight, seq_at * span, span, 2).astype(BF)
+    ffn_rows = in_rows + part
+    vec_rows = VEC_PAD * width // LANES
+    conv_rows = taps * in_rows
+    cot = cotangent.reshape(count, width)
+
+    conv_part, left_edge, right_edge = vmem_call(
+        functools.partial(cut_kernel, ns),
+        [((taps, in_rows, span), BF), ((rows, half, width), BF), ((rows, half, width), BF)],
+        slack=2,
+    )(conv_weight, tokens)
     got = [exchange(conv_part, "row", 2 * j) for j in range(1, nz)]
-    got = jnp.stack(got)
+    left = shift_along(right_edge, "seq", 1)
+    right = shift_along(left_edge, "seq", -1)
+    conv_own, ffn_own, ffn_part, vector_near = vmem_call(
+        functools.partial(round_kernel, ns),
+        [
+            (conv_weight.shape, BF),
+            ((ns * ffn_rows, width), BF),
+            ((ffn_rows, width), BF),
+            (vector_moments.shape, F32),
+        ],
+        slack=2,
+    )(conv_weight, inner_weight, outer_weight, vector_moments)
+    conv_other = exchange(conv_own, "row", 1)
+    ffn_other = exchange(ffn_own, "row", 1)
+    got[0], left, right = lax.optimization_barrier((got[0], left, right))
+    (got,) = vmem_call(stack_kernel, [((nz - 1, taps, in_rows, span), BF)], slack=2)(*got)
     conv_pieces = [got] + [exchange(got, "seq", k) for k in range(1, ns)]
-    conv_other = exchange(conv_own, "row", 1)
+    ffn_part, conv_pieces[1] = lax.optimization_barrier((ffn_part, conv_pieces[1]))
+    ffn_got = [exchange(ffn_part, "row", 2 * j) for j in range(1, nz)]
     conv_other_pieces = [exchange(p, "row", 1) for p in conv_pieces]
-
-    inner_own = inner_weight.astype(BF)
-    outer_own = outer_weight.astype(BF)
-    ffn_part = jnp.concatenate(
-        [
-            lax.dynamic_slice_in_dim(inner_weight, seq_at * quarter, quarter, 1),
-            lax.dynamic_slice_in_dim(outer_weight, seq_at * part, part, 0),
-        ],
-        axis=0,
-    ).astype(BF)
-    got = jnp.stack([exchange(ffn_part, "row", 2 * j) for j in range(1, nz)])
-    ffn_pieces = [got] + [exchange(got, "seq", k) for k in range(1, ns)]
-    inner_other = exchange(inner_own, "row", 1)
-    outer_other = exchange(outer_own, "row", 1)
-    ffn_other_pieces = [exchange(p, "row", 1) for p in ffn_pieces]
+    (ffn_got,) = vmem_call(stack_kernel, [((nz - 1, ffn_rows, width), BF)], slack=2)(*ffn_got)
+    ffn_pieces = [ffn_got] + [exchange(ffn_got, "seq", k) for k in range(1, ns)]
 
     pre, after, conv_full = vmem_call(
         functools.partial(conv_kernel, taps, nz, ns),
-        [((count, width), F32), ((count, width), F32), ((taps, width, width), BF)],
+        [((count, width), F32), ((count, width), F32), ((taps, nz, 2, in_rows, width), BF)],
         [
             pltpu.VMEM((length + 2 * half, width), F32),
             pltpu.VMEM((length + 2 * half, LANES), jnp.int32),
             pltpu.VMEM((count, taps * width), BF),
+            pltpu.SemaphoreType.DMA((2 * (1 + ns * (nz - 1)),)),
         ],
         smem=1,
-        inputs=6 + 2 * ns,
-        flops=2 * count * taps * width * width,
-        nbytes=4 * taps * width * width,
+        loose=range(5, 7 + 2 * ns),
     )(
         contig_lengths,
+        vectors,
         tokens,
         left,
         right,
-        vectors,
         conv_own,
         conv_other,
         *conv_pieces,
         *conv_other_pieces,
     )
 
-    tokens_late, _ = lax.optimization_barrier((tokens, ffn_pieces[-1]))
-    token_pieces = [tokens] + [exchange(tokens_late, "seq", k) for k in range(1, ns)]
-
-    results = vmem_call(
+    late = lax.optimization_barrier((pre, tokens, *ffn_pieces))
+    ffn_pieces = late[2:]
+    token_pieces = [tokens] + [exchange(late[1], "seq", k) for k in range(1, ns)]
+    ffn_other_pieces = [exchange(p, "row", 1) for p in ffn_pieces]
+
+    layer_out, low, hidden, outer_grad, inner_grad, inner_full, vec_sums = vmem_call(
         functools.partial(ffn_kernel, nz, ns),
-        [((count, width), BF), ((count, width), F32), ((count, width), BF)]
-        + [((count + 2 * VEC_PAD * width // LANES, span), BF)] * ns
-        + [((count, width), BF), ((count, hid), BF), ((count, width), BF), ((count, hid), BF)],
         [
-            pltpu.VMEM((width, hid), BF),
-            pltpu.VMEM((hid, width), BF),
+            ((count, width), BF),
+            ((count, width), BF),
+            ((count, hid), BF),
+            ((count, width), BF),
+            ((count, hid), BF),
+            ((nz, 2, in_rows, hid), BF),
+            ((VEC_PAD, width), F32),
+        ],
+        [
+            pltpu.VMEM((nz, 2, ns, part, width), BF),
             pltpu.VMEM((count, hid), F32),
             pltpu.VMEM((count, width), F32),
-            pltpu.VMEM((VEC_PAD, width), F32),
+            pltpu.SemaphoreType.DMA((4 * ns * nz,)),
         ],
-        inputs=8 + 2 * ns,
-        flops=8 * count * width * hid,
-        nbytes=20 * width * hid,
-    )(
-        pre,
-        after,
-        cotangent.reshape(count, width),
-        vectors,
-        inner_own,
-        outer_own,
-        inner_other,
-        outer_other,
-        *ffn_pieces,
-        *ffn_other_pieces,
-    )
-    layer_out, after_grad, conv_grad = results[:3]
-    grad_pieces = list(results[3 : 3 + ns])
-    low, hidden, outer_grad, inner_grad = results[3 + ns :]
-    grad_pieces = grad_pieces[:1] + [exchange(grad_pieces[k], "seq", k) for k in range(1, ns)]
-
-    conv_grad_rows = conv_grad.reshape(rows, length, width)
-    grad_left = shift_along(conv_grad_rows[:, length - half :], "seq", 1)
-    grad_right = shift_along(conv_grad_rows[:, :half], "seq", -1)
-
-    ffn_rows = in_rows + part
+        kept=(0,),
+        loose=range(3, 5 + 2 * ns),
+    )(after, cot, vectors, ffn_own, ffn_other, *ffn_pieces, *ffn_other_pieces)
+
     mine, theirs = vmem_call(
         functools.partial(ffn_weight_kernel, nz, ns, in_rows, out_rows),
         [((ns, nz, ffn_rows, width), BF)] * 2,
         [pltpu.VMEM((hid, width), BF), pltpu.VMEM((width, hid), BF)],
-        inputs=4,
-        flops=4 * count * width * hid,
-        nbytes=8 * width * hid,
     )(low, hidden, outer_grad, inner_grad)
+
+    late = lax.optimization_barrier((inner_grad, mine, *token_pieces))
+    inner_grad, mine, token_pieces = late[0], late[1], late[2:]
+    results = vmem_call(
+        functools.partial(back_kernel, ns),
+        [((count, width), F32), ((count, width), BF)]
+        + [((count + 2 * vec_rows, span), BF)] * ns,
+        [pltpu.VMEM((count, width), F32), pltpu.VMEM((VEC_PAD, width), F32)],
+    )(pre, cot, vectors, inner_grad, inner_full, vec_sums)
+    after_grad, conv_grad = results[:2]
+    grad_pieces = list(results[2:])
+    theirs, conv_grad = lax.optimization_barrier((theirs, conv_grad))
     arrived = exchange(theirs, "row", 1)
+    grad_pieces = grad_pieces[:1] + [exchange(grad_pieces[k], "seq", k) for k in range(1, ns)]
+    grad_rows = conv_grad.reshape(rows, length, width)
+    grad_left = shift_along(grad_rows[:, length - half :], "seq", 1)
+    grad_right = shift_along(grad_rows[:, :half], "seq", -1)
+    grad_pieces[0], grad_left, grad_right = lax.optimization_barrier(
+        (grad_pieces[0], grad_left, grad_right)
+    )
+
+    mine, grad_pieces[1] = lax.optimization_barrier((mine, grad_pieces[1]))
     flat = (ns * nz * ffn_rows, width)
-    sums = split_sum([mine.reshape(flat), arrived.reshape(flat)], ns)
-    sums = [sums[0]] + [exchange(sums[k], "seq", k) for k in range(1, ns)]
-    sums = split_sum(sums, nz)
-    sums = [sums[0]] + [exchange(sums[j], "row", 2 * j) for j in range(1, nz)]
-    ffn_sum, ffn_square = vmem_call(
-        functools.partial(final_kernel, nz, 0),
-        [((ffn_rows, width), BF), ((8, LANES), F32)],
-        inputs=nz,
-        flops=ffn_rows * width * nz,
-        nbytes=2 * ffn_rows * width * nz,
-    )(*sums)
-    ffn_sums = [ffn_sum] + [exchange(ffn_sum, "seq", k) for k in range(1, ns)]
-
-    vec_rows = VEC_PAD * width // LANES
-    conv_rows = taps * in_rows
+    ffn_sums = split_sum([mine.reshape(flat), arrived.reshape(flat)], ns)
+    ffn_sums = [ffn_sums[0]] + [exchange(ffn_sums[k], "seq", k) for k in range(1, ns)]
+
     mine, theirs = vmem_call(
         functools.partial(conv_weight_kernel, taps, nz, ns, in_rows),
         [((nz * conv_rows + 2 * vec_rows, span), BF)] * 2,
@@ -760,33 +898,19 @@
             pltpu.VMEM((ns * length + 2 * half, LANES), jnp.int32),
             pltpu.VMEM((ns * count, taps * span), BF),
             pltpu.VMEM((width, taps * span), F32),
+            pltpu.VMEM((ns, rows, length, width), BF),
+            pltpu.SemaphoreType.DMA((ns,)),
         ],
         smem=1,
-        inputs=2 * ns,
-        flops=2 * ns * count * width * taps * span,
-        nbytes=8 * count * width * ns,
+        loose=range(1, 1 + ns),
     )(contig_lengths, *token_pieces, *grad_pieces)
     arrived = exchange(theirs, "row", 1)
     sums = vmem_call(
         functools.partial(conv_core_kernel, conv_rows),
         [((conv_rows + 2 * vec_rows, span), BF)] * nz,
-        inputs=2,
-        flops=4 * conv_rows * nz * span,
-        nbytes=8 * conv_rows * nz * span,
+        slack=2,
     )(mine, arrived)
     sums = [sums[0]] + [exchange(sums[j], "row", 2 * j) for j in range(1, nz)]
-    conv_sum, conv_square, vec_sum = vmem_call(
-        functools.partial(final_kernel, nz, vec_rows),
-        [((conv_rows, span), BF), ((8, LANES), F32), ((VEC_PAD, width), F32)],
-        inputs=nz,
-        flops=conv_rows * span * nz,
-        nbytes=2 * conv_rows * span * nz,
-    )(*sums)
-    conv_sums = [conv_sum] + [exchange(conv_sum, "seq", k) for k in range(1, ns)]
-    square = conv_square + ffn_square
-    squares = lax.all_to_all(
-        jnp.broadcast_to(square[None], (ns * nr, 8, LANES)), ("seq", "row"), 0, 0
-    )
 
     (input_grad,) = vmem_call(
         functools.partial(input_grad_kernel, taps, ns),
@@ -797,49 +921,69 @@
             pltpu.VMEM((taps, count, width), BF),
         ],
         smem=1,
-        inputs=5,
-        flops=2 * count * taps * width * width,
-        nbytes=2 * taps * width * width,
+        kept=(0,),
     )(contig_lengths, conv_grad, grad_left, grad_right, after_grad, conv_full)
+    sums[0], input_grad = lax.optimization_barrier((sums[0], input_grad))
+
+    conv_sum, conv_square, vec_sum = vmem_call(
+        functools.partial(conv_final_kernel, nz, vec_rows),
+        [((conv_rows, span), BF), ((8, LANES), F32), ((VEC_PAD, width), F32)],
+        slack=2,
+    )(*sums)
+    conv_sums = [conv_sum] + [exchange(conv_sum, "seq", k) for k in range(1, ns)]
+
+    ffn_sums = split_sum(ffn_sums, nz)
+    ffn_sums = [ffn_sums[0]] + [exchange(ffn_sums[j], "row", 2 * j) for j in range(1, nz)]
+    ffn_sums[0], conv_sums[-1] = lax.optimization_barrier((ffn_sums[0], conv_sums[-1]))
+    (ffn_sum,) = vmem_call(
+        functools.partial(ffn_final_kernel, nz), [((ffn_rows + VEC_PAD, width), BF)], slack=2
+    )(*ffn_sums, conv_square)
+    ffn_sums = [ffn_sum] + [exchange(ffn_sum, "seq", k) for k in range(1, ns)]
+    (square,) = vmem_call(
+        functools.partial(square_kernel, ns), [((8, LANES), F32)], slack=2
+    )(*ffn_sums)
+    squares = [square] + [exchange(square, "row", 2 * j) for j in range(1, nz)]
+    (square,) = vmem_call(small_sum_kernel, [((8, LANES), F32)], slack=2)(*squares)
+    squares = [square, exchange(square, "row", 1)]
 
     second_width = taps * width + hid + (out_rows // in_rows) * width + vectors.shape[0]
+    results = [
+        (conv_weight.shape, F32),
+        (conv_weight.shape, F32),
+        (inner_weight.shape, F32),
+        (inner_weight.shape, F32),
+        (outer_weight.shape, F32),
+        (outer_weight.shape, F32),
+        ((in_rows, second_width), F32),
+    ]
     (
         norm,
+        new_vectors,
+        vector_first,
         new_conv,
         conv_first,
         new_inner,
         inner_first,
         new_outer,
         outer_first,
-        new_vectors,
-        vector_first,
         second_moments,
     ) = vmem_call(
         functools.partial(adam_kernel, taps, ns),
-        [
-            ((1, 1), F32),
-            (conv_weight.shape, F32),
-            (conv_weight.shape, F32),
-            (inner_weight.shape, F32),
-            (inner_weight.shape, F32),
-            (outer_weight.shape, F32),
-            (outer_weight.shape, F32),
-            (vectors.shape, F32),
-            (vectors.shape, F32),
-            ((in_rows, second_width), F32),
-        ],
-        [
+        [((1, 1), F32), (vectors.shape, F32), (vectors.shape, F32), *results],
+        [pltpu.VMEM(shape, dtype) for shape, dtype in results]
+        + [
             pltpu.VMEM((width // LANES, out_rows, LANES), F32),
             pltpu.VMEM((width, LANES), F32),
+            pltpu.SemaphoreType.DMA((8,)),
         ],
-        inputs=2 * ns + 10,
-        flops=20 * in_rows * second_width,
-        nbytes=28 * in_rows * second_width,
+        kept=range(3),
+        left=range(3, 10),
+        slack=3,
     )(
         *conv_sums,
         *ffn_sums,
         vec_sum,
-        squares,
+        *squares,
         conv_weight,
         inner_weight,
         outer_weight,
@@ -847,7 +991,7 @@
         conv_moments,
         inner_moments,
         outer_moments,
-        vector_moments,
+        vector_near,
     )
     return (
         layer_out.reshape(tokens.shape),

time: 247 us -> 204 us (0.83)
  Pallas kernels: 85.5 us -> 56.9 us
  local copies, waits for them, and re-layouts: 14.9 us -> 2.37 us
    pallas_call x11 -> x18, Pallas kernels: 85.5 us -> 56.9 us  [call(): pl.pallas_call(kernel, out_shape=[jax.ShapeDtypeStruct(shape, dtype) if i...]
    ppermute x4, waiting for transfers between devices: 2.74 us -> 13.5 us  [shift_along(): return lax.ppermute(value, axis, pairs)]
    ppermute x46 -> x49, waiting for transfers between devices: 74.4 us -> 65.5 us  [exchange(): return lax.ppermute(value, axis, [(i, i ^ mask) for i in range(size)])]
    unnamed x101 -> x27, local copies, waits for them, and re-layouts: 9.57 us -> 2.36 us
    all_to_all x1 -> x0, starting transfers between devices: 4.47 us -> none  [per_device(): lax.all_to_all(jnp.broadcast_to(square[None], (ns * nr, 8, LANES)), ('seq...]
    ppermute x46 -> x49, starting transfers between devices: 52.1 us -> 55.4 us  [exchange(): return lax.ppermute(value, axis, [(i, i ^ mask) for i in range(size)])]
  transfers between devices with their start and end apart: 51 -> 53, of which waited for: 17 -> 24; matrix products, arithmetic and copies ran while one was open for 2% -> 0% of each run, Pallas kernels for 18% -> 22%
where the time goes in v2:
time: 204 us
  waiting for transfers between devices  79 us (39%)
  starting transfers between devices  64.4 us (32%)
  Pallas kernels  56.9 us (28%)
  local copies, waits for them, and re-layouts  2.37 us (1%)
    ppermute x49, waiting for transfers between devices, exchange(): return lax.ppermute(value, axis, [(i, i ^ mask) for i in range(size)])  65.5 us
    pallas_call x18, Pallas kernels, call(): pl.pallas_call(kernel, out_shape=[jax.ShapeDtypeStruct(shape, dtype) if i...  56.9 us
    ppermute x49, starting transfers between devices, exchange(): return lax.ppermute(value, axis, [(i, i ^ mask) for i in range(size)])  55.4 us
    ppermute x4, waiting for transfers between devices, shift_along(): return lax.ppermute(value, axis, pairs)  13.5 us
    ppermute x4, starting transfers between devices, shift_along(): return lax.ppermute(value, axis, pairs)  9.07 us
  transfers between devices with their start and end apart: 53, of which 24 were waited for; matrix products, arithmetic and copies ran while one was open for 0% of the time, Pallas kernels for 22%

profile of v2, /device:TPU:0, one launch (start us, length us, event | category | flops | bytes accessed | tf_op | source)
XLA Modules:
  0.0 204.0 jit_solution(8842413579413917320)
XLA Ops:
  3.1 3.1 %collective-permute-start = (bf16[9,64,128]{2,1,0:T(8,128)(2,1)S(1)}, bf16[9,64,128]{2,1,0:T(8,128)(2,1)S(1)}, u32[]{:S(2)}, u32[]{:S(2)}) collective-permute-start(bf16[9,64,128]{2,1,0:T(8,128)(2,1)S(1)} %get-tuple-element.91), channel_id=1, source_target_pairs={{0,2},{1,3},{2,0},{3,1},{4,6},{5,7},{6,4},{7,5},{8,10},{9,11},{10,... | collective-permute-start | bytes 442376 | tf_op jit(solution)/shard_map/ppermute | solution.py:32
  6.2 2.6 %collective-permute-start.4 = (bf16[9,64,128]{2,1,0:T(8,128)(2,1)S(1)}, bf16[9,64,128]{2,1,0:T(8,128)(2,1)S(1)}, u32[]{:S(2)}, u32[]{:S(2)}) collective-permute-start(bf16[9,64,128]{2,1,0:T(8,128)(2,1)S(1)} %get-tuple-element.91), channel_id=1, source_target_pairs={{0,4},{1,5},{2,6},{3,7},{4,0},{5,1},{6,2},{7,3},{8,12},{9,13},{10,... | collective-permute-start | bytes 442376 | tf_op jit(solution)/shard_map/ppermute | solution.py:32
  8.7 3.6 %collective-permute-start.1 = (bf16[2,32,512]{2,1,0:T(8,128)(2,1)S(1)}, bf16[2,32,512]{2,1,0:T(8,128)(2,1)S(1)}, u32[]{:S(2)}, u32[]{:S(2)}) collective-permute-start(bf16[2,32,512]{2,1,0:T(8,128)(2,1)S(1)} %get-tuple-element.92), channel_id=1, source_target_pairs={{0,8},{8,16},{16,24},{1,9},{9,17},{17,25},{2,10},{10,18},{18,26},{... | collective-permute-start | bytes 196616 | tf_op jit(solution)/shard_map/ppermute | solution.py:38
  14.2 4.3 %collective-permute-done.2.right = bf16[2,32,512]{2,1,0:T(8,128)(2,1)S(1)} collective-permute-done((bf16[2,32,512]{2,1,0:T(8,128)(2,1)S(1)}, bf16[2,32,512]{2,1,0:T(8,128)(2,1)S(1)}, u32[]{:S(2)}, u32[]{:S(2)}) %collective-permute-start.2) | collective-permute-done | bytes 65568 | tf_op jit(solution)/shard_map/ppermute | solution.py:38
  24.5 8.9 %collective-permute-done.6.rest_1_ = bf16[3,9,64,128]{3,2,1,0:T(8,128)(2,1)S(1)} collective-permute-done((bf16[3,9,64,128]{3,2,1,0:T(8,128)(2,1)S(1)}, bf16[3,9,64,128]{3,2,1,0:T(8,128)(2,1)S(1)}, u32[]{:S(2)}, u32[]{:S(2)}) %collective-permute-start.6) | collective-permute-done | bytes 442400 | tf_op jit(solution)/shard_map/ppermute | solution.py:32
  33.4 7.0 %collective-permute-done.7.rest_2_ = bf16[3,9,64,128]{3,2,1,0:T(8,128)(2,1)S(1)} collective-permute-done((bf16[3,9,64,128]{3,2,1,0:T(8,128)(2,1)S(1)}, bf16[3,9,64,128]{3,2,1,0:T(8,128)(2,1)S(1)}, u32[]{:S(2)}, u32[]{:S(2)}) %collective-permute-start.7) | collective-permute-done | bytes 442400 | tf_op jit(solution)/shard_map/ppermute | solution.py:32
  40.4 3.6 %collective-permute-start.14 = (bf16[128,512]{1,0:T(8,128)(2,1)S(1)}, bf16[128,512]{1,0:T(8,128)(2,1)S(1)}, u32[]{:S(2)}, u32[]{:S(2)}) collective-permute-start(bf16[128,512]{1,0:T(8,128)(2,1)S(1)} %get-tuple-element.103), channel_id=1, source_target_pairs={{0,2},{1,3},{2,0},{3,1},{4,6},{5,7},{6,4},{7,5},{8,10},{9,11},{10,... | collective-permute-start | bytes 393224 | tf_op jit(solution)/shard_map/ppermute | solution.py:32
  45.2 2.4 %collective-permute-done.14.refs_0_ = bf16[128,512]{1,0:T(8,128)(2,1)S(1)} collective-permute-done((bf16[128,512]{1,0:T(8,128)(2,1)S(1)}, bf16[128,512]{1,0:T(8,128)(2,1)S(1)}, u32[]{:S(2)}, u32[]{:S(2)}) %collective-permute-start.14) | collective-permute-done | bytes 131104 | tf_op jit(solution)/shard_map/ppermute | solution.py:32
  47.6 3.7 %collective-permute-done.15.refs_1_ = bf16[128,512]{1,0:T(8,128)(2,1)S(1)} collective-permute-done((bf16[128,512]{1,0:T(8,128)(2,1)S(1)}, bf16[128,512]{1,0:T(8,128)(2,1)S(1)}, u32[]{:S(2)}, u32[]{:S(2)}) %collective-permute-start.15) | collective-permute-done | bytes 131104 | tf_op jit(solution)/shard_map/ppermute | solution.py:32
  51.3 2.3 %collective-permute-start.16 = (bf16[128,512]{1,0:T(8,128)(2,1)S(1)}, bf16[128,512]{1,0:T(8,128)(2,1)S(1)}, u32[]{:S(2)}, u32[]{:S(2)}) collective-permute-start(bf16[128,512]{1,0:T(8,128)(2,1)S(1)} %get-tuple-element.103), channel_id=1, source_target_pairs={{0,6},{1,7},{2,4},{3,5},{4,2},{5,3},{6,0},{7,1},{8,14},{9,15},{10,... | collective-permute-start | bytes 393224 | tf_op jit(solution)/shard_map/ppermute | solution.py:32
  53.6 4.5 %collective-permute-done.16.refs_2_ = bf16[128,512]{1,0:T(8,128)(2,1)S(1)} collective-permute-done((bf16[128,512]{1,0:T(8,128)(2,1)S(1)}, bf16[128,512]{1,0:T(8,128)(2,1)S(1)}, u32[]{:S(2)}, u32[]{:S(2)}) %collective-permute-start.16) | collective-permute-done | bytes 131104 | tf_op jit(solution)/shard_map/ppermute | solution.py:32
  58.2 2.0 collective-permute-start.18
  61.7 9.1 %shard_map.205 = (f32[512,512]{1,0:T(8,128)S(1)}, f32[512,512]{1,0:T(8,128)S(1)}, bf16[9,4,2,64,512]{4,3,2,1,0:T(8,128)(2,1)S(1)}) custom-call(s32[2,8]{1,0:T(2,128)S(1)} %copy-done.11, f32[10,512]{1,0:T(8,128)S(1)} %copy-done.10, bf16[2,256,512]{2,1,0:T(8,128)(2,1)S(1)} %copy-done.3, bf16[2,32,512]{2,1,0:T(8,128)(2,1)S(1)} %collective-permute-done.1.left, ...), custom_call_target="tpu_custom_call" | custom-call | flops 1 | bytes 1 | tf_op jit(solution)/shard_map/pallas_call | solution.py:118
  70.8 6.6 %collective-permute-done.18.refs_7_ = bf16[3,128,512]{2,1,0:T(8,128)(2,1)S(1)} collective-permute-done((bf16[3,128,512]{2,1,0:T(8,128)(2,1)S(1)}, bf16[3,128,512]{2,1,0:T(8,128)(2,1)S(1)}, u32[]{:S(2)}, u32[]{:S(2)}) %collective-permute-start.18) | collective-permute-done | bytes 393248 | tf_op jit(solution)/shard_map/ppermute | solution.py:32
  85.4 17.9 %shard_map.207 = (bf16[512,512]{1,0:T(8,128)(2,1)}, bf16[512,512]{1,0:T(8,128)(2,1)S(1)}, bf16[512,2048]{1,0:T(8,128)(2,1)S(1)}, bf16[512,512]{1,0:T(8,128)(2,1)...) custom-call(f32[512,512]{1,0:T(8,128)S(1)} %get-tuple-element.100.refs_0_, ...), custom_call_target="tpu_custom_call" | custom-call | flops 1 | bytes 1 | tf_op jit(solution)/shard_map/pallas_call | solution.py:118
  103.3 3.3 %shard_map.208 = (bf16[4,4,128,512]{3,2,1,0:T(8,128)(2,1)S(1)}, bf16[4,4,128,512]{3,2,1,0:T(8,128)(2,1)S(1)}) custom-call(bf16[512,512]{1,0:T(8,128)(2,1)S(1)} %get-tuple-element.110.refs_0_, bf16[512,2048]{1,0:T(8,128)(2,1)S(1)} %get-tuple-element.111.refs_1_, bf16[512,512]{1,0:T(8,128)(2,1)S(1)} %get-tuple-element.112.refs_2_, ...), custom_call_target="tpu_custom_call" | custom-call | flops 1 | bytes 1 | tf_op jit(solution)/shard_map/pallas_call | solution.py:118
  106.6 6.1 %shard_map.209 = (f32[512,512]{1,0:T(8,128)S(1)}, bf16[512,512]{1,0:T(8,128)(2,1)S(1)}, bf16[640,128]{1,0:T(8,128)(2,1)S(1)}, bf16[640,128]{1,0:T(8,128)(2,1)S(1...) custom-call(f32[512,512]{1,0:T(8,128)S(1)} %get-tuple-element.102.refs_0_, bf16[512,512]{1,0:T(8,128)(2,1)S(1)} %bitcast.10, ...), custom_call_target="tpu_custom_call" | custom-call | flops 1 | bytes 1 | tf_op jit(solution)/shard_map/pallas_call | solution.py:118
  116.4 2.7 %collective-permute-start.27 = (bf16[2,32,512]{2,1,0:T(8,128)(2,1)S(1)}, bf16[2,32,512]{2,1,0:T(8,128)(2,1)S(1)}, u32[]{:S(2)}, u32[]{:S(2)}) collective-permute-start(bf16[2,32,512]{2,1,0:T(8,128)(2,1)S(1)} %get-tuple-element.171), channel_id=1, source_target_pairs={{0,8},{8,16},{16,24},{1,9},{9,17},{17,25},{2,10},{10,18},{18,26},{... | collective-permute-start | bytes 196616 | tf_op jit(solution)/shard_map/ppermute | solution.py:38
  119.1 3.5 %collective-permute-done.27.refs_2_ = bf16[2,32,512]{2,1,0:T(8,128)(2,1)S(1)} collective-permute-done((bf16[2,32,512]{2,1,0:T(8,128)(2,1)S(1)}, bf16[2,32,512]{2,1,0:T(8,128)(2,1)S(1)}, u32[]{:S(2)}, u32[]{:S(2)}) %collective-permute-start.27) | collective-permute-done | bytes 65568 | tf_op jit(solution)/shard_map/ppermute | solution.py:38
  124.1 5.1 %collective-permute-done.28.refs_3_ = bf16[2,32,512]{2,1,0:T(8,128)(2,1)S(1)} collective-permute-done((bf16[2,32,512]{2,1,0:T(8,128)(2,1)S(1)}, bf16[2,32,512]{2,1,0:T(8,128)(2,1)S(1)}, u32[]{:S(2)}, u32[]{:S(2)}) %collective-permute-start.28) | collective-permute-done | bytes 65568 | tf_op jit(solution)/shard_map/ppermute | solution.py:38
  129.3 6.4 %shard_map.210 = (bf16[2432,128]{1,0:T(8,128)(2,1)S(1)}, bf16[2432,128]{1,0:T(8,128)(2,1)S(1)}) custom-call(s32[2,8]{1,0:T(2,128)S(1)} %copy-done.11, bf16[2,256,512]{2,1,0:T(8,128)(2,1)S(1)} %copy-done.3, bf16[2,256,512]{2,1,0:T(8,128)(2,1)S(1)} %collective-permute-done.24.refs_2_, bf16[2,256,512]{2,1,0:T(8,128)(2,1)S(1)} %collective-permute-done.25.refs_3_, ...), custom_call_target="tpu_custom_call" | custom-call | flops 1 | bytes 1 | tf_op jit(solution)/shard_map/pallas_call | solution.py:118
  136.5 3.0 %collective-permute-start.39 = (bf16[512,512]{1,0:T(8,128)(2,1)S(1)}, bf16[512,512]{1,0:T(8,128)(2,1)S(1)}, u32[]{:S(2)}, u32[]{:S(2)}) collective-permute-start(bf16[512,512]{1,0:T(8,128)(2,1)S(1)} %get-tuple-element.148), channel_id=1, source_target_pairs={{0,8},{8,0},{16,24},{24,16},{1,9},{9,1},{17,25},{25,17},{2,10},{10... | collective-permute-start | bytes 1572872 | tf_op jit(solution)/shard_map/ppermute | solution.py:32
  141.5 2.9 %collective-permute-start.34 = (bf16[704,128]{1,0:T(8,128)(2,1)S(1)}, bf16[704,128]{1,0:T(8,128)(2,1)S(1)}, u32[]{:S(2)}, u32[]{:S(2)}) collective-permute-start(bf16[704,128]{1,0:T(8,128)(2,1)S(1)} %get-tuple-element.142), channel_id=1, source_target_pairs={{0,4},{1,5},{2,6},{3,7},{4,0},{5,1},{6,2},{7,3},{8,12},{9,13},{10,... | collective-permute-start | bytes 540680 | tf_op jit(solution)/shard_map/ppermute | solution.py:32
  144.3 7.0 %collective-permute-done.33.refs_1_ = bf16[704,128]{1,0:T(8,128)(2,1)S(1)} collective-permute-done((bf16[704,128]{1,0:T(8,128)(2,1)S(1)}, bf16[704,128]{1,0:T(8,128)(2,1)S(1)}, u32[]{:S(2)}, u32[]{:S(2)}) %collective-permute-start.33) | collective-permute-done | bytes 180256 | tf_op jit(solution)/shard_map/ppermute | solution.py:32
  152.8 7.4 %shard_map.212 = f32[512,512]{1,0:T(8,128)} custom-call(s32[2,8]{1,0:T(2,128)S(1)} %copy-done.11, bf16[512,512]{1,0:T(8,128)(2,1)S(1)} %get-tuple-element.125.refs_1_, bf16[2,32,512]{2,1,0:T(8,128)(2,1)S(1)} %collective-permute-done.27.refs_2_, bf16[2,32,512]{2,1,0:T(8,128)(2,1)S(1)} %collective-permute-done.28.refs_3_, ...), custom_call_target="tpu_custom_call" | custom-call | flops 1 | bytes 1 | tf_op jit(solution)/shard_map/pallas_call | solution.py:118
  161.9 6.0 %collective-permute-done.40.refs_2_ = bf16[512,512]{1,0:T(8,128)(2,1)S(1)} collective-permute-done((bf16[512,512]{1,0:T(8,128)(2,1)S(1)}, bf16[512,512]{1,0:T(8,128)(2,1)S(1)}, u32[]{:S(2)}, u32[]{:S(2)}) %collective-permute-start.40) | collective-permute-done | bytes 524320 | tf_op jit(solution)/shard_map/ppermute | solution.py:32
  168.3 2.9 %collective-permute-start.44 = (bf16[128,512]{1,0:T(8,128)(2,1)S(1)}, bf16[128,512]{1,0:T(8,128)(2,1)S(1)}, u32[]{:S(2)}, u32[]{:S(2)}) collective-permute-start(bf16[128,512]{1,0:T(8,128)(2,1)S(1)} %get-tuple-element.155), channel_id=1, source_target_pairs={{0,4},{1,5},{2,6},{3,7},{4,0},{5,1},{6,2},{7,3},{8,12},{9,13},{10,... | collective-permute-start | bytes 393224 | tf_op jit(solution)/shard_map/ppermute | solution.py:32
  178.1 2.2 %collective-permute-start.46 = (bf16[144,512]{1,0:T(8,128)(2,1)S(1)}, bf16[144,512]{1,0:T(8,128)(2,1)S(1)}, u32[]{:S(2)}, u32[]{:S(2)}) collective-permute-start(bf16[144,512]{1,0:T(8,128)(2,1)S(1)} %shard_map.216.refs_0_.refs_4_), channel_id=1, source_target_pairs={{0,8},{8,0},{16,24},{24,16},{1,9},{9,1},{17,25},{25,17},{2,10},{10... | collective-permute-start | bytes 442376 | tf_op jit(solution)/shard_map/ppermute | solution.py:32
  185.0 2.8 %collective-permute-done.47.refs_2_.refs_6_ = bf16[144,512]{1,0:T(8,128)(2,1)S(1)} collective-permute-done((bf16[144,512]{1,0:T(8,128)(2,1)S(1)}, bf16[144,512]{1,0:T(8,128)(2,1)S(1)}, u32[]{:S(2)}, u32[]{:S(2)}) %collective-permute-start.47) | collective-permute-done | bytes 147488 | tf_op jit(solution)/shard_map/ppermute | solution.py:32
  187.8 3.6 %collective-permute-start.49 = (f32[8,128]{1,0:T(8,128)S(1)}, f32[8,128]{1,0:T(8,128)S(1)}, u32[]{:S(2)}, u32[]{:S(2)}) collective-permute-start(f32[8,128]{1,0:T(8,128)S(1)} %shard_map.217.refs_0_), channel_id=1, source_target_pairs={{0,2},{1,3},{2,0},{3,1},{4,6},{5,7},{6,4},{7,5},{8,10},{9,11},{10,... | collective-permute-start | bytes 12296 | tf_op jit(solution)/shard_map/ppermute | solution.py:32
  193.8 2.1 %collective-permute-done.50.refs_2_ = f32[8,128]{1,0:T(8,128)S(1)} collective-permute-done((f32[8,128]{1,0:T(8,128)S(1)}, f32[8,128]{1,0:T(8,128)S(1)}, u32[]{:S(2)}, u32[]{:S(2)}) %collective-permute-start.50) | collective-permute-done | bytes 4128 | tf_op jit(solution)/shard_map/ppermute | solution.py:32
  198.9 4.9 %shard_map.219 = (f32[1,1]{1,0:T(1,128)}, f32[10,512]{1,0:T(8,128)}, f32[10,512]{1,0:T(8,128)}, f32[9,64,512]{2,1,0:T(8,128)}, f32[9,64,512]{2,1,0:T(8,128)}, /*...) custom-call(bf16[576,128]{1,0:T(8,128)(2,1)S(1)} %get-tuple-element., ...), custom_call_target="tpu_custom_call" | custom-call | flops 1 | bytes 1 | tf_op jit(solution)/shard_map/pallas_call | solution.py:118
  (120 shorter events, 49.5 us)
Async XLA Ops:
  3.1 15.5 %collective-permute-start = (bf16[9,64,128]{2,1,0:T(8,128)(2,1)S(1)}, bf16[9,64,128]{2,1,0:T(8,128)(2,1)S(1)}, u32[]{:S(2)}, u32[]{:S(2)}) collective-permute-start(bf16[9,64,128]{2,1,0:T(8,128)(2,1)S(1)} %get-tuple-element.91), channel_id=1, source_target_pairs={{0,2},{1,3},{2,0},{3,1},{4,6},{5,7},{6,4},{7,5},{8,10},{9,11},{10,... | collective-permute-start | bytes 442376 | tf_op jit(solution)/shard_map/ppermute | solution.py:32
  6.2 14.0 %collective-permute-start.4 = (bf16[9,64,128]{2,1,0:T(8,128)(2,1)S(1)}, bf16[9,64,128]{2,1,0:T(8,128)(2,1)S(1)}, u32[]{:S(2)}, u32[]{:S(2)}) collective-permute-start(bf16[9,64,128]{2,1,0:T(8,128)(2,1)S(1)} %get-tuple-element.91), channel_id=1, source_target_pairs={{0,4},{1,5},{2,6},{3,7},{4,0},{5,1},{6,2},{7,3},{8,12},{9,13},{10,... | collective-permute-start | bytes 442376 | tf_op jit(solution)/shard_map/ppermute | solution.py:32
  8.7 11.4 %collective-permute-start.5 = (bf16[9,64,128]{2,1,0:T(8,128)(2,1)S(1)}, bf16[9,64,128]{2,1,0:T(8,128)(2,1)S(1)}, u32[]{:S(2)}, u32[]{:S(2)}) collective-permute-start(bf16[9,64,128]{2,1,0:T(8,128)(2,1)S(1)} %get-tuple-element.91), channel_id=1, source_target_pairs={{0,6},{1,7},{2,4},{3,5},{4,2},{5,3},{6,0},{7,1},{8,14},{9,15},{10,... | collective-permute-start | bytes 442376 | tf_op jit(solution)/shard_map/ppermute | solution.py:32
  20.2 13.2 %collective-permute-start.6 = (bf16[3,9,64,128]{3,2,1,0:T(8,128)(2,1)S(1)}, bf16[3,9,64,128]{3,2,1,0:T(8,128)(2,1)S(1)}, u32[]{:S(2)}, u32[]{:S(2)}) collective-permute-start(bf16[3,9,64,128]{3,2,1,0:T(8,128)(2,1)S(1)} %shard_map.204.rest_0_), channel_id=1, source_target_pairs={{0,8},{8,0},{16,24},{24,16},{1,9},{9,1},{17,25},{25,17},{2,10},{10... | collective-permute-start | bytes 1327112 | tf_op jit(solution)/shard_map/ppermute | solution.py:32
  21.7 18.6 %collective-permute-start.7 = (bf16[3,9,64,128]{3,2,1,0:T(8,128)(2,1)S(1)}, bf16[3,9,64,128]{3,2,1,0:T(8,128)(2,1)S(1)}, u32[]{:S(2)}, u32[]{:S(2)}) collective-permute-start(bf16[3,9,64,128]{3,2,1,0:T(8,128)(2,1)S(1)} %shard_map.204.rest_0_), channel_id=1, source_target_pairs={{0,16},{8,24},{16,0},{24,8},{1,17},{9,25},{17,1},{25,9},{2,18},{10... | collective-permute-start | bytes 1327112 | tf_op jit(solution)/shard_map/ppermute | solution.py:32
  23.3 20.7 %collective-permute-start.8 = (bf16[3,9,64,128]{3,2,1,0:T(8,128)(2,1)S(1)}, bf16[3,9,64,128]{3,2,1,0:T(8,128)(2,1)S(1)}, u32[]{:S(2)}, u32[]{:S(2)}) collective-permute-start(bf16[3,9,64,128]{3,2,1,0:T(8,128)(2,1)S(1)} %shard_map.204.rest_0_), channel_id=1, source_target_pairs={{0,24},{8,16},{16,8},{24,0},{1,25},{9,17},{17,9},{25,1},{2,26},{10... | collective-permute-start | bytes 1327112 | tf_op jit(solution)/shard_map/ppermute | solution.py:32
  23.9 34.2 %collective-permute-start.3 = (bf16[9,64,512]{2,1,0:T(8,128)(2,1)S(1)}, bf16[9,64,512]{2,1,0:T(8,128)(2,1)S(1)}, u32[]{:S(2)}, u32[]{:S(2)}) collective-permute-start(bf16[9,64,512]{2,1,0:T(8,128)(2,1)S(1)} %get-tuple-element.96.own), channel_id=1, source_target_pairs={{0,1},{1,0},{2,3},{3,2},{4,5},{5,4},{6,7},{7,6},{8,9},{9,8},{10,11... | collective-permute-start | bytes 1769480 | tf_op jit(solution)/shard_map/ppermute | solution.py:32
  24.0 34.1 %collective-permute-start.9 = (bf16[3,9,64,128]{3,2,1,0:T(8,128)(2,1)S(1)}, bf16[3,9,64,128]{3,2,1,0:T(8,128)(2,1)S(1)}, u32[]{:S(2)}, u32[]{:S(2)}) collective-permute-start(bf16[3,9,64,128]{3,2,1,0:T(8,128)(2,1)S(1)} %shard_map.204.rest_0_), channel_id=1, source_target_pairs={{0,1},{1,0},{2,3},{3,2},{4,5},{5,4},{6,7},{7,6},{8,9},{9,8},{10,11... | collective-permute-start | bytes 1327112 | tf_op jit(solution)/shard_map/ppermute | solution.py:32
  33.4 26.9 %collective-permute-start.10 = (bf16[3,9,64,128]{3,2,1,0:T(8,128)(2,1)S(1)}, bf16[3,9,64,128]{3,2,1,0:T(8,128)(2,1)S(1)}, u32[]{:S(2)}, u32[]{:S(2)}) collective-permute-start(bf16[3,9,64,128]{3,2,1,0:T(8,128)(2,1)S(1)} %collective-permute-done.6.rest_1_), channel_id=1, source_target_pairs={{0,1},{1,0},{2,3},{3,2},{4,5},{5,4},{6,7},{7,6},{8,9},{9,8},{10,11... | collective-permute-start | bytes 1327112 | tf_op jit(solution)/shard_map/ppermute | solution.py:32
  47.6 14.1 %collective-permute-start.11 = (bf16[3,9,64,128]{3,2,1,0:T(8,128)(2,1)S(1)}, bf16[3,9,64,128]{3,2,1,0:T(8,128)(2,1)S(1)}, u32[]{:S(2)}, u32[]{:S(2)}) collective-permute-start(bf16[3,9,64,128]{3,2,1,0:T(8,128)(2,1)S(1)} %collective-permute-done.7.rest_2_), channel_id=1, source_target_pairs={{0,1},{1,0},{2,3},{3,2},{4,5},{5,4},{6,7},{7,6},{8,9},{9,8},{10,11... | collective-permute-start | bytes 1327112 | tf_op jit(solution)/shard_map/ppermute | solution.py:32
  58.1 12.7 %collective-permute-start.17 = (bf16[3,128,512]{2,1,0:T(8,128)(2,1)S(1)}, bf16[3,128,512]{2,1,0:T(8,128)(2,1)S(1)}, u32[]{:S(2)}, u32[]{:S(2)}) collective-permute-start(bf16[3,128,512]{2,1,0:T(8,128)(2,1)S(1)} %shard_map.206.refs_5_), channel_id=1, source_target_pairs={{0,8},{8,0},{16,24},{24,16},{1,9},{9,1},{17,25},{25,17},{2,10},{10... | collective-permute-start | bytes 1179656 | tf_op jit(solution)/shard_map/ppermute | solution.py:32
  58.2 19.3 %collective-permute-start.18 = (bf16[3,128,512]{2,1,0:T(8,128)(2,1)S(1)}, bf16[3,128,512]{2,1,0:T(8,128)(2,1)S(1)}, u32[]{:S(2)}, u32[]{:S(2)}) collective-permute-start(bf16[3,128,512]{2,1,0:T(8,128)(2,1)S(1)} %shard_map.206.refs_5_), channel_id=1, source_target_pairs={{0,16},{8,24},{16,0},{24,8},{1,17},{9,25},{17,1},{25,9},{2,18},{10... | collective-permute-start | bytes 1179656 | tf_op jit(solution)/shard_map/ppermute | solution.py:32
  60.2 18.8 %collective-permute-start.19 = (bf16[3,128,512]{2,1,0:T(8,128)(2,1)S(1)}, bf16[3,128,512]{2,1,0:T(8,128)(2,1)S(1)}, u32[]{:S(2)}, u32[]{:S(2)}) collective-permute-start(bf16[3,128,512]{2,1,0:T(8,128)(2,1)S(1)} %shard_map.206.refs_5_), channel_id=1, source_target_pairs={{0,24},{8,16},{16,8},{24,0},{1,25},{9,17},{17,9},{25,1},{2,26},{10... | collective-permute-start | bytes 1179656 | tf_op jit(solution)/shard_map/ppermute | solution.py:32
  61.7 20.2 %collective-permute-start.13 = (bf16[512,512]{1,0:T(8,128)(2,1)S(1)}, bf16[512,512]{1,0:T(8,128)(2,1)S(1)}, u32[]{:S(2)}, u32[]{:S(2)}) collective-permute-start(bf16[512,512]{1,0:T(8,128)(2,1)S(1)} %get-tuple-element.101.refs_3_), channel_id=1, source_target_pairs={{0,1},{1,0},{2,3},{3,2},{4,5},{5,4},{6,7},{7,6},{8,9},{9,8},{10,11... | collective-permute-start | bytes 1572872 | tf_op jit(solution)/shard_map/ppermute | solution.py:32
  79.6 27.0 %collective-permute-start.24 = (bf16[2,256,512]{2,1,0:T(8,128)(2,1)S(1)}, bf16[2,256,512]{2,1,0:T(8,128)(2,1)S(1)}, u32[]{:S(2)}, u32[]{:S(2)}) collective-permute-start(bf16[2,256,512]{2,1,0:T(8,128)(2,1)S(1)} %copy-done.3), channel_id=1, source_target_pairs={{0,8},{8,0},{16,24},{24,16},{1,9},{9,1},{17,25},{25,17},{2,10},{10... | collective-permute-start | bytes 1572872 | tf_op jit(solution)/shard_map/ppermute | solution.py:32
  80.4 26.2 %collective-permute-start.25 = (bf16[2,256,512]{2,1,0:T(8,128)(2,1)S(1)}, bf16[2,256,512]{2,1,0:T(8,128)(2,1)S(1)}, u32[]{:S(2)}, u32[]{:S(2)}) collective-permute-start(bf16[2,256,512]{2,1,0:T(8,128)(2,1)S(1)} %copy-done.3), channel_id=1, source_target_pairs={{0,16},{8,24},{16,0},{24,8},{1,17},{9,25},{17,1},{25,9},{2,18},{10... | collective-permute-start | bytes 1572872 | tf_op jit(solution)/shard_map/ppermute | solution.py:32
  81.9 24.7 %collective-permute-start.26 = (bf16[2,256,512]{2,1,0:T(8,128)(2,1)S(1)}, bf16[2,256,512]{2,1,0:T(8,128)(2,1)S(1)}, u32[]{:S(2)}, u32[]{:S(2)}) collective-permute-start(bf16[2,256,512]{2,1,0:T(8,128)(2,1)S(1)} %copy-done.3), channel_id=1, source_target_pairs={{0,24},{8,16},{16,8},{24,0},{1,25},{9,17},{17,9},{25,1},{2,26},{10... | collective-permute-start | bytes 1572872 | tf_op jit(solution)/shard_map/ppermute | solution.py:32
  112.7 23.1 %collective-permute-start.38 = (bf16[4,4,128,512]{3,2,1,0:T(8,128)(2,1)S(1)}, bf16[4,4,128,512]{3,2,1,0:T(8,128)(2,1)S(1)}, u32[]{:S(2)}, u32[]{:S(2)}) collective-permute-start(bf16[4,4,128,512]{3,2,1,0:T(8,128)(2,1)S(1)} %get-tuple-element.146), channel_id=1, source_target_pairs={{0,1},{1,0},{2,3},{3,2},{4,5},{5,4},{6,7},{7,6},{8,9},{9,8},{10,11... | collective-permute-start | bytes 6291464 | tf_op jit(solution)/shard_map/ppermute | solution.py:32
  112.9 16.4 %collective-permute-start.29 = (bf16[640,128]{1,0:T(8,128)(2,1)S(1)}, bf16[640,128]{1,0:T(8,128)(2,1)S(1)}, u32[]{:S(2)}, u32[]{:S(2)}) collective-permute-start(bf16[640,128]{1,0:T(8,128)(2,1)S(1)} %get-tuple-element.128), channel_id=1, source_target_pairs={{0,8},{8,0},{16,24},{24,16},{1,9},{9,1},{17,25},{25,17},{2,10},{10... | collective-permute-start | bytes 491528 | tf_op jit(solution)/shard_map/ppermute | solution.py:32
  113.7 15.6 %collective-permute-start.30 = (bf16[640,128]{1,0:T(8,128)(2,1)S(1)}, bf16[640,128]{1,0:T(8,128)(2,1)S(1)}, u32[]{:S(2)}, u32[]{:S(2)}) collective-permute-start(bf16[640,128]{1,0:T(8,128)(2,1)S(1)} %get-tuple-element.130), channel_id=1, source_target_pairs={{0,16},{8,24},{16,0},{24,8},{1,17},{9,25},{17,1},{25,9},{2,18},{10... | collective-permute-start | bytes 491528 | tf_op jit(solution)/shard_map/ppermute | solution.py:32
  115.2 14.1 %collective-permute-start.31 = (bf16[640,128]{1,0:T(8,128)(2,1)S(1)}, bf16[640,128]{1,0:T(8,128)(2,1)S(1)}, u32[]{:S(2)}, u32[]{:S(2)}) collective-permute-start(bf16[640,128]{1,0:T(8,128)(2,1)S(1)} %get-tuple-element.131), channel_id=1, source_target_pairs={{0,24},{8,16},{16,8},{24,0},{1,25},{9,17},{17,9},{25,1},{2,26},{10... | collective-permute-start | bytes 491528 | tf_op jit(solution)/shard_map/ppermute | solution.py:32
  136.5 25.4 %collective-permute-start.39 = (bf16[512,512]{1,0:T(8,128)(2,1)S(1)}, bf16[512,512]{1,0:T(8,128)(2,1)S(1)}, u32[]{:S(2)}, u32[]{:S(2)}) collective-permute-start(bf16[512,512]{1,0:T(8,128)(2,1)S(1)} %get-tuple-element.148), channel_id=1, source_target_pairs={{0,8},{8,0},{16,24},{24,16},{1,9},{9,1},{17,25},{25,17},{2,10},{10... | collective-permute-start | bytes 1572872 | tf_op jit(solution)/shard_map/ppermute | solution.py:32
  139.5 28.4 %collective-permute-start.40 = (bf16[512,512]{1,0:T(8,128)(2,1)S(1)}, bf16[512,512]{1,0:T(8,128)(2,1)S(1)}, u32[]{:S(2)}, u32[]{:S(2)}) collective-permute-start(bf16[512,512]{1,0:T(8,128)(2,1)S(1)} %get-tuple-element.149), channel_id=1, source_target_pairs={{0,16},{8,24},{16,0},{24,8},{1,17},{9,25},{17,1},{25,9},{2,18},{10... | collective-permute-start | bytes 1572872 | tf_op jit(solution)/shard_map/ppermute | solution.py:32
  139.5 28.4 %collective-permute-start.41 = (bf16[512,512]{1,0:T(8,128)(2,1)S(1)}, bf16[512,512]{1,0:T(8,128)(2,1)S(1)}, u32[]{:S(2)}, u32[]{:S(2)}) collective-permute-start(bf16[512,512]{1,0:T(8,128)(2,1)S(1)} %get-tuple-element.150), channel_id=1, source_target_pairs={{0,24},{8,16},{16,8},{24,0},{1,25},{9,17},{17,9},{25,1},{2,26},{10... | collective-permute-start | bytes 1572872 | tf_op jit(solution)/shard_map/ppermute | solution.py:32
  141.4 9.9 %collective-permute-start.33 = (bf16[704,128]{1,0:T(8,128)(2,1)S(1)}, bf16[704,128]{1,0:T(8,128)(2,1)S(1)}, u32[]{:S(2)}, u32[]{:S(2)}) collective-permute-start(bf16[704,128]{1,0:T(8,128)(2,1)S(1)} %get-tuple-element.141), channel_id=1, source_target_pairs={{0,2},{1,3},{2,0},{3,1},{4,6},{5,7},{6,4},{7,5},{8,10},{9,11},{10,... | collective-permute-start | bytes 540680 | tf_op jit(solution)/shard_map/ppermute | solution.py:32
  141.5 18.8 %collective-permute-start.34 = (bf16[704,128]{1,0:T(8,128)(2,1)S(1)}, bf16[704,128]{1,0:T(8,128)(2,1)S(1)}, u32[]{:S(2)}, u32[]{:S(2)}) collective-permute-start(bf16[704,128]{1,0:T(8,128)(2,1)S(1)} %get-tuple-element.142), channel_id=1, source_target_pairs={{0,4},{1,5},{2,6},{3,7},{4,0},{5,1},{6,2},{7,3},{8,12},{9,13},{10,... | collective-permute-start | bytes 540680 | tf_op jit(solution)/shard_map/ppermute | solution.py:32
  151.3 8.9 %collective-permute-start.35 = (bf16[704,128]{1,0:T(8,128)(2,1)S(1)}, bf16[704,128]{1,0:T(8,128)(2,1)S(1)}, u32[]{:S(2)}, u32[]{:S(2)}) collective-permute-start(bf16[704,128]{1,0:T(8,128)(2,1)S(1)} %get-tuple-element.143), channel_id=1, source_target_pairs={{0,6},{1,7},{2,4},{3,5},{4,2},{5,3},{6,0},{7,1},{8,14},{9,15},{10,... | collective-permute-start | bytes 540680 | tf_op jit(solution)/shard_map/ppermute | solution.py:32
  160.4 12.2 %collective-permute-start.42 = (bf16[576,128]{1,0:T(8,128)(2,1)S(1)}, bf16[576,128]{1,0:T(8,128)(2,1)S(1)}, u32[]{:S(2)}, u32[]{:S(2)}) collective-permute-start(bf16[576,128]{1,0:T(8,128)(2,1)S(1)} %get-tuple-element.144.refs_0_), channel_id=1, source_target_pairs={{0,24},{8,16},{16,8},{24,0},{1,25},{9,17},{17,9},{25,1},{2,26},{10... | collective-permute-start | bytes 442376 | tf_op jit(solution)/shard_map/ppermute | solution.py:32
  168.3 8.1 %collective-permute-start.44 = (bf16[128,512]{1,0:T(8,128)(2,1)S(1)}, bf16[128,512]{1,0:T(8,128)(2,1)S(1)}, u32[]{:S(2)}, u32[]{:S(2)}) collective-permute-start(bf16[128,512]{1,0:T(8,128)(2,1)S(1)} %get-tuple-element.155), channel_id=1, source_target_pairs={{0,4},{1,5},{2,6},{3,7},{4,0},{5,1},{6,2},{7,3},{8,12},{9,13},{10,... | collective-permute-start | bytes 393224 | tf_op jit(solution)/shard_map/ppermute | solution.py:32
  180.3 7.4 %collective-permute-start.47 = (bf16[144,512]{1,0:T(8,128)(2,1)S(1)}, bf16[144,512]{1,0:T(8,128)(2,1)S(1)}, u32[]{:S(2)}, u32[]{:S(2)}) collective-permute-start(bf16[144,512]{1,0:T(8,128)(2,1)S(1)} %shard_map.216.refs_0_.refs_4_), channel_id=1, source_target_pairs={{0,16},{8,24},{16,0},{24,8},{1,17},{9,25},{17,1},{25,9},{2,18},{10... | collective-permute-start | bytes 442376 | tf_op jit(solution)/shard_map/ppermute | solution.py:32
  181.9 15.9 %collective-permute-start.36 = (bf16[576,128]{1,0:T(8,128)(2,1)S(1)}, bf16[576,128]{1,0:T(8,128)(2,1)S(1)}, u32[]{:S(2)}, u32[]{:S(2)}) collective-permute-start(bf16[576,128]{1,0:T(8,128)(2,1)S(1)} %get-tuple-element.144.refs_0_), channel_id=1, source_target_pairs={{0,8},{8,0},{16,24},{24,16},{1,9},{9,1},{17,25},{25,17},{2,10},{10... | collective-permute-start | bytes 442376 | tf_op jit(solution)/shard_map/ppermute | solution.py:32
  183.8 14.0 %collective-permute-start.37 = (bf16[576,128]{1,0:T(8,128)(2,1)S(1)}, bf16[576,128]{1,0:T(8,128)(2,1)S(1)}, u32[]{:S(2)}, u32[]{:S(2)}) collective-permute-start(bf16[576,128]{1,0:T(8,128)(2,1)S(1)} %get-tuple-element.144.refs_0_), channel_id=1, source_target_pairs={{0,16},{8,24},{16,0},{24,8},{1,17},{9,25},{17,1},{25,9},{2,18},{10... | collective-permute-start | bytes 442376 | tf_op jit(solution)/shard_map/ppermute | solution.py:32
  (34 other events, 520.2 us)

commit v3 on v2

--- a/solution.py
+++ b/solution.py
@@ -101,7 +101,7 @@
     return total
 
 
-def vmem_call(kernel, outs, scratch=(), smem=0, loose=(), kept=(), left=(), slack=6):
+def vmem_call(kernel, outs, scratch=(), smem=0, loose=(), far=(), kept=(), left=(), slack=6):
     space = pl.BlockSpec(memory_space=pltpu.VMEM)
     anywhere = pl.BlockSpec(memory_space=pl.ANY)
     grant = slack * 1024 * 1024
@@ -112,7 +112,7 @@
         fixed = [
             a
             if i < smem or i in loose
-            else pltpu.with_memory_space_constraint(a, pltpu.VMEM)
+            else pltpu.with_memory_space_constraint(a, pltpu.HBM if i in far else pltpu.VMEM)
             for i, a in enumerate(args)
         ]
         return pl.pallas_call(
@@ -122,7 +122,13 @@
                 for i, (shape, dtype) in enumerate(outs)
             ],
             in_specs=[
-                pl.BlockSpec(memory_space=pltpu.SMEM) if i < smem else anywhere if i in loose else space
+                pl.BlockSpec(memory_space=pltpu.SMEM)
+                if i < smem
+                else pl.BlockSpec(memory_space=pltpu.HBM)
+                if i in far
+                else anywhere
+                if i in loose
+                else space
                 for i in range(len(args))
             ],
             out_specs=[anywhere if i in left else space for i in range(len(outs))],
@@ -170,20 +176,30 @@
     lax.fori_loop(0, taps, body, 0)
 
 
-def cut_kernel(ns, conv, tok, part, left_edge, right_edge):
-    seq_at = lax.axis_index("seq")
+def round_kernel(ns, conv_far, inner_far, outer_far, tok_far, *refs):
+    conv_part, left_edge, right_edge, conv_own, ffn_own, ffn_part = refs[:6]
+    conv, inner, outer, sems = refs[6:]
     half = left_edge.shape[1]
-    part[...] = conv[:, :, at(seq_at, conv.shape[2] // ns)].astype(BF)
-    left_edge[...] = tok[:, :half, :]
-    right_edge[...] = tok[:, tok.shape[1] - half :, :]
-
-
-def round_kernel(ns, conv, inner, outer, vec_m, conv_own, ffn_own, ffn_part, vec_m_near):
+    copies = begin_copies(
+        [
+            (conv_far, conv),
+            (inner_far, inner),
+            (outer_far, outer),
+            (tok_far.at[:, :half], left_edge),
+            (tok_far.at[:, tok_far.shape[1] - half :], right_edge),
+        ],
+        sems,
+    )
     seq_at = lax.axis_index("seq")
     in_rows, hid = inner.shape
     quarter = hid // ns
     part = outer.shape[0] // ns
-    conv_own[...] = conv[...].astype(BF)
+    span = conv.shape[2] // ns
+    copies[0].wait()
+    for t in range(conv.shape[0]):
+        conv_own[t] = conv[t].astype(BF)
+        conv_part[t] = conv[t, :, at(seq_at, span)].astype(BF)
+    end_copies(copies[1:])
     for k in range(ns):
         ffn_own[k * in_rows : (k + 1) * in_rows, :] = inner[
             :, k * quarter : (k + 1) * quarter
@@ -191,12 +207,15 @@
     ffn_own[ns * in_rows :, :] = outer[...].astype(BF)
     ffn_part[:in_rows, :] = inner[:, at(seq_at, quarter)].astype(BF)
     ffn_part[in_rows:, :] = outer[at(seq_at, part), :].astype(BF)
-    vec_m_near[...] = vec_m[...]
-
-
-def stack_kernel(*refs):
-    for i, ref in enumerate(refs[:-1]):
-        refs[-1][i] = ref[...]
+
+
+def stack_kernel(count, *refs):
+    ins, rest = refs[:count], refs[count:]
+    out = rest[len(rest) // 2]
+    for i, ref in enumerate(ins):
+        out[i] = ref[...]
+    if len(rest) > 1:
+        rest[2][...] = rest[0][...]
 
 
 def conv_kernel(taps, nz, ns, lens, vec, tok, left, right, own, other, *rest):
@@ -357,7 +376,7 @@
     lax.fori_loop(0, blocks, down, 0)
 
 
-def back_kernel(ns, *refs):
+def back_kernel(ns, rows, *refs):
     pre, cot, vec, inner_grad, inner_full, partial_sums, after_grad, conv_grad = refs[:8]
     inner = inner_full.reshape(pre.shape[1], inner_grad.shape[1])
     sends = refs[8 : 8 + ns]
@@ -393,6 +412,17 @@
     for k in range(ns):
         sends[k][0:count, :] = conv_grad[:, at(seq_at ^ k, span)]
         encode(sends[k], count, spread(sums[...]))
+        begin = count + 2 * VEC_PAD * width // LANES
+        if sends[k].shape[0] > begin:
+            half = (sends[k].shape[0] - begin) // rows // (width // LANES)
+            length = count // rows
+            first = jnp.where((seq_at ^ k) > seq_at, length - half, 0)
+            for r in range(rows):
+                for a in range(width // LANES):
+                    sends[k][begin : begin + half, :] = conv_grad[
+                        at(r * (length // half) + first // half, half), a * LANES : (a + 1) * LANES
+                    ]
+                    begin += half
 
 
 def spread(v):
@@ -500,24 +530,39 @@
                 out[begin : begin + in_rows, :] = total[
                     at(block, in_rows), t * span : (t + 1) * span
                 ].astype(BF)
-    vec_rows = (grads[0].shape[0] - count) // 2
+    vec_rows = VEC_PAD * width // LANES
     summed = tree_sum([decode(g, count, vec_rows) for g in grads])
     for out in (mine, theirs):
         encode(out, nz * taps * in_rows, summed)
 
 
-def input_grad_kernel(taps, ns, *refs):
-    lens, grad, left, right, after_grad, full_blocks, out, ext, cid, cat = refs
+def input_grad_kernel(taps, ns, rows, masks, *refs):
+    lens, grad, after_grad, full_blocks = refs[:4]
+    pieces = refs[4 : 4 + len(masks)]
+    out, ext, cid, cat = refs[4 + len(masks) :]
     full = full_blocks.reshape(taps, grad.shape[1], grad.shape[1])
     seq_at = lax.axis_index("seq")
-    rows, half, width = left.shape
+    half = DILATION_STEP * (taps // 2)
+    width = grad.shape[1]
     length = grad.shape[0] // rows
     base = seq_at * length - half
     positions = base + lax.broadcasted_iota(jnp.int32, (length + 2 * half, LANES), 0)
+    ext[0:half, :] = jnp.zeros((half, width), F32)
+    ext[half + length :, :] = jnp.zeros((half, width), F32)
     for r in range(rows):
-        ext[0:half, :] = left[r].astype(F32)
         ext[half : half + length, :] = grad[r * length : (r + 1) * length, :].astype(F32)
-        ext[half + length :, :] = right[r].astype(F32)
+        for mask, piece in zip(masks, pieces):
+            for step, begin in ((-1, 0), (1, half + length)):
+
+                @pl.when((seq_at ^ mask) == seq_at + step)
+                def _(r=r, piece=piece, begin=begin):
+                    first = piece.shape[0] - rows * half * (width // LANES)
+                    for a in range(width // LANES):
+                        low = first + (r * (width // LANES) + a) * half
+                        ext[begin : begin + half, a * LANES : (a + 1) * LANES] = piece[
+                            low : low + half, :
+                        ].astype(F32)
+
         cid[...] = contigs(lens, r, positions, length * ns)
 
         def store(tap, a, value, r=r):
@@ -781,33 +826,53 @@
     conv_rows = taps * in_rows
     cot = cotangent.reshape(count, width)
 
-    conv_part, left_edge, right_edge = vmem_call(
-        functools.partial(cut_kernel, ns),
-        [((taps, in_rows, span), BF), ((rows, half, width), BF), ((rows, half, width), BF)],
-        slack=2,
-    )(conv_weight, tokens)
-    got = [exchange(conv_part, "row", 2 * j) for j in range(1, nz)]
-    left = shift_along(right_edge, "seq", 1)
-    right = shift_along(left_edge, "seq", -1)
-    conv_own, ffn_own, ffn_part, vector_near = vmem_call(
+    def edge_rows(k):
+        near = any(abs((i ^ k) - i) == 1 for i in range(ns))
+        return rows * half * (width // LANES) if near else 0
+
+    conv_part, left_edge, right_edge, conv_own, ffn_own, ffn_part = vmem_call(
         functools.partial(round_kernel, ns),
         [
+            ((taps, in_rows, span), BF),
+            ((rows, half, width), BF),
+            ((rows, half, width), BF),
             (conv_weight.shape, BF),
             ((ns * ffn_rows, width), BF),
             ((ffn_rows, width), BF),
-            (vector_moments.shape, F32),
         ],
+        [
+            pltpu.VMEM(conv_weight.shape, F32),
+            pltpu.VMEM(inner_weight.shape, F32),
+            pltpu.VMEM(outer_weight.shape, F32),
+            pltpu.SemaphoreType.DMA((5,)),
+        ],
+        far=range(4),
         slack=2,
-    )(conv_weight, inner_weight, outer_weight, vector_moments)
+    )(conv_weight, inner_weight, outer_weight, tokens)
+    got = [exchange(conv_part, "row", 2 * j) for j in range(1, nz)]
+    got[0], conv_own, ffn_own = lax.optimization_barrier((got[0], conv_own, ffn_own))
+    left = shift_along(right_edge, "seq", 1)
+    right = shift_along(left_edge, "seq", -1)
     conv_other = exchange(conv_own, "row", 1)
     ffn_other = exchange(ffn_own, "row", 1)
     got[0], left, right = lax.optimization_barrier((got[0], left, right))
-    (got,) = vmem_call(stack_kernel, [((nz - 1, taps, in_rows, span), BF)], slack=2)(*got)
+    (got,) = vmem_call(
+        functools.partial(stack_kernel, nz - 1), [((nz - 1, taps, in_rows, span), BF)], slack=2
+    )(*got)
     conv_pieces = [got] + [exchange(got, "seq", k) for k in range(1, ns)]
-    ffn_part, conv_pieces[1] = lax.optimization_barrier((ffn_part, conv_pieces[1]))
-    ffn_got = [exchange(ffn_part, "row", 2 * j) for j in range(1, nz)]
-    conv_other_pieces = [exchange(p, "row", 1) for p in conv_pieces]
-    (ffn_got,) = vmem_call(stack_kernel, [((nz - 1, ffn_rows, width), BF)], slack=2)(*ffn_got)
+    conv_other_pieces = [exchange(got, "row", 1)]
+    ffn_part, conv_other_pieces[0], conv_other, ffn_other = lax.optimization_barrier(
+        (ffn_part, conv_other_pieces[0], conv_other, ffn_other)
+    )
+    ffn_got = [exchange(ffn_part, "row", 2 * j) for j in range(nz - 1, 0, -1)][::-1]
+    late = lax.optimization_barrier((*ffn_got, *conv_pieces[1:]))
+    ffn_got, conv_pieces[1:] = late[: nz - 1], late[nz - 1 :]
+    conv_other_pieces += [exchange(p, "row", 1) for p in conv_pieces[1:]]
+    ffn_got, vector_near = vmem_call(
+        functools.partial(stack_kernel, nz - 1),
+        [((nz - 1, ffn_rows, width), BF), (vector_moments.shape, F32)],
+        slack=2,
+    )(*ffn_got, vector_moments)
     ffn_pieces = [ffn_got] + [exchange(ffn_got, "seq", k) for k in range(1, ns)]
 
     pre, after, conv_full = vmem_call(
@@ -833,9 +898,10 @@
         *conv_other_pieces,
     )
 
-    late = lax.optimization_barrier((pre, tokens, *ffn_pieces))
-    ffn_pieces = late[2:]
-    token_pieces = [tokens] + [exchange(late[1], "seq", k) for k in range(1, ns)]
+    pre, tokens_late = lax.optimization_barrier((pre, tokens))
+    token_pieces = [tokens] + [exchange(tokens_late, "seq", k) for k in range(1, ns)]
+    late = lax.optimization_barrier((pre, *ffn_pieces))
+    pre, ffn_pieces = late[0], late[1:]
     ffn_other_pieces = [exchange(p, "row", 1) for p in ffn_pieces]
 
     layer_out, low, hidden, outer_grad, inner_grad, inner_full, vec_sums = vmem_call(
@@ -865,26 +931,22 @@
         [pltpu.VMEM((hid, width), BF), pltpu.VMEM((width, hid), BF)],
     )(low, hidden, outer_grad, inner_grad)
 
-    late = lax.optimization_barrier((inner_grad, mine, *token_pieces))
-    inner_grad, mine, token_pieces = late[0], late[1], late[2:]
+    inner_grad, mine = lax.optimization_barrier((inner_grad, mine))
     results = vmem_call(
-        functools.partial(back_kernel, ns),
+        functools.partial(back_kernel, ns, rows),
         [((count, width), F32), ((count, width), BF)]
-        + [((count + 2 * vec_rows, span), BF)] * ns,
+        + [
+            ((count + 2 * vec_rows + edge_rows(k), span), BF)
+            for k in range(ns)
+        ],
         [pltpu.VMEM((count, width), F32), pltpu.VMEM((VEC_PAD, width), F32)],
     )(pre, cot, vectors, inner_grad, inner_full, vec_sums)
     after_grad, conv_grad = results[:2]
     grad_pieces = list(results[2:])
-    theirs, conv_grad = lax.optimization_barrier((theirs, conv_grad))
+    late = lax.optimization_barrier((theirs, *grad_pieces, *token_pieces))
+    theirs, grad_pieces, token_pieces = late[0], list(late[1 : 1 + ns]), late[1 + ns :]
     arrived = exchange(theirs, "row", 1)
     grad_pieces = grad_pieces[:1] + [exchange(grad_pieces[k], "seq", k) for k in range(1, ns)]
-    grad_rows = conv_grad.reshape(rows, length, width)
-    grad_left = shift_along(grad_rows[:, length - half :], "seq", 1)
-    grad_right = shift_along(grad_rows[:, :half], "seq", -1)
-    grad_pieces[0], grad_left, grad_right = lax.optimization_barrier(
-        (grad_pieces[0], grad_left, grad_right)
-    )
-
     mine, grad_pieces[1] = lax.optimization_barrier((mine, grad_pieces[1]))
     flat = (ns * nz * ffn_rows, width)
     ffn_sums = split_sum([mine.reshape(flat), arrived.reshape(flat)], ns)
@@ -912,8 +974,9 @@
     )(mine, arrived)
     sums = [sums[0]] + [exchange(sums[j], "row", 2 * j) for j in range(1, nz)]
 
+    masks = [k for k in range(ns) if edge_rows(k)]
     (input_grad,) = vmem_call(
-        functools.partial(input_grad_kernel, taps, ns),
+        functools.partial(input_grad_kernel, taps, ns, rows, masks),
         [((count, width), F32)],
         [
             pltpu.VMEM((length + 2 * half, width), F32),
@@ -922,7 +985,7 @@
         ],
         smem=1,
         kept=(0,),
-    )(contig_lengths, conv_grad, grad_left, grad_right, after_grad, conv_full)
+    )(contig_lengths, conv_grad, after_grad, conv_full, *[grad_pieces[k] for k in masks])
     sums[0], input_grad = lax.optimization_barrier((sums[0], input_grad))
 
     conv_sum, conv_square, vec_sum = vmem_call(

time: 204 us -> 187 us (0.917)
  waiting for transfers between devices: 79 us -> 64.6 us
  local copies, waits for them, and re-layouts: 2.37 us -> 0.06 us
  starting transfers between devices: 64.4 us -> 62.1 us
    ppermute x4 -> x2, waiting for transfers between devices: 13.5 us -> 4.85 us  [shift_along(): return lax.ppermute(value, axis, pairs)]
    ppermute x49, waiting for transfers between devices: 65.5 us -> 59.8 us  [exchange(): return lax.ppermute(value, axis, [(i, i ^ mask) for i in range(size)])]
    ppermute x4 -> x2, starting transfers between devices: 9.07 us -> 4.9 us  [shift_along(): return lax.ppermute(value, axis, pairs)]
    unnamed x27 -> x23, local copies, waits for them, and re-layouts: 2.36 us -> 0.06 us
    pallas_call x18 -> x17, Pallas kernels: 56.9 us -> 58.7 us  [call(): pl.pallas_call(kernel, out_shape=[jax.ShapeDtypeStruct(shape, dtype) if i...]
  transfers between devices with their start and end apart: 53 -> 51, of which waited for: 24 -> 21; matrix products, arithmetic and copies ran while one was open for 0% -> 0% of each run, Pallas kernels for 22% -> 28%
where the time goes in v3:
time: 187 us
  waiting for transfers between devices  64.6 us (35%)
  starting transfers between devices  62.1 us (33%)
  Pallas kernels  58.7 us (31%)
    ppermute x49, waiting for transfers between devices, exchange(): return lax.ppermute(value, axis, [(i, i ^ mask) for i in range(size)])  59.8 us
    pallas_call x17, Pallas kernels, call(): pl.pallas_call(kernel, out_shape=[jax.ShapeDtypeStruct(shape, dtype) if i...  58.7 us
    ppermute x49, starting transfers between devices, exchange(): return lax.ppermute(value, axis, [(i, i ^ mask) for i in range(size)])  57.2 us
    ppermute x2, starting transfers between devices, shift_along(): return lax.ppermute(value, axis, pairs)  4.9 us
    ppermute x2, waiting for transfers between devices, shift_along(): return lax.ppermute(value, axis, pairs)  4.85 us
  transfers between devices with their start and end apart: 51, of which 21 were waited for; matrix products, arithmetic and copies ran while one was open for 0% of the time, Pallas kernels for 28%

profile of v3, /device:TPU:0, one launch (start us, length us, event | category | flops | bytes accessed | tf_op | source)
XLA Modules:
  0.0 186.6 jit_solution(4734251312866694017)
XLA Ops:
  0.7 1.7 shard_map.202
  2.4 3.1 %collective-permute-start = (bf16[9,64,128]{2,1,0:T(8,128)(2,1)S(1)}, bf16[9,64,128]{2,1,0:T(8,128)(2,1)S(1)}, u32[]{:S(2)}, u32[]{:S(2)}) collective-permute-start(bf16[9,64,128]{2,1,0:T(8,128)(2,1)S(1)} %get-tuple-element.105), channel_id=1, source_target_pairs={{0,2},{1,3},{2,0},{3,1},{4,6},{5,7},{6,4},{7,5},{8,10},{9,11},{10,... | collective-permute-start | bytes 442376 | tf_op jit(solution)/shard_map/ppermute | solution.py:32
  5.5 2.6 %collective-permute-start.3 = (bf16[9,64,128]{2,1,0:T(8,128)(2,1)S(1)}, bf16[9,64,128]{2,1,0:T(8,128)(2,1)S(1)}, u32[]{:S(2)}, u32[]{:S(2)}) collective-permute-start(bf16[9,64,128]{2,1,0:T(8,128)(2,1)S(1)} %get-tuple-element.105), channel_id=1, source_target_pairs={{0,4},{1,5},{2,6},{3,7},{4,0},{5,1},{6,2},{7,3},{8,12},{9,13},{10,... | collective-permute-start | bytes 442376 | tf_op jit(solution)/shard_map/ppermute | solution.py:32
  8.1 3.6 %collective-permute-start.1 = (bf16[2,32,512]{2,1,0:T(8,128)(2,1)S(1)}, bf16[2,32,512]{2,1,0:T(8,128)(2,1)S(1)}, u32[]{:S(2)}, u32[]{:S(2)}) collective-permute-start(bf16[2,32,512]{2,1,0:T(8,128)(2,1)S(1)} %get-tuple-element.109), channel_id=1, source_target_pairs={{0,8},{8,16},{16,24},{1,9},{9,17},{17,25},{2,10},{10,18},{18,26},{... | collective-permute-start | bytes 196616 | tf_op jit(solution)/shard_map/ppermute | solution.py:38
  13.6 4.3 %collective-permute-done.2.right = bf16[2,32,512]{2,1,0:T(8,128)(2,1)S(1)} collective-permute-done((bf16[2,32,512]{2,1,0:T(8,128)(2,1)S(1)}, bf16[2,32,512]{2,1,0:T(8,128)(2,1)S(1)}, u32[]{:S(2)}, u32[]{:S(2)}) %collective-permute-start.2) | collective-permute-done | bytes 65568 | tf_op jit(solution)/shard_map/ppermute | solution.py:38
  17.9 1.6 collective-permute-done.3.refs_1_
  23.8 2.3 %collective-permute-start.10 = (bf16[128,512]{1,0:T(8,128)(2,1)S(1)}, bf16[128,512]{1,0:T(8,128)(2,1)S(1)}, u32[]{:S(2)}, u32[]{:S(2)}) collective-permute-start(bf16[128,512]{1,0:T(8,128)(2,1)S(1)} %get-tuple-element.118), channel_id=1, source_target_pairs={{0,6},{1,7},{2,4},{3,5},{4,2},{5,3},{6,0},{7,1},{8,14},{9,15},{10,... | collective-permute-start | bytes 393224 | tf_op jit(solution)/shard_map/ppermute | solution.py:32
  27.7 5.4 %collective-permute-done.11.rest_1_ = bf16[3,9,64,128]{3,2,1,0:T(8,128)(2,1)S(1)} collective-permute-done((bf16[3,9,64,128]{3,2,1,0:T(8,128)(2,1)S(1)}, bf16[3,9,64,128]{3,2,1,0:T(8,128)(2,1)S(1)}, u32[]{:S(2)}, u32[]{:S(2)}) %collective-permute-start.11) | collective-permute-done | bytes 442400 | tf_op jit(solution)/shard_map/ppermute | solution.py:32
  33.2 3.3 %collective-permute-start.9 = (bf16[128,512]{1,0:T(8,128)(2,1)S(1)}, bf16[128,512]{1,0:T(8,128)(2,1)S(1)}, u32[]{:S(2)}, u32[]{:S(2)}) collective-permute-start(bf16[128,512]{1,0:T(8,128)(2,1)S(1)} %get-tuple-element.118), channel_id=1, source_target_pairs={{0,4},{1,5},{2,6},{3,7},{4,0},{5,1},{6,2},{7,3},{8,12},{9,13},{10,... | collective-permute-start | bytes 393224 | tf_op jit(solution)/shard_map/ppermute | solution.py:32
  36.5 6.9 %collective-permute-done.12.rest_2_ = bf16[3,9,64,128]{3,2,1,0:T(8,128)(2,1)S(1)} collective-permute-done((bf16[3,9,64,128]{3,2,1,0:T(8,128)(2,1)S(1)}, bf16[3,9,64,128]{3,2,1,0:T(8,128)(2,1)S(1)}, u32[]{:S(2)}, u32[]{:S(2)}) %collective-permute-start.12) | collective-permute-done | bytes 442400 | tf_op jit(solution)/shard_map/ppermute | solution.py:32
  47.7 9.1 %shard_map.204 = (f32[512,512]{1,0:T(8,128)S(1)}, f32[512,512]{1,0:T(8,128)S(1)}, bf16[9,4,2,64,512]{4,3,2,1,0:T(8,128)(2,1)S(1)}) custom-call(s32[2,8]{1,0:T(2,128)S(1)} %copy-done.9, f32[10,512]{1,0:T(8,128)S(1)} %copy-done.8, bf16[2,256,512]{2,1,0:T(8,128)(2,1)S(1)} %copy-done.1, bf16[2,32,512]{2,1,0:T(8,128)(2,1)S(1)} %collective-permute-done.1.left, ...), custom_call_target="tpu_custom_call" | custom-call | flops 1 | bytes 1 | tf_op jit(solution)/shard_map/pallas_call | solution.py:118
  56.9 6.6 %collective-permute-done.18.refs_7_ = bf16[3,128,512]{2,1,0:T(8,128)(2,1)S(1)} collective-permute-done((bf16[3,128,512]{2,1,0:T(8,128)(2,1)S(1)}, bf16[3,128,512]{2,1,0:T(8,128)(2,1)S(1)}, u32[]{:S(2)}, u32[]{:S(2)}) %collective-permute-start.18) | collective-permute-done | bytes 393248 | tf_op jit(solution)/shard_map/ppermute | solution.py:32
  63.4 1.6 collective-permute-done.19.refs_8_
  71.4 17.9 %shard_map.206 = (bf16[512,512]{1,0:T(8,128)(2,1)}, bf16[512,512]{1,0:T(8,128)(2,1)S(1)}, bf16[512,2048]{1,0:T(8,128)(2,1)S(1)}, bf16[512,512]{1,0:T(8,128)(2,1)...) custom-call(f32[512,512]{1,0:T(8,128)S(1)} %get-tuple-element.123.refs_0_, ...), custom_call_target="tpu_custom_call" | custom-call | flops 1 | bytes 1 | tf_op jit(solution)/shard_map/pallas_call | solution.py:118
  89.3 3.3 %shard_map.207 = (bf16[4,4,128,512]{3,2,1,0:T(8,128)(2,1)S(1)}, bf16[4,4,128,512]{3,2,1,0:T(8,128)(2,1)S(1)}) custom-call(bf16[512,512]{1,0:T(8,128)(2,1)S(1)} %get-tuple-element.136.refs_0_, bf16[512,2048]{1,0:T(8,128)(2,1)S(1)} %get-tuple-element.137.refs_1_, bf16[512,512]{1,0:T(8,128)(2,1)S(1)} %get-tuple-element.138.refs_2_, ...), custom_call_target="tpu_custom_call" | custom-call | flops 1 | bytes 1 | tf_op jit(solution)/shard_map/pallas_call | solution.py:118
  92.6 6.1 %shard_map.208 = (f32[512,512]{1,0:T(8,128)S(1)}, bf16[512,512]{1,0:T(8,128)(2,1)S(1)}, bf16[640,128]{1,0:T(8,128)(2,1)S(1)}, bf16[896,128]{1,0:T(8,128)(2,1)S(1...) custom-call(f32[512,512]{1,0:T(8,128)S(1)} %get-tuple-element.141.refs_0_, bf16[512,512]{1,0:T(8,128)(2,1)S(1)} %bitcast.9, ...), custom_call_target="tpu_custom_call" | custom-call | flops 1 | bytes 1 | tf_op jit(solution)/shard_map/pallas_call | solution.py:118
  102.4 4.9 %collective-permute-done.27.refs_6_.refs_4_ = bf16[896,128]{1,0:T(8,128)(2,1)S(1)} collective-permute-done((bf16[896,128]{1,0:T(8,128)(2,1)S(1)}, bf16[896,128]{1,0:T(8,128)(2,1)S(1)}, u32[]{:S(2)}, u32[]{:S(2)}) %collective-permute-start.27) | collective-permute-done | bytes 229408 | tf_op jit(solution)/shard_map/ppermute | solution.py:32
  107.7 4.4 %collective-permute-done.29.refs_8_.refs_5_ = bf16[896,128]{1,0:T(8,128)(2,1)S(1)} collective-permute-done((bf16[896,128]{1,0:T(8,128)(2,1)S(1)}, bf16[896,128]{1,0:T(8,128)(2,1)S(1)}, u32[]{:S(2)}, u32[]{:S(2)}) %collective-permute-start.29) | collective-permute-done | bytes 229408 | tf_op jit(solution)/shard_map/ppermute | solution.py:32
  112.1 6.6 %shard_map.209 = (bf16[2432,128]{1,0:T(8,128)(2,1)S(1)}, bf16[2432,128]{1,0:T(8,128)(2,1)S(1)}) custom-call(s32[2,8]{1,0:T(2,128)S(1)} %copy-done.9, bf16[2,256,512]{2,1,0:T(8,128)(2,1)S(1)} %copy-done.1, bf16[2,256,512]{2,1,0:T(8,128)(2,1)S(1)} %collective-permute-done.24.refs_2_, bf16[2,256,512]{2,1,0:T(8,128)(2,1)S(1)} %collective-permute-done.25.refs_3_, ...), custom_call_target="tpu_custom_call" | custom-call | flops 1 | bytes 1 | tf_op jit(solution)/shard_map/pallas_call | solution.py:118
  123.3 2.4 %collective-permute-start.31 = (bf16[704,128]{1,0:T(8,128)(2,1)S(1)}, bf16[704,128]{1,0:T(8,128)(2,1)S(1)}, u32[]{:S(2)}, u32[]{:S(2)}) collective-permute-start(bf16[704,128]{1,0:T(8,128)(2,1)S(1)} %get-tuple-element.169), channel_id=1, source_target_pairs={{0,2},{1,3},{2,0},{3,1},{4,6},{5,7},{6,4},{7,5},{8,10},{9,11},{10,... | collective-permute-start | bytes 540680 | tf_op jit(solution)/shard_map/ppermute | solution.py:32
  126.8 6.6 %collective-permute-done.31.refs_1_ = bf16[704,128]{1,0:T(8,128)(2,1)S(1)} collective-permute-done((bf16[704,128]{1,0:T(8,128)(2,1)S(1)}, bf16[704,128]{1,0:T(8,128)(2,1)S(1)}, u32[]{:S(2)}, u32[]{:S(2)}) %collective-permute-start.31) | collective-permute-done | bytes 180256 | tf_op jit(solution)/shard_map/ppermute | solution.py:32
  133.4 1.7 collective-permute-start.33
  135.2 7.4 %shard_map.211 = f32[512,512]{1,0:T(8,128)} custom-call(s32[2,8]{1,0:T(2,128)S(1)} %copy-done.9, bf16[512,512]{1,0:T(8,128)(2,1)S(1)} %get-tuple-element.164.refs_1_, f32[512,512]{1,0:T(8,128)S(1)} %get-tuple-element.165.refs_2_, bf16[9,4,2,64,512]{4,3,2,1,0:T(8,128)(2,1)S(1)} %get-tuple-element.166.refs_3_, ...), custom_call_target="tpu_custom_call" | custom-call | flops 1 | bytes 1 | tf_op jit(solution)/shard_map/pallas_call | solution.py:118
  144.3 5.1 %collective-permute-done.38.refs_2_ = bf16[512,512]{1,0:T(8,128)(2,1)S(1)} collective-permute-done((bf16[512,512]{1,0:T(8,128)(2,1)S(1)}, bf16[512,512]{1,0:T(8,128)(2,1)S(1)}, u32[]{:S(2)}, u32[]{:S(2)}) %collective-permute-start.38) | collective-permute-done | bytes 524320 | tf_op jit(solution)/shard_map/ppermute | solution.py:32
  149.7 2.4 %collective-permute-start.41 = (bf16[128,512]{1,0:T(8,128)(2,1)S(1)}, bf16[128,512]{1,0:T(8,128)(2,1)S(1)}, u32[]{:S(2)}, u32[]{:S(2)}) collective-permute-start(bf16[128,512]{1,0:T(8,128)(2,1)S(1)} %get-tuple-element.182), channel_id=1, source_target_pairs={{0,2},{1,3},{2,0},{3,1},{4,6},{5,7},{6,4},{7,5},{8,10},{9,11},{10,... | collective-permute-start | bytes 393224 | tf_op jit(solution)/shard_map/ppermute | solution.py:32
  154.5 1.9 %collective-permute-done.41.refs_1_ = bf16[128,512]{1,0:T(8,128)(2,1)S(1)} collective-permute-done((bf16[128,512]{1,0:T(8,128)(2,1)S(1)}, bf16[128,512]{1,0:T(8,128)(2,1)S(1)}, u32[]{:S(2)}, u32[]{:S(2)}) %collective-permute-start.41) | collective-permute-done | bytes 131104 | tf_op jit(solution)/shard_map/ppermute | solution.py:32
  156.5 4.7 %collective-permute-done.42.refs_2_ = bf16[128,512]{1,0:T(8,128)(2,1)S(1)} collective-permute-done((bf16[128,512]{1,0:T(8,128)(2,1)S(1)}, bf16[128,512]{1,0:T(8,128)(2,1)S(1)}, u32[]{:S(2)}, u32[]{:S(2)}) %collective-permute-start.42) | collective-permute-done | bytes 131104 | tf_op jit(solution)/shard_map/ppermute | solution.py:32
  167.7 2.0 %collective-permute-done.46.refs_3_.refs_7_ = bf16[144,512]{1,0:T(8,128)(2,1)S(1)} collective-permute-done((bf16[144,512]{1,0:T(8,128)(2,1)S(1)}, bf16[144,512]{1,0:T(8,128)(2,1)S(1)}, u32[]{:S(2)}, u32[]{:S(2)}) %collective-permute-start.46) | collective-permute-done | bytes 147488 | tf_op jit(solution)/shard_map/ppermute | solution.py:32
  169.7 3.8 %collective-permute-start.47 = (f32[8,128]{1,0:T(8,128)S(1)}, f32[8,128]{1,0:T(8,128)S(1)}, u32[]{:S(2)}, u32[]{:S(2)}) collective-permute-start(f32[8,128]{1,0:T(8,128)S(1)} %shard_map.216.refs_0_), channel_id=1, source_target_pairs={{0,2},{1,3},{2,0},{3,1},{4,6},{5,7},{6,4},{7,5},{8,10},{9,11},{10,... | collective-permute-start | bytes 12296 | tf_op jit(solution)/shard_map/ppermute | solution.py:32
  176.4 1.7 collective-permute-done.48.refs_2_
  178.0 2.4 %collective-permute-done.49.refs_3_ = f32[8,128]{1,0:T(8,128)S(1)} collective-permute-done((f32[8,128]{1,0:T(8,128)S(1)}, f32[8,128]{1,0:T(8,128)S(1)}, u32[]{:S(2)}, u32[]{:S(2)}) %collective-permute-start.49) | collective-permute-done | bytes 4128 | tf_op jit(solution)/shard_map/ppermute | solution.py:32
  181.6 4.9 %shard_map.218 = (f32[1,1]{1,0:T(1,128)}, f32[10,512]{1,0:T(8,128)}, f32[10,512]{1,0:T(8,128)}, f32[9,64,512]{2,1,0:T(8,128)}, f32[9,64,512]{2,1,0:T(8,128)}, /*...) custom-call(bf16[576,128]{1,0:T(8,128)(2,1)S(1)} %get-tuple-element., ...), custom_call_target="tpu_custom_call" | custom-call | flops 1 | bytes 1 | tf_op jit(solution)/shard_map/pallas_call | solution.py:118
  (110 shorter events, 43.3 us)
Async XLA Ops:
  2.4 10.6 %collective-permute-start = (bf16[9,64,128]{2,1,0:T(8,128)(2,1)S(1)}, bf16[9,64,128]{2,1,0:T(8,128)(2,1)S(1)}, u32[]{:S(2)}, u32[]{:S(2)}) collective-permute-start(bf16[9,64,128]{2,1,0:T(8,128)(2,1)S(1)} %get-tuple-element.105), channel_id=1, source_target_pairs={{0,2},{1,3},{2,0},{3,1},{4,6},{5,7},{6,4},{7,5},{8,10},{9,11},{10,... | collective-permute-start | bytes 442376 | tf_op jit(solution)/shard_map/ppermute | solution.py:32
  5.5 14.0 %collective-permute-start.3 = (bf16[9,64,128]{2,1,0:T(8,128)(2,1)S(1)}, bf16[9,64,128]{2,1,0:T(8,128)(2,1)S(1)}, u32[]{:S(2)}, u32[]{:S(2)}) collective-permute-start(bf16[9,64,128]{2,1,0:T(8,128)(2,1)S(1)} %get-tuple-element.105), channel_id=1, source_target_pairs={{0,4},{1,5},{2,6},{3,7},{4,0},{5,1},{6,2},{7,3},{8,12},{9,13},{10,... | collective-permute-start | bytes 442376 | tf_op jit(solution)/shard_map/ppermute | solution.py:32
  8.1 11.4 %collective-permute-start.4 = (bf16[9,64,128]{2,1,0:T(8,128)(2,1)S(1)}, bf16[9,64,128]{2,1,0:T(8,128)(2,1)S(1)}, u32[]{:S(2)}, u32[]{:S(2)}) collective-permute-start(bf16[9,64,128]{2,1,0:T(8,128)(2,1)S(1)} %get-tuple-element.105), channel_id=1, source_target_pairs={{0,6},{1,7},{2,4},{3,5},{4,2},{5,3},{6,0},{7,1},{8,14},{9,15},{10,... | collective-permute-start | bytes 442376 | tf_op jit(solution)/shard_map/ppermute | solution.py:32
  20.2 13.0 %collective-permute-start.11 = (bf16[3,9,64,128]{3,2,1,0:T(8,128)(2,1)S(1)}, bf16[3,9,64,128]{3,2,1,0:T(8,128)(2,1)S(1)}, u32[]{:S(2)}, u32[]{:S(2)}) collective-permute-start(bf16[3,9,64,128]{3,2,1,0:T(8,128)(2,1)S(1)} %shard_map.203.rest_0_), channel_id=1, source_target_pairs={{0,8},{8,0},{16,24},{24,16},{1,9},{9,1},{17,25},{25,17},{2,10},{10... | collective-permute-start | bytes 1327112 | tf_op jit(solution)/shard_map/ppermute | solution.py:32
  21.7 21.7 %collective-permute-start.12 = (bf16[3,9,64,128]{3,2,1,0:T(8,128)(2,1)S(1)}, bf16[3,9,64,128]{3,2,1,0:T(8,128)(2,1)S(1)}, u32[]{:S(2)}, u32[]{:S(2)}) collective-permute-start(bf16[3,9,64,128]{3,2,1,0:T(8,128)(2,1)S(1)} %shard_map.203.rest_0_), channel_id=1, source_target_pairs={{0,16},{8,24},{16,0},{24,8},{1,17},{9,25},{17,1},{25,9},{2,18},{10... | collective-permute-start | bytes 1327112 | tf_op jit(solution)/shard_map/ppermute | solution.py:32
  23.2 20.2 %collective-permute-start.13 = (bf16[3,9,64,128]{3,2,1,0:T(8,128)(2,1)S(1)}, bf16[3,9,64,128]{3,2,1,0:T(8,128)(2,1)S(1)}, u32[]{:S(2)}, u32[]{:S(2)}) collective-permute-start(bf16[3,9,64,128]{3,2,1,0:T(8,128)(2,1)S(1)} %shard_map.203.rest_0_), channel_id=1, source_target_pairs={{0,24},{8,16},{16,8},{24,0},{1,25},{9,17},{17,9},{25,1},{2,26},{10... | collective-permute-start | bytes 1327112 | tf_op jit(solution)/shard_map/ppermute | solution.py:32
  23.8 19.6 %collective-permute-start.10 = (bf16[128,512]{1,0:T(8,128)(2,1)S(1)}, bf16[128,512]{1,0:T(8,128)(2,1)S(1)}, u32[]{:S(2)}, u32[]{:S(2)}) collective-permute-start(bf16[128,512]{1,0:T(8,128)(2,1)S(1)} %get-tuple-element.118), channel_id=1, source_target_pairs={{0,6},{1,7},{2,4},{3,5},{4,2},{5,3},{6,0},{7,1},{8,14},{9,15},{10,... | collective-permute-start | bytes 393224 | tf_op jit(solution)/shard_map/ppermute | solution.py:32
  26.1 17.3 %collective-permute-start.8 = (bf16[128,512]{1,0:T(8,128)(2,1)S(1)}, bf16[128,512]{1,0:T(8,128)(2,1)S(1)}, u32[]{:S(2)}, u32[]{:S(2)}) collective-permute-start(bf16[128,512]{1,0:T(8,128)(2,1)S(1)} %get-tuple-element.118), channel_id=1, source_target_pairs={{0,2},{1,3},{2,0},{3,1},{4,6},{5,7},{6,4},{7,5},{8,10},{9,11},{10,... | collective-permute-start | bytes 393224 | tf_op jit(solution)/shard_map/ppermute | solution.py:32
  33.2 10.3 %collective-permute-start.9 = (bf16[128,512]{1,0:T(8,128)(2,1)S(1)}, bf16[128,512]{1,0:T(8,128)(2,1)S(1)}, u32[]{:S(2)}, u32[]{:S(2)}) collective-permute-start(bf16[128,512]{1,0:T(8,128)(2,1)S(1)} %get-tuple-element.118), channel_id=1, source_target_pairs={{0,4},{1,5},{2,6},{3,7},{4,0},{5,1},{6,2},{7,3},{8,12},{9,13},{10,... | collective-permute-start | bytes 393224 | tf_op jit(solution)/shard_map/ppermute | solution.py:32
  44.2 12.7 %collective-permute-start.17 = (bf16[3,128,512]{2,1,0:T(8,128)(2,1)S(1)}, bf16[3,128,512]{2,1,0:T(8,128)(2,1)S(1)}, u32[]{:S(2)}, u32[]{:S(2)}) collective-permute-start(bf16[3,128,512]{2,1,0:T(8,128)(2,1)S(1)} %get-tuple-element.131.refs_5_), channel_id=1, source_target_pairs={{0,8},{8,0},{16,24},{24,16},{1,9},{9,1},{17,25},{25,17},{2,10},{10... | collective-permute-start | bytes 1179656 | tf_op jit(solution)/shard_map/ppermute | solution.py:32
  45.4 18.0 %collective-permute-start.18 = (bf16[3,128,512]{2,1,0:T(8,128)(2,1)S(1)}, bf16[3,128,512]{2,1,0:T(8,128)(2,1)S(1)}, u32[]{:S(2)}, u32[]{:S(2)}) collective-permute-start(bf16[3,128,512]{2,1,0:T(8,128)(2,1)S(1)} %get-tuple-element.131.refs_5_), channel_id=1, source_target_pairs={{0,16},{8,24},{16,0},{24,8},{1,17},{9,25},{17,1},{25,9},{2,18},{10... | collective-permute-start | bytes 1179656 | tf_op jit(solution)/shard_map/ppermute | solution.py:32
  46.3 18.8 %collective-permute-start.19 = (bf16[3,128,512]{2,1,0:T(8,128)(2,1)S(1)}, bf16[3,128,512]{2,1,0:T(8,128)(2,1)S(1)}, u32[]{:S(2)}, u32[]{:S(2)}) collective-permute-start(bf16[3,128,512]{2,1,0:T(8,128)(2,1)S(1)} %get-tuple-element.131.refs_5_), channel_id=1, source_target_pairs={{0,24},{8,16},{16,8},{24,0},{1,25},{9,17},{17,9},{25,1},{2,26},{10... | collective-permute-start | bytes 1179656 | tf_op jit(solution)/shard_map/ppermute | solution.py:32
  65.6 33.1 %collective-permute-start.24 = (bf16[2,256,512]{2,1,0:T(8,128)(2,1)S(1)}, bf16[2,256,512]{2,1,0:T(8,128)(2,1)S(1)}, u32[]{:S(2)}, u32[]{:S(2)}) collective-permute-start(bf16[2,256,512]{2,1,0:T(8,128)(2,1)S(1)} %copy-done.1), channel_id=1, source_target_pairs={{0,8},{8,0},{16,24},{24,16},{1,9},{9,1},{17,25},{25,17},{2,10},{10... | collective-permute-start | bytes 1572872 | tf_op jit(solution)/shard_map/ppermute | solution.py:32
  66.4 32.3 %collective-permute-start.25 = (bf16[2,256,512]{2,1,0:T(8,128)(2,1)S(1)}, bf16[2,256,512]{2,1,0:T(8,128)(2,1)S(1)}, u32[]{:S(2)}, u32[]{:S(2)}) collective-permute-start(bf16[2,256,512]{2,1,0:T(8,128)(2,1)S(1)} %copy-done.1), channel_id=1, source_target_pairs={{0,16},{8,24},{16,0},{24,8},{1,17},{9,25},{17,1},{25,9},{2,18},{10... | collective-permute-start | bytes 1572872 | tf_op jit(solution)/shard_map/ppermute | solution.py:32
  67.9 30.8 %collective-permute-start.26 = (bf16[2,256,512]{2,1,0:T(8,128)(2,1)S(1)}, bf16[2,256,512]{2,1,0:T(8,128)(2,1)S(1)}, u32[]{:S(2)}, u32[]{:S(2)}) collective-permute-start(bf16[2,256,512]{2,1,0:T(8,128)(2,1)S(1)} %copy-done.1), channel_id=1, source_target_pairs={{0,24},{8,16},{16,8},{24,0},{1,25},{9,17},{17,9},{25,1},{2,26},{10... | collective-permute-start | bytes 1572872 | tf_op jit(solution)/shard_map/ppermute | solution.py:32
  98.7 20.0 %collective-permute-start.36 = (bf16[4,4,128,512]{3,2,1,0:T(8,128)(2,1)S(1)}, bf16[4,4,128,512]{3,2,1,0:T(8,128)(2,1)S(1)}, u32[]{:S(2)}, u32[]{:S(2)}) collective-permute-start(bf16[4,4,128,512]{3,2,1,0:T(8,128)(2,1)S(1)} %get-tuple-element.174), channel_id=1, source_target_pairs={{0,1},{1,0},{2,3},{3,2},{4,5},{5,4},{6,7},{7,6},{8,9},{9,8},{10,11... | collective-permute-start | bytes 6291464 | tf_op jit(solution)/shard_map/ppermute | solution.py:32
  98.9 8.4 %collective-permute-start.27 = (bf16[896,128]{1,0:T(8,128)(2,1)S(1)}, bf16[896,128]{1,0:T(8,128)(2,1)S(1)}, u32[]{:S(2)}, u32[]{:S(2)}) collective-permute-start(bf16[896,128]{1,0:T(8,128)(2,1)S(1)} %get-tuple-element.157), channel_id=1, source_target_pairs={{0,8},{8,0},{16,24},{24,16},{1,9},{9,1},{17,25},{25,17},{2,10},{10... | collective-permute-start | bytes 688136 | tf_op jit(solution)/shard_map/ppermute | solution.py:32
  99.7 12.3 %collective-permute-start.29 = (bf16[896,128]{1,0:T(8,128)(2,1)S(1)}, bf16[896,128]{1,0:T(8,128)(2,1)S(1)}, u32[]{:S(2)}, u32[]{:S(2)}) collective-permute-start(bf16[896,128]{1,0:T(8,128)(2,1)S(1)} %get-tuple-element.160), channel_id=1, source_target_pairs={{0,24},{8,16},{16,8},{24,0},{1,25},{9,17},{17,9},{25,1},{2,26},{10... | collective-permute-start | bytes 688136 | tf_op jit(solution)/shard_map/ppermute | solution.py:32
  101.2 6.5 %collective-permute-start.28 = (bf16[640,128]{1,0:T(8,128)(2,1)S(1)}, bf16[640,128]{1,0:T(8,128)(2,1)S(1)}, u32[]{:S(2)}, u32[]{:S(2)}) collective-permute-start(bf16[640,128]{1,0:T(8,128)(2,1)S(1)} %get-tuple-element.159), channel_id=1, source_target_pairs={{0,16},{8,24},{16,0},{24,8},{1,17},{9,25},{17,1},{25,9},{2,18},{10... | collective-permute-start | bytes 491528 | tf_op jit(solution)/shard_map/ppermute | solution.py:32
  119.4 24.9 %collective-permute-start.37 = (bf16[512,512]{1,0:T(8,128)(2,1)S(1)}, bf16[512,512]{1,0:T(8,128)(2,1)S(1)}, u32[]{:S(2)}, u32[]{:S(2)}) collective-permute-start(bf16[512,512]{1,0:T(8,128)(2,1)S(1)} %get-tuple-element.176), channel_id=1, source_target_pairs={{0,8},{8,0},{16,24},{24,16},{1,9},{9,1},{17,25},{25,17},{2,10},{10... | collective-permute-start | bytes 1572872 | tf_op jit(solution)/shard_map/ppermute | solution.py:32
  121.0 28.4 %collective-permute-start.38 = (bf16[512,512]{1,0:T(8,128)(2,1)S(1)}, bf16[512,512]{1,0:T(8,128)(2,1)S(1)}, u32[]{:S(2)}, u32[]{:S(2)}) collective-permute-start(bf16[512,512]{1,0:T(8,128)(2,1)S(1)} %get-tuple-element.177), channel_id=1, source_target_pairs={{0,16},{8,24},{16,0},{24,8},{1,17},{9,25},{17,1},{25,9},{2,18},{10... | collective-permute-start | bytes 1572872 | tf_op jit(solution)/shard_map/ppermute | solution.py:32
  121.5 27.9 %collective-permute-start.39 = (bf16[512,512]{1,0:T(8,128)(2,1)S(1)}, bf16[512,512]{1,0:T(8,128)(2,1)S(1)}, u32[]{:S(2)}, u32[]{:S(2)}) collective-permute-start(bf16[512,512]{1,0:T(8,128)(2,1)S(1)} %get-tuple-element.178), channel_id=1, source_target_pairs={{0,24},{8,16},{16,8},{24,0},{1,25},{9,17},{17,9},{25,1},{2,26},{10... | collective-permute-start | bytes 1572872 | tf_op jit(solution)/shard_map/ppermute | solution.py:32
  123.3 10.1 %collective-permute-start.31 = (bf16[704,128]{1,0:T(8,128)(2,1)S(1)}, bf16[704,128]{1,0:T(8,128)(2,1)S(1)}, u32[]{:S(2)}, u32[]{:S(2)}) collective-permute-start(bf16[704,128]{1,0:T(8,128)(2,1)S(1)} %get-tuple-element.169), channel_id=1, source_target_pairs={{0,2},{1,3},{2,0},{3,1},{4,6},{5,7},{6,4},{7,5},{8,10},{9,11},{10,... | collective-permute-start | bytes 540680 | tf_op jit(solution)/shard_map/ppermute | solution.py:32
  125.7 16.9 %collective-permute-start.32 = (bf16[704,128]{1,0:T(8,128)(2,1)S(1)}, bf16[704,128]{1,0:T(8,128)(2,1)S(1)}, u32[]{:S(2)}, u32[]{:S(2)}) collective-permute-start(bf16[704,128]{1,0:T(8,128)(2,1)S(1)} %get-tuple-element.170), channel_id=1, source_target_pairs={{0,4},{1,5},{2,6},{3,7},{4,0},{5,1},{6,2},{7,3},{8,12},{9,13},{10,... | collective-permute-start | bytes 540680 | tf_op jit(solution)/shard_map/ppermute | solution.py:32
  133.4 9.2 %collective-permute-start.33 = (bf16[704,128]{1,0:T(8,128)(2,1)S(1)}, bf16[704,128]{1,0:T(8,128)(2,1)S(1)}, u32[]{:S(2)}, u32[]{:S(2)}) collective-permute-start(bf16[704,128]{1,0:T(8,128)(2,1)S(1)} %get-tuple-element.171), channel_id=1, source_target_pairs={{0,6},{1,7},{2,4},{3,5},{4,2},{5,3},{6,0},{7,1},{8,14},{9,15},{10,... | collective-permute-start | bytes 540680 | tf_op jit(solution)/shard_map/ppermute | solution.py:32
  142.8 11.8 %collective-permute-start.40 = (bf16[576,128]{1,0:T(8,128)(2,1)S(1)}, bf16[576,128]{1,0:T(8,128)(2,1)S(1)}, u32[]{:S(2)}, u32[]{:S(2)}) collective-permute-start(bf16[576,128]{1,0:T(8,128)(2,1)S(1)} %get-tuple-element.172.refs_0_), channel_id=1, source_target_pairs={{0,24},{8,16},{16,8},{24,0},{1,25},{9,17},{17,9},{25,1},{2,26},{10... | collective-permute-start | bytes 442376 | tf_op jit(solution)/shard_map/ppermute | solution.py:32
  149.7 6.8 %collective-permute-start.41 = (bf16[128,512]{1,0:T(8,128)(2,1)S(1)}, bf16[128,512]{1,0:T(8,128)(2,1)S(1)}, u32[]{:S(2)}, u32[]{:S(2)}) collective-permute-start(bf16[128,512]{1,0:T(8,128)(2,1)S(1)} %get-tuple-element.182), channel_id=1, source_target_pairs={{0,2},{1,3},{2,0},{3,1},{4,6},{5,7},{6,4},{7,5},{8,10},{9,11},{10,... | collective-permute-start | bytes 393224 | tf_op jit(solution)/shard_map/ppermute | solution.py:32
  152.1 9.1 %collective-permute-start.42 = (bf16[128,512]{1,0:T(8,128)(2,1)S(1)}, bf16[128,512]{1,0:T(8,128)(2,1)S(1)}, u32[]{:S(2)}, u32[]{:S(2)}) collective-permute-start(bf16[128,512]{1,0:T(8,128)(2,1)S(1)} %get-tuple-element.183), channel_id=1, source_target_pairs={{0,4},{1,5},{2,6},{3,7},{4,0},{5,1},{6,2},{7,3},{8,12},{9,13},{10,... | collective-permute-start | bytes 393224 | tf_op jit(solution)/shard_map/ppermute | solution.py:32
  153.1 8.0 %collective-permute-start.43 = (bf16[128,512]{1,0:T(8,128)(2,1)S(1)}, bf16[128,512]{1,0:T(8,128)(2,1)S(1)}, u32[]{:S(2)}, u32[]{:S(2)}) collective-permute-start(bf16[128,512]{1,0:T(8,128)(2,1)S(1)} %get-tuple-element.184), channel_id=1, source_target_pairs={{0,6},{1,7},{2,4},{3,5},{4,2},{5,3},{6,0},{7,1},{8,14},{9,15},{10,... | collective-permute-start | bytes 393224 | tf_op jit(solution)/shard_map/ppermute | solution.py:32
  164.8 15.6 %collective-permute-start.34 = (bf16[576,128]{1,0:T(8,128)(2,1)S(1)}, bf16[576,128]{1,0:T(8,128)(2,1)S(1)}, u32[]{:S(2)}, u32[]{:S(2)}) collective-permute-start(bf16[576,128]{1,0:T(8,128)(2,1)S(1)} %get-tuple-element.172.refs_0_), channel_id=1, source_target_pairs={{0,8},{8,0},{16,24},{24,16},{1,9},{9,1},{17,25},{25,17},{2,10},{10... | collective-permute-start | bytes 442376 | tf_op jit(solution)/shard_map/ppermute | solution.py:32
  165.6 14.8 %collective-permute-start.35 = (bf16[576,128]{1,0:T(8,128)(2,1)S(1)}, bf16[576,128]{1,0:T(8,128)(2,1)S(1)}, u32[]{:S(2)}, u32[]{:S(2)}) collective-permute-start(bf16[576,128]{1,0:T(8,128)(2,1)S(1)} %get-tuple-element.172.refs_0_), channel_id=1, source_target_pairs={{0,16},{8,24},{16,0},{24,8},{1,17},{9,25},{17,1},{25,9},{2,18},{10... | collective-permute-start | bytes 442376 | tf_op jit(solution)/shard_map/ppermute | solution.py:32
  169.7 6.6 %collective-permute-start.47 = (f32[8,128]{1,0:T(8,128)S(1)}, f32[8,128]{1,0:T(8,128)S(1)}, u32[]{:S(2)}, u32[]{:S(2)}) collective-permute-start(f32[8,128]{1,0:T(8,128)S(1)} %shard_map.216.refs_0_), channel_id=1, source_target_pairs={{0,2},{1,3},{2,0},{3,1},{4,6},{5,7},{6,4},{7,5},{8,10},{9,11},{10,... | collective-permute-start | bytes 12296 | tf_op jit(solution)/shard_map/ppermute | solution.py:32
  (30 other events, 547.2 us)

commit v4 on v3

--- a/solution.py
+++ b/solution.py
@@ -260,15 +260,15 @@
     for r in range(rows):
 
         def norm(begin, carry, r=r):
-            where = pl.ds(r * length + begin, 32)
+            where = pl.ds(r * length + begin, 256)
             active, _ = gelu_parts(pre[where, :])
             unit, _ = normalized(active)
             after[where, :] = (
-                tok[r, pl.ds(begin, 32), :].astype(F32) + unit * vec[1:2, :] + vec[2:3, :]
+                tok[r, pl.ds(begin, 256), :].astype(F32) + unit * vec[1:2, :] + vec[2:3, :]
             )
             return carry
 
-        loop_rows(length, 32, norm)
+        loop_rows(length, 256, norm)
 
 
 def ffn_kernel(nz, ns, *refs):
@@ -276,7 +276,7 @@
     wholes = refs[3:5]
     pieces = (refs[5 : 5 + ns], refs[5 + ns : 5 + 2 * ns])
     rest = refs[5 + 2 * ns :]
-    layer, low, hidden, outer_grad, inner_grad, inner_full, sums, outer_full, slope, tmp, sems = rest
+    layer, low, hidden, outer_grad, inner_grad, inner_full, sums, outer_full, slope, tmp = rest
     seq_at, z_at, core_at = place()
     count, width = after.shape
     hid = inner_full.shape[3]
@@ -286,30 +286,21 @@
     inner = inner_full.reshape(width, hid)
     outer = outer_full.reshape(hid, width)
     part = outer_full.shape[3]
-    pairs = []
     for i, whole in enumerate(wholes):
         core = core_at ^ i
         for q in range(ns):
-            pairs.append(
-                (
-                    whole.at[q * in_rows : (q + 1) * in_rows],
-                    inner_full.at[z_at, core, :, q * quarter : (q + 1) * quarter],
-                )
-            )
-            pairs.append(
-                (
-                    whole.at[ns * in_rows + q * part : ns * in_rows + (q + 1) * part],
-                    outer_full.at[z_at, core, q],
-                )
-            )
+            inner_full[z_at, core, :, q * quarter : (q + 1) * quarter] = whole[
+                q * in_rows : (q + 1) * in_rows
+            ]
+            begin = ns * in_rows + q * part
+            outer_full[z_at, core, q] = whole[begin : begin + part]
         for k in range(ns):
             piece = pieces[i][k]
             q = seq_at ^ k
             for j in range(1, nz):
                 z = z_at ^ j
-                pairs.append((piece.at[j - 1, :in_rows], inner_full.at[z, core, :, at(q, quarter)]))
-                pairs.append((piece.at[j - 1, in_rows:], outer_full.at[z, core, q]))
-    copies = begin_copies(pairs, sems)
+                inner_full[z, core, :, at(q, quarter)] = piece[j - 1, :in_rows]
+                outer_full[z, core, q] = piece[j - 1, in_rows:]
 
     def lower(begin, carry):
         where = pl.ds(begin, 64)
@@ -317,21 +308,20 @@
         return carry
 
     loop_rows(count, 64, lower)
-    end_copies(copies)
 
     def up(b, carry):
         cols = at(b, width)
         tmp[...] = dot(low[...], inner[:, cols]) + vec[pl.ds(6 + b, 1), :]
 
         def act(begin, inside):
-            where = pl.ds(begin, 32)
+            where = pl.ds(begin, 128)
             v = tmp[where, :]
             active, cdf = gelu_parts(v)
             hidden[where, cols] = active.astype(BF)
             slope[where, cols] = gelu_slope(v, cdf)
             return inside
 
-        loop_rows(count, 32, act)
+        loop_rows(count, 128, act)
         return carry
 
     lax.fori_loop(0, blocks, up, 0)
@@ -340,7 +330,7 @@
 
     def second(begin, carry):
         bias_sum, gain_sum, shift_sum = carry
-        where = pl.ds(begin, 32)
+        where = pl.ds(begin, 256)
         unit, scale = normalized(tmp[where, :])
         gain = vec[4:5, :]
         layer[where, :] = (after[where, :] + unit * gain + vec[5:6, :]).astype(BF)
@@ -354,7 +344,7 @@
             shift_sum + fold_rows(dy),
         )
 
-    totals = loop_rows(count, 32, second, (zero, zero, zero))
+    totals = loop_rows(count, 256, second, (zero, zero, zero))
     sums[...] = jnp.zeros(sums.shape, F32)
     for i, total in enumerate(totals):
         sums[3 + i : 4 + i, :] = column_sum(total)
@@ -364,12 +354,12 @@
         tmp[...] = dot_nt(outer_grad[...], outer[cols, :])
 
         def act(begin, total):
-            where = pl.ds(begin, 32)
+            where = pl.ds(begin, 128)
             grad = (tmp[where, :] * slope[where, cols]).astype(BF)
             inner_grad[where, cols] = grad
             return total + fold_rows(grad.astype(F32))
 
-        total = loop_rows(count, 32, act, zero)
+        total = loop_rows(count, 128, act, zero)
         sums[pl.ds(6 + b, 1), :] = column_sum(total)
         return carry
 
@@ -389,7 +379,7 @@
 
     def first(begin, carry):
         bias_sum, gain_sum, shift_sum = carry
-        where = pl.ds(begin, 32)
+        where = pl.ds(begin, 256)
         upstream = cot[where, :].astype(F32) + tmp[where, :]
         after_grad[where, :] = upstream
         v = pre[where, :]
@@ -405,7 +395,7 @@
             shift_sum + fold_rows(upstream),
         )
 
-    totals = loop_rows(count, 32, first, (zero, zero, zero))
+    totals = loop_rows(count, 256, first, (zero, zero, zero))
     for i, total in enumerate(totals):
         sums[i : i + 1, :] = column_sum(total)
     span = width // ns
@@ -919,10 +909,8 @@
             pltpu.VMEM((nz, 2, ns, part, width), BF),
             pltpu.VMEM((count, hid), F32),
             pltpu.VMEM((count, width), F32),
-            pltpu.SemaphoreType.DMA((4 * ns * nz,)),
         ],
         kept=(0,),
-        loose=range(3, 5 + 2 * ns),
     )(after, cot, vectors, ffn_own, ffn_other, *ffn_pieces, *ffn_other_pieces)
 
     mine, theirs = vmem_call(

time: 187 us -> 179 us (0.957)
  Pallas kernels: 58.7 us -> 44.5 us
  waiting for transfers between devices: 64.6 us -> 71.5 us
    pallas_call x17, Pallas kernels: 58.7 us -> 44.5 us  [call(): pl.pallas_call(kernel, out_shape=[jax.ShapeDtypeStruct(shape, dtype) if i...]
    ppermute x49, waiting for transfers between devices: 59.8 us -> 66.7 us  [exchange(): return lax.ppermute(value, axis, [(i, i ^ mask) for i in range(size)])]
  transfers between devices with their start and end apart: 51 -> 51, of which waited for: 21 -> 23; matrix products, arithmetic and copies ran while one was open for 0% -> 0% of each run, Pallas kernels for 28% -> 21%
where the time goes in v4:
time: 179 us
  waiting for transfers between devices  71.5 us (40%)
  starting transfers between devices  61.8 us (35%)
  Pallas kernels  44.5 us (25%)
    ppermute x49, waiting for transfers between devices, exchange(): return lax.ppermute(value, axis, [(i, i ^ mask) for i in range(size)])  66.7 us
    ppermute x49, starting transfers between devices, exchange(): return lax.ppermute(value, axis, [(i, i ^ mask) for i in range(size)])  56.9 us
    pallas_call x17, Pallas kernels, call(): pl.pallas_call(kernel, out_shape=[jax.ShapeDtypeStruct(shape, dtype) if i...  44.5 us
    ppermute x2, starting transfers between devices, shift_along(): return lax.ppermute(value, axis, pairs)  4.9 us
    ppermute x2, waiting for transfers between devices, shift_along(): return lax.ppermute(value, axis, pairs)  4.85 us
  transfers between devices with their start and end apart: 51, of which 23 were waited for; matrix products, arithmetic and copies ran while one was open for 0% of the time, Pallas kernels for 21%

profile of v4, /device:TPU:0, one launch (start us, length us, event | category | flops | bytes accessed | tf_op | source)
XLA Modules:
  0.0 179.1 jit_solution(10684892661195353890)
XLA Ops:
  0.7 1.7 shard_map.202
  2.4 3.1 %collective-permute-start = (bf16[9,64,128]{2,1,0:T(8,128)(2,1)S(1)}, bf16[9,64,128]{2,1,0:T(8,128)(2,1)S(1)}, u32[]{:S(2)}, u32[]{:S(2)}) collective-permute-start(bf16[9,64,128]{2,1,0:T(8,128)(2,1)S(1)} %get-tuple-element.105), channel_id=1, source_target_pairs={{0,2},{1,3},{2,0},{3,1},{4,6},{5,7},{6,4},{7,5},{8,10},{9,11},{10,... | collective-permute-start | bytes 442376 | tf_op jit(solution)/shard_map/ppermute | solution.py:32
  5.5 2.6 %collective-permute-start.3 = (bf16[9,64,128]{2,1,0:T(8,128)(2,1)S(1)}, bf16[9,64,128]{2,1,0:T(8,128)(2,1)S(1)}, u32[]{:S(2)}, u32[]{:S(2)}) collective-permute-start(bf16[9,64,128]{2,1,0:T(8,128)(2,1)S(1)} %get-tuple-element.105), channel_id=1, source_target_pairs={{0,4},{1,5},{2,6},{3,7},{4,0},{5,1},{6,2},{7,3},{8,12},{9,13},{10,... | collective-permute-start | bytes 442376 | tf_op jit(solution)/shard_map/ppermute | solution.py:32
  8.1 3.6 %collective-permute-start.1 = (bf16[2,32,512]{2,1,0:T(8,128)(2,1)S(1)}, bf16[2,32,512]{2,1,0:T(8,128)(2,1)S(1)}, u32[]{:S(2)}, u32[]{:S(2)}) collective-permute-start(bf16[2,32,512]{2,1,0:T(8,128)(2,1)S(1)} %get-tuple-element.109), channel_id=1, source_target_pairs={{0,8},{8,16},{16,24},{1,9},{9,17},{17,25},{2,10},{10,18},{18,26},{... | collective-permute-start | bytes 196616 | tf_op jit(solution)/shard_map/ppermute | solution.py:38
  13.6 4.3 %collective-permute-done.2.right = bf16[2,32,512]{2,1,0:T(8,128)(2,1)S(1)} collective-permute-done((bf16[2,32,512]{2,1,0:T(8,128)(2,1)S(1)}, bf16[2,32,512]{2,1,0:T(8,128)(2,1)S(1)}, u32[]{:S(2)}, u32[]{:S(2)}) %collective-permute-start.2) | collective-permute-done | bytes 65568 | tf_op jit(solution)/shard_map/ppermute | solution.py:38
  23.8 2.3 %collective-permute-start.10 = (bf16[128,512]{1,0:T(8,128)(2,1)S(1)}, bf16[128,512]{1,0:T(8,128)(2,1)S(1)}, u32[]{:S(2)}, u32[]{:S(2)}) collective-permute-start(bf16[128,512]{1,0:T(8,128)(2,1)S(1)} %get-tuple-element.118), channel_id=1, source_target_pairs={{0,6},{1,7},{2,4},{3,5},{4,2},{5,3},{6,0},{7,1},{8,14},{9,15},{10,... | collective-permute-start | bytes 393224 | tf_op jit(solution)/shard_map/ppermute | solution.py:32
  27.7 5.4 %collective-permute-done.11.rest_1_ = bf16[3,9,64,128]{3,2,1,0:T(8,128)(2,1)S(1)} collective-permute-done((bf16[3,9,64,128]{3,2,1,0:T(8,128)(2,1)S(1)}, bf16[3,9,64,128]{3,2,1,0:T(8,128)(2,1)S(1)}, u32[]{:S(2)}, u32[]{:S(2)}) %collective-permute-start.11) | collective-permute-done | bytes 442400 | tf_op jit(solution)/shard_map/ppermute | solution.py:32
  33.2 3.3 %collective-permute-start.9 = (bf16[128,512]{1,0:T(8,128)(2,1)S(1)}, bf16[128,512]{1,0:T(8,128)(2,1)S(1)}, u32[]{:S(2)}, u32[]{:S(2)}) collective-permute-start(bf16[128,512]{1,0:T(8,128)(2,1)S(1)} %get-tuple-element.118), channel_id=1, source_target_pairs={{0,4},{1,5},{2,6},{3,7},{4,0},{5,1},{6,2},{7,3},{8,12},{9,13},{10,... | collective-permute-start | bytes 393224 | tf_op jit(solution)/shard_map/ppermute | solution.py:32
  36.5 6.9 %collective-permute-done.12.rest_2_ = bf16[3,9,64,128]{3,2,1,0:T(8,128)(2,1)S(1)} collective-permute-done((bf16[3,9,64,128]{3,2,1,0:T(8,128)(2,1)S(1)}, bf16[3,9,64,128]{3,2,1,0:T(8,128)(2,1)S(1)}, u32[]{:S(2)}, u32[]{:S(2)}) %collective-permute-start.12) | collective-permute-done | bytes 442400 | tf_op jit(solution)/shard_map/ppermute | solution.py:32
  47.7 6.6 %shard_map.204 = (f32[512,512]{1,0:T(8,128)S(1)}, f32[512,512]{1,0:T(8,128)S(1)}, bf16[9,4,2,64,512]{4,3,2,1,0:T(8,128)(2,1)S(1)}) custom-call(s32[2,8]{1,0:T(2,128)S(1)} %copy-done.9, f32[10,512]{1,0:T(8,128)S(1)} %copy-done.8, bf16[2,256,512]{2,1,0:T(8,128)(2,1)S(1)} %copy-done.1, bf16[2,32,512]{2,1,0:T(8,128)(2,1)S(1)} %collective-permute-done.1.left, ...), custom_call_target="tpu_custom_call" | custom-call | flops 1 | bytes 1 | tf_op jit(solution)/shard_map/pallas_call | solution.py:118
  54.3 1.8 %collective-permute-done.17.refs_6_ = bf16[3,128,512]{2,1,0:T(8,128)(2,1)S(1)} collective-permute-done((bf16[3,128,512]{2,1,0:T(8,128)(2,1)S(1)}, bf16[3,128,512]{2,1,0:T(8,128)(2,1)S(1)}, u32[]{:S(2)}, u32[]{:S(2)}) %collective-permute-start.17) | collective-permute-done | bytes 393248 | tf_op jit(solution)/shard_map/ppermute | solution.py:32
  56.1 7.3 %collective-permute-done.18.refs_7_ = bf16[3,128,512]{2,1,0:T(8,128)(2,1)S(1)} collective-permute-done((bf16[3,128,512]{2,1,0:T(8,128)(2,1)S(1)}, bf16[3,128,512]{2,1,0:T(8,128)(2,1)S(1)}, u32[]{:S(2)}, u32[]{:S(2)}) %collective-permute-start.18) | collective-permute-done | bytes 393248 | tf_op jit(solution)/shard_map/ppermute | solution.py:32
  71.4 9.7 %shard_map.206 = (bf16[512,512]{1,0:T(8,128)(2,1)}, bf16[512,512]{1,0:T(8,128)(2,1)S(1)}, bf16[512,2048]{1,0:T(8,128)(2,1)S(1)}, bf16[512,512]{1,0:T(8,128)(2,1)...) custom-call(f32[512,512]{1,0:T(8,128)S(1)} %get-tuple-element.123.refs_0_, ...), custom_call_target="tpu_custom_call" | custom-call | flops 1 | bytes 1 | tf_op jit(solution)/shard_map/pallas_call | solution.py:118
  81.1 3.3 %shard_map.207 = (bf16[4,4,128,512]{3,2,1,0:T(8,128)(2,1)S(1)}, bf16[4,4,128,512]{3,2,1,0:T(8,128)(2,1)S(1)}) custom-call(bf16[512,512]{1,0:T(8,128)(2,1)S(1)} %get-tuple-element.136.refs_0_, bf16[512,2048]{1,0:T(8,128)(2,1)S(1)} %get-tuple-element.137.refs_1_, bf16[512,512]{1,0:T(8,128)(2,1)S(1)} %get-tuple-element.138.refs_2_, ...), custom_call_target="tpu_custom_call" | custom-call | flops 1 | bytes 1 | tf_op jit(solution)/shard_map/pallas_call | solution.py:118
  84.3 2.7 %shard_map.208 = (f32[512,512]{1,0:T(8,128)S(1)}, bf16[512,512]{1,0:T(8,128)(2,1)S(1)}, bf16[640,128]{1,0:T(8,128)(2,1)S(1)}, bf16[896,128]{1,0:T(8,128)(2,1)S(1...) custom-call(f32[512,512]{1,0:T(8,128)S(1)} %get-tuple-element.141.refs_0_, bf16[512,512]{1,0:T(8,128)(2,1)S(1)} %bitcast.9, ...), custom_call_target="tpu_custom_call" | custom-call | flops 1 | bytes 1 | tf_op jit(solution)/shard_map/pallas_call | solution.py:118
  87.0 4.1 %collective-permute-done.25.refs_3_ = bf16[2,256,512]{2,1,0:T(8,128)(2,1)S(1)} collective-permute-done((bf16[2,256,512]{2,1,0:T(8,128)(2,1)S(1)}, bf16[2,256,512]{2,1,0:T(8,128)(2,1)S(1)}, u32[]{:S(2)}, u32[]{:S(2)}) %collective-permute-start.25) | collective-permute-done | bytes 524320 | tf_op jit(solution)/shard_map/ppermute | solution.py:32
  92.4 1.8 collective-permute-start.29
  94.7 4.9 %collective-permute-done.27.refs_6_.refs_4_ = bf16[896,128]{1,0:T(8,128)(2,1)S(1)} collective-permute-done((bf16[896,128]{1,0:T(8,128)(2,1)S(1)}, bf16[896,128]{1,0:T(8,128)(2,1)S(1)}, u32[]{:S(2)}, u32[]{:S(2)}) %collective-permute-start.27) | collective-permute-done | bytes 229408 | tf_op jit(solution)/shard_map/ppermute | solution.py:32
  100.6 4.5 %collective-permute-done.29.refs_8_.refs_5_ = bf16[896,128]{1,0:T(8,128)(2,1)S(1)} collective-permute-done((bf16[896,128]{1,0:T(8,128)(2,1)S(1)}, bf16[896,128]{1,0:T(8,128)(2,1)S(1)}, u32[]{:S(2)}, u32[]{:S(2)}) %collective-permute-start.29) | collective-permute-done | bytes 229408 | tf_op jit(solution)/shard_map/ppermute | solution.py:32
  105.1 6.6 %shard_map.209 = (bf16[2432,128]{1,0:T(8,128)(2,1)S(1)}, bf16[2432,128]{1,0:T(8,128)(2,1)S(1)}) custom-call(s32[2,8]{1,0:T(2,128)S(1)} %copy-done.9, bf16[2,256,512]{2,1,0:T(8,128)(2,1)S(1)} %copy-done.1, bf16[2,256,512]{2,1,0:T(8,128)(2,1)S(1)} %collective-permute-done.24.refs_2_, bf16[2,256,512]{2,1,0:T(8,128)(2,1)S(1)} %collective-permute-done.25.refs_3_, ...), custom_call_target="tpu_custom_call" | custom-call | flops 1 | bytes 1 | tf_op jit(solution)/shard_map/pallas_call | solution.py:118
  114.3 1.7 collective-permute-start.39
  116.4 2.4 %collective-permute-start.31 = (bf16[704,128]{1,0:T(8,128)(2,1)S(1)}, bf16[704,128]{1,0:T(8,128)(2,1)S(1)}, u32[]{:S(2)}, u32[]{:S(2)}) collective-permute-start(bf16[704,128]{1,0:T(8,128)(2,1)S(1)} %get-tuple-element.169), channel_id=1, source_target_pairs={{0,2},{1,3},{2,0},{3,1},{4,6},{5,7},{6,4},{7,5},{8,10},{9,11},{10,... | collective-permute-start | bytes 540680 | tf_op jit(solution)/shard_map/ppermute | solution.py:32
  119.9 6.6 %collective-permute-done.31.refs_1_ = bf16[704,128]{1,0:T(8,128)(2,1)S(1)} collective-permute-done((bf16[704,128]{1,0:T(8,128)(2,1)S(1)}, bf16[704,128]{1,0:T(8,128)(2,1)S(1)}, u32[]{:S(2)}, u32[]{:S(2)}) %collective-permute-start.31) | collective-permute-done | bytes 180256 | tf_op jit(solution)/shard_map/ppermute | solution.py:32
  126.5 1.7 collective-permute-start.33
  128.2 7.4 %shard_map.211 = f32[512,512]{1,0:T(8,128)} custom-call(s32[2,8]{1,0:T(2,128)S(1)} %copy-done.9, bf16[512,512]{1,0:T(8,128)(2,1)S(1)} %get-tuple-element.164.refs_1_, f32[512,512]{1,0:T(8,128)S(1)} %get-tuple-element.165.refs_2_, bf16[9,4,2,64,512]{4,3,2,1,0:T(8,128)(2,1)S(1)} %get-tuple-element.166.refs_3_, ...), custom_call_target="tpu_custom_call" | custom-call | flops 1 | bytes 1 | tf_op jit(solution)/shard_map/pallas_call | solution.py:118
  137.1 2.8 %collective-permute-done.38.refs_2_ = bf16[512,512]{1,0:T(8,128)(2,1)S(1)} collective-permute-done((bf16[512,512]{1,0:T(8,128)(2,1)S(1)}, bf16[512,512]{1,0:T(8,128)(2,1)S(1)}, u32[]{:S(2)}, u32[]{:S(2)}) %collective-permute-start.38) | collective-permute-done | bytes 524320 | tf_op jit(solution)/shard_map/ppermute | solution.py:32
  141.0 2.7 %collective-permute-start.42 = (bf16[128,512]{1,0:T(8,128)(2,1)S(1)}, bf16[128,512]{1,0:T(8,128)(2,1)S(1)}, u32[]{:S(2)}, u32[]{:S(2)}) collective-permute-start(bf16[128,512]{1,0:T(8,128)(2,1)S(1)} %get-tuple-element.183), channel_id=1, source_target_pairs={{0,4},{1,5},{2,6},{3,7},{4,0},{5,1},{6,2},{7,3},{8,12},{9,13},{10,... | collective-permute-start | bytes 393224 | tf_op jit(solution)/shard_map/ppermute | solution.py:32
  146.4 7.1 %collective-permute-done.42.refs_2_ = bf16[128,512]{1,0:T(8,128)(2,1)S(1)} collective-permute-done((bf16[128,512]{1,0:T(8,128)(2,1)S(1)}, bf16[128,512]{1,0:T(8,128)(2,1)S(1)}, u32[]{:S(2)}, u32[]{:S(2)}) %collective-permute-start.42) | collective-permute-done | bytes 131104 | tf_op jit(solution)/shard_map/ppermute | solution.py:32
  160.1 1.7 collective-permute-done.46.refs_3_.refs_7_
  161.8 4.0 %collective-permute-start.47 = (f32[8,128]{1,0:T(8,128)S(1)}, f32[8,128]{1,0:T(8,128)S(1)}, u32[]{:S(2)}, u32[]{:S(2)}) collective-permute-start(f32[8,128]{1,0:T(8,128)S(1)} %shard_map.216.refs_0_), channel_id=1, source_target_pairs={{0,2},{1,3},{2,0},{3,1},{4,6},{5,7},{6,4},{7,5},{8,10},{9,11},{10,... | collective-permute-start | bytes 12296 | tf_op jit(solution)/shard_map/ppermute | solution.py:32
  170.3 2.5 %collective-permute-done.49.refs_3_ = f32[8,128]{1,0:T(8,128)S(1)} collective-permute-done((f32[8,128]{1,0:T(8,128)S(1)}, f32[8,128]{1,0:T(8,128)S(1)}, u32[]{:S(2)}, u32[]{:S(2)}) %collective-permute-start.49) | collective-permute-done | bytes 4128 | tf_op jit(solution)/shard_map/ppermute | solution.py:32
  174.0 4.9 %shard_map.218 = (f32[1,1]{1,0:T(1,128)}, f32[10,512]{1,0:T(8,128)}, f32[10,512]{1,0:T(8,128)}, f32[9,64,512]{2,1,0:T(8,128)}, f32[9,64,512]{2,1,0:T(8,128)}, /*...) custom-call(bf16[576,128]{1,0:T(8,128)(2,1)S(1)} %get-tuple-element., ...), custom_call_target="tpu_custom_call" | custom-call | flops 1 | bytes 1 | tf_op jit(solution)/shard_map/pallas_call | solution.py:118
  (110 shorter events, 45.9 us)
Async XLA Ops:
  2.4 10.6 %collective-permute-start = (bf16[9,64,128]{2,1,0:T(8,128)(2,1)S(1)}, bf16[9,64,128]{2,1,0:T(8,128)(2,1)S(1)}, u32[]{:S(2)}, u32[]{:S(2)}) collective-permute-start(bf16[9,64,128]{2,1,0:T(8,128)(2,1)S(1)} %get-tuple-element.105), channel_id=1, source_target_pairs={{0,2},{1,3},{2,0},{3,1},{4,6},{5,7},{6,4},{7,5},{8,10},{9,11},{10,... | collective-permute-start | bytes 442376 | tf_op jit(solution)/shard_map/ppermute | solution.py:32
  5.5 14.0 %collective-permute-start.3 = (bf16[9,64,128]{2,1,0:T(8,128)(2,1)S(1)}, bf16[9,64,128]{2,1,0:T(8,128)(2,1)S(1)}, u32[]{:S(2)}, u32[]{:S(2)}) collective-permute-start(bf16[9,64,128]{2,1,0:T(8,128)(2,1)S(1)} %get-tuple-element.105), channel_id=1, source_target_pairs={{0,4},{1,5},{2,6},{3,7},{4,0},{5,1},{6,2},{7,3},{8,12},{9,13},{10,... | collective-permute-start | bytes 442376 | tf_op jit(solution)/shard_map/ppermute | solution.py:32
  8.1 11.4 %collective-permute-start.4 = (bf16[9,64,128]{2,1,0:T(8,128)(2,1)S(1)}, bf16[9,64,128]{2,1,0:T(8,128)(2,1)S(1)}, u32[]{:S(2)}, u32[]{:S(2)}) collective-permute-start(bf16[9,64,128]{2,1,0:T(8,128)(2,1)S(1)} %get-tuple-element.105), channel_id=1, source_target_pairs={{0,6},{1,7},{2,4},{3,5},{4,2},{5,3},{6,0},{7,1},{8,14},{9,15},{10,... | collective-permute-start | bytes 442376 | tf_op jit(solution)/shard_map/ppermute | solution.py:32
  11.7 6.2 %collective-permute-start.2 = (bf16[2,32,512]{2,1,0:T(8,128)(2,1)S(1)}, bf16[2,32,512]{2,1,0:T(8,128)(2,1)S(1)}, u32[]{:S(2)}, u32[]{:S(2)}) collective-permute-start(bf16[2,32,512]{2,1,0:T(8,128)(2,1)S(1)} %get-tuple-element.110), channel_id=1, source_target_pairs={{8,0},{16,8},{24,16},{9,1},{17,9},{25,17},{10,2},{18,10},{26,18},{... | collective-permute-start | bytes 196616 | tf_op jit(solution)/shard_map/ppermute | solution.py:38
  20.2 13.0 %collective-permute-start.11 = (bf16[3,9,64,128]{3,2,1,0:T(8,128)(2,1)S(1)}, bf16[3,9,64,128]{3,2,1,0:T(8,128)(2,1)S(1)}, u32[]{:S(2)}, u32[]{:S(2)}) collective-permute-start(bf16[3,9,64,128]{3,2,1,0:T(8,128)(2,1)S(1)} %shard_map.203.rest_0_), channel_id=1, source_target_pairs={{0,8},{8,0},{16,24},{24,16},{1,9},{9,1},{17,25},{25,17},{2,10},{10... | collective-permute-start | bytes 1327112 | tf_op jit(solution)/shard_map/ppermute | solution.py:32
  21.7 21.7 %collective-permute-start.12 = (bf16[3,9,64,128]{3,2,1,0:T(8,128)(2,1)S(1)}, bf16[3,9,64,128]{3,2,1,0:T(8,128)(2,1)S(1)}, u32[]{:S(2)}, u32[]{:S(2)}) collective-permute-start(bf16[3,9,64,128]{3,2,1,0:T(8,128)(2,1)S(1)} %shard_map.203.rest_0_), channel_id=1, source_target_pairs={{0,16},{8,24},{16,0},{24,8},{1,17},{9,25},{17,1},{25,9},{2,18},{10... | collective-permute-start | bytes 1327112 | tf_op jit(solution)/shard_map/ppermute | solution.py:32
  23.2 20.2 %collective-permute-start.13 = (bf16[3,9,64,128]{3,2,1,0:T(8,128)(2,1)S(1)}, bf16[3,9,64,128]{3,2,1,0:T(8,128)(2,1)S(1)}, u32[]{:S(2)}, u32[]{:S(2)}) collective-permute-start(bf16[3,9,64,128]{3,2,1,0:T(8,128)(2,1)S(1)} %shard_map.203.rest_0_), channel_id=1, source_target_pairs={{0,24},{8,16},{16,8},{24,0},{1,25},{9,17},{17,9},{25,1},{2,26},{10... | collective-permute-start | bytes 1327112 | tf_op jit(solution)/shard_map/ppermute | solution.py:32
  23.8 19.6 %collective-permute-start.10 = (bf16[128,512]{1,0:T(8,128)(2,1)S(1)}, bf16[128,512]{1,0:T(8,128)(2,1)S(1)}, u32[]{:S(2)}, u32[]{:S(2)}) collective-permute-start(bf16[128,512]{1,0:T(8,128)(2,1)S(1)} %get-tuple-element.118), channel_id=1, source_target_pairs={{0,6},{1,7},{2,4},{3,5},{4,2},{5,3},{6,0},{7,1},{8,14},{9,15},{10,... | collective-permute-start | bytes 393224 | tf_op jit(solution)/shard_map/ppermute | solution.py:32
  26.1 17.3 %collective-permute-start.8 = (bf16[128,512]{1,0:T(8,128)(2,1)S(1)}, bf16[128,512]{1,0:T(8,128)(2,1)S(1)}, u32[]{:S(2)}, u32[]{:S(2)}) collective-permute-start(bf16[128,512]{1,0:T(8,128)(2,1)S(1)} %get-tuple-element.118), channel_id=1, source_target_pairs={{0,2},{1,3},{2,0},{3,1},{4,6},{5,7},{6,4},{7,5},{8,10},{9,11},{10,... | collective-permute-start | bytes 393224 | tf_op jit(solution)/shard_map/ppermute | solution.py:32
  33.2 10.3 %collective-permute-start.9 = (bf16[128,512]{1,0:T(8,128)(2,1)S(1)}, bf16[128,512]{1,0:T(8,128)(2,1)S(1)}, u32[]{:S(2)}, u32[]{:S(2)}) collective-permute-start(bf16[128,512]{1,0:T(8,128)(2,1)S(1)} %get-tuple-element.118), channel_id=1, source_target_pairs={{0,4},{1,5},{2,6},{3,7},{4,0},{5,1},{6,2},{7,3},{8,12},{9,13},{10,... | collective-permute-start | bytes 393224 | tf_op jit(solution)/shard_map/ppermute | solution.py:32
  44.2 12.0 %collective-permute-start.17 = (bf16[3,128,512]{2,1,0:T(8,128)(2,1)S(1)}, bf16[3,128,512]{2,1,0:T(8,128)(2,1)S(1)}, u32[]{:S(2)}, u32[]{:S(2)}) collective-permute-start(bf16[3,128,512]{2,1,0:T(8,128)(2,1)S(1)} %get-tuple-element.131.refs_5_), channel_id=1, source_target_pairs={{0,8},{8,0},{16,24},{24,16},{1,9},{9,1},{17,25},{25,17},{2,10},{10... | collective-permute-start | bytes 1179656 | tf_op jit(solution)/shard_map/ppermute | solution.py:32
  45.4 18.0 %collective-permute-start.18 = (bf16[3,128,512]{2,1,0:T(8,128)(2,1)S(1)}, bf16[3,128,512]{2,1,0:T(8,128)(2,1)S(1)}, u32[]{:S(2)}, u32[]{:S(2)}) collective-permute-start(bf16[3,128,512]{2,1,0:T(8,128)(2,1)S(1)} %get-tuple-element.131.refs_5_), channel_id=1, source_target_pairs={{0,16},{8,24},{16,0},{24,8},{1,17},{9,25},{17,1},{25,9},{2,18},{10... | collective-permute-start | bytes 1179656 | tf_op jit(solution)/shard_map/ppermute | solution.py:32
  46.3 18.8 %collective-permute-start.19 = (bf16[3,128,512]{2,1,0:T(8,128)(2,1)S(1)}, bf16[3,128,512]{2,1,0:T(8,128)(2,1)S(1)}, u32[]{:S(2)}, u32[]{:S(2)}) collective-permute-start(bf16[3,128,512]{2,1,0:T(8,128)(2,1)S(1)} %get-tuple-element.131.refs_5_), channel_id=1, source_target_pairs={{0,24},{8,16},{16,8},{24,0},{1,25},{9,17},{17,9},{25,1},{2,26},{10... | collective-permute-start | bytes 1179656 | tf_op jit(solution)/shard_map/ppermute | solution.py:32
  65.6 21.4 %collective-permute-start.24 = (bf16[2,256,512]{2,1,0:T(8,128)(2,1)S(1)}, bf16[2,256,512]{2,1,0:T(8,128)(2,1)S(1)}, u32[]{:S(2)}, u32[]{:S(2)}) collective-permute-start(bf16[2,256,512]{2,1,0:T(8,128)(2,1)S(1)} %copy-done.1), channel_id=1, source_target_pairs={{0,8},{8,0},{16,24},{24,16},{1,9},{9,1},{17,25},{25,17},{2,10},{10... | collective-permute-start | bytes 1572872 | tf_op jit(solution)/shard_map/ppermute | solution.py:32
  66.4 24.8 %collective-permute-start.25 = (bf16[2,256,512]{2,1,0:T(8,128)(2,1)S(1)}, bf16[2,256,512]{2,1,0:T(8,128)(2,1)S(1)}, u32[]{:S(2)}, u32[]{:S(2)}) collective-permute-start(bf16[2,256,512]{2,1,0:T(8,128)(2,1)S(1)} %copy-done.1), channel_id=1, source_target_pairs={{0,16},{8,24},{16,0},{24,8},{1,17},{9,25},{17,1},{25,9},{2,18},{10... | collective-permute-start | bytes 1572872 | tf_op jit(solution)/shard_map/ppermute | solution.py:32
  67.9 23.3 %collective-permute-start.26 = (bf16[2,256,512]{2,1,0:T(8,128)(2,1)S(1)}, bf16[2,256,512]{2,1,0:T(8,128)(2,1)S(1)}, u32[]{:S(2)}, u32[]{:S(2)}) collective-permute-start(bf16[2,256,512]{2,1,0:T(8,128)(2,1)S(1)} %copy-done.1), channel_id=1, source_target_pairs={{0,24},{8,16},{16,8},{24,0},{1,25},{9,17},{17,9},{25,1},{2,26},{10... | collective-permute-start | bytes 1572872 | tf_op jit(solution)/shard_map/ppermute | solution.py:32
  91.2 20.6 %collective-permute-start.36 = (bf16[4,4,128,512]{3,2,1,0:T(8,128)(2,1)S(1)}, bf16[4,4,128,512]{3,2,1,0:T(8,128)(2,1)S(1)}, u32[]{:S(2)}, u32[]{:S(2)}) collective-permute-start(bf16[4,4,128,512]{3,2,1,0:T(8,128)(2,1)S(1)} %get-tuple-element.174), channel_id=1, source_target_pairs={{0,1},{1,0},{2,3},{3,2},{4,5},{5,4},{6,7},{7,6},{8,9},{9,8},{10,11... | collective-permute-start | bytes 6291464 | tf_op jit(solution)/shard_map/ppermute | solution.py:32
  91.2 8.4 %collective-permute-start.27 = (bf16[896,128]{1,0:T(8,128)(2,1)S(1)}, bf16[896,128]{1,0:T(8,128)(2,1)S(1)}, u32[]{:S(2)}, u32[]{:S(2)}) collective-permute-start(bf16[896,128]{1,0:T(8,128)(2,1)S(1)} %get-tuple-element.157), channel_id=1, source_target_pairs={{0,8},{8,0},{16,24},{24,16},{1,9},{9,1},{17,25},{25,17},{2,10},{10... | collective-permute-start | bytes 688136 | tf_op jit(solution)/shard_map/ppermute | solution.py:32
  92.4 12.7 %collective-permute-start.29 = (bf16[896,128]{1,0:T(8,128)(2,1)S(1)}, bf16[896,128]{1,0:T(8,128)(2,1)S(1)}, u32[]{:S(2)}, u32[]{:S(2)}) collective-permute-start(bf16[896,128]{1,0:T(8,128)(2,1)S(1)} %get-tuple-element.160), channel_id=1, source_target_pairs={{0,24},{8,16},{16,8},{24,0},{1,25},{9,17},{17,9},{25,1},{2,26},{10... | collective-permute-start | bytes 688136 | tf_op jit(solution)/shard_map/ppermute | solution.py:32
  94.1 6.4 %collective-permute-start.28 = (bf16[640,128]{1,0:T(8,128)(2,1)S(1)}, bf16[640,128]{1,0:T(8,128)(2,1)S(1)}, u32[]{:S(2)}, u32[]{:S(2)}) collective-permute-start(bf16[640,128]{1,0:T(8,128)(2,1)S(1)} %get-tuple-element.159), channel_id=1, source_target_pairs={{0,16},{8,24},{16,0},{24,8},{1,17},{9,25},{17,1},{25,9},{2,18},{10... | collective-permute-start | bytes 491528 | tf_op jit(solution)/shard_map/ppermute | solution.py:32
  112.5 24.6 %collective-permute-start.37 = (bf16[512,512]{1,0:T(8,128)(2,1)S(1)}, bf16[512,512]{1,0:T(8,128)(2,1)S(1)}, u32[]{:S(2)}, u32[]{:S(2)}) collective-permute-start(bf16[512,512]{1,0:T(8,128)(2,1)S(1)} %get-tuple-element.176), channel_id=1, source_target_pairs={{0,8},{8,0},{16,24},{24,16},{1,9},{9,1},{17,25},{25,17},{2,10},{10... | collective-permute-start | bytes 1572872 | tf_op jit(solution)/shard_map/ppermute | solution.py:32
  113.1 26.8 %collective-permute-start.38 = (bf16[512,512]{1,0:T(8,128)(2,1)S(1)}, bf16[512,512]{1,0:T(8,128)(2,1)S(1)}, u32[]{:S(2)}, u32[]{:S(2)}) collective-permute-start(bf16[512,512]{1,0:T(8,128)(2,1)S(1)} %get-tuple-element.177), channel_id=1, source_target_pairs={{0,16},{8,24},{16,0},{24,8},{1,17},{9,25},{17,1},{25,9},{2,18},{10... | collective-permute-start | bytes 1572872 | tf_op jit(solution)/shard_map/ppermute | solution.py:32
  114.3 25.6 %collective-permute-start.39 = (bf16[512,512]{1,0:T(8,128)(2,1)S(1)}, bf16[512,512]{1,0:T(8,128)(2,1)S(1)}, u32[]{:S(2)}, u32[]{:S(2)}) collective-permute-start(bf16[512,512]{1,0:T(8,128)(2,1)S(1)} %get-tuple-element.178), channel_id=1, source_target_pairs={{0,24},{8,16},{16,8},{24,0},{1,25},{9,17},{17,9},{25,1},{2,26},{10... | collective-permute-start | bytes 1572872 | tf_op jit(solution)/shard_map/ppermute | solution.py:32
  116.4 10.1 %collective-permute-start.31 = (bf16[704,128]{1,0:T(8,128)(2,1)S(1)}, bf16[704,128]{1,0:T(8,128)(2,1)S(1)}, u32[]{:S(2)}, u32[]{:S(2)}) collective-permute-start(bf16[704,128]{1,0:T(8,128)(2,1)S(1)} %get-tuple-element.169), channel_id=1, source_target_pairs={{0,2},{1,3},{2,0},{3,1},{4,6},{5,7},{6,4},{7,5},{8,10},{9,11},{10,... | collective-permute-start | bytes 540680 | tf_op jit(solution)/shard_map/ppermute | solution.py:32
  118.8 16.9 %collective-permute-start.32 = (bf16[704,128]{1,0:T(8,128)(2,1)S(1)}, bf16[704,128]{1,0:T(8,128)(2,1)S(1)}, u32[]{:S(2)}, u32[]{:S(2)}) collective-permute-start(bf16[704,128]{1,0:T(8,128)(2,1)S(1)} %get-tuple-element.170), channel_id=1, source_target_pairs={{0,4},{1,5},{2,6},{3,7},{4,0},{5,1},{6,2},{7,3},{8,12},{9,13},{10,... | collective-permute-start | bytes 540680 | tf_op jit(solution)/shard_map/ppermute | solution.py:32
  126.5 9.2 %collective-permute-start.33 = (bf16[704,128]{1,0:T(8,128)(2,1)S(1)}, bf16[704,128]{1,0:T(8,128)(2,1)S(1)}, u32[]{:S(2)}, u32[]{:S(2)}) collective-permute-start(bf16[704,128]{1,0:T(8,128)(2,1)S(1)} %get-tuple-element.171), channel_id=1, source_target_pairs={{0,6},{1,7},{2,4},{3,5},{4,2},{5,3},{6,0},{7,1},{8,14},{9,15},{10,... | collective-permute-start | bytes 540680 | tf_op jit(solution)/shard_map/ppermute | solution.py:32
  135.9 9.2 %collective-permute-start.40 = (bf16[576,128]{1,0:T(8,128)(2,1)S(1)}, bf16[576,128]{1,0:T(8,128)(2,1)S(1)}, u32[]{:S(2)}, u32[]{:S(2)}) collective-permute-start(bf16[576,128]{1,0:T(8,128)(2,1)S(1)} %get-tuple-element.172.refs_0_), channel_id=1, source_target_pairs={{0,24},{8,16},{16,8},{24,0},{1,25},{9,17},{17,9},{25,1},{2,26},{10... | collective-permute-start | bytes 442376 | tf_op jit(solution)/shard_map/ppermute | solution.py:32
  141.0 12.5 %collective-permute-start.42 = (bf16[128,512]{1,0:T(8,128)(2,1)S(1)}, bf16[128,512]{1,0:T(8,128)(2,1)S(1)}, u32[]{:S(2)}, u32[]{:S(2)}) collective-permute-start(bf16[128,512]{1,0:T(8,128)(2,1)S(1)} %get-tuple-element.183), channel_id=1, source_target_pairs={{0,4},{1,5},{2,6},{3,7},{4,0},{5,1},{6,2},{7,3},{8,12},{9,13},{10,... | collective-permute-start | bytes 393224 | tf_op jit(solution)/shard_map/ppermute | solution.py:32
  143.7 9.8 %collective-permute-start.43 = (bf16[128,512]{1,0:T(8,128)(2,1)S(1)}, bf16[128,512]{1,0:T(8,128)(2,1)S(1)}, u32[]{:S(2)}, u32[]{:S(2)}) collective-permute-start(bf16[128,512]{1,0:T(8,128)(2,1)S(1)} %get-tuple-element.184), channel_id=1, source_target_pairs={{0,6},{1,7},{2,4},{3,5},{4,2},{5,3},{6,0},{7,1},{8,14},{9,15},{10,... | collective-permute-start | bytes 393224 | tf_op jit(solution)/shard_map/ppermute | solution.py:32
  157.1 15.7 %collective-permute-start.34 = (bf16[576,128]{1,0:T(8,128)(2,1)S(1)}, bf16[576,128]{1,0:T(8,128)(2,1)S(1)}, u32[]{:S(2)}, u32[]{:S(2)}) collective-permute-start(bf16[576,128]{1,0:T(8,128)(2,1)S(1)} %get-tuple-element.172.refs_0_), channel_id=1, source_target_pairs={{0,8},{8,0},{16,24},{24,16},{1,9},{9,1},{17,25},{25,17},{2,10},{10... | collective-permute-start | bytes 442376 | tf_op jit(solution)/shard_map/ppermute | solution.py:32
  158.4 14.4 %collective-permute-start.35 = (bf16[576,128]{1,0:T(8,128)(2,1)S(1)}, bf16[576,128]{1,0:T(8,128)(2,1)S(1)}, u32[]{:S(2)}, u32[]{:S(2)}) collective-permute-start(bf16[576,128]{1,0:T(8,128)(2,1)S(1)} %get-tuple-element.172.refs_0_), channel_id=1, source_target_pairs={{0,16},{8,24},{16,0},{24,8},{1,17},{9,25},{17,1},{25,9},{2,18},{10... | collective-permute-start | bytes 442376 | tf_op jit(solution)/shard_map/ppermute | solution.py:32
  161.8 7.0 %collective-permute-start.47 = (f32[8,128]{1,0:T(8,128)S(1)}, f32[8,128]{1,0:T(8,128)S(1)}, u32[]{:S(2)}, u32[]{:S(2)}) collective-permute-start(f32[8,128]{1,0:T(8,128)S(1)} %shard_map.216.refs_0_), channel_id=1, source_target_pairs={{0,2},{1,3},{2,0},{3,1},{4,6},{5,7},{6,4},{7,5},{8,10},{9,11},{10,... | collective-permute-start | bytes 12296 | tf_op jit(solution)/shard_map/ppermute | solution.py:32
  (30 other events, 542.6 us)

commit v5 on v4

--- a/solution.py
+++ b/solution.py
@@ -176,21 +176,17 @@
     lax.fori_loop(0, taps, body, 0)
 
 
-def round_kernel(ns, conv_far, inner_far, outer_far, tok_far, *refs):
-    conv_part, left_edge, right_edge, conv_own, ffn_own, ffn_part = refs[:6]
-    conv, inner, outer, sems = refs[6:]
-    half = left_edge.shape[1]
-    copies = begin_copies(
-        [
-            (conv_far, conv),
-            (inner_far, inner),
-            (outer_far, outer),
-            (tok_far.at[:, :half], left_edge),
-            (tok_far.at[:, tok_far.shape[1] - half :], right_edge),
-        ],
-        sems,
-    )
+def round_kernel(ns, masks, conv_far, inner_far, outer_far, tok_far, *refs):
+    conv_part, conv_own, ffn_own, ffn_part = refs[:4]
+    edges = refs[4 : 4 + len(masks)]
+    conv, inner, outer, sems = refs[4 + len(masks) :]
     seq_at = lax.axis_index("seq")
+    pairs = [(conv_far, conv), (inner_far, inner), (outer_far, outer)]
+    for mask, edge in zip(masks, edges):
+        half = edge.shape[1]
+        last = jnp.where((seq_at ^ mask) > seq_at, tok_far.shape[1] // half - 1, 0)
+        pairs.append((tok_far.at[:, at(last, half)], edge))
+    copies = begin_copies(pairs, sems)
     in_rows, hid = inner.shape
     quarter = hid // ns
     part = outer.shape[0] // ns
@@ -218,7 +214,8 @@
         rest[2][...] = rest[0][...]
 
 
-def conv_kernel(taps, nz, ns, lens, vec, tok, left, right, own, other, *rest):
+def conv_kernel(taps, nz, ns, masks, lens, vec, tok, own, other, *rest):
+    edges, rest = rest[: len(masks)], rest[len(masks) :]
     pieces = (rest[:ns], rest[ns : 2 * ns])
     pre, after, full, ext, cid, cat, sems = rest[2 * ns :]
     seq_at, z_at, core_at = place()
@@ -237,10 +234,17 @@
     span = length + 2 * half
     base = seq_at * length - half
     positions = base + lax.broadcasted_iota(jnp.int32, (span, LANES), 0)
+    ext[0:half, :] = jnp.zeros((half, width), F32)
+    ext[half + length :, :] = jnp.zeros((half, width), F32)
     for r in range(rows):
-        ext[0:half, :] = left[r].astype(F32)
         ext[half : half + length, :] = tok[r].astype(F32)
-        ext[half + length :, :] = right[r].astype(F32)
+        for mask, edge in zip(masks, edges):
+            for step, to, begin in ((-1, 0, edge.shape[1] - half), (1, half + length, 0)):
+
+                @pl.when((seq_at ^ mask) == seq_at + step)
+                def _(r=r, edge=edge, to=to, begin=begin):
+                    ext[to : to + half, :] = edge[r, begin : begin + half, :].astype(F32)
+
         cid[...] = contigs(lens, r, positions, length * ns)
 
         def store(tap, a, value, r=r):
@@ -662,8 +666,8 @@
     clipped = gradient * clip
     first = beta_one * first + (1.0 - beta_one) * clipped
     second = beta_two * second + (1.0 - beta_two) * clipped * clipped
-    first_hat = first / (1.0 - beta_one**step_count)
-    second_hat = second / (1.0 - beta_two**step_count)
+    first_hat = first * (1.0 / (1.0 - beta_one**step_count))
+    second_hat = second * (1.0 / (1.0 - beta_two**step_count))
     weight = weight - rate * (first_hat / (jnp.sqrt(second_hat) + adam_eps) + decay * weight)
     return weight, first, second
 
@@ -721,49 +725,37 @@
     send(0, new_conv, outs[0])
     send(1, conv_first, outs[1])
     send(2, second.at[:, : taps * width], outs[6].at[:, : taps * width])
-    chunks = quarter // LANES
-
     for k in range(ns):
-
-        def inner_step(a, carry, k=k):
-            lanes = at((seq_at ^ k) * chunks + a, LANES)
-            w, m, v = adam_math(
-                inner[:, lanes],
-                inner_m[0, :, lanes],
-                inner_m[1, :, lanes],
-                ffn_grads[k][0:in_rows, at(a, LANES)].astype(F32),
-                clip,
-                matrix_rate,
-                weight_decay,
-            )
-            new_inner[:, lanes] = w
-            inner_first[:, lanes] = m
-            second[:, at(taps * width // LANES + (seq_at ^ k) * chunks + a, LANES)] = v
-            return carry
-
-        lax.fori_loop(0, chunks, inner_step, 0)
+        lanes = at(seq_at ^ k, quarter)
+        w, m, v = adam_math(
+            inner[:, lanes],
+            inner_m[0, :, lanes],
+            inner_m[1, :, lanes],
+            ffn_grads[k][0:in_rows, :].astype(F32),
+            clip,
+            matrix_rate,
+            weight_decay,
+        )
+        new_inner[:, lanes] = w
+        inner_first[:, lanes] = m
+        second[:, at(taps * width // quarter + (seq_at ^ k), quarter)] = v
     send(3, new_inner, outs[2])
     send(4, inner_first, outs[3])
     for k in range(ns):
         where = at(seq_at ^ k, part)
-
-        def outer_step(a, carry, k=k, where=where):
-            lanes = at(a, LANES)
-            w, m, v = adam_math(
-                outer[where, lanes],
-                outer_m[0, where, lanes],
-                outer_m[1, where, lanes],
-                ffn_grads[k][in_rows : in_rows + part, lanes].astype(F32),
-                clip,
-                matrix_rate,
-                weight_decay,
-            )
-            new_outer[where, lanes] = w
-            outer_first[where, lanes] = m
-            outer_second[a, where, :] = v
-            return carry
-
-        lax.fori_loop(0, width // LANES, outer_step, 0)
+        w, m, v = adam_math(
+            outer[where, :],
+            outer_m[0, where, :],
+            outer_m[1, where, :],
+            ffn_grads[k][in_rows : in_rows + part, :].astype(F32),
+            clip,
+            matrix_rate,
+            weight_decay,
+        )
+        new_outer[where, :] = w
+        outer_first[where, :] = m
+        for a in range(width // LANES):
+            outer_second[a, where, :] = v[:, a * LANES : (a + 1) * LANES]
     send(5, new_outer, outs[4])
     send(6, outer_first, outs[5])
     ratio = out_rows // in_rows
@@ -820,35 +812,41 @@
         near = any(abs((i ^ k) - i) == 1 for i in range(ns))
         return rows * half * (width // LANES) if near else 0
 
-    conv_part, left_edge, right_edge, conv_own, ffn_own, ffn_part = vmem_call(
-        functools.partial(round_kernel, ns),
+    masks = [k for k in range(ns) if edge_rows(k)]
+    far_masks = [k for k in masks if k > 1]
+    rounded = vmem_call(
+        functools.partial(round_kernel, ns, far_masks),
         [
             ((taps, in_rows, span), BF),
-            ((rows, half, width), BF),
-            ((rows, half, width), BF),
             (conv_weight.shape, BF),
             ((ns * ffn_rows, width), BF),
             ((ffn_rows, width), BF),
-        ],
+        ]
+        + [((rows, half, width), BF)] * len(far_masks),
         [
             pltpu.VMEM(conv_weight.shape, F32),
             pltpu.VMEM(inner_weight.shape, F32),
             pltpu.VMEM(outer_weight.shape, F32),
-            pltpu.SemaphoreType.DMA((5,)),
+            pltpu.SemaphoreType.DMA((3 + len(far_masks),)),
         ],
         far=range(4),
         slack=2,
     )(conv_weight, inner_weight, outer_weight, tokens)
+    conv_part, conv_own, ffn_own, ffn_part = rounded[:4]
     got = [exchange(conv_part, "row", 2 * j) for j in range(1, nz)]
-    got[0], conv_own, ffn_own = lax.optimization_barrier((got[0], conv_own, ffn_own))
-    left = shift_along(right_edge, "seq", 1)
-    right = shift_along(left_edge, "seq", -1)
-    conv_other = exchange(conv_own, "row", 1)
-    ffn_other = exchange(ffn_own, "row", 1)
-    got[0], left, right = lax.optimization_barrier((got[0], left, right))
+    edges = [exchange(rounded[4 + i], "seq", k) for i, k in enumerate(far_masks)]
+    tokens_now = lax.optimization_barrier((tokens, got[0]))[0]
+    token_pieces = [tokens] + [
+        exchange(tokens_now, "seq", k) for k in range(1, ns) if k & (k - 1) == 0
+    ]
+    late = lax.optimization_barrier((got[0], *edges, *token_pieces[1:]))
+    got[0], edges, token_pieces[1:] = late[0], late[1 : 1 + len(edges)], late[1 + len(edges) :]
     (got,) = vmem_call(
         functools.partial(stack_kernel, nz - 1), [((nz - 1, taps, in_rows, span), BF)], slack=2
     )(*got)
+    conv_own, ffn_own = lax.optimization_barrier((conv_own, ffn_own, got))[:2]
+    conv_other = exchange(conv_own, "row", 1)
+    ffn_other = exchange(ffn_own, "row", 1)
     conv_pieces = [got] + [exchange(got, "seq", k) for k in range(1, ns)]
     conv_other_pieces = [exchange(got, "row", 1)]
     ffn_part, conv_other_pieces[0], conv_other, ffn_other = lax.optimization_barrier(
@@ -866,7 +864,7 @@
     ffn_pieces = [ffn_got] + [exchange(ffn_got, "seq", k) for k in range(1, ns)]
 
     pre, after, conv_full = vmem_call(
-        functools.partial(conv_kernel, taps, nz, ns),
+        functools.partial(conv_kernel, taps, nz, ns, masks),
         [((count, width), F32), ((count, width), F32), ((taps, nz, 2, in_rows, width), BF)],
         [
             pltpu.VMEM((length + 2 * half, width), F32),
@@ -875,21 +873,25 @@
             pltpu.SemaphoreType.DMA((2 * (1 + ns * (nz - 1)),)),
         ],
         smem=1,
-        loose=range(5, 7 + 2 * ns),
+        loose=[i for i in range(3, 6 + len(far_masks) + 2 * ns) if not 5 <= i < 6 + len(far_masks)],
     )(
         contig_lengths,
         vectors,
         tokens,
-        left,
-        right,
         conv_own,
         conv_other,
+        token_pieces[1],
+        *edges,
         *conv_pieces,
         *conv_other_pieces,
     )
 
-    pre, tokens_late = lax.optimization_barrier((pre, tokens))
-    token_pieces = [tokens] + [exchange(tokens_late, "seq", k) for k in range(1, ns)]
+    tokens_late = lax.optimization_barrier((tokens, pre, *ffn_pieces))[0]
+    near = [k for k in range(1, ns) if k & (k - 1) == 0]
+    token_pieces = [tokens] + [
+        token_pieces[1 + near.index(k)] if k in near else exchange(tokens_late, "seq", k)
+        for k in range(1, ns)
+    ]
     late = lax.optimization_barrier((pre, *ffn_pieces))
     pre, ffn_pieces = late[0], late[1:]
     ffn_other_pieces = [exchange(p, "row", 1) for p in ffn_pieces]

time: 179 us -> 175 us (0.978)
  starting transfers between devices: 61.8 us -> 51.1 us
  waiting for transfers between devices: 71.5 us -> 78 us
    ppermute x49 -> x50, waiting for transfers between devices: 66.7 us -> 78 us  [exchange(): return lax.ppermute(value, axis, [(i, i ^ mask) for i in range(size)])]
    ppermute x49 -> x50, starting transfers between devices: 56.9 us -> 51.1 us  [exchange(): return lax.ppermute(value, axis, [(i, i ^ mask) for i in range(size)])]
    ppermute x2 -> x0, starting transfers between devices: 4.9 us -> none  [shift_along(): return lax.ppermute(value, axis, pairs)]
    ppermute x2 -> x0, waiting for transfers between devices: 4.85 us -> none  [shift_along(): return lax.ppermute(value, axis, pairs)]
  transfers between devices with their start and end apart: 51 -> 50, of which waited for: 23 -> 25; matrix products, arithmetic and copies ran while one was open for 0% -> 0% of each run, Pallas kernels for 21% -> 22%
where the time goes in v5:
time: 175 us
  waiting for transfers between devices  78 us (45%)
  starting transfers between devices  51.1 us (29%)
  Pallas kernels  44.6 us (25%)
    ppermute x50, waiting for transfers between devices, exchange(): return lax.ppermute(value, axis, [(i, i ^ mask) for i in range(size)])  78 us
    ppermute x50, starting transfers between devices, exchange(): return lax.ppermute(value, axis, [(i, i ^ mask) for i in range(size)])  51.1 us
    pallas_call x17, Pallas kernels, call(): pl.pallas_call(kernel, out_shape=[jax.ShapeDtypeStruct(shape, dtype) if i...  44.6 us
  transfers between devices with their start and end apart: 50, of which 25 were waited for; matrix products, arithmetic and copies ran while one was open for 0% of the time, Pallas kernels for 22%

profile of v5, /device:TPU:0, one launch (start us, length us, event | category | flops | bytes accessed | tf_op | source)
XLA Modules:
  0.0 174.8 jit_solution(1086451680318273657)
XLA Ops:
  0.7 1.7 shard_map.202
  2.4 3.1 %collective-permute-start = (bf16[9,64,128]{2,1,0:T(8,128)(2,1)S(1)}, bf16[9,64,128]{2,1,0:T(8,128)(2,1)S(1)}, u32[]{:S(2)}, u32[]{:S(2)}) collective-permute-start(bf16[9,64,128]{2,1,0:T(8,128)(2,1)S(1)} %get-tuple-element.106), channel_id=1, source_target_pairs={{0,2},{1,3},{2,0},{3,1},{4,6},{5,7},{6,4},{7,5},{8,10},{9,11},{10,... | collective-permute-start | bytes 442376 | tf_op jit(solution)/shard_map/ppermute | solution.py:32
  5.5 3.8 %collective-permute-done.refs_0_ = bf16[9,64,128]{2,1,0:T(8,128)(2,1)S(1)} collective-permute-done((bf16[9,64,128]{2,1,0:T(8,128)(2,1)S(1)}, bf16[9,64,128]{2,1,0:T(8,128)(2,1)S(1)}, u32[]{:S(2)}, u32[]{:S(2)}) %collective-permute-start) | collective-permute-done | bytes 147488 | tf_op jit(solution)/shard_map/ppermute | solution.py:32
  9.3 1.7 collective-permute-start.3
  12.5 3.6 %collective-permute-start.5 = (bf16[9,64,128]{2,1,0:T(8,128)(2,1)S(1)}, bf16[9,64,128]{2,1,0:T(8,128)(2,1)S(1)}, u32[]{:S(2)}, u32[]{:S(2)}) collective-permute-start(bf16[9,64,128]{2,1,0:T(8,128)(2,1)S(1)} %get-tuple-element.106), channel_id=1, source_target_pairs={{0,6},{1,7},{2,4},{3,5},{4,2},{5,3},{6,0},{7,1},{8,14},{9,15},{10,... | collective-permute-start | bytes 442376 | tf_op jit(solution)/shard_map/ppermute | solution.py:32
  16.6 8.4 %collective-permute-done.1.rest_1_ = bf16[2,32,512]{2,1,0:T(8,128)(2,1)S(1)} collective-permute-done((bf16[2,32,512]{2,1,0:T(8,128)(2,1)S(1)}, bf16[2,32,512]{2,1,0:T(8,128)(2,1)S(1)}, u32[]{:S(2)}, u32[]{:S(2)}) %collective-permute-start.1) | collective-permute-done | bytes 65568 | tf_op jit(solution)/shard_map/ppermute | solution.py:32
  25.1 2.1 %collective-permute-done.4.refs_1_ = bf16[9,64,128]{2,1,0:T(8,128)(2,1)S(1)} collective-permute-done((bf16[9,64,128]{2,1,0:T(8,128)(2,1)S(1)}, bf16[9,64,128]{2,1,0:T(8,128)(2,1)S(1)}, u32[]{:S(2)}, u32[]{:S(2)}) %collective-permute-start.4) | collective-permute-done | bytes 147488 | tf_op jit(solution)/shard_map/ppermute | solution.py:32
  28.3 1.5 collective-permute-start.13
  31.4 2.5 %collective-permute-start.11 = (bf16[128,512]{1,0:T(8,128)(2,1)S(1)}, bf16[128,512]{1,0:T(8,128)(2,1)S(1)}, u32[]{:S(2)}, u32[]{:S(2)}) collective-permute-start(bf16[128,512]{1,0:T(8,128)(2,1)S(1)} %get-tuple-element.116), channel_id=1, source_target_pairs={{0,6},{1,7},{2,4},{3,5},{4,2},{5,3},{6,0},{7,1},{8,14},{9,15},{10,... | collective-permute-start | bytes 393224 | tf_op jit(solution)/shard_map/ppermute | solution.py:32
  33.8 7.9 %collective-permute-done.14.rest_5_ = bf16[3,9,64,128]{3,2,1,0:T(8,128)(2,1)S(1)} collective-permute-done((bf16[3,9,64,128]{3,2,1,0:T(8,128)(2,1)S(1)}, bf16[3,9,64,128]{3,2,1,0:T(8,128)(2,1)S(1)}, u32[]{:S(2)}, u32[]{:S(2)}) %collective-permute-start.14) | collective-permute-done | bytes 442400 | tf_op jit(solution)/shard_map/ppermute | solution.py:32
  41.8 8.3 %collective-permute-done.13.rest_4_ = bf16[3,9,64,128]{3,2,1,0:T(8,128)(2,1)S(1)} collective-permute-done((bf16[3,9,64,128]{3,2,1,0:T(8,128)(2,1)S(1)}, bf16[3,9,64,128]{3,2,1,0:T(8,128)(2,1)S(1)}, u32[]{:S(2)}, u32[]{:S(2)}) %collective-permute-start.13) | collective-permute-done | bytes 442400 | tf_op jit(solution)/shard_map/ppermute | solution.py:32
  54.4 6.6 %shard_map.204 = (f32[512,512]{1,0:T(8,128)S(1)}, f32[512,512]{1,0:T(8,128)S(1)}, bf16[9,4,2,64,512]{4,3,2,1,0:T(8,128)(2,1)S(1)}) custom-call(s32[2,8]{1,0:T(2,128)S(1)} %copy-done.9, f32[10,512]{1,0:T(8,128)S(1)} %copy-done.8, bf16[2,256,512]{2,1,0:T(8,128)(2,1)S(1)} %copy-done.1, bf16[9,64,512]{2,1,0:T(8,128)(2,1)S(1)} %get-tuple-element.110.own, ...), custom_call_target="tpu_custom_call" | custom-call | flops 1 | bytes 1 | tf_op jit(solution)/shard_map/pallas_call | solution.py:118
  61.0 2.7 %collective-permute-done.20.refs_8_ = bf16[3,128,512]{2,1,0:T(8,128)(2,1)S(1)} collective-permute-done((bf16[3,128,512]{2,1,0:T(8,128)(2,1)S(1)}, bf16[3,128,512]{2,1,0:T(8,128)(2,1)S(1)}, u32[]{:S(2)}, u32[]{:S(2)}) %collective-permute-start.20) | collective-permute-done | bytes 393248 | tf_op jit(solution)/shard_map/ppermute | solution.py:32
  63.7 7.9 %collective-permute-done.19.refs_7_ = bf16[3,128,512]{2,1,0:T(8,128)(2,1)S(1)} collective-permute-done((bf16[3,128,512]{2,1,0:T(8,128)(2,1)S(1)}, bf16[3,128,512]{2,1,0:T(8,128)(2,1)S(1)}, u32[]{:S(2)}, u32[]{:S(2)}) %collective-permute-start.19) | collective-permute-done | bytes 393248 | tf_op jit(solution)/shard_map/ppermute | solution.py:32
  76.4 9.7 %shard_map.206 = (bf16[512,512]{1,0:T(8,128)(2,1)}, bf16[512,512]{1,0:T(8,128)(2,1)S(1)}, bf16[512,2048]{1,0:T(8,128)(2,1)S(1)}, bf16[512,512]{1,0:T(8,128)(2,1)...) custom-call(f32[512,512]{1,0:T(8,128)S(1)} %get-tuple-element.121.refs_0_, ...), custom_call_target="tpu_custom_call" | custom-call | flops 1 | bytes 1 | tf_op jit(solution)/shard_map/pallas_call | solution.py:118
  86.1 3.3 %shard_map.207 = (bf16[4,4,128,512]{3,2,1,0:T(8,128)(2,1)S(1)}, bf16[4,4,128,512]{3,2,1,0:T(8,128)(2,1)S(1)}) custom-call(bf16[512,512]{1,0:T(8,128)(2,1)S(1)} %get-tuple-element.133.refs_0_, bf16[512,2048]{1,0:T(8,128)(2,1)S(1)} %get-tuple-element.134.refs_1_, bf16[512,512]{1,0:T(8,128)(2,1)S(1)} %get-tuple-element.135.refs_2_, ...), custom_call_target="tpu_custom_call" | custom-call | flops 1 | bytes 1 | tf_op jit(solution)/shard_map/pallas_call | solution.py:118
  89.3 2.7 %shard_map.208 = (f32[512,512]{1,0:T(8,128)S(1)}, bf16[512,512]{1,0:T(8,128)(2,1)S(1)}, bf16[640,128]{1,0:T(8,128)(2,1)S(1)}, bf16[896,128]{1,0:T(8,128)(2,1)S(1...) custom-call(f32[512,512]{1,0:T(8,128)S(1)} %get-tuple-element.138.refs_0_, bf16[512,512]{1,0:T(8,128)(2,1)S(1)} %bitcast.9, ...), custom_call_target="tpu_custom_call" | custom-call | flops 1 | bytes 1 | tf_op jit(solution)/shard_map/pallas_call | solution.py:118
  92.2 1.5 collective-permute-start.26
  95.7 4.9 %collective-permute-done.26.refs_6_.refs_4_ = bf16[896,128]{1,0:T(8,128)(2,1)S(1)} collective-permute-done((bf16[896,128]{1,0:T(8,128)(2,1)S(1)}, bf16[896,128]{1,0:T(8,128)(2,1)S(1)}, u32[]{:S(2)}, u32[]{:S(2)}) %collective-permute-start.26) | collective-permute-done | bytes 229408 | tf_op jit(solution)/shard_map/ppermute | solution.py:32
  101.6 4.3 %collective-permute-done.28.refs_8_.refs_5_ = bf16[896,128]{1,0:T(8,128)(2,1)S(1)} collective-permute-done((bf16[896,128]{1,0:T(8,128)(2,1)S(1)}, bf16[896,128]{1,0:T(8,128)(2,1)S(1)}, u32[]{:S(2)}, u32[]{:S(2)}) %collective-permute-start.28) | collective-permute-done | bytes 229408 | tf_op jit(solution)/shard_map/ppermute | solution.py:32
  105.9 6.6 %shard_map.209 = (bf16[2432,128]{1,0:T(8,128)(2,1)S(1)}, bf16[2432,128]{1,0:T(8,128)(2,1)S(1)}) custom-call(s32[2,8]{1,0:T(2,128)S(1)} %copy-done.9, bf16[2,256,512]{2,1,0:T(8,128)(2,1)S(1)} %copy-done.1, bf16[2,256,512]{2,1,0:T(8,128)(2,1)S(1)} %collective-permute-done.2.rest_0_.refs_2_, bf16[2,256,512]{2,1,0:T(8,128)(2,1)S(1)} %collective-permute-done.3.refs_3_, ...), custom_call_target="tpu_custom_call" | custom-call | flops 1 | bytes 1 | tf_op jit(solution)/shard_map/pallas_call | solution.py:118
  117.7 2.7 %collective-permute-start.31 = (bf16[704,128]{1,0:T(8,128)(2,1)S(1)}, bf16[704,128]{1,0:T(8,128)(2,1)S(1)}, u32[]{:S(2)}, u32[]{:S(2)}) collective-permute-start(bf16[704,128]{1,0:T(8,128)(2,1)S(1)} %get-tuple-element.168), channel_id=1, source_target_pairs={{0,4},{1,5},{2,6},{3,7},{4,0},{5,1},{6,2},{7,3},{8,12},{9,13},{10,... | collective-permute-start | bytes 540680 | tf_op jit(solution)/shard_map/ppermute | solution.py:32
  120.3 6.8 %collective-permute-done.30.refs_1_ = bf16[704,128]{1,0:T(8,128)(2,1)S(1)} collective-permute-done((bf16[704,128]{1,0:T(8,128)(2,1)S(1)}, bf16[704,128]{1,0:T(8,128)(2,1)S(1)}, u32[]{:S(2)}, u32[]{:S(2)}) %collective-permute-start.30) | collective-permute-done | bytes 180256 | tf_op jit(solution)/shard_map/ppermute | solution.py:32
  128.5 7.4 %shard_map.211 = f32[512,512]{1,0:T(8,128)} custom-call(s32[2,8]{1,0:T(2,128)S(1)} %copy-done.9, bf16[512,512]{1,0:T(8,128)(2,1)S(1)} %get-tuple-element.162.refs_1_, f32[512,512]{1,0:T(8,128)S(1)} %get-tuple-element.163.refs_2_, bf16[9,4,2,64,512]{4,3,2,1,0:T(8,128)(2,1)S(1)} %get-tuple-element.164.refs_3_, ...), custom_call_target="tpu_custom_call" | custom-call | flops 1 | bytes 1 | tf_op jit(solution)/shard_map/pallas_call | solution.py:118
  136.1 1.5 collective-permute-start.39
  137.7 4.9 %collective-permute-done.37.refs_2_ = bf16[512,512]{1,0:T(8,128)(2,1)S(1)} collective-permute-done((bf16[512,512]{1,0:T(8,128)(2,1)S(1)}, bf16[512,512]{1,0:T(8,128)(2,1)S(1)}, u32[]{:S(2)}, u32[]{:S(2)}) %collective-permute-start.37) | collective-permute-done | bytes 524320 | tf_op jit(solution)/shard_map/ppermute | solution.py:32
  143.0 3.7 %collective-permute-start.41 = (bf16[128,512]{1,0:T(8,128)(2,1)S(1)}, bf16[128,512]{1,0:T(8,128)(2,1)S(1)}, u32[]{:S(2)}, u32[]{:S(2)}) collective-permute-start(bf16[128,512]{1,0:T(8,128)(2,1)S(1)} %get-tuple-element.181), channel_id=1, source_target_pairs={{0,4},{1,5},{2,6},{3,7},{4,0},{5,1},{6,2},{7,3},{8,12},{9,13},{10,... | collective-permute-start | bytes 393224 | tf_op jit(solution)/shard_map/ppermute | solution.py:32
  147.4 2.6 %collective-permute-done.40.refs_1_ = bf16[128,512]{1,0:T(8,128)(2,1)S(1)} collective-permute-done((bf16[128,512]{1,0:T(8,128)(2,1)S(1)}, bf16[128,512]{1,0:T(8,128)(2,1)S(1)}, u32[]{:S(2)}, u32[]{:S(2)}) %collective-permute-start.40) | collective-permute-done | bytes 131104 | tf_op jit(solution)/shard_map/ppermute | solution.py:32
  149.9 1.9 %collective-permute-done.41.refs_2_ = bf16[128,512]{1,0:T(8,128)(2,1)S(1)} collective-permute-done((bf16[128,512]{1,0:T(8,128)(2,1)S(1)}, bf16[128,512]{1,0:T(8,128)(2,1)S(1)}, u32[]{:S(2)}, u32[]{:S(2)}) %collective-permute-start.41) | collective-permute-done | bytes 131104 | tf_op jit(solution)/shard_map/ppermute | solution.py:32
  151.9 1.7 collective-permute-done.42.refs_3_
  161.4 2.2 %collective-permute-start.48 = (f32[8,128]{1,0:T(8,128)S(1)}, f32[8,128]{1,0:T(8,128)S(1)}, u32[]{:S(2)}, u32[]{:S(2)}) collective-permute-start(f32[8,128]{1,0:T(8,128)S(1)} %shard_map.216.refs_0_), channel_id=1, source_target_pairs={{0,6},{1,7},{2,4},{3,5},{4,2},{5,3},{6,0},{7,1},{8,14},{9,15},{10,... | collective-permute-start | bytes 12296 | tf_op jit(solution)/shard_map/ppermute | solution.py:32
  169.8 4.9 %shard_map.218 = (f32[1,1]{1,0:T(1,128)}, f32[10,512]{1,0:T(8,128)}, f32[10,512]{1,0:T(8,128)}, f32[9,64,512]{2,1,0:T(8,128)}, f32[9,64,512]{2,1,0:T(8,128)}, /*...) custom-call(bf16[576,128]{1,0:T(8,128)(2,1)S(1)} %get-tuple-element., ...), custom_call_target="tpu_custom_call" | custom-call | flops 1 | bytes 1 | tf_op jit(solution)/shard_map/pallas_call | solution.py:118
  (108 shorter events, 38.4 us)
Async XLA Ops:
  2.4 6.9 %collective-permute-start = (bf16[9,64,128]{2,1,0:T(8,128)(2,1)S(1)}, bf16[9,64,128]{2,1,0:T(8,128)(2,1)S(1)}, u32[]{:S(2)}, u32[]{:S(2)}) collective-permute-start(bf16[9,64,128]{2,1,0:T(8,128)(2,1)S(1)} %get-tuple-element.106), channel_id=1, source_target_pairs={{0,2},{1,3},{2,0},{3,1},{4,6},{5,7},{6,4},{7,5},{8,10},{9,11},{10,... | collective-permute-start | bytes 442376 | tf_op jit(solution)/shard_map/ppermute | solution.py:32
  9.3 15.7 %collective-permute-start.3 = (bf16[2,256,512]{2,1,0:T(8,128)(2,1)S(1)}, bf16[2,256,512]{2,1,0:T(8,128)(2,1)S(1)}, u32[]{:S(2)}, u32[]{:S(2)}) collective-permute-start(bf16[2,256,512]{2,1,0:T(8,128)(2,1)S(1)} %copy-done.1), channel_id=1, source_target_pairs={{0,16},{8,24},{16,0},{24,8},{1,17},{9,25},{17,1},{25,9},{2,18},{10... | collective-permute-start | bytes 1572872 | tf_op jit(solution)/shard_map/ppermute | solution.py:32
  11.0 14.0 %collective-permute-start.2 = (bf16[2,256,512]{2,1,0:T(8,128)(2,1)S(1)}, bf16[2,256,512]{2,1,0:T(8,128)(2,1)S(1)}, u32[]{:S(2)}, u32[]{:S(2)}) collective-permute-start(bf16[2,256,512]{2,1,0:T(8,128)(2,1)S(1)} %copy-done.1), channel_id=1, source_target_pairs={{0,8},{8,0},{16,24},{24,16},{1,9},{9,1},{17,25},{25,17},{2,10},{10... | collective-permute-start | bytes 1572872 | tf_op jit(solution)/shard_map/ppermute | solution.py:32
  12.5 12.5 %collective-permute-start.5 = (bf16[9,64,128]{2,1,0:T(8,128)(2,1)S(1)}, bf16[9,64,128]{2,1,0:T(8,128)(2,1)S(1)}, u32[]{:S(2)}, u32[]{:S(2)}) collective-permute-start(bf16[9,64,128]{2,1,0:T(8,128)(2,1)S(1)} %get-tuple-element.106), channel_id=1, source_target_pairs={{0,6},{1,7},{2,4},{3,5},{4,2},{5,3},{6,0},{7,1},{8,14},{9,15},{10,... | collective-permute-start | bytes 442376 | tf_op jit(solution)/shard_map/ppermute | solution.py:32
  16.1 11.0 %collective-permute-start.4 = (bf16[9,64,128]{2,1,0:T(8,128)(2,1)S(1)}, bf16[9,64,128]{2,1,0:T(8,128)(2,1)S(1)}, u32[]{:S(2)}, u32[]{:S(2)}) collective-permute-start(bf16[9,64,128]{2,1,0:T(8,128)(2,1)S(1)} %get-tuple-element.106), channel_id=1, source_target_pairs={{0,4},{1,5},{2,6},{3,7},{4,0},{5,1},{6,2},{7,3},{8,12},{9,13},{10,... | collective-permute-start | bytes 442376 | tf_op jit(solution)/shard_map/ppermute | solution.py:32
  16.1 8.9 %collective-permute-start.1 = (bf16[2,32,512]{2,1,0:T(8,128)(2,1)S(1)}, bf16[2,32,512]{2,1,0:T(8,128)(2,1)S(1)}, u32[]{:S(2)}, u32[]{:S(2)}) collective-permute-start(bf16[2,32,512]{2,1,0:T(8,128)(2,1)S(1)} %get-tuple-element.107), channel_id=1, source_target_pairs={{0,24},{8,16},{16,8},{24,0},{1,25},{9,17},{17,9},{25,1},{2,26},{10... | collective-permute-start | bytes 196616 | tf_op jit(solution)/shard_map/ppermute | solution.py:32
  27.9 13.9 %collective-permute-start.14 = (bf16[3,9,64,128]{3,2,1,0:T(8,128)(2,1)S(1)}, bf16[3,9,64,128]{3,2,1,0:T(8,128)(2,1)S(1)}, u32[]{:S(2)}, u32[]{:S(2)}) collective-permute-start(bf16[3,9,64,128]{3,2,1,0:T(8,128)(2,1)S(1)} %shard_map.203.rest_2_), channel_id=1, source_target_pairs={{0,24},{8,16},{16,8},{24,0},{1,25},{9,17},{17,9},{25,1},{2,26},{10... | collective-permute-start | bytes 1327112 | tf_op jit(solution)/shard_map/ppermute | solution.py:32
  28.3 21.7 %collective-permute-start.13 = (bf16[3,9,64,128]{3,2,1,0:T(8,128)(2,1)S(1)}, bf16[3,9,64,128]{3,2,1,0:T(8,128)(2,1)S(1)}, u32[]{:S(2)}, u32[]{:S(2)}) collective-permute-start(bf16[3,9,64,128]{3,2,1,0:T(8,128)(2,1)S(1)} %shard_map.203.rest_2_), channel_id=1, source_target_pairs={{0,16},{8,24},{16,0},{24,8},{1,17},{9,25},{17,1},{25,9},{2,18},{10... | collective-permute-start | bytes 1327112 | tf_op jit(solution)/shard_map/ppermute | solution.py:32
  29.9 20.2 %collective-permute-start.12 = (bf16[3,9,64,128]{3,2,1,0:T(8,128)(2,1)S(1)}, bf16[3,9,64,128]{3,2,1,0:T(8,128)(2,1)S(1)}, u32[]{:S(2)}, u32[]{:S(2)}) collective-permute-start(bf16[3,9,64,128]{3,2,1,0:T(8,128)(2,1)S(1)} %shard_map.203.rest_2_), channel_id=1, source_target_pairs={{0,8},{8,0},{16,24},{24,16},{1,9},{9,1},{17,25},{25,17},{2,10},{10... | collective-permute-start | bytes 1327112 | tf_op jit(solution)/shard_map/ppermute | solution.py:32
  31.4 18.7 %collective-permute-start.11 = (bf16[128,512]{1,0:T(8,128)(2,1)S(1)}, bf16[128,512]{1,0:T(8,128)(2,1)S(1)}, u32[]{:S(2)}, u32[]{:S(2)}) collective-permute-start(bf16[128,512]{1,0:T(8,128)(2,1)S(1)} %get-tuple-element.116), channel_id=1, source_target_pairs={{0,6},{1,7},{2,4},{3,5},{4,2},{5,3},{6,0},{7,1},{8,14},{9,15},{10,... | collective-permute-start | bytes 393224 | tf_op jit(solution)/shard_map/ppermute | solution.py:32
  33.8 16.2 %collective-permute-start.10 = (bf16[128,512]{1,0:T(8,128)(2,1)S(1)}, bf16[128,512]{1,0:T(8,128)(2,1)S(1)}, u32[]{:S(2)}, u32[]{:S(2)}) collective-permute-start(bf16[128,512]{1,0:T(8,128)(2,1)S(1)} %get-tuple-element.116), channel_id=1, source_target_pairs={{0,4},{1,5},{2,6},{3,7},{4,0},{5,1},{6,2},{7,3},{8,12},{9,13},{10,... | collective-permute-start | bytes 393224 | tf_op jit(solution)/shard_map/ppermute | solution.py:32
  41.8 8.3 %collective-permute-start.9 = (bf16[128,512]{1,0:T(8,128)(2,1)S(1)}, bf16[128,512]{1,0:T(8,128)(2,1)S(1)}, u32[]{:S(2)}, u32[]{:S(2)}) collective-permute-start(bf16[128,512]{1,0:T(8,128)(2,1)S(1)} %get-tuple-element.116), channel_id=1, source_target_pairs={{0,2},{1,3},{2,0},{3,1},{4,6},{5,7},{6,4},{7,5},{8,10},{9,11},{10,... | collective-permute-start | bytes 393224 | tf_op jit(solution)/shard_map/ppermute | solution.py:32
  50.8 12.9 %collective-permute-start.20 = (bf16[3,128,512]{2,1,0:T(8,128)(2,1)S(1)}, bf16[3,128,512]{2,1,0:T(8,128)(2,1)S(1)}, u32[]{:S(2)}, u32[]{:S(2)}) collective-permute-start(bf16[3,128,512]{2,1,0:T(8,128)(2,1)S(1)} %get-tuple-element.128.refs_5_), channel_id=1, source_target_pairs={{0,24},{8,16},{16,8},{24,0},{1,25},{9,17},{17,9},{25,1},{2,26},{10... | collective-permute-start | bytes 1179656 | tf_op jit(solution)/shard_map/ppermute | solution.py:32
  52.1 19.5 %collective-permute-start.19 = (bf16[3,128,512]{2,1,0:T(8,128)(2,1)S(1)}, bf16[3,128,512]{2,1,0:T(8,128)(2,1)S(1)}, u32[]{:S(2)}, u32[]{:S(2)}) collective-permute-start(bf16[3,128,512]{2,1,0:T(8,128)(2,1)S(1)} %get-tuple-element.128.refs_5_), channel_id=1, source_target_pairs={{0,16},{8,24},{16,0},{24,8},{1,17},{9,25},{17,1},{25,9},{2,18},{10... | collective-permute-start | bytes 1179656 | tf_op jit(solution)/shard_map/ppermute | solution.py:32
  53.6 18.1 %collective-permute-start.18 = (bf16[3,128,512]{2,1,0:T(8,128)(2,1)S(1)}, bf16[3,128,512]{2,1,0:T(8,128)(2,1)S(1)}, u32[]{:S(2)}, u32[]{:S(2)}) collective-permute-start(bf16[3,128,512]{2,1,0:T(8,128)(2,1)S(1)} %get-tuple-element.128.refs_5_), channel_id=1, source_target_pairs={{0,8},{8,0},{16,24},{24,16},{1,9},{9,1},{17,25},{25,17},{2,10},{10... | collective-permute-start | bytes 1179656 | tf_op jit(solution)/shard_map/ppermute | solution.py:32
  71.7 20.4 %collective-permute-start.25 = (bf16[2,256,512]{2,1,0:T(8,128)(2,1)S(1)}, bf16[2,256,512]{2,1,0:T(8,128)(2,1)S(1)}, u32[]{:S(2)}, u32[]{:S(2)}) collective-permute-start(bf16[2,256,512]{2,1,0:T(8,128)(2,1)S(1)} %copy-done.1), channel_id=1, source_target_pairs={{0,24},{8,16},{16,8},{24,0},{1,25},{9,17},{17,9},{25,1},{2,26},{10... | collective-permute-start | bytes 1572872 | tf_op jit(solution)/shard_map/ppermute | solution.py:32
  92.0 20.6 %collective-permute-start.35 = (bf16[4,4,128,512]{3,2,1,0:T(8,128)(2,1)S(1)}, bf16[4,4,128,512]{3,2,1,0:T(8,128)(2,1)S(1)}, u32[]{:S(2)}, u32[]{:S(2)}) collective-permute-start(bf16[4,4,128,512]{3,2,1,0:T(8,128)(2,1)S(1)} %get-tuple-element.172), channel_id=1, source_target_pairs={{0,1},{1,0},{2,3},{3,2},{4,5},{5,4},{6,7},{7,6},{8,9},{9,8},{10,11... | collective-permute-start | bytes 6291464 | tf_op jit(solution)/shard_map/ppermute | solution.py:32
  92.2 8.4 %collective-permute-start.26 = (bf16[896,128]{1,0:T(8,128)(2,1)S(1)}, bf16[896,128]{1,0:T(8,128)(2,1)S(1)}, u32[]{:S(2)}, u32[]{:S(2)}) collective-permute-start(bf16[896,128]{1,0:T(8,128)(2,1)S(1)} %get-tuple-element.155), channel_id=1, source_target_pairs={{0,8},{8,0},{16,24},{24,16},{1,9},{9,1},{17,25},{25,17},{2,10},{10... | collective-permute-start | bytes 688136 | tf_op jit(solution)/shard_map/ppermute | solution.py:32
  93.7 12.2 %collective-permute-start.28 = (bf16[896,128]{1,0:T(8,128)(2,1)S(1)}, bf16[896,128]{1,0:T(8,128)(2,1)S(1)}, u32[]{:S(2)}, u32[]{:S(2)}) collective-permute-start(bf16[896,128]{1,0:T(8,128)(2,1)S(1)} %get-tuple-element.158), channel_id=1, source_target_pairs={{0,24},{8,16},{16,8},{24,0},{1,25},{9,17},{17,9},{25,1},{2,26},{10... | collective-permute-start | bytes 688136 | tf_op jit(solution)/shard_map/ppermute | solution.py:32
  95.1 6.5 %collective-permute-start.27 = (bf16[640,128]{1,0:T(8,128)(2,1)S(1)}, bf16[640,128]{1,0:T(8,128)(2,1)S(1)}, u32[]{:S(2)}, u32[]{:S(2)}) collective-permute-start(bf16[640,128]{1,0:T(8,128)(2,1)S(1)} %get-tuple-element.157), channel_id=1, source_target_pairs={{0,16},{8,24},{16,0},{24,8},{1,17},{9,25},{17,1},{25,9},{2,18},{10... | collective-permute-start | bytes 491528 | tf_op jit(solution)/shard_map/ppermute | solution.py:32
  113.3 24.4 %collective-permute-start.36 = (bf16[512,512]{1,0:T(8,128)(2,1)S(1)}, bf16[512,512]{1,0:T(8,128)(2,1)S(1)}, u32[]{:S(2)}, u32[]{:S(2)}) collective-permute-start(bf16[512,512]{1,0:T(8,128)(2,1)S(1)} %get-tuple-element.174), channel_id=1, source_target_pairs={{0,8},{8,0},{16,24},{24,16},{1,9},{9,1},{17,25},{25,17},{2,10},{10... | collective-permute-start | bytes 1572872 | tf_op jit(solution)/shard_map/ppermute | solution.py:32
  114.2 28.4 %collective-permute-start.37 = (bf16[512,512]{1,0:T(8,128)(2,1)S(1)}, bf16[512,512]{1,0:T(8,128)(2,1)S(1)}, u32[]{:S(2)}, u32[]{:S(2)}) collective-permute-start(bf16[512,512]{1,0:T(8,128)(2,1)S(1)} %get-tuple-element.175), channel_id=1, source_target_pairs={{0,16},{8,24},{16,0},{24,8},{1,17},{9,25},{17,1},{25,9},{2,18},{10... | collective-permute-start | bytes 1572872 | tf_op jit(solution)/shard_map/ppermute | solution.py:32
  115.5 27.1 %collective-permute-start.38 = (bf16[512,512]{1,0:T(8,128)(2,1)S(1)}, bf16[512,512]{1,0:T(8,128)(2,1)S(1)}, u32[]{:S(2)}, u32[]{:S(2)}) collective-permute-start(bf16[512,512]{1,0:T(8,128)(2,1)S(1)} %get-tuple-element.176), channel_id=1, source_target_pairs={{0,24},{8,16},{16,8},{24,0},{1,25},{9,17},{17,9},{25,1},{2,26},{10... | collective-permute-start | bytes 1572872 | tf_op jit(solution)/shard_map/ppermute | solution.py:32
  117.2 9.9 %collective-permute-start.30 = (bf16[704,128]{1,0:T(8,128)(2,1)S(1)}, bf16[704,128]{1,0:T(8,128)(2,1)S(1)}, u32[]{:S(2)}, u32[]{:S(2)}) collective-permute-start(bf16[704,128]{1,0:T(8,128)(2,1)S(1)} %get-tuple-element.167), channel_id=1, source_target_pairs={{0,2},{1,3},{2,0},{3,1},{4,6},{5,7},{6,4},{7,5},{8,10},{9,11},{10,... | collective-permute-start | bytes 540680 | tf_op jit(solution)/shard_map/ppermute | solution.py:32
  117.7 18.2 %collective-permute-start.31 = (bf16[704,128]{1,0:T(8,128)(2,1)S(1)}, bf16[704,128]{1,0:T(8,128)(2,1)S(1)}, u32[]{:S(2)}, u32[]{:S(2)}) collective-permute-start(bf16[704,128]{1,0:T(8,128)(2,1)S(1)} %get-tuple-element.168), channel_id=1, source_target_pairs={{0,4},{1,5},{2,6},{3,7},{4,0},{5,1},{6,2},{7,3},{8,12},{9,13},{10,... | collective-permute-start | bytes 540680 | tf_op jit(solution)/shard_map/ppermute | solution.py:32
  127.1 8.8 %collective-permute-start.32 = (bf16[704,128]{1,0:T(8,128)(2,1)S(1)}, bf16[704,128]{1,0:T(8,128)(2,1)S(1)}, u32[]{:S(2)}, u32[]{:S(2)}) collective-permute-start(bf16[704,128]{1,0:T(8,128)(2,1)S(1)} %get-tuple-element.169), channel_id=1, source_target_pairs={{0,6},{1,7},{2,4},{3,5},{4,2},{5,3},{6,0},{7,1},{8,14},{9,15},{10,... | collective-permute-start | bytes 540680 | tf_op jit(solution)/shard_map/ppermute | solution.py:32
  136.1 11.2 %collective-permute-start.39 = (bf16[576,128]{1,0:T(8,128)(2,1)S(1)}, bf16[576,128]{1,0:T(8,128)(2,1)S(1)}, u32[]{:S(2)}, u32[]{:S(2)}) collective-permute-start(bf16[576,128]{1,0:T(8,128)(2,1)S(1)} %get-tuple-element.170.refs_0_), channel_id=1, source_target_pairs={{0,24},{8,16},{16,8},{24,0},{1,25},{9,17},{17,9},{25,1},{2,26},{10... | collective-permute-start | bytes 442376 | tf_op jit(solution)/shard_map/ppermute | solution.py:32
  142.9 7.0 %collective-permute-start.40 = (bf16[128,512]{1,0:T(8,128)(2,1)S(1)}, bf16[128,512]{1,0:T(8,128)(2,1)S(1)}, u32[]{:S(2)}, u32[]{:S(2)}) collective-permute-start(bf16[128,512]{1,0:T(8,128)(2,1)S(1)} %get-tuple-element.180), channel_id=1, source_target_pairs={{0,2},{1,3},{2,0},{3,1},{4,6},{5,7},{6,4},{7,5},{8,10},{9,11},{10,... | collective-permute-start | bytes 393224 | tf_op jit(solution)/shard_map/ppermute | solution.py:32
  143.0 8.9 %collective-permute-start.41 = (bf16[128,512]{1,0:T(8,128)(2,1)S(1)}, bf16[128,512]{1,0:T(8,128)(2,1)S(1)}, u32[]{:S(2)}, u32[]{:S(2)}) collective-permute-start(bf16[128,512]{1,0:T(8,128)(2,1)S(1)} %get-tuple-element.181), channel_id=1, source_target_pairs={{0,4},{1,5},{2,6},{3,7},{4,0},{5,1},{6,2},{7,3},{8,12},{9,13},{10,... | collective-permute-start | bytes 393224 | tf_op jit(solution)/shard_map/ppermute | solution.py:32
  146.7 6.9 %collective-permute-start.42 = (bf16[128,512]{1,0:T(8,128)(2,1)S(1)}, bf16[128,512]{1,0:T(8,128)(2,1)S(1)}, u32[]{:S(2)}, u32[]{:S(2)}) collective-permute-start(bf16[128,512]{1,0:T(8,128)(2,1)S(1)} %get-tuple-element.182), channel_id=1, source_target_pairs={{0,6},{1,7},{2,4},{3,5},{4,2},{5,3},{6,0},{7,1},{8,14},{9,15},{10,... | collective-permute-start | bytes 393224 | tf_op jit(solution)/shard_map/ppermute | solution.py:32
  157.3 11.4 %collective-permute-start.34 = (bf16[576,128]{1,0:T(8,128)(2,1)S(1)}, bf16[576,128]{1,0:T(8,128)(2,1)S(1)}, u32[]{:S(2)}, u32[]{:S(2)}) collective-permute-start(bf16[576,128]{1,0:T(8,128)(2,1)S(1)} %get-tuple-element.170.refs_0_), channel_id=1, source_target_pairs={{0,16},{8,24},{16,0},{24,8},{1,17},{9,25},{17,1},{25,9},{2,18},{10... | collective-permute-start | bytes 442376 | tf_op jit(solution)/shard_map/ppermute | solution.py:32
  157.9 10.8 %collective-permute-start.33 = (bf16[576,128]{1,0:T(8,128)(2,1)S(1)}, bf16[576,128]{1,0:T(8,128)(2,1)S(1)}, u32[]{:S(2)}, u32[]{:S(2)}) collective-permute-start(bf16[576,128]{1,0:T(8,128)(2,1)S(1)} %get-tuple-element.170.refs_0_), channel_id=1, source_target_pairs={{0,8},{8,0},{16,24},{24,16},{1,9},{9,1},{17,25},{25,17},{2,10},{10... | collective-permute-start | bytes 442376 | tf_op jit(solution)/shard_map/ppermute | solution.py:32
  (29 other events, 485.5 us)

commit v6 on v5

--- a/solution.py
+++ b/solution.py
@@ -834,8 +834,11 @@
     )(conv_weight, inner_weight, outer_weight, tokens)
     conv_part, conv_own, ffn_own, ffn_part = rounded[:4]
     got = [exchange(conv_part, "row", 2 * j) for j in range(1, nz)]
-    edges = [exchange(rounded[4 + i], "seq", k) for i, k in enumerate(far_masks)]
-    tokens_now = lax.optimization_barrier((tokens, got[0]))[0]
+    edges = [
+        exchange(lax.optimization_barrier((rounded[4 + i], got[0]))[0], "seq", k)
+        for i, k in enumerate(far_masks)
+    ]
+    tokens_now = lax.optimization_barrier((tokens, conv_part))[0]
     token_pieces = [tokens] + [
         exchange(tokens_now, "seq", k) for k in range(1, ns) if k & (k - 1) == 0
     ]

time: 175 us -> 172 us (0.983)
  waiting for transfers between devices: 78 us -> 75.6 us
    ppermute x50, waiting for transfers between devices: 78 us -> 75.6 us  [exchange(): return lax.ppermute(value, axis, [(i, i ^ mask) for i in range(size)])]
  transfers between devices with their start and end apart: 50 -> 50, of which waited for: 25 -> 26; matrix products, arithmetic and copies ran while one was open for 0% -> 0% of each run, Pallas kernels for 22% -> 22%
where the time goes in v6:
time: 172 us
  waiting for transfers between devices  75.6 us (44%)
  starting transfers between devices  50.4 us (29%)
  Pallas kernels  44.6 us (26%)
    ppermute x50, waiting for transfers between devices, exchange(): return lax.ppermute(value, axis, [(i, i ^ mask) for i in range(size)])  75.6 us
    ppermute x50, starting transfers between devices, exchange(): return lax.ppermute(value, axis, [(i, i ^ mask) for i in range(size)])  50.4 us
    pallas_call x17, Pallas kernels, call(): pl.pallas_call(kernel, out_shape=[jax.ShapeDtypeStruct(shape, dtype) if i...  44.6 us
  transfers between devices with their start and end apart: 50, of which 26 were waited for; matrix products, arithmetic and copies ran while one was open for 0% of the time, Pallas kernels for 22%

profile of v6, /device:TPU:0, one launch (start us, length us, event | category | flops | bytes accessed | tf_op | source)
XLA Modules:
  0.0 171.8 jit_solution(10969155946814990793)
XLA Ops:
  0.7 1.7 shard_map.202
  2.4 3.0 %collective-permute-start.3 = (bf16[2,256,512]{2,1,0:T(8,128)(2,1)S(1)}, bf16[2,256,512]{2,1,0:T(8,128)(2,1)S(1)}, u32[]{:S(2)}, u32[]{:S(2)}) collective-permute-start(bf16[2,256,512]{2,1,0:T(8,128)(2,1)S(1)} %copy-done.1), channel_id=1, source_target_pairs={{0,16},{8,24},{16,0},{24,8},{1,17},{9,25},{17,1},{25,9},{2,18},{10... | collective-permute-start | bytes 1572872 | tf_op jit(solution)/shard_map/ppermute | solution.py:32
  6.9 1.6 collective-permute-start
  8.5 2.5 %collective-permute-start.5 = (bf16[9,64,128]{2,1,0:T(8,128)(2,1)S(1)}, bf16[9,64,128]{2,1,0:T(8,128)(2,1)S(1)}, u32[]{:S(2)}, u32[]{:S(2)}) collective-permute-start(bf16[9,64,128]{2,1,0:T(8,128)(2,1)S(1)} %get-tuple-element.107), channel_id=1, source_target_pairs={{0,6},{1,7},{2,4},{3,5},{4,2},{5,3},{6,0},{7,1},{8,14},{9,15},{10,... | collective-permute-start | bytes 442376 | tf_op jit(solution)/shard_map/ppermute | solution.py:32
  12.8 7.2 %collective-permute-done.1.rest_1_ = bf16[2,32,512]{2,1,0:T(8,128)(2,1)S(1)} collective-permute-done((bf16[2,32,512]{2,1,0:T(8,128)(2,1)S(1)}, bf16[2,32,512]{2,1,0:T(8,128)(2,1)S(1)}, u32[]{:S(2)}, u32[]{:S(2)}) %collective-permute-start.1) | collective-permute-done | bytes 65568 | tf_op jit(solution)/shard_map/ppermute | solution.py:32
  20.0 3.5 %collective-permute-done.4.refs_1_ = bf16[9,64,128]{2,1,0:T(8,128)(2,1)S(1)} collective-permute-done((bf16[9,64,128]{2,1,0:T(8,128)(2,1)S(1)}, bf16[9,64,128]{2,1,0:T(8,128)(2,1)S(1)}, u32[]{:S(2)}, u32[]{:S(2)}) %collective-permute-start.4) | collective-permute-done | bytes 147488 | tf_op jit(solution)/shard_map/ppermute | solution.py:32
  24.8 1.5 collective-permute-start.13
  27.8 2.6 %collective-permute-start.11 = (bf16[128,512]{1,0:T(8,128)(2,1)S(1)}, bf16[128,512]{1,0:T(8,128)(2,1)S(1)}, u32[]{:S(2)}, u32[]{:S(2)}) collective-permute-start(bf16[128,512]{1,0:T(8,128)(2,1)S(1)} %get-tuple-element.118), channel_id=1, source_target_pairs={{0,6},{1,7},{2,4},{3,5},{4,2},{5,3},{6,0},{7,1},{8,14},{9,15},{10,... | collective-permute-start | bytes 393224 | tf_op jit(solution)/shard_map/ppermute | solution.py:32
  30.4 7.8 %collective-permute-done.14.rest_5_ = bf16[3,9,64,128]{3,2,1,0:T(8,128)(2,1)S(1)} collective-permute-done((bf16[3,9,64,128]{3,2,1,0:T(8,128)(2,1)S(1)}, bf16[3,9,64,128]{3,2,1,0:T(8,128)(2,1)S(1)}, u32[]{:S(2)}, u32[]{:S(2)}) %collective-permute-start.14) | collective-permute-done | bytes 442400 | tf_op jit(solution)/shard_map/ppermute | solution.py:32
  38.2 8.3 %collective-permute-done.13.rest_4_ = bf16[3,9,64,128]{3,2,1,0:T(8,128)(2,1)S(1)} collective-permute-done((bf16[3,9,64,128]{3,2,1,0:T(8,128)(2,1)S(1)}, bf16[3,9,64,128]{3,2,1,0:T(8,128)(2,1)S(1)}, u32[]{:S(2)}, u32[]{:S(2)}) %collective-permute-start.13) | collective-permute-done | bytes 442400 | tf_op jit(solution)/shard_map/ppermute | solution.py:32
  50.8 6.6 %shard_map.204 = (f32[512,512]{1,0:T(8,128)S(1)}, f32[512,512]{1,0:T(8,128)S(1)}, bf16[9,4,2,64,512]{4,3,2,1,0:T(8,128)(2,1)S(1)}) custom-call(s32[2,8]{1,0:T(2,128)S(1)} %copy-done.9, f32[10,512]{1,0:T(8,128)S(1)} %copy-done.8, bf16[2,256,512]{2,1,0:T(8,128)(2,1)S(1)} %copy-done.1, bf16[9,64,512]{2,1,0:T(8,128)(2,1)S(1)} %get-tuple-element.112.own, ...), custom_call_target="tpu_custom_call" | custom-call | flops 1 | bytes 1 | tf_op jit(solution)/shard_map/pallas_call | solution.py:118
  57.4 2.7 %collective-permute-done.20.refs_8_ = bf16[3,128,512]{2,1,0:T(8,128)(2,1)S(1)} collective-permute-done((bf16[3,128,512]{2,1,0:T(8,128)(2,1)S(1)}, bf16[3,128,512]{2,1,0:T(8,128)(2,1)S(1)}, u32[]{:S(2)}, u32[]{:S(2)}) %collective-permute-start.20) | collective-permute-done | bytes 393248 | tf_op jit(solution)/shard_map/ppermute | solution.py:32
  60.1 7.9 %collective-permute-done.19.refs_7_ = bf16[3,128,512]{2,1,0:T(8,128)(2,1)S(1)} collective-permute-done((bf16[3,128,512]{2,1,0:T(8,128)(2,1)S(1)}, bf16[3,128,512]{2,1,0:T(8,128)(2,1)S(1)}, u32[]{:S(2)}, u32[]{:S(2)}) %collective-permute-start.19) | collective-permute-done | bytes 393248 | tf_op jit(solution)/shard_map/ppermute | solution.py:32
  72.8 9.7 %shard_map.206 = (bf16[512,512]{1,0:T(8,128)(2,1)}, bf16[512,512]{1,0:T(8,128)(2,1)S(1)}, bf16[512,2048]{1,0:T(8,128)(2,1)S(1)}, bf16[512,512]{1,0:T(8,128)(2,1)...) custom-call(f32[512,512]{1,0:T(8,128)S(1)} %get-tuple-element.123.refs_0_, ...), custom_call_target="tpu_custom_call" | custom-call | flops 1 | bytes 1 | tf_op jit(solution)/shard_map/pallas_call | solution.py:118
  82.5 3.3 %shard_map.207 = (bf16[4,4,128,512]{3,2,1,0:T(8,128)(2,1)S(1)}, bf16[4,4,128,512]{3,2,1,0:T(8,128)(2,1)S(1)}) custom-call(bf16[512,512]{1,0:T(8,128)(2,1)S(1)} %get-tuple-element.135.refs_0_, bf16[512,2048]{1,0:T(8,128)(2,1)S(1)} %get-tuple-element.136.refs_1_, bf16[512,512]{1,0:T(8,128)(2,1)S(1)} %get-tuple-element.137.refs_2_, ...), custom_call_target="tpu_custom_call" | custom-call | flops 1 | bytes 1 | tf_op jit(solution)/shard_map/pallas_call | solution.py:118
  85.8 2.7 %shard_map.208 = (f32[512,512]{1,0:T(8,128)S(1)}, bf16[512,512]{1,0:T(8,128)(2,1)S(1)}, bf16[640,128]{1,0:T(8,128)(2,1)S(1)}, bf16[896,128]{1,0:T(8,128)(2,1)S(1...) custom-call(f32[512,512]{1,0:T(8,128)S(1)} %get-tuple-element.140.refs_0_, bf16[512,512]{1,0:T(8,128)(2,1)S(1)} %bitcast.9, ...), custom_call_target="tpu_custom_call" | custom-call | flops 1 | bytes 1 | tf_op jit(solution)/shard_map/pallas_call | solution.py:118
  88.6 1.5 collective-permute-start.26
  92.2 4.9 %collective-permute-done.26.refs_6_.refs_4_ = bf16[896,128]{1,0:T(8,128)(2,1)S(1)} collective-permute-done((bf16[896,128]{1,0:T(8,128)(2,1)S(1)}, bf16[896,128]{1,0:T(8,128)(2,1)S(1)}, u32[]{:S(2)}, u32[]{:S(2)}) %collective-permute-start.26) | collective-permute-done | bytes 229408 | tf_op jit(solution)/shard_map/ppermute | solution.py:32
  98.0 4.3 %collective-permute-done.28.refs_8_.refs_5_ = bf16[896,128]{1,0:T(8,128)(2,1)S(1)} collective-permute-done((bf16[896,128]{1,0:T(8,128)(2,1)S(1)}, bf16[896,128]{1,0:T(8,128)(2,1)S(1)}, u32[]{:S(2)}, u32[]{:S(2)}) %collective-permute-start.28) | collective-permute-done | bytes 229408 | tf_op jit(solution)/shard_map/ppermute | solution.py:32
  102.4 6.6 %shard_map.209 = (bf16[2432,128]{1,0:T(8,128)(2,1)S(1)}, bf16[2432,128]{1,0:T(8,128)(2,1)S(1)}) custom-call(s32[2,8]{1,0:T(2,128)S(1)} %copy-done.9, bf16[2,256,512]{2,1,0:T(8,128)(2,1)S(1)} %copy-done.1, bf16[2,256,512]{2,1,0:T(8,128)(2,1)S(1)} %collective-permute-done.2.rest_0_.refs_2_, bf16[2,256,512]{2,1,0:T(8,128)(2,1)S(1)} %collective-permute-done.3.refs_3_, ...), custom_call_target="tpu_custom_call" | custom-call | flops 1 | bytes 1 | tf_op jit(solution)/shard_map/pallas_call | solution.py:118
  113.7 3.2 %collective-permute-start.31 = (bf16[704,128]{1,0:T(8,128)(2,1)S(1)}, bf16[704,128]{1,0:T(8,128)(2,1)S(1)}, u32[]{:S(2)}, u32[]{:S(2)}) collective-permute-start(bf16[704,128]{1,0:T(8,128)(2,1)S(1)} %get-tuple-element.170), channel_id=1, source_target_pairs={{0,4},{1,5},{2,6},{3,7},{4,0},{5,1},{6,2},{7,3},{8,12},{9,13},{10,... | collective-permute-start | bytes 540680 | tf_op jit(solution)/shard_map/ppermute | solution.py:32
  116.9 6.5 %collective-permute-done.30.refs_1_ = bf16[704,128]{1,0:T(8,128)(2,1)S(1)} collective-permute-done((bf16[704,128]{1,0:T(8,128)(2,1)S(1)}, bf16[704,128]{1,0:T(8,128)(2,1)S(1)}, u32[]{:S(2)}, u32[]{:S(2)}) %collective-permute-start.30) | collective-permute-done | bytes 180256 | tf_op jit(solution)/shard_map/ppermute | solution.py:32
  124.8 7.4 %shard_map.211 = f32[512,512]{1,0:T(8,128)} custom-call(s32[2,8]{1,0:T(2,128)S(1)} %copy-done.9, bf16[512,512]{1,0:T(8,128)(2,1)S(1)} %get-tuple-element.164.refs_1_, f32[512,512]{1,0:T(8,128)S(1)} %get-tuple-element.165.refs_2_, bf16[9,4,2,64,512]{4,3,2,1,0:T(8,128)(2,1)S(1)} %get-tuple-element.166.refs_3_, ...), custom_call_target="tpu_custom_call" | custom-call | flops 1 | bytes 1 | tf_op jit(solution)/shard_map/pallas_call | solution.py:118
  132.5 1.6 collective-permute-start.39
  134.1 4.9 %collective-permute-done.37.refs_2_ = bf16[512,512]{1,0:T(8,128)(2,1)S(1)} collective-permute-done((bf16[512,512]{1,0:T(8,128)(2,1)S(1)}, bf16[512,512]{1,0:T(8,128)(2,1)S(1)}, u32[]{:S(2)}, u32[]{:S(2)}) %collective-permute-start.37) | collective-permute-done | bytes 524320 | tf_op jit(solution)/shard_map/ppermute | solution.py:32
  139.4 3.2 %collective-permute-start.41 = (bf16[128,512]{1,0:T(8,128)(2,1)S(1)}, bf16[128,512]{1,0:T(8,128)(2,1)S(1)}, u32[]{:S(2)}, u32[]{:S(2)}) collective-permute-start(bf16[128,512]{1,0:T(8,128)(2,1)S(1)} %get-tuple-element.183), channel_id=1, source_target_pairs={{0,4},{1,5},{2,6},{3,7},{4,0},{5,1},{6,2},{7,3},{8,12},{9,13},{10,... | collective-permute-start | bytes 393224 | tf_op jit(solution)/shard_map/ppermute | solution.py:32
  143.8 2.2 %collective-permute-done.40.refs_1_ = bf16[128,512]{1,0:T(8,128)(2,1)S(1)} collective-permute-done((bf16[128,512]{1,0:T(8,128)(2,1)S(1)}, bf16[128,512]{1,0:T(8,128)(2,1)S(1)}, u32[]{:S(2)}, u32[]{:S(2)}) %collective-permute-start.40) | collective-permute-done | bytes 131104 | tf_op jit(solution)/shard_map/ppermute | solution.py:32
  146.0 1.7 %collective-permute-done.41.refs_2_ = bf16[128,512]{1,0:T(8,128)(2,1)S(1)} collective-permute-done((bf16[128,512]{1,0:T(8,128)(2,1)S(1)}, bf16[128,512]{1,0:T(8,128)(2,1)S(1)}, u32[]{:S(2)}, u32[]{:S(2)}) %collective-permute-start.41) | collective-permute-done | bytes 131104 | tf_op jit(solution)/shard_map/ppermute | solution.py:32
  147.7 1.7 %collective-permute-done.42.refs_3_ = bf16[128,512]{1,0:T(8,128)(2,1)S(1)} collective-permute-done((bf16[128,512]{1,0:T(8,128)(2,1)S(1)}, bf16[128,512]{1,0:T(8,128)(2,1)S(1)}, u32[]{:S(2)}, u32[]{:S(2)}) %collective-permute-start.42) | collective-permute-done | bytes 131104 | tf_op jit(solution)/shard_map/ppermute | solution.py:32
  157.5 2.4 %collective-permute-start.48 = (f32[8,128]{1,0:T(8,128)S(1)}, f32[8,128]{1,0:T(8,128)S(1)}, u32[]{:S(2)}, u32[]{:S(2)}) collective-permute-start(f32[8,128]{1,0:T(8,128)S(1)} %shard_map.216.refs_0_), channel_id=1, source_target_pairs={{0,6},{1,7},{2,4},{3,5},{4,2},{5,3},{6,0},{7,1},{8,14},{9,15},{10,... | collective-permute-start | bytes 12296 | tf_op jit(solution)/shard_map/ppermute | solution.py:32
  159.9 2.1 %collective-permute-start.47 = (f32[8,128]{1,0:T(8,128)S(1)}, f32[8,128]{1,0:T(8,128)S(1)}, u32[]{:S(2)}, u32[]{:S(2)}) collective-permute-start(f32[8,128]{1,0:T(8,128)S(1)} %shard_map.216.refs_0_), channel_id=1, source_target_pairs={{0,4},{1,5},{2,6},{3,7},{4,0},{5,1},{6,2},{7,3},{8,12},{9,13},{10,... | collective-permute-start | bytes 12296 | tf_op jit(solution)/shard_map/ppermute | solution.py:32
  166.8 4.9 %shard_map.218 = (f32[1,1]{1,0:T(1,128)}, f32[10,512]{1,0:T(8,128)}, f32[10,512]{1,0:T(8,128)}, f32[9,64,512]{2,1,0:T(8,128)}, f32[9,64,512]{2,1,0:T(8,128)}, /*...) custom-call(bf16[576,128]{1,0:T(8,128)(2,1)S(1)} %get-tuple-element., ...), custom_call_target="tpu_custom_call" | custom-call | flops 1 | bytes 1 | tf_op jit(solution)/shard_map/pallas_call | solution.py:118
  (108 shorter events, 38.8 us)
Async XLA Ops:
  2.4 17.6 %collective-permute-start.3 = (bf16[2,256,512]{2,1,0:T(8,128)(2,1)S(1)}, bf16[2,256,512]{2,1,0:T(8,128)(2,1)S(1)}, u32[]{:S(2)}, u32[]{:S(2)}) collective-permute-start(bf16[2,256,512]{2,1,0:T(8,128)(2,1)S(1)} %copy-done.1), channel_id=1, source_target_pairs={{0,16},{8,24},{16,0},{24,8},{1,17},{9,25},{17,1},{25,9},{2,18},{10... | collective-permute-start | bytes 1572872 | tf_op jit(solution)/shard_map/ppermute | solution.py:32
  5.4 14.6 %collective-permute-start.2 = (bf16[2,256,512]{2,1,0:T(8,128)(2,1)S(1)}, bf16[2,256,512]{2,1,0:T(8,128)(2,1)S(1)}, u32[]{:S(2)}, u32[]{:S(2)}) collective-permute-start(bf16[2,256,512]{2,1,0:T(8,128)(2,1)S(1)} %copy-done.1), channel_id=1, source_target_pairs={{0,8},{8,0},{16,24},{24,16},{1,9},{9,1},{17,25},{25,17},{2,10},{10... | collective-permute-start | bytes 1572872 | tf_op jit(solution)/shard_map/ppermute | solution.py:32
  8.5 11.5 %collective-permute-start.5 = (bf16[9,64,128]{2,1,0:T(8,128)(2,1)S(1)}, bf16[9,64,128]{2,1,0:T(8,128)(2,1)S(1)}, u32[]{:S(2)}, u32[]{:S(2)}) collective-permute-start(bf16[9,64,128]{2,1,0:T(8,128)(2,1)S(1)} %get-tuple-element.107), channel_id=1, source_target_pairs={{0,6},{1,7},{2,4},{3,5},{4,2},{5,3},{6,0},{7,1},{8,14},{9,15},{10,... | collective-permute-start | bytes 442376 | tf_op jit(solution)/shard_map/ppermute | solution.py:32
  11.0 12.6 %collective-permute-start.4 = (bf16[9,64,128]{2,1,0:T(8,128)(2,1)S(1)}, bf16[9,64,128]{2,1,0:T(8,128)(2,1)S(1)}, u32[]{:S(2)}, u32[]{:S(2)}) collective-permute-start(bf16[9,64,128]{2,1,0:T(8,128)(2,1)S(1)} %get-tuple-element.107), channel_id=1, source_target_pairs={{0,4},{1,5},{2,6},{3,7},{4,0},{5,1},{6,2},{7,3},{8,12},{9,13},{10,... | collective-permute-start | bytes 442376 | tf_op jit(solution)/shard_map/ppermute | solution.py:32
  12.3 7.7 %collective-permute-start.1 = (bf16[2,32,512]{2,1,0:T(8,128)(2,1)S(1)}, bf16[2,32,512]{2,1,0:T(8,128)(2,1)S(1)}, u32[]{:S(2)}, u32[]{:S(2)}) collective-permute-start(bf16[2,32,512]{2,1,0:T(8,128)(2,1)S(1)} %get-tuple-element.109), channel_id=1, source_target_pairs={{0,24},{8,16},{16,8},{24,0},{1,25},{9,17},{17,9},{25,1},{2,26},{10... | collective-permute-start | bytes 196616 | tf_op jit(solution)/shard_map/ppermute | solution.py:32
  24.3 13.9 %collective-permute-start.14 = (bf16[3,9,64,128]{3,2,1,0:T(8,128)(2,1)S(1)}, bf16[3,9,64,128]{3,2,1,0:T(8,128)(2,1)S(1)}, u32[]{:S(2)}, u32[]{:S(2)}) collective-permute-start(bf16[3,9,64,128]{3,2,1,0:T(8,128)(2,1)S(1)} %shard_map.203.rest_2_), channel_id=1, source_target_pairs={{0,24},{8,16},{16,8},{24,0},{1,25},{9,17},{17,9},{25,1},{2,26},{10... | collective-permute-start | bytes 1327112 | tf_op jit(solution)/shard_map/ppermute | solution.py:32
  24.8 21.7 %collective-permute-start.13 = (bf16[3,9,64,128]{3,2,1,0:T(8,128)(2,1)S(1)}, bf16[3,9,64,128]{3,2,1,0:T(8,128)(2,1)S(1)}, u32[]{:S(2)}, u32[]{:S(2)}) collective-permute-start(bf16[3,9,64,128]{3,2,1,0:T(8,128)(2,1)S(1)} %shard_map.203.rest_2_), channel_id=1, source_target_pairs={{0,16},{8,24},{16,0},{24,8},{1,17},{9,25},{17,1},{25,9},{2,18},{10... | collective-permute-start | bytes 1327112 | tf_op jit(solution)/shard_map/ppermute | solution.py:32
  26.3 20.2 %collective-permute-start.12 = (bf16[3,9,64,128]{3,2,1,0:T(8,128)(2,1)S(1)}, bf16[3,9,64,128]{3,2,1,0:T(8,128)(2,1)S(1)}, u32[]{:S(2)}, u32[]{:S(2)}) collective-permute-start(bf16[3,9,64,128]{3,2,1,0:T(8,128)(2,1)S(1)} %shard_map.203.rest_2_), channel_id=1, source_target_pairs={{0,8},{8,0},{16,24},{24,16},{1,9},{9,1},{17,25},{25,17},{2,10},{10... | collective-permute-start | bytes 1327112 | tf_op jit(solution)/shard_map/ppermute | solution.py:32
  27.8 18.7 %collective-permute-start.11 = (bf16[128,512]{1,0:T(8,128)(2,1)S(1)}, bf16[128,512]{1,0:T(8,128)(2,1)S(1)}, u32[]{:S(2)}, u32[]{:S(2)}) collective-permute-start(bf16[128,512]{1,0:T(8,128)(2,1)S(1)} %get-tuple-element.118), channel_id=1, source_target_pairs={{0,6},{1,7},{2,4},{3,5},{4,2},{5,3},{6,0},{7,1},{8,14},{9,15},{10,... | collective-permute-start | bytes 393224 | tf_op jit(solution)/shard_map/ppermute | solution.py:32
  30.4 16.1 %collective-permute-start.10 = (bf16[128,512]{1,0:T(8,128)(2,1)S(1)}, bf16[128,512]{1,0:T(8,128)(2,1)S(1)}, u32[]{:S(2)}, u32[]{:S(2)}) collective-permute-start(bf16[128,512]{1,0:T(8,128)(2,1)S(1)} %get-tuple-element.118), channel_id=1, source_target_pairs={{0,4},{1,5},{2,6},{3,7},{4,0},{5,1},{6,2},{7,3},{8,12},{9,13},{10,... | collective-permute-start | bytes 393224 | tf_op jit(solution)/shard_map/ppermute | solution.py:32
  38.2 8.3 %collective-permute-start.9 = (bf16[128,512]{1,0:T(8,128)(2,1)S(1)}, bf16[128,512]{1,0:T(8,128)(2,1)S(1)}, u32[]{:S(2)}, u32[]{:S(2)}) collective-permute-start(bf16[128,512]{1,0:T(8,128)(2,1)S(1)} %get-tuple-element.118), channel_id=1, source_target_pairs={{0,2},{1,3},{2,0},{3,1},{4,6},{5,7},{6,4},{7,5},{8,10},{9,11},{10,... | collective-permute-start | bytes 393224 | tf_op jit(solution)/shard_map/ppermute | solution.py:32
  47.2 12.9 %collective-permute-start.20 = (bf16[3,128,512]{2,1,0:T(8,128)(2,1)S(1)}, bf16[3,128,512]{2,1,0:T(8,128)(2,1)S(1)}, u32[]{:S(2)}, u32[]{:S(2)}) collective-permute-start(bf16[3,128,512]{2,1,0:T(8,128)(2,1)S(1)} %get-tuple-element.130.refs_5_), channel_id=1, source_target_pairs={{0,24},{8,16},{16,8},{24,0},{1,25},{9,17},{17,9},{25,1},{2,26},{10... | collective-permute-start | bytes 1179656 | tf_op jit(solution)/shard_map/ppermute | solution.py:32
  48.6 19.5 %collective-permute-start.19 = (bf16[3,128,512]{2,1,0:T(8,128)(2,1)S(1)}, bf16[3,128,512]{2,1,0:T(8,128)(2,1)S(1)}, u32[]{:S(2)}, u32[]{:S(2)}) collective-permute-start(bf16[3,128,512]{2,1,0:T(8,128)(2,1)S(1)} %get-tuple-element.130.refs_5_), channel_id=1, source_target_pairs={{0,16},{8,24},{16,0},{24,8},{1,17},{9,25},{17,1},{25,9},{2,18},{10... | collective-permute-start | bytes 1179656 | tf_op jit(solution)/shard_map/ppermute | solution.py:32
  50.0 18.1 %collective-permute-start.18 = (bf16[3,128,512]{2,1,0:T(8,128)(2,1)S(1)}, bf16[3,128,512]{2,1,0:T(8,128)(2,1)S(1)}, u32[]{:S(2)}, u32[]{:S(2)}) collective-permute-start(bf16[3,128,512]{2,1,0:T(8,128)(2,1)S(1)} %get-tuple-element.130.refs_5_), channel_id=1, source_target_pairs={{0,8},{8,0},{16,24},{24,16},{1,9},{9,1},{17,25},{25,17},{2,10},{10... | collective-permute-start | bytes 1179656 | tf_op jit(solution)/shard_map/ppermute | solution.py:32
  68.1 20.4 %collective-permute-start.25 = (bf16[2,256,512]{2,1,0:T(8,128)(2,1)S(1)}, bf16[2,256,512]{2,1,0:T(8,128)(2,1)S(1)}, u32[]{:S(2)}, u32[]{:S(2)}) collective-permute-start(bf16[2,256,512]{2,1,0:T(8,128)(2,1)S(1)} %copy-done.1), channel_id=1, source_target_pairs={{0,24},{8,16},{16,8},{24,0},{1,25},{9,17},{17,9},{25,1},{2,26},{10... | collective-permute-start | bytes 1572872 | tf_op jit(solution)/shard_map/ppermute | solution.py:32
  88.4 20.6 %collective-permute-start.35 = (bf16[4,4,128,512]{3,2,1,0:T(8,128)(2,1)S(1)}, bf16[4,4,128,512]{3,2,1,0:T(8,128)(2,1)S(1)}, u32[]{:S(2)}, u32[]{:S(2)}) collective-permute-start(bf16[4,4,128,512]{3,2,1,0:T(8,128)(2,1)S(1)} %get-tuple-element.174), channel_id=1, source_target_pairs={{0,1},{1,0},{2,3},{3,2},{4,5},{5,4},{6,7},{7,6},{8,9},{9,8},{10,11... | collective-permute-start | bytes 6291464 | tf_op jit(solution)/shard_map/ppermute | solution.py:32
  88.6 8.4 %collective-permute-start.26 = (bf16[896,128]{1,0:T(8,128)(2,1)S(1)}, bf16[896,128]{1,0:T(8,128)(2,1)S(1)}, u32[]{:S(2)}, u32[]{:S(2)}) collective-permute-start(bf16[896,128]{1,0:T(8,128)(2,1)S(1)} %get-tuple-element.157), channel_id=1, source_target_pairs={{0,8},{8,0},{16,24},{24,16},{1,9},{9,1},{17,25},{25,17},{2,10},{10... | collective-permute-start | bytes 688136 | tf_op jit(solution)/shard_map/ppermute | solution.py:32
  90.2 12.2 %collective-permute-start.28 = (bf16[896,128]{1,0:T(8,128)(2,1)S(1)}, bf16[896,128]{1,0:T(8,128)(2,1)S(1)}, u32[]{:S(2)}, u32[]{:S(2)}) collective-permute-start(bf16[896,128]{1,0:T(8,128)(2,1)S(1)} %get-tuple-element.160), channel_id=1, source_target_pairs={{0,24},{8,16},{16,8},{24,0},{1,25},{9,17},{17,9},{25,1},{2,26},{10... | collective-permute-start | bytes 688136 | tf_op jit(solution)/shard_map/ppermute | solution.py:32
  91.6 6.5 %collective-permute-start.27 = (bf16[640,128]{1,0:T(8,128)(2,1)S(1)}, bf16[640,128]{1,0:T(8,128)(2,1)S(1)}, u32[]{:S(2)}, u32[]{:S(2)}) collective-permute-start(bf16[640,128]{1,0:T(8,128)(2,1)S(1)} %get-tuple-element.159), channel_id=1, source_target_pairs={{0,16},{8,24},{16,0},{24,8},{1,17},{9,25},{17,1},{25,9},{2,18},{10... | collective-permute-start | bytes 491528 | tf_op jit(solution)/shard_map/ppermute | solution.py:32
  109.7 24.4 %collective-permute-start.36 = (bf16[512,512]{1,0:T(8,128)(2,1)S(1)}, bf16[512,512]{1,0:T(8,128)(2,1)S(1)}, u32[]{:S(2)}, u32[]{:S(2)}) collective-permute-start(bf16[512,512]{1,0:T(8,128)(2,1)S(1)} %get-tuple-element.176), channel_id=1, source_target_pairs={{0,8},{8,0},{16,24},{24,16},{1,9},{9,1},{17,25},{25,17},{2,10},{10... | collective-permute-start | bytes 1572872 | tf_op jit(solution)/shard_map/ppermute | solution.py:32
  110.6 28.4 %collective-permute-start.37 = (bf16[512,512]{1,0:T(8,128)(2,1)S(1)}, bf16[512,512]{1,0:T(8,128)(2,1)S(1)}, u32[]{:S(2)}, u32[]{:S(2)}) collective-permute-start(bf16[512,512]{1,0:T(8,128)(2,1)S(1)} %get-tuple-element.177), channel_id=1, source_target_pairs={{0,16},{8,24},{16,0},{24,8},{1,17},{9,25},{17,1},{25,9},{2,18},{10... | collective-permute-start | bytes 1572872 | tf_op jit(solution)/shard_map/ppermute | solution.py:32
  111.9 27.1 %collective-permute-start.38 = (bf16[512,512]{1,0:T(8,128)(2,1)S(1)}, bf16[512,512]{1,0:T(8,128)(2,1)S(1)}, u32[]{:S(2)}, u32[]{:S(2)}) collective-permute-start(bf16[512,512]{1,0:T(8,128)(2,1)S(1)} %get-tuple-element.178), channel_id=1, source_target_pairs={{0,24},{8,16},{16,8},{24,0},{1,25},{9,17},{17,9},{25,1},{2,26},{10... | collective-permute-start | bytes 1572872 | tf_op jit(solution)/shard_map/ppermute | solution.py:32
  113.7 9.8 %collective-permute-start.30 = (bf16[704,128]{1,0:T(8,128)(2,1)S(1)}, bf16[704,128]{1,0:T(8,128)(2,1)S(1)}, u32[]{:S(2)}, u32[]{:S(2)}) collective-permute-start(bf16[704,128]{1,0:T(8,128)(2,1)S(1)} %get-tuple-element.169), channel_id=1, source_target_pairs={{0,2},{1,3},{2,0},{3,1},{4,6},{5,7},{6,4},{7,5},{8,10},{9,11},{10,... | collective-permute-start | bytes 540680 | tf_op jit(solution)/shard_map/ppermute | solution.py:32
  113.7 18.5 %collective-permute-start.31 = (bf16[704,128]{1,0:T(8,128)(2,1)S(1)}, bf16[704,128]{1,0:T(8,128)(2,1)S(1)}, u32[]{:S(2)}, u32[]{:S(2)}) collective-permute-start(bf16[704,128]{1,0:T(8,128)(2,1)S(1)} %get-tuple-element.170), channel_id=1, source_target_pairs={{0,4},{1,5},{2,6},{3,7},{4,0},{5,1},{6,2},{7,3},{8,12},{9,13},{10,... | collective-permute-start | bytes 540680 | tf_op jit(solution)/shard_map/ppermute | solution.py:32
  123.5 8.8 %collective-permute-start.32 = (bf16[704,128]{1,0:T(8,128)(2,1)S(1)}, bf16[704,128]{1,0:T(8,128)(2,1)S(1)}, u32[]{:S(2)}, u32[]{:S(2)}) collective-permute-start(bf16[704,128]{1,0:T(8,128)(2,1)S(1)} %get-tuple-element.171), channel_id=1, source_target_pairs={{0,6},{1,7},{2,4},{3,5},{4,2},{5,3},{6,0},{7,1},{8,14},{9,15},{10,... | collective-permute-start | bytes 540680 | tf_op jit(solution)/shard_map/ppermute | solution.py:32
  132.5 11.3 %collective-permute-start.39 = (bf16[576,128]{1,0:T(8,128)(2,1)S(1)}, bf16[576,128]{1,0:T(8,128)(2,1)S(1)}, u32[]{:S(2)}, u32[]{:S(2)}) collective-permute-start(bf16[576,128]{1,0:T(8,128)(2,1)S(1)} %get-tuple-element.172.refs_0_), channel_id=1, source_target_pairs={{0,24},{8,16},{16,8},{24,0},{1,25},{9,17},{17,9},{25,1},{2,26},{10... | collective-permute-start | bytes 442376 | tf_op jit(solution)/shard_map/ppermute | solution.py:32
  139.3 6.7 %collective-permute-start.40 = (bf16[128,512]{1,0:T(8,128)(2,1)S(1)}, bf16[128,512]{1,0:T(8,128)(2,1)S(1)}, u32[]{:S(2)}, u32[]{:S(2)}) collective-permute-start(bf16[128,512]{1,0:T(8,128)(2,1)S(1)} %get-tuple-element.182), channel_id=1, source_target_pairs={{0,2},{1,3},{2,0},{3,1},{4,6},{5,7},{6,4},{7,5},{8,10},{9,11},{10,... | collective-permute-start | bytes 393224 | tf_op jit(solution)/shard_map/ppermute | solution.py:32
  139.4 8.3 %collective-permute-start.41 = (bf16[128,512]{1,0:T(8,128)(2,1)S(1)}, bf16[128,512]{1,0:T(8,128)(2,1)S(1)}, u32[]{:S(2)}, u32[]{:S(2)}) collective-permute-start(bf16[128,512]{1,0:T(8,128)(2,1)S(1)} %get-tuple-element.183), channel_id=1, source_target_pairs={{0,4},{1,5},{2,6},{3,7},{4,0},{5,1},{6,2},{7,3},{8,12},{9,13},{10,... | collective-permute-start | bytes 393224 | tf_op jit(solution)/shard_map/ppermute | solution.py:32
  142.6 6.9 %collective-permute-start.42 = (bf16[128,512]{1,0:T(8,128)(2,1)S(1)}, bf16[128,512]{1,0:T(8,128)(2,1)S(1)}, u32[]{:S(2)}, u32[]{:S(2)}) collective-permute-start(bf16[128,512]{1,0:T(8,128)(2,1)S(1)} %get-tuple-element.184), channel_id=1, source_target_pairs={{0,6},{1,7},{2,4},{3,5},{4,2},{5,3},{6,0},{7,1},{8,14},{9,15},{10,... | collective-permute-start | bytes 393224 | tf_op jit(solution)/shard_map/ppermute | solution.py:32
  151.0 6.4 %collective-permute-start.44 = (bf16[144,512]{1,0:T(8,128)(2,1)S(1)}, bf16[144,512]{1,0:T(8,128)(2,1)S(1)}, u32[]{:S(2)}, u32[]{:S(2)}) collective-permute-start(bf16[144,512]{1,0:T(8,128)(2,1)S(1)} %shard_map.215.refs_0_.refs_4_), channel_id=1, source_target_pairs={{0,16},{8,24},{16,0},{24,8},{1,17},{9,25},{17,1},{25,9},{2,18},{10... | collective-permute-start | bytes 442376 | tf_op jit(solution)/shard_map/ppermute | solution.py:32
  153.1 12.4 %collective-permute-start.34 = (bf16[576,128]{1,0:T(8,128)(2,1)S(1)}, bf16[576,128]{1,0:T(8,128)(2,1)S(1)}, u32[]{:S(2)}, u32[]{:S(2)}) collective-permute-start(bf16[576,128]{1,0:T(8,128)(2,1)S(1)} %get-tuple-element.172.refs_0_), channel_id=1, source_target_pairs={{0,16},{8,24},{16,0},{24,8},{1,17},{9,25},{17,1},{25,9},{2,18},{10... | collective-permute-start | bytes 442376 | tf_op jit(solution)/shard_map/ppermute | solution.py:32
  154.4 11.1 %collective-permute-start.33 = (bf16[576,128]{1,0:T(8,128)(2,1)S(1)}, bf16[576,128]{1,0:T(8,128)(2,1)S(1)}, u32[]{:S(2)}, u32[]{:S(2)}) collective-permute-start(bf16[576,128]{1,0:T(8,128)(2,1)S(1)} %get-tuple-element.172.refs_0_), channel_id=1, source_target_pairs={{0,8},{8,0},{16,24},{24,16},{1,9},{9,1},{17,25},{25,17},{2,10},{10... | collective-permute-start | bytes 442376 | tf_op jit(solution)/shard_map/ppermute | solution.py:32
  (29 other events, 470.1 us)

commit v7 on v6

--- a/solution.py
+++ b/solution.py
@@ -22,6 +22,7 @@
 F32 = jnp.float32
 BF = jnp.bfloat16
 VEC_PAD = 16
+VEC_ROWS = 10
 LANES = 128
 SQRT_HALF = 0.7071067811865476
 PDF_SCALE = 0.3989422804014327
@@ -406,7 +407,7 @@
     for k in range(ns):
         sends[k][0:count, :] = conv_grad[:, at(seq_at ^ k, span)]
         encode(sends[k], count, spread(sums[...]))
-        begin = count + 2 * VEC_PAD * width // LANES
+        begin = count + 2 * VEC_ROWS * width // LANES
         if sends[k].shape[0] > begin:
             half = (sends[k].shape[0] - begin) // rows // (width // LANES)
             length = count // rows
@@ -420,6 +421,7 @@
 
 
 def spread(v):
+    v = v[:VEC_ROWS]
     return jnp.concatenate(
         [v[:, a * LANES : (a + 1) * LANES] for a in range(v.shape[1] // LANES)], axis=0
     )
@@ -427,7 +429,7 @@
 
 def gathered(v):
     return jnp.concatenate(
-        [v[a * VEC_PAD : (a + 1) * VEC_PAD, :] for a in range(v.shape[0] // VEC_PAD)], axis=1
+        [v[a * VEC_ROWS : (a + 1) * VEC_ROWS, :] for a in range(v.shape[0] // VEC_ROWS)], axis=1
     )
 
 
@@ -524,7 +526,7 @@
                 out[begin : begin + in_rows, :] = total[
                     at(block, in_rows), t * span : (t + 1) * span
                 ].astype(BF)
-    vec_rows = VEC_PAD * width // LANES
+    vec_rows = VEC_ROWS * width // LANES
     summed = tree_sum([decode(g, count, vec_rows) for g in grads])
     for out in (mine, theirs):
         encode(out, nz * taps * in_rows, summed)
@@ -721,10 +723,6 @@
             second[:, at(t * ns + (seq_at ^ k), span)] = v
         return carry
 
-    lax.fori_loop(0, taps, conv_step, 0)
-    send(0, new_conv, outs[0])
-    send(1, conv_first, outs[1])
-    send(2, second.at[:, : taps * width], outs[6].at[:, : taps * width])
     for k in range(ns):
         lanes = at(seq_at ^ k, quarter)
         w, m, v = adam_math(
@@ -739,8 +737,8 @@
         new_inner[:, lanes] = w
         inner_first[:, lanes] = m
         second[:, at(taps * width // quarter + (seq_at ^ k), quarter)] = v
-    send(3, new_inner, outs[2])
-    send(4, inner_first, outs[3])
+    send(0, new_inner, outs[2])
+    send(1, inner_first, outs[3])
     for k in range(ns):
         where = at(seq_at ^ k, part)
         w, m, v = adam_math(
@@ -756,8 +754,8 @@
         outer_first[where, :] = m
         for a in range(width // LANES):
             outer_second[a, where, :] = v[:, a * LANES : (a + 1) * LANES]
-    send(5, new_outer, outs[4])
-    send(6, outer_first, outs[5])
+    send(2, new_outer, outs[4])
+    send(3, outer_first, outs[5])
     ratio = out_rows // in_rows
     base = taps * width + hid
     for e in range(ratio):
@@ -772,7 +770,15 @@
     begin = base + ratio * width
     block = z_at * 2 + core_at
     second[:, begin : begin + vec_count] = vec_second[at(block, in_rows), :][:, 0:vec_count]
-    send(7, second.at[:, taps * width :], outs[6].at[:, taps * width :])
+    send(4, second.at[:, taps * width :], outs[6].at[:, taps * width :])
+    parts = 3
+    for p in range(parts):
+        low, high = taps * p // parts, taps * (p + 1) // parts
+        lax.fori_loop(low, high, conv_step, 0)
+        send(5 + 3 * p, new_conv.at[low:high], outs[0].at[low:high])
+        send(6 + 3 * p, conv_first.at[low:high], outs[1].at[low:high])
+        cols = slice(low * width, high * width)
+        send(7 + 3 * p, second.at[:, cols], outs[6].at[:, cols])
     end_copies(going)
 
 
@@ -804,7 +810,7 @@
     part = out_rows // ns
 
     ffn_rows = in_rows + part
-    vec_rows = VEC_PAD * width // LANES
+    vec_rows = VEC_ROWS * width // LANES
     conv_rows = taps * in_rows
     cot = cotangent.reshape(count, width)
 
@@ -866,6 +872,7 @@
     )(*ffn_got, vector_moments)
     ffn_pieces = [ffn_got] + [exchange(ffn_got, "seq", k) for k in range(1, ns)]
 
+    ffn_near, conv_own = lax.optimization_barrier((exchange(ffn_got, "row", 1), conv_own))
     pre, after, conv_full = vmem_call(
         functools.partial(conv_kernel, taps, nz, ns, masks),
         [((count, width), F32), ((count, width), F32), ((taps, nz, 2, in_rows, width), BF)],
@@ -895,9 +902,9 @@
         token_pieces[1 + near.index(k)] if k in near else exchange(tokens_late, "seq", k)
         for k in range(1, ns)
     ]
-    late = lax.optimization_barrier((pre, *ffn_pieces))
-    pre, ffn_pieces = late[0], late[1:]
-    ffn_other_pieces = [exchange(p, "row", 1) for p in ffn_pieces]
+    late = lax.optimization_barrier((pre, *ffn_pieces[1:]))
+    pre, ffn_pieces = late[0], [ffn_got, *late[1:]]
+    ffn_other_pieces = [ffn_near] + [exchange(p, "row", 1) for p in ffn_pieces[1:]]
 
     layer_out, low, hidden, outer_grad, inner_grad, inner_full, vec_sums = vmem_call(
         functools.partial(ffn_kernel, nz, ns),
@@ -983,7 +990,7 @@
 
     conv_sum, conv_square, vec_sum = vmem_call(
         functools.partial(conv_final_kernel, nz, vec_rows),
-        [((conv_rows, span), BF), ((8, LANES), F32), ((VEC_PAD, width), F32)],
+        [((conv_rows, span), BF), ((8, LANES), F32), ((VEC_ROWS, width), F32)],
         slack=2,
     )(*sums)
     conv_sums = [conv_sum] + [exchange(conv_sum, "seq", k) for k in range(1, ns)]
@@ -1030,7 +1037,7 @@
         + [
             pltpu.VMEM((width // LANES, out_rows, LANES), F32),
             pltpu.VMEM((width, LANES), F32),
-            pltpu.SemaphoreType.DMA((8,)),
+            pltpu.SemaphoreType.DMA((14,)),
         ],
         kept=range(3),
         left=range(3, 10),

time: 172 us -> 171 us (level)
  transfers between devices with their start and end apart: 50 -> 50, of which waited for: 26 -> 25; matrix products, arithmetic and copies ran while one was open for 0% -> 0% of each run, Pallas kernels for 22% -> 22%
where the time goes in v7:
time: 171 us
  waiting for transfers between devices  74.9 us (44%)
  starting transfers between devices  50.3 us (29%)
  Pallas kernels  44.4 us (26%)
    ppermute x50, waiting for transfers between devices, exchange(): return lax.ppermute(value, axis, [(i, i ^ mask) for i in range(size)])  74.9 us
    ppermute x50, starting transfers between devices, exchange(): return lax.ppermute(value, axis, [(i, i ^ mask) for i in range(size)])  50.3 us
    pallas_call x17, Pallas kernels, call(): pl.pallas_call(kernel, out_shape=[jax.ShapeDtypeStruct(shape, dtype) if i...  44.4 us
  transfers between devices with their start and end apart: 50, of which 25 were waited for; matrix products, arithmetic and copies ran while one was open for 0% of the time, Pallas kernels for 22%

profile of v7, /device:TPU:0, one launch (start us, length us, event | category | flops | bytes accessed | tf_op | source)
XLA Modules:
  0.0 170.8 jit_solution(17415085427125818645)
XLA Ops:
  0.7 1.7 %shard_map.202 = (bf16[9,64,128]{2,1,0:T(8,128)(2,1)S(1)}, bf16[9,64,512]{2,1,0:T(8,128)(2,1)S(1)}, bf16[512,512]{1,0:T(8,128)(2,1)S(1)}, bf16[128,512]{1,0:T(8,128)(2,1)S(1)}, bf16[2,32,512]{2,1,0:T(8,128)(2,1)S(1)}) custom-call(f32[9,64,512]{2,1,0:T(8,128)} %refs_11_.1, f32[64,2048]{1,0:T(8,128)} %refs_12_.1, f32[256,512]{1,0:T(8,128)} %refs_13_.1, ...), custom_call_target="tpu_custom_call" | custom-call | flops 1 | bytes 1 | tf_op jit(solution)/shard_map/pallas_call | solution.py:119
  2.4 3.0 %collective-permute-start.3 = (bf16[2,256,512]{2,1,0:T(8,128)(2,1)S(1)}, bf16[2,256,512]{2,1,0:T(8,128)(2,1)S(1)}, u32[]{:S(2)}, u32[]{:S(2)}) collective-permute-start(bf16[2,256,512]{2,1,0:T(8,128)(2,1)S(1)} %copy-done.1), channel_id=1, source_target_pairs={{0,16},{8,24},{16,0},{24,8},{1,17},{9,25},{17,1},{25,9},{2,18},{10... | collective-permute-start | bytes 1572872 | tf_op jit(solution)/shard_map/ppermute | solution.py:33
  6.9 1.6 collective-permute-start
  8.5 2.5 %collective-permute-start.5 = (bf16[9,64,128]{2,1,0:T(8,128)(2,1)S(1)}, bf16[9,64,128]{2,1,0:T(8,128)(2,1)S(1)}, u32[]{:S(2)}, u32[]{:S(2)}) collective-permute-start(bf16[9,64,128]{2,1,0:T(8,128)(2,1)S(1)} %get-tuple-element.107), channel_id=1, source_target_pairs={{0,6},{1,7},{2,4},{3,5},{4,2},{5,3},{6,0},{7,1},{8,14},{9,15},{10,... | collective-permute-start | bytes 442376 | tf_op jit(solution)/shard_map/ppermute | solution.py:33
  12.8 7.2 %collective-permute-done.1.rest_1_ = bf16[2,32,512]{2,1,0:T(8,128)(2,1)S(1)} collective-permute-done((bf16[2,32,512]{2,1,0:T(8,128)(2,1)S(1)}, bf16[2,32,512]{2,1,0:T(8,128)(2,1)S(1)}, u32[]{:S(2)}, u32[]{:S(2)}) %collective-permute-start.1) | collective-permute-done | bytes 65568 | tf_op jit(solution)/shard_map/ppermute | solution.py:33
  20.0 3.5 %collective-permute-done.4.refs_1_ = bf16[9,64,128]{2,1,0:T(8,128)(2,1)S(1)} collective-permute-done((bf16[9,64,128]{2,1,0:T(8,128)(2,1)S(1)}, bf16[9,64,128]{2,1,0:T(8,128)(2,1)S(1)}, u32[]{:S(2)}, u32[]{:S(2)}) %collective-permute-start.4) | collective-permute-done | bytes 147488 | tf_op jit(solution)/shard_map/ppermute | solution.py:33
  24.8 1.5 collective-permute-start.13
  27.8 2.6 %collective-permute-start.11 = (bf16[128,512]{1,0:T(8,128)(2,1)S(1)}, bf16[128,512]{1,0:T(8,128)(2,1)S(1)}, u32[]{:S(2)}, u32[]{:S(2)}) collective-permute-start(bf16[128,512]{1,0:T(8,128)(2,1)S(1)} %get-tuple-element.116), channel_id=1, source_target_pairs={{0,6},{1,7},{2,4},{3,5},{4,2},{5,3},{6,0},{7,1},{8,14},{9,15},{10,... | collective-permute-start | bytes 393224 | tf_op jit(solution)/shard_map/ppermute | solution.py:33
  30.4 7.8 %collective-permute-done.14.rest_5_ = bf16[3,9,64,128]{3,2,1,0:T(8,128)(2,1)S(1)} collective-permute-done((bf16[3,9,64,128]{3,2,1,0:T(8,128)(2,1)S(1)}, bf16[3,9,64,128]{3,2,1,0:T(8,128)(2,1)S(1)}, u32[]{:S(2)}, u32[]{:S(2)}) %collective-permute-start.14) | collective-permute-done | bytes 442400 | tf_op jit(solution)/shard_map/ppermute | solution.py:33
  38.2 8.3 %collective-permute-done.13.rest_4_ = bf16[3,9,64,128]{3,2,1,0:T(8,128)(2,1)S(1)} collective-permute-done((bf16[3,9,64,128]{3,2,1,0:T(8,128)(2,1)S(1)}, bf16[3,9,64,128]{3,2,1,0:T(8,128)(2,1)S(1)}, u32[]{:S(2)}, u32[]{:S(2)}) %collective-permute-start.13) | collective-permute-done | bytes 442400 | tf_op jit(solution)/shard_map/ppermute | solution.py:33
  51.2 6.6 %shard_map.205 = (f32[512,512]{1,0:T(8,128)S(1)}, f32[512,512]{1,0:T(8,128)S(1)}, bf16[9,4,2,64,512]{4,3,2,1,0:T(8,128)(2,1)S(1)}) custom-call(s32[2,8]{1,0:T(2,128)S(1)} %copy-done.9, f32[10,512]{1,0:T(8,128)S(1)} %copy-done.8, bf16[2,256,512]{2,1,0:T(8,128)(2,1)S(1)} %copy-done.1, bf16[9,64,512]{2,1,0:T(8,128)(2,1)S(1)} %get-tuple-element.121.own, ...), custom_call_target="tpu_custom_call" | custom-call | flops 1 | bytes 1 | tf_op jit(solution)/shard_map/pallas_call | solution.py:119
  57.9 2.8 %collective-permute-done.21.refs_8_ = bf16[3,128,512]{2,1,0:T(8,128)(2,1)S(1)} collective-permute-done((bf16[3,128,512]{2,1,0:T(8,128)(2,1)S(1)}, bf16[3,128,512]{2,1,0:T(8,128)(2,1)S(1)}, u32[]{:S(2)}, u32[]{:S(2)}) %collective-permute-start.21) | collective-permute-done | bytes 393248 | tf_op jit(solution)/shard_map/ppermute | solution.py:33
  60.6 7.5 %collective-permute-done.20.refs_7_ = bf16[3,128,512]{2,1,0:T(8,128)(2,1)S(1)} collective-permute-done((bf16[3,128,512]{2,1,0:T(8,128)(2,1)S(1)}, bf16[3,128,512]{2,1,0:T(8,128)(2,1)S(1)}, u32[]{:S(2)}, u32[]{:S(2)}) %collective-permute-start.20) | collective-permute-done | bytes 393248 | tf_op jit(solution)/shard_map/ppermute | solution.py:33
  72.3 9.7 %shard_map.206 = (bf16[512,512]{1,0:T(8,128)(2,1)}, bf16[512,512]{1,0:T(8,128)(2,1)S(1)}, bf16[512,2048]{1,0:T(8,128)(2,1)S(1)}, bf16[512,512]{1,0:T(8,128)(2,1)...) custom-call(f32[512,512]{1,0:T(8,128)S(1)} %get-tuple-element.129.refs_0_, ...), custom_call_target="tpu_custom_call" | custom-call | flops 1 | bytes 1 | tf_op jit(solution)/shard_map/pallas_call | solution.py:119
  82.0 3.3 %shard_map.207 = (bf16[4,4,128,512]{3,2,1,0:T(8,128)(2,1)S(1)}, bf16[4,4,128,512]{3,2,1,0:T(8,128)(2,1)S(1)}) custom-call(bf16[512,512]{1,0:T(8,128)(2,1)S(1)} %get-tuple-element.137.refs_0_, bf16[512,2048]{1,0:T(8,128)(2,1)S(1)} %get-tuple-element.138.refs_1_, bf16[512,512]{1,0:T(8,128)(2,1)S(1)} %get-tuple-element.139.refs_2_, ...), custom_call_target="tpu_custom_call" | custom-call | flops 1 | bytes 1 | tf_op jit(solution)/shard_map/pallas_call | solution.py:119
  85.3 2.7 %shard_map.208 = (f32[512,512]{1,0:T(8,128)S(1)}, bf16[512,512]{1,0:T(8,128)(2,1)S(1)}, bf16[592,128]{1,0:T(8,128)(2,1)S(1)}, bf16[848,128]{1,0:T(8,128)(2,1)S(1...) custom-call(f32[512,512]{1,0:T(8,128)S(1)} %get-tuple-element.142.refs_0_, bf16[512,512]{1,0:T(8,128)(2,1)S(1)} %bitcast.9, ...), custom_call_target="tpu_custom_call" | custom-call | flops 1 | bytes 1 | tf_op jit(solution)/shard_map/pallas_call | solution.py:119
  91.7 4.7 %collective-permute-done.26.refs_6_.refs_4_ = bf16[848,128]{1,0:T(8,128)(2,1)S(1)} collective-permute-done((bf16[848,128]{1,0:T(8,128)(2,1)S(1)}, bf16[848,128]{1,0:T(8,128)(2,1)S(1)}, u32[]{:S(2)}, u32[]{:S(2)}) %collective-permute-start.26) | collective-permute-done | bytes 217120 | tf_op jit(solution)/shard_map/ppermute | solution.py:33
  97.3 4.1 %collective-permute-done.28.refs_8_.refs_5_ = bf16[848,128]{1,0:T(8,128)(2,1)S(1)} collective-permute-done((bf16[848,128]{1,0:T(8,128)(2,1)S(1)}, bf16[848,128]{1,0:T(8,128)(2,1)S(1)}, u32[]{:S(2)}, u32[]{:S(2)}) %collective-permute-start.28) | collective-permute-done | bytes 217120 | tf_op jit(solution)/shard_map/ppermute | solution.py:33
  101.3 6.6 %shard_map.209 = (bf16[2384,128]{1,0:T(8,128)(2,1)S(1)}, bf16[2384,128]{1,0:T(8,128)(2,1)S(1)}) custom-call(s32[2,8]{1,0:T(2,128)S(1)} %copy-done.9, bf16[2,256,512]{2,1,0:T(8,128)(2,1)S(1)} %copy-done.1, bf16[2,256,512]{2,1,0:T(8,128)(2,1)S(1)} %collective-permute-done.2.rest_0_.refs_2_, bf16[2,256,512]{2,1,0:T(8,128)(2,1)S(1)} %collective-permute-done.3.refs_3_, ...), custom_call_target="tpu_custom_call" | custom-call | flops 1 | bytes 1 | tf_op jit(solution)/shard_map/pallas_call | solution.py:119
  112.7 3.2 %collective-permute-start.31 = (bf16[656,128]{1,0:T(8,128)(2,1)S(1)}, bf16[656,128]{1,0:T(8,128)(2,1)S(1)}, u32[]{:S(2)}, u32[]{:S(2)}) collective-permute-start(bf16[656,128]{1,0:T(8,128)(2,1)S(1)} %get-tuple-element.172), channel_id=1, source_target_pairs={{0,4},{1,5},{2,6},{3,7},{4,0},{5,1},{6,2},{7,3},{8,12},{9,13},{10,... | collective-permute-start | bytes 503816 | tf_op jit(solution)/shard_map/ppermute | solution.py:33
  115.9 6.0 %collective-permute-done.30.refs_1_ = bf16[656,128]{1,0:T(8,128)(2,1)S(1)} collective-permute-done((bf16[656,128]{1,0:T(8,128)(2,1)S(1)}, bf16[656,128]{1,0:T(8,128)(2,1)S(1)}, u32[]{:S(2)}, u32[]{:S(2)}) %collective-permute-start.30) | collective-permute-done | bytes 167968 | tf_op jit(solution)/shard_map/ppermute | solution.py:33
  123.3 7.4 %shard_map.211 = f32[512,512]{1,0:T(8,128)} custom-call(s32[2,8]{1,0:T(2,128)S(1)} %copy-done.9, bf16[512,512]{1,0:T(8,128)(2,1)S(1)} %get-tuple-element.166.refs_1_, f32[512,512]{1,0:T(8,128)S(1)} %get-tuple-element.167.refs_2_, bf16[9,4,2,64,512]{4,3,2,1,0:T(8,128)(2,1)S(1)} %get-tuple-element.168.refs_3_, ...), custom_call_target="tpu_custom_call" | custom-call | flops 1 | bytes 1 | tf_op jit(solution)/shard_map/pallas_call | solution.py:119
  130.9 1.6 collective-permute-start.39
  132.5 5.5 %collective-permute-done.37.refs_2_ = bf16[512,512]{1,0:T(8,128)(2,1)S(1)} collective-permute-done((bf16[512,512]{1,0:T(8,128)(2,1)S(1)}, bf16[512,512]{1,0:T(8,128)(2,1)S(1)}, u32[]{:S(2)}, u32[]{:S(2)}) %collective-permute-start.37) | collective-permute-done | bytes 524320 | tf_op jit(solution)/shard_map/ppermute | solution.py:33
  138.5 3.0 %collective-permute-start.41 = (bf16[128,512]{1,0:T(8,128)(2,1)S(1)}, bf16[128,512]{1,0:T(8,128)(2,1)S(1)}, u32[]{:S(2)}, u32[]{:S(2)}) collective-permute-start(bf16[128,512]{1,0:T(8,128)(2,1)S(1)} %get-tuple-element.185), channel_id=1, source_target_pairs={{0,4},{1,5},{2,6},{3,7},{4,0},{5,1},{6,2},{7,3},{8,12},{9,13},{10,... | collective-permute-start | bytes 393224 | tf_op jit(solution)/shard_map/ppermute | solution.py:33
  142.8 2.2 %collective-permute-done.40.refs_1_ = bf16[128,512]{1,0:T(8,128)(2,1)S(1)} collective-permute-done((bf16[128,512]{1,0:T(8,128)(2,1)S(1)}, bf16[128,512]{1,0:T(8,128)(2,1)S(1)}, u32[]{:S(2)}, u32[]{:S(2)}) %collective-permute-start.40) | collective-permute-done | bytes 131104 | tf_op jit(solution)/shard_map/ppermute | solution.py:33
  145.0 1.7 %collective-permute-done.41.refs_2_ = bf16[128,512]{1,0:T(8,128)(2,1)S(1)} collective-permute-done((bf16[128,512]{1,0:T(8,128)(2,1)S(1)}, bf16[128,512]{1,0:T(8,128)(2,1)S(1)}, u32[]{:S(2)}, u32[]{:S(2)}) %collective-permute-start.41) | collective-permute-done | bytes 131104 | tf_op jit(solution)/shard_map/ppermute | solution.py:33
  146.7 1.7 %collective-permute-done.42.refs_3_ = bf16[128,512]{1,0:T(8,128)(2,1)S(1)} collective-permute-done((bf16[128,512]{1,0:T(8,128)(2,1)S(1)}, bf16[128,512]{1,0:T(8,128)(2,1)S(1)}, u32[]{:S(2)}, u32[]{:S(2)}) %collective-permute-start.42) | collective-permute-done | bytes 131104 | tf_op jit(solution)/shard_map/ppermute | solution.py:33
  149.8 1.5 collective-permute-start.44
  156.5 2.4 %collective-permute-start.48 = (f32[8,128]{1,0:T(8,128)S(1)}, f32[8,128]{1,0:T(8,128)S(1)}, u32[]{:S(2)}, u32[]{:S(2)}) collective-permute-start(f32[8,128]{1,0:T(8,128)S(1)} %shard_map.216.refs_0_), channel_id=1, source_target_pairs={{0,6},{1,7},{2,4},{3,5},{4,2},{5,3},{6,0},{7,1},{8,14},{9,15},{10,... | collective-permute-start | bytes 12296 | tf_op jit(solution)/shard_map/ppermute | solution.py:33
  158.8 2.2 %collective-permute-start.47 = (f32[8,128]{1,0:T(8,128)S(1)}, f32[8,128]{1,0:T(8,128)S(1)}, u32[]{:S(2)}, u32[]{:S(2)}) collective-permute-start(f32[8,128]{1,0:T(8,128)S(1)} %shard_map.216.refs_0_), channel_id=1, source_target_pairs={{0,4},{1,5},{2,6},{3,7},{4,0},{5,1},{6,2},{7,3},{8,12},{9,13},{10,... | collective-permute-start | bytes 12296 | tf_op jit(solution)/shard_map/ppermute | solution.py:33
  165.9 4.7 %shard_map.218 = (f32[1,1]{1,0:T(1,128)}, f32[10,512]{1,0:T(8,128)}, f32[10,512]{1,0:T(8,128)}, f32[9,64,512]{2,1,0:T(8,128)}, f32[9,64,512]{2,1,0:T(8,128)}, /*...) custom-call(bf16[576,128]{1,0:T(8,128)(2,1)S(1)} %get-tuple-element., ...), custom_call_target="tpu_custom_call" | custom-call | flops 1 | bytes 1 | tf_op jit(solution)/shard_map/pallas_call | solution.py:119
  (108 shorter events, 38.7 us)
Async XLA Ops:
  2.4 17.6 %collective-permute-start.3 = (bf16[2,256,512]{2,1,0:T(8,128)(2,1)S(1)}, bf16[2,256,512]{2,1,0:T(8,128)(2,1)S(1)}, u32[]{:S(2)}, u32[]{:S(2)}) collective-permute-start(bf16[2,256,512]{2,1,0:T(8,128)(2,1)S(1)} %copy-done.1), channel_id=1, source_target_pairs={{0,16},{8,24},{16,0},{24,8},{1,17},{9,25},{17,1},{25,9},{2,18},{10... | collective-permute-start | bytes 1572872 | tf_op jit(solution)/shard_map/ppermute | solution.py:33
  5.4 14.6 %collective-permute-start.2 = (bf16[2,256,512]{2,1,0:T(8,128)(2,1)S(1)}, bf16[2,256,512]{2,1,0:T(8,128)(2,1)S(1)}, u32[]{:S(2)}, u32[]{:S(2)}) collective-permute-start(bf16[2,256,512]{2,1,0:T(8,128)(2,1)S(1)} %copy-done.1), channel_id=1, source_target_pairs={{0,8},{8,0},{16,24},{24,16},{1,9},{9,1},{17,25},{25,17},{2,10},{10... | collective-permute-start | bytes 1572872 | tf_op jit(solution)/shard_map/ppermute | solution.py:33
  8.5 11.5 %collective-permute-start.5 = (bf16[9,64,128]{2,1,0:T(8,128)(2,1)S(1)}, bf16[9,64,128]{2,1,0:T(8,128)(2,1)S(1)}, u32[]{:S(2)}, u32[]{:S(2)}) collective-permute-start(bf16[9,64,128]{2,1,0:T(8,128)(2,1)S(1)} %get-tuple-element.107), channel_id=1, source_target_pairs={{0,6},{1,7},{2,4},{3,5},{4,2},{5,3},{6,0},{7,1},{8,14},{9,15},{10,... | collective-permute-start | bytes 442376 | tf_op jit(solution)/shard_map/ppermute | solution.py:33
  11.0 12.6 %collective-permute-start.4 = (bf16[9,64,128]{2,1,0:T(8,128)(2,1)S(1)}, bf16[9,64,128]{2,1,0:T(8,128)(2,1)S(1)}, u32[]{:S(2)}, u32[]{:S(2)}) collective-permute-start(bf16[9,64,128]{2,1,0:T(8,128)(2,1)S(1)} %get-tuple-element.107), channel_id=1, source_target_pairs={{0,4},{1,5},{2,6},{3,7},{4,0},{5,1},{6,2},{7,3},{8,12},{9,13},{10,... | collective-permute-start | bytes 442376 | tf_op jit(solution)/shard_map/ppermute | solution.py:33
  12.3 7.7 %collective-permute-start.1 = (bf16[2,32,512]{2,1,0:T(8,128)(2,1)S(1)}, bf16[2,32,512]{2,1,0:T(8,128)(2,1)S(1)}, u32[]{:S(2)}, u32[]{:S(2)}) collective-permute-start(bf16[2,32,512]{2,1,0:T(8,128)(2,1)S(1)} %get-tuple-element.109), channel_id=1, source_target_pairs={{0,24},{8,16},{16,8},{24,0},{1,25},{9,17},{17,9},{25,1},{2,26},{10... | collective-permute-start | bytes 196616 | tf_op jit(solution)/shard_map/ppermute | solution.py:33
  24.3 13.9 %collective-permute-start.14 = (bf16[3,9,64,128]{3,2,1,0:T(8,128)(2,1)S(1)}, bf16[3,9,64,128]{3,2,1,0:T(8,128)(2,1)S(1)}, u32[]{:S(2)}, u32[]{:S(2)}) collective-permute-start(bf16[3,9,64,128]{3,2,1,0:T(8,128)(2,1)S(1)} %shard_map.203.rest_2_), channel_id=1, source_target_pairs={{0,24},{8,16},{16,8},{24,0},{1,25},{9,17},{17,9},{25,1},{2,26},{10... | collective-permute-start | bytes 1327112 | tf_op jit(solution)/shard_map/ppermute | solution.py:33
  24.8 21.7 %collective-permute-start.13 = (bf16[3,9,64,128]{3,2,1,0:T(8,128)(2,1)S(1)}, bf16[3,9,64,128]{3,2,1,0:T(8,128)(2,1)S(1)}, u32[]{:S(2)}, u32[]{:S(2)}) collective-permute-start(bf16[3,9,64,128]{3,2,1,0:T(8,128)(2,1)S(1)} %shard_map.203.rest_2_), channel_id=1, source_target_pairs={{0,16},{8,24},{16,0},{24,8},{1,17},{9,25},{17,1},{25,9},{2,18},{10... | collective-permute-start | bytes 1327112 | tf_op jit(solution)/shard_map/ppermute | solution.py:33
  26.3 20.2 %collective-permute-start.12 = (bf16[3,9,64,128]{3,2,1,0:T(8,128)(2,1)S(1)}, bf16[3,9,64,128]{3,2,1,0:T(8,128)(2,1)S(1)}, u32[]{:S(2)}, u32[]{:S(2)}) collective-permute-start(bf16[3,9,64,128]{3,2,1,0:T(8,128)(2,1)S(1)} %shard_map.203.rest_2_), channel_id=1, source_target_pairs={{0,8},{8,0},{16,24},{24,16},{1,9},{9,1},{17,25},{25,17},{2,10},{10... | collective-permute-start | bytes 1327112 | tf_op jit(solution)/shard_map/ppermute | solution.py:33
  27.8 18.7 %collective-permute-start.11 = (bf16[128,512]{1,0:T(8,128)(2,1)S(1)}, bf16[128,512]{1,0:T(8,128)(2,1)S(1)}, u32[]{:S(2)}, u32[]{:S(2)}) collective-permute-start(bf16[128,512]{1,0:T(8,128)(2,1)S(1)} %get-tuple-element.116), channel_id=1, source_target_pairs={{0,6},{1,7},{2,4},{3,5},{4,2},{5,3},{6,0},{7,1},{8,14},{9,15},{10,... | collective-permute-start | bytes 393224 | tf_op jit(solution)/shard_map/ppermute | solution.py:33
  30.4 16.1 %collective-permute-start.10 = (bf16[128,512]{1,0:T(8,128)(2,1)S(1)}, bf16[128,512]{1,0:T(8,128)(2,1)S(1)}, u32[]{:S(2)}, u32[]{:S(2)}) collective-permute-start(bf16[128,512]{1,0:T(8,128)(2,1)S(1)} %get-tuple-element.116), channel_id=1, source_target_pairs={{0,4},{1,5},{2,6},{3,7},{4,0},{5,1},{6,2},{7,3},{8,12},{9,13},{10,... | collective-permute-start | bytes 393224 | tf_op jit(solution)/shard_map/ppermute | solution.py:33
  38.2 8.3 %collective-permute-start.9 = (bf16[128,512]{1,0:T(8,128)(2,1)S(1)}, bf16[128,512]{1,0:T(8,128)(2,1)S(1)}, u32[]{:S(2)}, u32[]{:S(2)}) collective-permute-start(bf16[128,512]{1,0:T(8,128)(2,1)S(1)} %get-tuple-element.116), channel_id=1, source_target_pairs={{0,2},{1,3},{2,0},{3,1},{4,6},{5,7},{6,4},{7,5},{8,10},{9,11},{10,... | collective-permute-start | bytes 393224 | tf_op jit(solution)/shard_map/ppermute | solution.py:33
  47.7 12.9 %collective-permute-start.21 = (bf16[3,128,512]{2,1,0:T(8,128)(2,1)S(1)}, bf16[3,128,512]{2,1,0:T(8,128)(2,1)S(1)}, u32[]{:S(2)}, u32[]{:S(2)}) collective-permute-start(bf16[3,128,512]{2,1,0:T(8,128)(2,1)S(1)} %get-tuple-element.120.refs_5_), channel_id=1, source_target_pairs={{0,24},{8,16},{16,8},{24,0},{1,25},{9,17},{17,9},{25,1},{2,26},{10... | collective-permute-start | bytes 1179656 | tf_op jit(solution)/shard_map/ppermute | solution.py:33
  49.0 19.2 %collective-permute-start.20 = (bf16[3,128,512]{2,1,0:T(8,128)(2,1)S(1)}, bf16[3,128,512]{2,1,0:T(8,128)(2,1)S(1)}, u32[]{:S(2)}, u32[]{:S(2)}) collective-permute-start(bf16[3,128,512]{2,1,0:T(8,128)(2,1)S(1)} %get-tuple-element.120.refs_5_), channel_id=1, source_target_pairs={{0,16},{8,24},{16,0},{24,8},{1,17},{9,25},{17,1},{25,9},{2,18},{10... | collective-permute-start | bytes 1179656 | tf_op jit(solution)/shard_map/ppermute | solution.py:33
  50.4 17.7 %collective-permute-start.19 = (bf16[3,128,512]{2,1,0:T(8,128)(2,1)S(1)}, bf16[3,128,512]{2,1,0:T(8,128)(2,1)S(1)}, u32[]{:S(2)}, u32[]{:S(2)}) collective-permute-start(bf16[3,128,512]{2,1,0:T(8,128)(2,1)S(1)} %get-tuple-element.120.refs_5_), channel_id=1, source_target_pairs={{0,8},{8,0},{16,24},{24,16},{1,9},{9,1},{17,25},{25,17},{2,10},{10... | collective-permute-start | bytes 1179656 | tf_op jit(solution)/shard_map/ppermute | solution.py:33
  68.1 19.8 %collective-permute-start.25 = (bf16[2,256,512]{2,1,0:T(8,128)(2,1)S(1)}, bf16[2,256,512]{2,1,0:T(8,128)(2,1)S(1)}, u32[]{:S(2)}, u32[]{:S(2)}) collective-permute-start(bf16[2,256,512]{2,1,0:T(8,128)(2,1)S(1)} %copy-done.1), channel_id=1, source_target_pairs={{0,24},{8,16},{16,8},{24,0},{1,25},{9,17},{17,9},{25,1},{2,26},{10... | collective-permute-start | bytes 1572872 | tf_op jit(solution)/shard_map/ppermute | solution.py:33
  87.9 20.1 %collective-permute-start.35 = (bf16[4,4,128,512]{3,2,1,0:T(8,128)(2,1)S(1)}, bf16[4,4,128,512]{3,2,1,0:T(8,128)(2,1)S(1)}, u32[]{:S(2)}, u32[]{:S(2)}) collective-permute-start(bf16[4,4,128,512]{3,2,1,0:T(8,128)(2,1)S(1)} %get-tuple-element.176), channel_id=1, source_target_pairs={{0,1},{1,0},{2,3},{3,2},{4,5},{5,4},{6,7},{7,6},{8,9},{9,8},{10,11... | collective-permute-start | bytes 6291464 | tf_op jit(solution)/shard_map/ppermute | solution.py:33
  88.2 8.2 %collective-permute-start.26 = (bf16[848,128]{1,0:T(8,128)(2,1)S(1)}, bf16[848,128]{1,0:T(8,128)(2,1)S(1)}, u32[]{:S(2)}, u32[]{:S(2)}) collective-permute-start(bf16[848,128]{1,0:T(8,128)(2,1)S(1)} %get-tuple-element.159), channel_id=1, source_target_pairs={{0,8},{8,0},{16,24},{24,16},{1,9},{9,1},{17,25},{25,17},{2,10},{10... | collective-permute-start | bytes 651272 | tf_op jit(solution)/shard_map/ppermute | solution.py:33
  89.7 11.7 %collective-permute-start.28 = (bf16[848,128]{1,0:T(8,128)(2,1)S(1)}, bf16[848,128]{1,0:T(8,128)(2,1)S(1)}, u32[]{:S(2)}, u32[]{:S(2)}) collective-permute-start(bf16[848,128]{1,0:T(8,128)(2,1)S(1)} %get-tuple-element.162), channel_id=1, source_target_pairs={{0,24},{8,16},{16,8},{24,0},{1,25},{9,17},{17,9},{25,1},{2,26},{10... | collective-permute-start | bytes 651272 | tf_op jit(solution)/shard_map/ppermute | solution.py:33
  108.7 23.8 %collective-permute-start.36 = (bf16[512,512]{1,0:T(8,128)(2,1)S(1)}, bf16[512,512]{1,0:T(8,128)(2,1)S(1)}, u32[]{:S(2)}, u32[]{:S(2)}) collective-permute-start(bf16[512,512]{1,0:T(8,128)(2,1)S(1)} %get-tuple-element.178), channel_id=1, source_target_pairs={{0,8},{8,0},{16,24},{24,16},{1,9},{9,1},{17,25},{25,17},{2,10},{10... | collective-permute-start | bytes 1572872 | tf_op jit(solution)/shard_map/ppermute | solution.py:33
  109.6 28.4 %collective-permute-start.37 = (bf16[512,512]{1,0:T(8,128)(2,1)S(1)}, bf16[512,512]{1,0:T(8,128)(2,1)S(1)}, u32[]{:S(2)}, u32[]{:S(2)}) collective-permute-start(bf16[512,512]{1,0:T(8,128)(2,1)S(1)} %get-tuple-element.179), channel_id=1, source_target_pairs={{0,16},{8,24},{16,0},{24,8},{1,17},{9,25},{17,1},{25,9},{2,18},{10... | collective-permute-start | bytes 1572872 | tf_op jit(solution)/shard_map/ppermute | solution.py:33
  110.9 27.1 %collective-permute-start.38 = (bf16[512,512]{1,0:T(8,128)(2,1)S(1)}, bf16[512,512]{1,0:T(8,128)(2,1)S(1)}, u32[]{:S(2)}, u32[]{:S(2)}) collective-permute-start(bf16[512,512]{1,0:T(8,128)(2,1)S(1)} %get-tuple-element.180), channel_id=1, source_target_pairs={{0,24},{8,16},{16,8},{24,0},{1,25},{9,17},{17,9},{25,1},{2,26},{10... | collective-permute-start | bytes 1572872 | tf_op jit(solution)/shard_map/ppermute | solution.py:33
  112.6 9.3 %collective-permute-start.30 = (bf16[656,128]{1,0:T(8,128)(2,1)S(1)}, bf16[656,128]{1,0:T(8,128)(2,1)S(1)}, u32[]{:S(2)}, u32[]{:S(2)}) collective-permute-start(bf16[656,128]{1,0:T(8,128)(2,1)S(1)} %get-tuple-element.171), channel_id=1, source_target_pairs={{0,2},{1,3},{2,0},{3,1},{4,6},{5,7},{6,4},{7,5},{8,10},{9,11},{10,... | collective-permute-start | bytes 503816 | tf_op jit(solution)/shard_map/ppermute | solution.py:33
  112.7 18.0 %collective-permute-start.31 = (bf16[656,128]{1,0:T(8,128)(2,1)S(1)}, bf16[656,128]{1,0:T(8,128)(2,1)S(1)}, u32[]{:S(2)}, u32[]{:S(2)}) collective-permute-start(bf16[656,128]{1,0:T(8,128)(2,1)S(1)} %get-tuple-element.172), channel_id=1, source_target_pairs={{0,4},{1,5},{2,6},{3,7},{4,0},{5,1},{6,2},{7,3},{8,12},{9,13},{10,... | collective-permute-start | bytes 503816 | tf_op jit(solution)/shard_map/ppermute | solution.py:33
  121.9 8.8 %collective-permute-start.32 = (bf16[656,128]{1,0:T(8,128)(2,1)S(1)}, bf16[656,128]{1,0:T(8,128)(2,1)S(1)}, u32[]{:S(2)}, u32[]{:S(2)}) collective-permute-start(bf16[656,128]{1,0:T(8,128)(2,1)S(1)} %get-tuple-element.173), channel_id=1, source_target_pairs={{0,6},{1,7},{2,4},{3,5},{4,2},{5,3},{6,0},{7,1},{8,14},{9,15},{10,... | collective-permute-start | bytes 503816 | tf_op jit(solution)/shard_map/ppermute | solution.py:33
  130.9 11.8 %collective-permute-start.39 = (bf16[576,128]{1,0:T(8,128)(2,1)S(1)}, bf16[576,128]{1,0:T(8,128)(2,1)S(1)}, u32[]{:S(2)}, u32[]{:S(2)}) collective-permute-start(bf16[576,128]{1,0:T(8,128)(2,1)S(1)} %get-tuple-element.174.refs_0_), channel_id=1, source_target_pairs={{0,24},{8,16},{16,8},{24,0},{1,25},{9,17},{17,9},{25,1},{2,26},{10... | collective-permute-start | bytes 442376 | tf_op jit(solution)/shard_map/ppermute | solution.py:33
  138.3 6.7 %collective-permute-start.40 = (bf16[128,512]{1,0:T(8,128)(2,1)S(1)}, bf16[128,512]{1,0:T(8,128)(2,1)S(1)}, u32[]{:S(2)}, u32[]{:S(2)}) collective-permute-start(bf16[128,512]{1,0:T(8,128)(2,1)S(1)} %get-tuple-element.184), channel_id=1, source_target_pairs={{0,2},{1,3},{2,0},{3,1},{4,6},{5,7},{6,4},{7,5},{8,10},{9,11},{10,... | collective-permute-start | bytes 393224 | tf_op jit(solution)/shard_map/ppermute | solution.py:33
  138.5 8.2 %collective-permute-start.41 = (bf16[128,512]{1,0:T(8,128)(2,1)S(1)}, bf16[128,512]{1,0:T(8,128)(2,1)S(1)}, u32[]{:S(2)}, u32[]{:S(2)}) collective-permute-start(bf16[128,512]{1,0:T(8,128)(2,1)S(1)} %get-tuple-element.185), channel_id=1, source_target_pairs={{0,4},{1,5},{2,6},{3,7},{4,0},{5,1},{6,2},{7,3},{8,12},{9,13},{10,... | collective-permute-start | bytes 393224 | tf_op jit(solution)/shard_map/ppermute | solution.py:33
  141.6 6.9 %collective-permute-start.42 = (bf16[128,512]{1,0:T(8,128)(2,1)S(1)}, bf16[128,512]{1,0:T(8,128)(2,1)S(1)}, u32[]{:S(2)}, u32[]{:S(2)}) collective-permute-start(bf16[128,512]{1,0:T(8,128)(2,1)S(1)} %get-tuple-element.186), channel_id=1, source_target_pairs={{0,6},{1,7},{2,4},{3,5},{4,2},{5,3},{6,0},{7,1},{8,14},{9,15},{10,... | collective-permute-start | bytes 393224 | tf_op jit(solution)/shard_map/ppermute | solution.py:33
  148.6 6.2 %collective-permute-start.45 = (bf16[144,512]{1,0:T(8,128)(2,1)S(1)}, bf16[144,512]{1,0:T(8,128)(2,1)S(1)}, u32[]{:S(2)}, u32[]{:S(2)}) collective-permute-start(bf16[144,512]{1,0:T(8,128)(2,1)S(1)} %shard_map.215.refs_0_.refs_4_), channel_id=1, source_target_pairs={{0,24},{8,16},{16,8},{24,0},{1,25},{9,17},{17,9},{25,1},{2,26},{10... | collective-permute-start | bytes 442376 | tf_op jit(solution)/shard_map/ppermute | solution.py:33
  149.8 6.5 %collective-permute-start.44 = (bf16[144,512]{1,0:T(8,128)(2,1)S(1)}, bf16[144,512]{1,0:T(8,128)(2,1)S(1)}, u32[]{:S(2)}, u32[]{:S(2)}) collective-permute-start(bf16[144,512]{1,0:T(8,128)(2,1)S(1)} %shard_map.215.refs_0_.refs_4_), channel_id=1, source_target_pairs={{0,16},{8,24},{16,0},{24,8},{1,17},{9,25},{17,1},{25,9},{2,18},{10... | collective-permute-start | bytes 442376 | tf_op jit(solution)/shard_map/ppermute | solution.py:33
  152.1 12.6 %collective-permute-start.34 = (bf16[576,128]{1,0:T(8,128)(2,1)S(1)}, bf16[576,128]{1,0:T(8,128)(2,1)S(1)}, u32[]{:S(2)}, u32[]{:S(2)}) collective-permute-start(bf16[576,128]{1,0:T(8,128)(2,1)S(1)} %get-tuple-element.174.refs_0_), channel_id=1, source_target_pairs={{0,16},{8,24},{16,0},{24,8},{1,17},{9,25},{17,1},{25,9},{2,18},{10... | collective-permute-start | bytes 442376 | tf_op jit(solution)/shard_map/ppermute | solution.py:33
  153.4 11.3 %collective-permute-start.33 = (bf16[576,128]{1,0:T(8,128)(2,1)S(1)}, bf16[576,128]{1,0:T(8,128)(2,1)S(1)}, u32[]{:S(2)}, u32[]{:S(2)}) collective-permute-start(bf16[576,128]{1,0:T(8,128)(2,1)S(1)} %get-tuple-element.174.refs_0_), channel_id=1, source_target_pairs={{0,8},{8,0},{16,24},{24,16},{1,9},{9,1},{17,25},{25,17},{2,10},{10... | collective-permute-start | bytes 442376 | tf_op jit(solution)/shard_map/ppermute | solution.py:33
  (29 other events, 474.3 us)
